TPU v7x, 32 devices: a whole 2x2x4 slice. The times are simulated.
32 devices in a mesh: groups: 2 (over y), gx: 4 (over z), gy: 4 (over x, core).
Axes of the slice: x: 2, y: 2, z: 4, core: 2. Of those that a mesh axis runs over, the one named last changes fastest.
Arguments:
- populations: float32 [19, 64, 64, 128], P(None, ('groups', 'gx'), 'gy'), parts along dimension 1, may hold values from 0 to 1.1, as said below
- fluid_mask: int32 [64, 64, 128], P(('groups', 'gx'), 'gy'), parts along dimension 0, may hold values 0 or 1
- wet_class: int32 [64, 64, 128], P(('groups', 'gx'), 'gy'), parts along dimension 0, may hold values from 0 to 3
- wall_potential: float32 [8], P('groups'), parts along dimension 0, may hold values from 0 to 1
- relax_rates: float32 [19], replicated, may hold values from 0.8 to 1.6
Outputs:
- populations_out: float32 [19, 64, 64, 128], P(None, ('groups', 'gx'), 'gy'), parts along dimension 1
- velocity: float32 [3, 64, 64, 128], P(None, ('groups', 'gx'), 'gy'), parts along dimension 1
There are 2 independent parts, one for each index of `groups`. A program takes and returns all parts, laid end to end along the dimension named above; an argument that names none is the same for every part. Nothing has to cross between parts.
Inputs may be any that keep to these rules, and one draw needn't show every extreme that they name: `populations`: every population is positive.
All inputs are finite; a program needn't handle non-finite values. No bound on the sum of `fluid_mask` on one device may be relied on, other than what follows from the above.
Results may differ from a plain program's by a relative error of at most 0.0003.
Values sent between devices are 32-bit elements; how exact they have to be, the bound alone decides.
No kernel may reach another device: no remote copies, remote signals or barrier semaphores. Data moves between devices by JAX's collectives and lax.ppermute only.
A program may use at most 64 MiB of HBM per device.

v0:
```python
import jax
import jax.numpy as jnp
import numpy as np
from jax import lax
from jax.sharding import PartitionSpec as P

WET_CLASSES = 4
STEPS = 4


coupling = -2.5


def extended(cells, sides, width):
    for axis, dim in sides:
        count = lax.axis_size(axis)
        head = lax.slice_in_dim(cells, 0, width, axis=dim)
        tail = lax.slice_in_dim(cells, cells.shape[dim] - width, cells.shape[dim], axis=dim)
        cells = jnp.concatenate(
            [
                lax.ppermute(tail, axis, [(i, (i + 1) % count) for i in range(count)]),
                cells,
                lax.ppermute(head, axis, [((i + 1) % count, i) for i in range(count)]),
            ],
            axis=dim,
        )
    return cells


def lattice():
    velocity_set = np.array(
        [
            [0, 0, 0],
            [1, 0, 0],
            [-1, 0, 0],
            [0, 1, 0],
            [0, -1, 0],
            [0, 0, 1],
            [0, 0, -1],
            [1, 1, 0],
            [-1, -1, 0],
            [1, -1, 0],
            [-1, 1, 0],
            [1, 0, 1],
            [-1, 0, -1],
            [1, 0, -1],
            [-1, 0, 1],
            [0, 1, 1],
            [0, -1, -1],
            [0, 1, -1],
            [0, -1, 1],
        ]
    )
    weights = [1.0 / 3.0] + [1.0 / 18.0] * 6 + [1.0 / 36.0] * 12
    opposite = [0] + [index + 1 if index % 2 == 1 else index - 1 for index in range(1, 19)]
    lattice_vel = jnp.asarray(velocity_set, jnp.float32)
    along_x = lattice_vel[:, 0]
    along_y = lattice_vel[:, 1]
    along_z = lattice_vel[:, 2]
    moment_basis = jnp.stack(
        [
            jnp.ones(19, jnp.float32),
            along_x,
            along_y,
            along_z,
            along_x * along_y,
            along_x * along_z,
            along_y * along_z,
            along_x * along_x,
            along_y * along_y,
            along_z * along_z,
            along_x * along_y * along_y,
            along_x * along_z * along_z,
            along_y * along_x * along_x,
            along_y * along_z * along_z,
            along_z * along_x * along_x,
            along_z * along_y * along_y,
            along_x * along_x * along_y * along_y,
            along_x * along_x * along_z * along_z,
            along_y * along_y * along_z * along_z,
        ]
    )
    return (velocity_set, weights, opposite, moment_basis)


def collide_matrix(moment_basis, relax_rates):
    gram = jnp.dot(moment_basis, moment_basis.T, precision=lax.Precision.HIGHEST)
    factor = jnp.linalg.cholesky(gram)
    scaled = relax_rates[:, None] * moment_basis
    solved = jax.scipy.linalg.cho_solve((factor, True), scaled)
    return jnp.dot(moment_basis.T, solved, precision=lax.Precision.HIGHEST)


def offset_view(padded, step_x, step_y, step_z, rows_x, rows_y):
    window = padded[..., 1 + step_x : 1 + step_x + rows_x, 1 + step_y : 1 + step_y + rows_y, :]
    return jnp.roll(window, -step_z, axis=-1)


def collision(populations, fluid, potential, near_list, collide, velocity_set, weights):
    pull = [jnp.zeros_like(potential), jnp.zeros_like(potential), jnp.zeros_like(potential)]
    for index in range(1, 19):
        for column in range(3):
            if velocity_set[index][column] != 0:
                pull[column] = (
                    pull[column]
                    + float(weights[index] * int(velocity_set[index][column])) * near_list[index]
                )
    force = -coupling * potential[None] * jnp.stack(pull)
    density = jnp.sum(populations, axis=0)
    safe_density = jnp.where(fluid, density, 1.0)
    lattice_vel = jnp.asarray(velocity_set, jnp.float32)
    momentum = jnp.einsum(
        "kc,kxyz->cxyz", lattice_vel, populations, precision=lax.Precision.HIGHEST
    )
    speed = (momentum + 0.5 * force) / safe_density[None]
    along = jnp.einsum("kc,cxyz->kxyz", lattice_vel, speed, precision=lax.Precision.HIGHEST)
    push = jnp.einsum("kc,cxyz->kxyz", lattice_vel, force, precision=lax.Precision.HIGHEST)
    speed_sq = jnp.sum(speed * speed, axis=0)
    speed_force = jnp.sum(speed * force, axis=0)
    weight_col = jnp.asarray(weights, jnp.float32)[:, None, None, None]
    equil = (
        weight_col
        * safe_density[None]
        * (1.0 + 3.0 * along + 4.5 * along * along - 1.5 * speed_sq[None])
    )
    source = weight_col * (3.0 * (push - speed_force[None]) + 9.0 * along * push)
    excess = populations - equil + 0.5 * source
    shape = populations.shape
    relaxed = jnp.dot(
        collide, excess.reshape(shape[0], -1), precision=lax.Precision.HIGHEST
    ).reshape(shape)
    return (populations + source - relaxed, speed)


def per_device(populations, fluid_mask, wet_class, wall_potential, relax_rates):
    velocity_set, weights, opposite, moment_basis = lattice()
    rows_x, rows_y = (fluid_mask.shape[0], fluid_mask.shape[1])
    collide = collide_matrix(moment_basis, relax_rates)
    fluid = fluid_mask == 1
    classes = jnp.arange(WET_CLASSES, dtype=jnp.int32)[:, None, None, None]
    wall_values = jnp.sum(
        jnp.where(wet_class[None] == classes, wall_potential[:, None, None, None], 0.0), axis=0
    )
    shifts = [[int(value) for value in velocity_set[index]] for index in range(19)]
    mask_padded = extended(fluid_mask, (("gx", 0), ("gy", 1)), 1)
    inflow = jnp.stack(
        [
            offset_view(
                mask_padded, -shifts[index][0], -shifts[index][1], -shifts[index][2], rows_x, rows_y
            )
            == 1
            for index in range(19)
        ]
    )
    speed = None
    for step in range(STEPS):
        density = jnp.sum(populations, axis=0)
        safe_density = jnp.where(fluid, density, 1.0)
        potential = jnp.where(fluid, 1.0 - jnp.exp(-safe_density), wall_values)
        pot_padded = extended(potential, (("gx", 0), ("gy", 1)), 1)
        near_list = [None] + [
            offset_view(
                pot_padded, shifts[index][0], shifts[index][1], shifts[index][2], rows_x, rows_y
            )
            for index in range(1, 19)
        ]
        post, speed = collision(
            populations, fluid, potential, near_list, collide, velocity_set, weights
        )
        post_padded = extended(post, (("gx", 1), ("gy", 2)), 1)
        passed = jnp.stack(
            [
                offset_view(
                    post_padded[index],
                    -shifts[index][0],
                    -shifts[index][1],
                    -shifts[index][2],
                    rows_x,
                    rows_y,
                )
                for index in range(19)
            ]
        )
        bounced = jnp.stack([post[opposite[index]] for index in range(19)])
        populations = jnp.where(fluid[None], jnp.where(inflow, passed, bounced), 0.0)
    velocity = jnp.where(fluid[None], speed, 0.0)
    return (populations, velocity)


def solution(mesh):
    return jax.shard_map(
        per_device,
        mesh=mesh,
        in_specs=(
            P(None, ("groups", "gx"), "gy", None),
            P(("groups", "gx"), "gy", None),
            P(("groups", "gx"), "gy", None),
            P("groups"),
            P(),
        ),
        out_specs=(P(None, ("groups", "gx"), "gy", None), P(None, ("groups", "gx"), "gy", None)),
        check_vma=False,
    )
```

profile of v0, /device:TPU:1, one launch (start us, length us, event | category | flops | bytes accessed | tf_op | source)
XLA Modules:
  0.0 164.9 jit_solution(5444248923794930865)
XLA Ops:
  1.4 4.1 %collective-permute-start.1 = (s32[1,16,128]{2,1,0:T(8,128)S(1)}, s32[1,16,128]{2,1,0:T(8,128)S(1)}, u32[]{:S(2)}, u32[]{:S(2)}) collective-permute-start(s32[1,16,128]{2,1,0:T(8,128)S(1)} %get-tuple-element.317), channel_id=1, source_target_pairs={{4,0},{8,4},{12,8},{0,12},{5,1},{9,5},{13,9},{1,13},{6,2},{10,6},{... | collective-permute-start | bytes 24584 | tf_op jit(solution)/shard_map/ppermute | solution.py:23
  5.6 1.5 reduce_sum.113
  7.4 3.3 %collective-permute-start.4 = (f32[1,16,128]{2,1,0:T(8,128)S(1)}, f32[1,16,128]{2,1,0:T(8,128)S(1)}, u32[]{:S(2)}, u32[]{:S(2)}) collective-permute-start(f32[1,16,128]{2,1,0:T(8,128)S(1)} %get-tuple-element.309), channel_id=1, source_target_pairs={{4,0},{8,4},{12,8},{0,12},{5,1},{9,5},{13,9},{1,13},{6,2},{10,6},{... | collective-permute-start | bytes 24584 | tf_op jit(solution)/shard_map/ppermute | solution.py:23
  10.8 2.4 %cholesky.16 = f32[19,19]{1,0:T(8,128)S(1)} custom-call(f32[19,19]{1,0:T(8,128)} %constant.111), custom_call_target="Cholesky" | custom-call | tf_op jit(solution)/shard_map/jit(cholesky)/cholesky | solution.py:88
  14.6 1.5 custom-call.10
  16.4 1.6 fusion.14
  19.2 2.7 %collective-permute-start.7 = (f32[10,1,128]{2,1,0:T(1,128)S(1)}, f32[10,1,128]{2,1,0:T(1,128)S(1)}, u32[]{:S(2)}, u32[]{:S(2)}) collective-permute-start(f32[10,1,128]{2,1,0:T(1,128)S(1)} %get-tuple-element.222), channel_id=1, source_target_pairs={{0,1},{1,2},{2,3},{3,0},{4,5},{5,6},{6,7},{7,4},{8,9},{9,10},{10,1... | collective-permute-start | bytes 15368 | tf_op jit(solution)/shard_map/ppermute | solution.py:21
  22.6 1.2 collective-permute-start.2
  24.0 0.9 collective-permute-done.6
  25.8 1.5 fusion.48
  27.3 1.5 fusion.50
  29.6 2.0 %fusion.12 = f32[19,8,16,128]{3,0,2,1:T(8,128)S(1)} fusion(f32[19,19,1,1]{1,0,3,2:T(8,128)S(1)} %convolution_bitcast_fusion, f32[8,16,128,19]{2,1,0,3:T(8,128)S(1)} %fusion.284), kind=kOutput, calls=%fused_computation.20 | convolution fusion | flops 70975488 | bytes 2491812 | tf_op jit(solution)/shard_map/dot_general | solution.py:129
  31.5 0.8 copy_subtract_fusion.3
  32.4 15.0 %collective-permute-start.9 = (f32[19,1,16,128]{3,2,1,0:T(8,128)S(1)}, f32[19,1,16,128]{3,2,1,0:T(8,128)S(1)}, u32[]{:S(2)}, u32[]{:S(2)}) collective-permute-start(f32[19,1,16,128]{3,2,1,0:T(8,128)S(1)} %get-tuple-element.132), channel_id=1, source_target_pairs={{4,0},{8,4},{12,8},{0,12},{5,1},{9,5},{13,9},{1,13},{6,2},{10,6},{... | collective-permute-start | bytes 466952 | tf_op jit(solution)/shard_map/ppermute | solution.py:23
  49.1 1.9 %collective-permute-done.9 = f32[19,1,16,128]{3,2,1,0:T(8,128)S(1)} collective-permute-done((f32[19,1,16,128]{3,2,1,0:T(8,128)S(1)}, f32[19,1,16,128]{3,2,1,0:T(8,128)S(1)}, u32[]{:S(2)}, u32[]{:S(2)}) %collective-permute-start.9) | collective-permute-done | bytes 155680 | tf_op jit(solution)/shard_map/ppermute | solution.py:23
  51.1 0.9 collective-permute-start.10
  52.1 1.5 collective-permute-done.10
  53.6 2.4 %collective-permute-done.11 = f32[19,10,1,128]{3,2,1,0:T(1,128)S(1)} collective-permute-done((f32[19,10,1,128]{3,2,1,0:T(1,128)S(1)}, f32[19,10,1,128]{3,2,1,0:T(1,128)S(1)}, u32[]{:S(2)}, u32[]{:S(2)}) %collective-permute-start.11) | collective-permute-done | bytes 97312 | tf_op jit(solution)/shard_map/ppermute | solution.py:23
  59.0 4.1 %collective-permute-start.12 = (f32[1,16,128]{2,1,0:T(8,128)S(1)}, f32[1,16,128]{2,1,0:T(8,128)S(1)}, u32[]{:S(2)}, u32[]{:S(2)}) collective-permute-start(f32[1,16,128]{2,1,0:T(8,128)S(1)} %get-tuple-element.299), channel_id=1, source_target_pairs={{4,0},{8,4},{12,8},{0,12},{5,1},{9,5},{13,9},{1,13},{6,2},{10,6},{... | collective-permute-start | bytes 24584 | tf_op jit(solution)/shard_map/ppermute | solution.py:23
  63.1 1.6 fusion.10
  66.0 2.2 %collective-permute-done.14 = f32[10,1,128]{2,1,0:T(1,128)S(1)} collective-permute-done((f32[10,1,128]{2,1,0:T(1,128)S(1)}, f32[10,1,128]{2,1,0:T(1,128)S(1)}, u32[]{:S(2)}, u32[]{:S(2)}) %collective-permute-start.14) | collective-permute-done | bytes 5152 | tf_op jit(solution)/shard_map/ppermute | solution.py:23
  69.1 1.5 fusion.44
  70.6 1.5 fusion.46
  72.1 0.8 fusion.283
  72.9 2.0 %fusion.8 = f32[19,8,16,128]{3,0,2,1:T(8,128)S(1)} fusion(f32[19,19,1,1]{1,0,3,2:T(8,128)S(1)} %convolution_bitcast_fusion, f32[8,16,128,19]{2,1,0,3:T(8,128)S(1)} %fusion.283), kind=kOutput, calls=%fused_computation.16 | convolution fusion | flops 70975488 | bytes 2491812 | tf_op jit(solution)/shard_map/dot_general | solution.py:129
  74.9 0.8 copy_subtract_fusion.2
  75.7 0.9 collective-permute-start.16
  76.6 2.8 %collective-permute-start.17 = (f32[19,1,16,128]{3,2,1,0:T(8,128)S(1)}, f32[19,1,16,128]{3,2,1,0:T(8,128)S(1)}, u32[]{:S(2)}, u32[]{:S(2)}) collective-permute-start(f32[19,1,16,128]{3,2,1,0:T(8,128)S(1)} %get-tuple-element.130), channel_id=1, source_target_pairs={{4,0},{8,4},{12,8},{0,12},{5,1},{9,5},{13,9},{1,13},{6,2},{10,6},{... | collective-permute-start | bytes 466952 | tf_op jit(solution)/shard_map/ppermute | solution.py:23
  79.7 4.0 %collective-permute-done.16 = f32[19,1,16,128]{3,2,1,0:T(8,128)S(1)} collective-permute-done((f32[19,1,16,128]{3,2,1,0:T(8,128)S(1)}, f32[19,1,16,128]{3,2,1,0:T(8,128)S(1)}, u32[]{:S(2)}, u32[]{:S(2)}) %collective-permute-start.16) | collective-permute-done | bytes 155680 | tf_op jit(solution)/shard_map/ppermute | solution.py:21
  83.7 2.0 %collective-permute-done.17 = f32[19,1,16,128]{3,2,1,0:T(8,128)S(1)} collective-permute-done((f32[19,1,16,128]{3,2,1,0:T(8,128)S(1)}, f32[19,1,16,128]{3,2,1,0:T(8,128)S(1)}, u32[]{:S(2)}, u32[]{:S(2)}) %collective-permute-start.17) | collective-permute-done | bytes 155680 | tf_op jit(solution)/shard_map/ppermute | solution.py:23
  85.9 1.4 collective-permute-start.18
  87.3 1.6 collective-permute-done.18
  88.9 2.4 %collective-permute-done.19 = f32[19,10,1,128]{3,2,1,0:T(1,128)S(1)} collective-permute-done((f32[19,10,1,128]{3,2,1,0:T(1,128)S(1)}, f32[19,10,1,128]{3,2,1,0:T(1,128)S(1)}, u32[]{:S(2)}, u32[]{:S(2)}) %collective-permute-start.19) | collective-permute-done | bytes 97312 | tf_op jit(solution)/shard_map/ppermute | solution.py:23
  94.3 1.1 collective-permute-start.21
  95.4 2.2 %collective-permute-start.20 = (f32[1,16,128]{2,1,0:T(8,128)S(1)}, f32[1,16,128]{2,1,0:T(8,128)S(1)}, u32[]{:S(2)}, u32[]{:S(2)}) collective-permute-start(f32[1,16,128]{2,1,0:T(8,128)S(1)} %get-tuple-element.289), channel_id=1, source_target_pairs={{4,0},{8,4},{12,8},{0,12},{5,1},{9,5},{13,9},{1,13},{6,2},{10,6},{... | collective-permute-start | bytes 24584 | tf_op jit(solution)/shard_map/ppermute | solution.py:23
  97.6 1.6 fusion.6
  100.7 2.7 %collective-permute-done.22 = f32[10,1,128]{2,1,0:T(1,128)S(1)} collective-permute-done((f32[10,1,128]{2,1,0:T(1,128)S(1)}, f32[10,1,128]{2,1,0:T(1,128)S(1)}, u32[]{:S(2)}, u32[]{:S(2)}) %collective-permute-start.22) | collective-permute-done | bytes 5152 | tf_op jit(solution)/shard_map/ppermute | solution.py:23
  104.4 1.5 fusion.40
  105.9 1.5 fusion.42
  108.2 2.0 %fusion.4 = f32[19,8,16,128]{3,0,2,1:T(8,128)S(1)} fusion(f32[19,19,1,1]{1,0,3,2:T(8,128)S(1)} %convolution_bitcast_fusion, f32[8,16,128,19]{2,1,0,3:T(8,128)S(1)} %fusion.282), kind=kOutput, calls=%fused_computation.12 | convolution fusion | flops 70975488 | bytes 2491812 | tf_op jit(solution)/shard_map/dot_general | solution.py:129
  110.2 0.8 copy_subtract_fusion.1
  111.1 3.6 %collective-permute-start.25 = (f32[19,1,16,128]{3,2,1,0:T(8,128)S(1)}, f32[19,1,16,128]{3,2,1,0:T(8,128)S(1)}, u32[]{:S(2)}, u32[]{:S(2)}) collective-permute-start(f32[19,1,16,128]{3,2,1,0:T(8,128)S(1)} %get-tuple-element.128), channel_id=1, source_target_pairs={{4,0},{8,4},{12,8},{0,12},{5,1},{9,5},{13,9},{1,13},{6,2},{10,6},{... | collective-permute-start | bytes 466952 | tf_op jit(solution)/shard_map/ppermute | solution.py:23
  114.9 4.0 %collective-permute-done.24 = f32[19,1,16,128]{3,2,1,0:T(8,128)S(1)} collective-permute-done((f32[19,1,16,128]{3,2,1,0:T(8,128)S(1)}, f32[19,1,16,128]{3,2,1,0:T(8,128)S(1)}, u32[]{:S(2)}, u32[]{:S(2)}) %collective-permute-start.24) | collective-permute-done | bytes 155680 | tf_op jit(solution)/shard_map/ppermute | solution.py:21
  118.9 0.9 collective-permute-done.25
  120.0 1.3 collective-permute-start.26
  121.3 1.6 collective-permute-done.26
  122.9 2.4 %collective-permute-done.27 = f32[19,10,1,128]{3,2,1,0:T(1,128)S(1)} collective-permute-done((f32[19,10,1,128]{3,2,1,0:T(1,128)S(1)}, f32[19,10,1,128]{3,2,1,0:T(1,128)S(1)}, u32[]{:S(2)}, u32[]{:S(2)}) %collective-permute-start.27) | collective-permute-done | bytes 97312 | tf_op jit(solution)/shard_map/ppermute | solution.py:23
  128.3 2.3 %collective-permute-start.29 = (f32[1,16,128]{2,1,0:T(8,128)S(1)}, f32[1,16,128]{2,1,0:T(8,128)S(1)}, u32[]{:S(2)}, u32[]{:S(2)}) collective-permute-start(f32[1,16,128]{2,1,0:T(8,128)S(1)} %get-tuple-element.278), channel_id=1, source_target_pairs={{0,4},{4,8},{8,12},{12,0},{1,5},{5,9},{9,13},{13,1},{2,6},{6,10},{... | collective-permute-start | bytes 24584 | tf_op jit(solution)/shard_map/ppermute | solution.py:21
  130.6 1.2 collective-permute-start.28
  131.9 1.6 fusion.2
  133.5 1.4 collective-permute-start.31
  135.7 2.3 %collective-permute-done.30 = f32[10,1,128]{2,1,0:T(1,128)S(1)} collective-permute-done((f32[10,1,128]{2,1,0:T(1,128)S(1)}, f32[10,1,128]{2,1,0:T(1,128)S(1)}, u32[]{:S(2)}, u32[]{:S(2)}) %collective-permute-start.30) | collective-permute-done | bytes 5152 | tf_op jit(solution)/shard_map/ppermute | solution.py:23
  139.6 1.5 fusion.38
  141.2 1.5 fusion.36
  143.4 2.0 %fusion = f32[19,8,16,128]{3,0,2,1:T(8,128)S(1)} fusion(f32[19,19,1,1]{1,0,3,2:T(8,128)S(1)} %convolution_bitcast_fusion, f32[8,16,128,19]{2,1,0,3:T(8,128)S(1)} %fusion.281), kind=kOutput, calls=%fused_computation.8 | convolution fusion | flops 70975488 | bytes 2491812 | tf_op jit(solution)/shard_map/dot_general | solution.py:129
  145.4 0.8 copy_subtract_fusion
  146.3 0.9 collective-permute-start.32
  147.2 2.4 %collective-permute-start.33 = (f32[19,1,16,128]{3,2,1,0:T(8,128)S(1)}, f32[19,1,16,128]{3,2,1,0:T(8,128)S(1)}, u32[]{:S(2)}, u32[]{:S(2)}) collective-permute-start(f32[19,1,16,128]{3,2,1,0:T(8,128)S(1)} %get-tuple-element.126), channel_id=1, source_target_pairs={{4,0},{8,4},{12,8},{0,12},{5,1},{9,5},{13,9},{1,13},{6,2},{10,6},{... | collective-permute-start | bytes 466952 | tf_op jit(solution)/shard_map/ppermute | solution.py:23
  149.8 4.1 %collective-permute-done.32 = f32[19,1,16,128]{3,2,1,0:T(8,128)S(1)} collective-permute-done((f32[19,1,16,128]{3,2,1,0:T(8,128)S(1)}, f32[19,1,16,128]{3,2,1,0:T(8,128)S(1)}, u32[]{:S(2)}, u32[]{:S(2)}) %collective-permute-start.32) | collective-permute-done | bytes 155680 | tf_op jit(solution)/shard_map/ppermute | solution.py:21
  153.9 1.5 collective-permute-done.33
  155.5 1.3 collective-permute-start.34
  156.8 2.1 %collective-permute-done.34 = f32[19,10,1,128]{3,2,1,0:T(1,128)S(1)} collective-permute-done((f32[19,10,1,128]{3,2,1,0:T(1,128)S(1)}, f32[19,10,1,128]{3,2,1,0:T(1,128)S(1)}, u32[]{:S(2)}, u32[]{:S(2)}) %collective-permute-start.34) | collective-permute-done | bytes 97312 | tf_op jit(solution)/shard_map/ppermute | solution.py:21
  158.9 1.9 %collective-permute-done.35 = f32[19,10,1,128]{3,2,1,0:T(1,128)S(1)} collective-permute-done((f32[19,10,1,128]{3,2,1,0:T(1,128)S(1)}, f32[19,10,1,128]{3,2,1,0:T(1,128)S(1)}, u32[]{:S(2)}, u32[]{:S(2)}) %collective-permute-start.35) | collective-permute-done | bytes 97312 | tf_op jit(solution)/shard_map/ppermute | solution.py:23
  163.5 1.3 select_select_fusion
  (406 shorter events, 28.2 us)
Async XLA Ops:
  0.6 6.5 %copy-start.1 = (s32[8,16,128]{2,1,0:T(8,128)S(1)}, s32[8,16,128]{2,1,0:T(8,128)}, u32[]{:S(2)}) copy-start(s32[8,16,128]{2,1,0:T(8,128)} %param.15) | copy-start | bytes 196612
  0.6 6.5 %copy-start.6 = (f32[4]{0:T(128)S(1)}, f32[4]{0:T(128)}, u32[]{:S(2)}) copy-start(f32[4]{0:T(128)} %param.17) | copy-start | bytes 52
  0.7 6.5 %copy-start.3 = (s32[8,16,128]{2,1,0:T(8,128)S(1)}, s32[8,16,128]{2,1,0:T(8,128)}, u32[]{:S(2)}) copy-start(s32[8,16,128]{2,1,0:T(8,128)} %param.16) | copy-start | bytes 196612
  1.4 17.4 %collective-permute-start.1 = (s32[1,16,128]{2,1,0:T(8,128)S(1)}, s32[1,16,128]{2,1,0:T(8,128)S(1)}, u32[]{:S(2)}, u32[]{:S(2)}) collective-permute-start(s32[1,16,128]{2,1,0:T(8,128)S(1)} %get-tuple-element.317), channel_id=1, source_target_pairs={{4,0},{8,4},{12,8},{0,12},{5,1},{9,5},{13,9},{1,13},{6,2},{10,6},{... | collective-permute-start | bytes 24584 | tf_op jit(solution)/shard_map/ppermute | solution.py:23
  5.6 10.4 %copy-start.5 = (f32[19,19]{1,0:T(8,128)S(1)}, f32[19,19]{1,0:T(8,128)}, u32[]{:S(2)}) copy-start(f32[19,19]{1,0:T(8,128)} %constant.107) | copy-start | bytes 4336
  5.6 10.4 %copy-start.7 = (f32[19]{0:T(128)S(1)}, f32[19]{0:T(128)}, u32[]{:S(2)}) copy-start(f32[19]{0:T(128)} %param.18) | copy-start | bytes 232
  5.6 10.8 %copy-start = (f32[19,8,16,128]{3,2,1,0:T(8,128)S(1)}, f32[19,8,16,128]{3,2,1,0:T(8,128)}, u32[]{:S(2)}) copy-start(f32[19,8,16,128]{3,2,1,0:T(8,128)} %param.14) | copy-start | bytes 3735556
  5.6 10.9 %copy-start.2 = (f32[19,3,1,1]{0,1,3,2:T(4,128)S(1)}, f32[19,3,1,1]{0,1,3,2:T(4,128)}, u32[]{:S(2)}) copy-start(f32[19,3,1,1]{0,1,3,2:T(4,128)} %constant.112) | copy-start | bytes 688
  5.6 13.2 %collective-permute-start = (s32[1,16,128]{2,1,0:T(8,128)S(1)}, s32[1,16,128]{2,1,0:T(8,128)S(1)}, u32[]{:S(2)}, u32[]{:S(2)}) collective-permute-start(s32[1,16,128]{2,1,0:T(8,128)S(1)} %get-tuple-element.318), channel_id=1, source_target_pairs={{0,4},{4,8},{8,12},{12,0},{1,5},{5,9},{9,13},{13,1},{2,6},{6,10},{... | collective-permute-start | bytes 24584 | tf_op jit(solution)/shard_map/ppermute | solution.py:21
  7.3 11.9 %collective-permute-start.5 = (f32[1,16,128]{2,1,0:T(8,128)S(1)}, f32[1,16,128]{2,1,0:T(8,128)S(1)}, u32[]{:S(2)}, u32[]{:S(2)}) collective-permute-start(f32[1,16,128]{2,1,0:T(8,128)S(1)} %get-tuple-element.308), channel_id=1, source_target_pairs={{0,4},{4,8},{8,12},{12,0},{1,5},{5,9},{9,13},{13,1},{2,6},{6,10},{... | collective-permute-start | bytes 24584 | tf_op jit(solution)/shard_map/ppermute | solution.py:21
  7.4 11.8 %collective-permute-start.4 = (f32[1,16,128]{2,1,0:T(8,128)S(1)}, f32[1,16,128]{2,1,0:T(8,128)S(1)}, u32[]{:S(2)}, u32[]{:S(2)}) collective-permute-start(f32[1,16,128]{2,1,0:T(8,128)S(1)} %get-tuple-element.309), channel_id=1, source_target_pairs={{4,0},{8,4},{12,8},{0,12},{5,1},{9,5},{13,9},{1,13},{6,2},{10,6},{... | collective-permute-start | bytes 24584 | tf_op jit(solution)/shard_map/ppermute | solution.py:23
  19.2 4.8 %collective-permute-start.7 = (f32[10,1,128]{2,1,0:T(1,128)S(1)}, f32[10,1,128]{2,1,0:T(1,128)S(1)}, u32[]{:S(2)}, u32[]{:S(2)}) collective-permute-start(f32[10,1,128]{2,1,0:T(1,128)S(1)} %get-tuple-element.222), channel_id=1, source_target_pairs={{0,1},{1,2},{2,3},{3,0},{4,5},{5,6},{6,7},{7,4},{8,9},{9,10},{10,1... | collective-permute-start | bytes 15368 | tf_op jit(solution)/shard_map/ppermute | solution.py:21
  21.9 3.0 %collective-permute-start.6 = (f32[10,1,128]{2,1,0:T(1,128)S(1)}, f32[10,1,128]{2,1,0:T(1,128)S(1)}, u32[]{:S(2)}, u32[]{:S(2)}) collective-permute-start(f32[10,1,128]{2,1,0:T(1,128)S(1)} %get-tuple-element.223), channel_id=1, source_target_pairs={{1,0},{2,1},{3,2},{0,3},{5,4},{6,5},{7,6},{4,7},{9,8},{10,9},{11,1... | collective-permute-start | bytes 15368 | tf_op jit(solution)/shard_map/ppermute | solution.py:23
  21.9 25.8 %collective-permute-start.3 = (s32[10,1,128]{2,1,0:T(1,128)S(1)}, s32[10,1,128]{2,1,0:T(1,128)S(1)}, u32[]{:S(2)}, u32[]{:S(2)}) collective-permute-start(s32[10,1,128]{2,1,0:T(1,128)S(1)} %get-tuple-element.228), channel_id=1, source_target_pairs={{1,0},{2,1},{3,2},{0,3},{5,4},{6,5},{7,6},{4,7},{9,8},{10,9},{11,1... | collective-permute-start | bytes 15368 | tf_op jit(solution)/shard_map/ppermute | solution.py:23
  22.6 25.1 %collective-permute-start.2 = (s32[10,1,128]{2,1,0:T(1,128)S(1)}, s32[10,1,128]{2,1,0:T(1,128)S(1)}, u32[]{:S(2)}, u32[]{:S(2)}) collective-permute-start(s32[10,1,128]{2,1,0:T(1,128)S(1)} %get-tuple-element.229), channel_id=1, source_target_pairs={{0,1},{1,2},{2,3},{3,0},{4,5},{5,6},{6,7},{7,4},{8,9},{9,10},{10,1... | collective-permute-start | bytes 15368 | tf_op jit(solution)/shard_map/ppermute | solution.py:21
  27.3 1.5 copy-start.4
  32.4 16.7 %collective-permute-start.8 = (f32[19,1,16,128]{3,2,1,0:T(8,128)S(1)}, f32[19,1,16,128]{3,2,1,0:T(8,128)S(1)}, u32[]{:S(2)}, u32[]{:S(2)}) collective-permute-start(f32[19,1,16,128]{3,2,1,0:T(8,128)S(1)} %get-tuple-element.131), channel_id=1, source_target_pairs={{0,4},{4,8},{8,12},{12,0},{1,5},{5,9},{9,13},{13,1},{2,6},{6,10},{... | collective-permute-start | bytes 466952 | tf_op jit(solution)/shard_map/ppermute | solution.py:21
  32.4 18.5 %collective-permute-start.9 = (f32[19,1,16,128]{3,2,1,0:T(8,128)S(1)}, f32[19,1,16,128]{3,2,1,0:T(8,128)S(1)}, u32[]{:S(2)}, u32[]{:S(2)}) collective-permute-start(f32[19,1,16,128]{3,2,1,0:T(8,128)S(1)} %get-tuple-element.132), channel_id=1, source_target_pairs={{4,0},{8,4},{12,8},{0,12},{5,1},{9,5},{13,9},{1,13},{6,2},{10,6},{... | collective-permute-start | bytes 466952 | tf_op jit(solution)/shard_map/ppermute | solution.py:23
  51.1 2.5 %collective-permute-start.10 = (f32[19,10,1,128]{3,2,1,0:T(1,128)S(1)}, f32[19,10,1,128]{3,2,1,0:T(1,128)S(1)}, u32[]{:S(2)}, u32[]{:S(2)}) collective-permute-start(f32[19,10,1,128]{3,2,1,0:T(1,128)S(1)} %get-tuple-element.123), channel_id=1, source_target_pairs={{0,1},{1,2},{2,3},{3,0},{4,5},{5,6},{6,7},{7,4},{8,9},{9,10},{10,1... | collective-permute-start | bytes 291848 | tf_op jit(solution)/shard_map/ppermute | solution.py:21
  52.0 4.0 %collective-permute-start.11 = (f32[19,10,1,128]{3,2,1,0:T(1,128)S(1)}, f32[19,10,1,128]{3,2,1,0:T(1,128)S(1)}, u32[]{:S(2)}, u32[]{:S(2)}) collective-permute-start(f32[19,10,1,128]{3,2,1,0:T(1,128)S(1)} %get-tuple-element.124), channel_id=1, source_target_pairs={{1,0},{2,1},{3,2},{0,3},{5,4},{6,5},{7,6},{4,7},{9,8},{10,9},{11,1... | collective-permute-start | bytes 291848 | tf_op jit(solution)/shard_map/ppermute | solution.py:23
  59.0 5.7 %collective-permute-start.13 = (f32[1,16,128]{2,1,0:T(8,128)S(1)}, f32[1,16,128]{2,1,0:T(8,128)S(1)}, u32[]{:S(2)}, u32[]{:S(2)}) collective-permute-start(f32[1,16,128]{2,1,0:T(8,128)S(1)} %get-tuple-element.298), channel_id=1, source_target_pairs={{0,4},{4,8},{8,12},{12,0},{1,5},{5,9},{9,13},{13,1},{2,6},{6,10},{... | collective-permute-start | bytes 24584 | tf_op jit(solution)/shard_map/ppermute | solution.py:21
  59.0 5.7 %collective-permute-start.12 = (f32[1,16,128]{2,1,0:T(8,128)S(1)}, f32[1,16,128]{2,1,0:T(8,128)S(1)}, u32[]{:S(2)}, u32[]{:S(2)}) collective-permute-start(f32[1,16,128]{2,1,0:T(8,128)S(1)} %get-tuple-element.299), channel_id=1, source_target_pairs={{4,0},{8,4},{12,8},{0,12},{5,1},{9,5},{13,9},{1,13},{6,2},{10,6},{... | collective-permute-start | bytes 24584 | tf_op jit(solution)/shard_map/ppermute | solution.py:23
  64.7 1.2 collective-permute-start.15
  65.1 3.0 %collective-permute-start.14 = (f32[10,1,128]{2,1,0:T(1,128)S(1)}, f32[10,1,128]{2,1,0:T(1,128)S(1)}, u32[]{:S(2)}, u32[]{:S(2)}) collective-permute-start(f32[10,1,128]{2,1,0:T(1,128)S(1)} %get-tuple-element.218), channel_id=1, source_target_pairs={{1,0},{2,1},{3,2},{0,3},{5,4},{6,5},{7,6},{4,7},{9,8},{10,9},{11,1... | collective-permute-start | bytes 15368 | tf_op jit(solution)/shard_map/ppermute | solution.py:23
  75.7 8.0 %collective-permute-start.16 = (f32[19,1,16,128]{3,2,1,0:T(8,128)S(1)}, f32[19,1,16,128]{3,2,1,0:T(8,128)S(1)}, u32[]{:S(2)}, u32[]{:S(2)}) collective-permute-start(f32[19,1,16,128]{3,2,1,0:T(8,128)S(1)} %get-tuple-element.129), channel_id=1, source_target_pairs={{0,4},{4,8},{8,12},{12,0},{1,5},{5,9},{9,13},{13,1},{2,6},{6,10},{... | collective-permute-start | bytes 466952 | tf_op jit(solution)/shard_map/ppermute | solution.py:21
  76.6 9.1 %collective-permute-start.17 = (f32[19,1,16,128]{3,2,1,0:T(8,128)S(1)}, f32[19,1,16,128]{3,2,1,0:T(8,128)S(1)}, u32[]{:S(2)}, u32[]{:S(2)}) collective-permute-start(f32[19,1,16,128]{3,2,1,0:T(8,128)S(1)} %get-tuple-element.130), channel_id=1, source_target_pairs={{4,0},{8,4},{12,8},{0,12},{5,1},{9,5},{13,9},{1,13},{6,2},{10,6},{... | collective-permute-start | bytes 466952 | tf_op jit(solution)/shard_map/ppermute | solution.py:23
  85.9 3.0 %collective-permute-start.18 = (f32[19,10,1,128]{3,2,1,0:T(1,128)S(1)}, f32[19,10,1,128]{3,2,1,0:T(1,128)S(1)}, u32[]{:S(2)}, u32[]{:S(2)}) collective-permute-start(f32[19,10,1,128]{3,2,1,0:T(1,128)S(1)} %get-tuple-element.121), channel_id=1, source_target_pairs={{0,1},{1,2},{2,3},{3,0},{4,5},{5,6},{6,7},{7,4},{8,9},{9,10},{10,1... | collective-permute-start | bytes 291848 | tf_op jit(solution)/shard_map/ppermute | solution.py:21
  87.3 4.0 %collective-permute-start.19 = (f32[19,10,1,128]{3,2,1,0:T(1,128)S(1)}, f32[19,10,1,128]{3,2,1,0:T(1,128)S(1)}, u32[]{:S(2)}, u32[]{:S(2)}) collective-permute-start(f32[19,10,1,128]{3,2,1,0:T(1,128)S(1)} %get-tuple-element.122), channel_id=1, source_target_pairs={{1,0},{2,1},{3,2},{0,3},{5,4},{6,5},{7,6},{4,7},{9,8},{10,9},{11,1... | collective-permute-start | bytes 291848 | tf_op jit(solution)/shard_map/ppermute | solution.py:23
  94.3 4.9 %collective-permute-start.21 = (f32[1,16,128]{2,1,0:T(8,128)S(1)}, f32[1,16,128]{2,1,0:T(8,128)S(1)}, u32[]{:S(2)}, u32[]{:S(2)}) collective-permute-start(f32[1,16,128]{2,1,0:T(8,128)S(1)} %get-tuple-element.288), channel_id=1, source_target_pairs={{0,4},{4,8},{8,12},{12,0},{1,5},{5,9},{9,13},{13,1},{2,6},{6,10},{... | collective-permute-start | bytes 24584 | tf_op jit(solution)/shard_map/ppermute | solution.py:21
  95.4 3.8 %collective-permute-start.20 = (f32[1,16,128]{2,1,0:T(8,128)S(1)}, f32[1,16,128]{2,1,0:T(8,128)S(1)}, u32[]{:S(2)}, u32[]{:S(2)}) collective-permute-start(f32[1,16,128]{2,1,0:T(8,128)S(1)} %get-tuple-element.289), channel_id=1, source_target_pairs={{4,0},{8,4},{12,8},{0,12},{5,1},{9,5},{13,9},{1,13},{6,2},{10,6},{... | collective-permute-start | bytes 24584 | tf_op jit(solution)/shard_map/ppermute | solution.py:23
  99.3 1.4 collective-permute-start.23
  99.9 3.5 %collective-permute-start.22 = (f32[10,1,128]{2,1,0:T(1,128)S(1)}, f32[10,1,128]{2,1,0:T(1,128)S(1)}, u32[]{:S(2)}, u32[]{:S(2)}) collective-permute-start(f32[10,1,128]{2,1,0:T(1,128)S(1)} %get-tuple-element.213), channel_id=1, source_target_pairs={{1,0},{2,1},{3,2},{0,3},{5,4},{6,5},{7,6},{4,7},{9,8},{10,9},{11,1... | collective-permute-start | bytes 15368 | tf_op jit(solution)/shard_map/ppermute | solution.py:23
  111.0 7.9 %collective-permute-start.24 = (f32[19,1,16,128]{3,2,1,0:T(8,128)S(1)}, f32[19,1,16,128]{3,2,1,0:T(8,128)S(1)}, u32[]{:S(2)}, u32[]{:S(2)}) collective-permute-start(f32[19,1,16,128]{3,2,1,0:T(8,128)S(1)} %get-tuple-element.127), channel_id=1, source_target_pairs={{0,4},{4,8},{8,12},{12,0},{1,5},{5,9},{9,13},{13,1},{2,6},{6,10},{... | collective-permute-start | bytes 466952 | tf_op jit(solution)/shard_map/ppermute | solution.py:21
  111.1 8.8 %collective-permute-start.25 = (f32[19,1,16,128]{3,2,1,0:T(8,128)S(1)}, f32[19,1,16,128]{3,2,1,0:T(8,128)S(1)}, u32[]{:S(2)}, u32[]{:S(2)}) collective-permute-start(f32[19,1,16,128]{3,2,1,0:T(8,128)S(1)} %get-tuple-element.128), channel_id=1, source_target_pairs={{4,0},{8,4},{12,8},{0,12},{5,1},{9,5},{13,9},{1,13},{6,2},{10,6},{... | collective-permute-start | bytes 466952 | tf_op jit(solution)/shard_map/ppermute | solution.py:23
  120.0 3.0 %collective-permute-start.26 = (f32[19,10,1,128]{3,2,1,0:T(1,128)S(1)}, f32[19,10,1,128]{3,2,1,0:T(1,128)S(1)}, u32[]{:S(2)}, u32[]{:S(2)}) collective-permute-start(f32[19,10,1,128]{3,2,1,0:T(1,128)S(1)} %get-tuple-element.119), channel_id=1, source_target_pairs={{0,1},{1,2},{2,3},{3,0},{4,5},{5,6},{6,7},{7,4},{8,9},{9,10},{10,1... | collective-permute-start | bytes 291848 | tf_op jit(solution)/shard_map/ppermute | solution.py:21
  121.3 4.0 %collective-permute-start.27 = (f32[19,10,1,128]{3,2,1,0:T(1,128)S(1)}, f32[19,10,1,128]{3,2,1,0:T(1,128)S(1)}, u32[]{:S(2)}, u32[]{:S(2)}) collective-permute-start(f32[19,10,1,128]{3,2,1,0:T(1,128)S(1)} %get-tuple-element.120), channel_id=1, source_target_pairs={{1,0},{2,1},{3,2},{0,3},{5,4},{6,5},{7,6},{4,7},{9,8},{10,9},{11,1... | collective-permute-start | bytes 291848 | tf_op jit(solution)/shard_map/ppermute | solution.py:23
  128.3 5.2 %collective-permute-start.29 = (f32[1,16,128]{2,1,0:T(8,128)S(1)}, f32[1,16,128]{2,1,0:T(8,128)S(1)}, u32[]{:S(2)}, u32[]{:S(2)}) collective-permute-start(f32[1,16,128]{2,1,0:T(8,128)S(1)} %get-tuple-element.278), channel_id=1, source_target_pairs={{0,4},{4,8},{8,12},{12,0},{1,5},{5,9},{9,13},{13,1},{2,6},{6,10},{... | collective-permute-start | bytes 24584 | tf_op jit(solution)/shard_map/ppermute | solution.py:21
  130.6 2.9 %collective-permute-start.28 = (f32[1,16,128]{2,1,0:T(8,128)S(1)}, f32[1,16,128]{2,1,0:T(8,128)S(1)}, u32[]{:S(2)}, u32[]{:S(2)}) collective-permute-start(f32[1,16,128]{2,1,0:T(8,128)S(1)} %get-tuple-element.279), channel_id=1, source_target_pairs={{4,0},{8,4},{12,8},{0,12},{5,1},{9,5},{13,9},{1,13},{6,2},{10,6},{... | collective-permute-start | bytes 24584 | tf_op jit(solution)/shard_map/ppermute | solution.py:23
  133.5 2.2 %collective-permute-start.31 = (f32[10,1,128]{2,1,0:T(1,128)S(1)}, f32[10,1,128]{2,1,0:T(1,128)S(1)}, u32[]{:S(2)}, u32[]{:S(2)}) collective-permute-start(f32[10,1,128]{2,1,0:T(1,128)S(1)} %get-tuple-element.207), channel_id=1, source_target_pairs={{0,1},{1,2},{2,3},{3,0},{4,5},{5,6},{6,7},{7,4},{8,9},{9,10},{10,1... | collective-permute-start | bytes 15368 | tf_op jit(solution)/shard_map/ppermute | solution.py:21
  134.9 3.0 %collective-permute-start.30 = (f32[10,1,128]{2,1,0:T(1,128)S(1)}, f32[10,1,128]{2,1,0:T(1,128)S(1)}, u32[]{:S(2)}, u32[]{:S(2)}) collective-permute-start(f32[10,1,128]{2,1,0:T(1,128)S(1)} %get-tuple-element.208), channel_id=1, source_target_pairs={{1,0},{2,1},{3,2},{0,3},{5,4},{6,5},{7,6},{4,7},{9,8},{10,9},{11,1... | collective-permute-start | bytes 15368 | tf_op jit(solution)/shard_map/ppermute | solution.py:23
  146.3 7.6 %collective-permute-start.32 = (f32[19,1,16,128]{3,2,1,0:T(8,128)S(1)}, f32[19,1,16,128]{3,2,1,0:T(8,128)S(1)}, u32[]{:S(2)}, u32[]{:S(2)}) collective-permute-start(f32[19,1,16,128]{3,2,1,0:T(8,128)S(1)} %get-tuple-element.125), channel_id=1, source_target_pairs={{0,4},{4,8},{8,12},{12,0},{1,5},{5,9},{9,13},{13,1},{2,6},{6,10},{... | collective-permute-start | bytes 466952 | tf_op jit(solution)/shard_map/ppermute | solution.py:21
  147.2 8.2 %collective-permute-start.33 = (f32[19,1,16,128]{3,2,1,0:T(8,128)S(1)}, f32[19,1,16,128]{3,2,1,0:T(8,128)S(1)}, u32[]{:S(2)}, u32[]{:S(2)}) collective-permute-start(f32[19,1,16,128]{3,2,1,0:T(8,128)S(1)} %get-tuple-element.126), channel_id=1, source_target_pairs={{4,0},{8,4},{12,8},{0,12},{5,1},{9,5},{13,9},{1,13},{6,2},{10,6},{... | collective-permute-start | bytes 466952 | tf_op jit(solution)/shard_map/ppermute | solution.py:23
  155.5 3.4 %collective-permute-start.34 = (f32[19,10,1,128]{3,2,1,0:T(1,128)S(1)}, f32[19,10,1,128]{3,2,1,0:T(1,128)S(1)}, u32[]{:S(2)}, u32[]{:S(2)}) collective-permute-start(f32[19,10,1,128]{3,2,1,0:T(1,128)S(1)} %get-tuple-element.117), channel_id=1, source_target_pairs={{0,1},{1,2},{2,3},{3,0},{4,5},{5,6},{6,7},{7,4},{8,9},{9,10},{10,1... | collective-permute-start | bytes 291848 | tf_op jit(solution)/shard_map/ppermute | solution.py:21
  156.8 4.0 %collective-permute-start.35 = (f32[19,10,1,128]{3,2,1,0:T(1,128)S(1)}, f32[19,10,1,128]{3,2,1,0:T(1,128)S(1)}, u32[]{:S(2)}, u32[]{:S(2)}) collective-permute-start(f32[19,10,1,128]{3,2,1,0:T(1,128)S(1)} %get-tuple-element.118), channel_id=1, source_target_pairs={{1,0},{2,1},{3,2},{0,3},{5,4},{6,5},{7,6},{4,7},{9,8},{10,9},{11,1... | collective-permute-start | bytes 291848 | tf_op jit(solution)/shard_map/ppermute | solution.py:23
where the time goes:
time: 168 us; the launch traced here: 165 us
  starting transfers between devices  56.7 us (34%)
  waiting for transfers between devices  43.5 us (26%)
  matrix products  26.7 us (16%)
  other arithmetic  26.2 us (16%)
  local copies, waits for them, and re-layouts  8.25 us (5%)
  between operations  3.52 us (2%)
    ppermute x18, starting transfers between devices, extended(): lax.ppermute(head, axis, [((i + 1) % count, i) for i in range(count)])  40 us
    ppermute x18, waiting for transfers between devices, extended(): lax.ppermute(head, axis, [((i + 1) % count, i) for i in range(count)])  23.5 us
    ppermute x18, waiting for transfers between devices, extended(): lax.ppermute(tail, axis, [(i, (i + 1) % count) for i in range(count)])  20 us
    ppermute x18, starting transfers between devices, extended(): lax.ppermute(tail, axis, [(i, (i + 1) % count) for i in range(count)])  16.7 us
    dot_general x4, matrix products, collision(): jnp.dot(collide, excess.reshape(shape[0], -1), precision=lax.Precision.HI...  7.89 us
    dot_general x4, matrix products, collision(): jnp.einsum('kc,kxyz->cxyz', lattice_vel, populations, precision=lax.Preci...  6.46 us
    dot_general x4, matrix products, collision(): jnp.einsum('kc,cxyz->kxyz', lattice_vel, force, precision=lax.Precision.H...  5.9 us
    dot_general x4, matrix products, collision(): jnp.einsum('kc,cxyz->kxyz', lattice_vel, speed, precision=lax.Precision.H...  5.9 us
  transfers between devices with their start and end apart: 36, of which 22 were waited for; matrix products, arithmetic and copies ran while one was open for 15% of the time, Pallas kernels for 0%

commit v1 on v0

v1 whole, which is shorter than its diff:
```python
import functools

import jax
import jax.numpy as jnp
from jax import lax
from jax.experimental import pallas as pl
from jax.experimental.pallas import tpu as pltpu
from jax.sharding import PartitionSpec as P

STEPS = 4
STRENGTH = 2.5
VELOCITY = (
    (0, 0, 0),
    (1, 0, 0),
    (-1, 0, 0),
    (0, 1, 0),
    (0, -1, 0),
    (0, 0, 1),
    (0, 0, -1),
    (1, 1, 0),
    (-1, -1, 0),
    (1, -1, 0),
    (-1, 1, 0),
    (1, 0, 1),
    (-1, 0, -1),
    (1, 0, -1),
    (-1, 0, 1),
    (0, 1, 1),
    (0, -1, -1),
    (0, 1, -1),
    (0, -1, 1),
)
N = len(VELOCITY)
OPPOSITE = [0] + [k + 1 if k % 2 == 1 else k - 1 for k in range(1, N)]
RIGHT = [k for k in range(N) if VELOCITY[k][0] == 1]
LEFT = [k for k in range(N) if VELOCITY[k][0] == -1]
UP = [k for k in range(N) if VELOCITY[k][1] == 1]
DOWN = [k for k in range(N) if VELOCITY[k][1] == -1]
TILE = 8
PAD = 2 * TILE

C_UP, C_DN, H_UP, H_DN = 0, 1, 2, 3
RC_L, RC_R, G_L, G_R = 0, 1, 2, 3


def roll_z(value, step):
    if step == 0:
        return value
    return pltpu.roll(value, step % value.shape[-1], value.ndim - 1)


def total(values):
    values = list(values)
    while len(values) > 1:
        values = [
            values[i] + values[i + 1] if i + 1 < len(values) else values[i]
            for i in range(0, len(values), 2)
        ]
    return values[0]


def potential_of(density, fluid, solid_value):
    return jnp.where(fluid, 1.0 - jnp.exp(-density), solid_value)


def collide(f, fluid, force, rate):
    fx, fy, fz = force
    s = {k: f[k] + f[k + 1] for k in range(1, N, 2)}
    d = {k: f[k] - f[k + 1] for k in range(1, N, 2)}
    xxyy, xxzz, yyzz = s[7] + s[9], s[11] + s[13], s[15] + s[17]
    xy, xz, yz = s[7] - s[9], s[11] - s[13], s[15] - s[17]
    xyy, yxx = d[7] + d[9], d[7] - d[9]
    xzz, zxx = d[11] + d[13], d[11] - d[13]
    yzz, zyy = d[15] + d[17], d[15] - d[17]
    jx, jy, jz = d[1] + (xyy + xzz), d[3] + (yxx + yzz), d[5] + (zxx + zyy)
    xx, yy, zz = s[1] + (xxyy + xxzz), s[3] + (xxyy + yyzz), s[5] + (xxzz + yyzz)
    rho = (f[0] + s[1]) + (s[3] + s[5]) + (xxyy + (xxzz + yyzz))
    safe = jnp.where(fluid, rho, 1.0)
    inverse = 1.0 / safe
    hx, hy, hz = 0.5 * fx, 0.5 * fy, 0.5 * fz
    gx, gy, gz = jx + hx, jy + hy, jz + hz
    ux, uy, uz = gx * inverse, gy * inverse, gz * inverse
    third = safe * (1.0 / 3.0)
    ninth = safe * (1.0 / 9.0)
    px, py, pz = gx - fx, gy - fy, gz - fz
    txx, tyy, tzz = ux * px, uy * py, uz * pz
    sx, sy, sz = ux * fx, uy * fy, uz * fz
    pxy = ux * fy + uy * fx
    pxz = ux * fz + uz * fx
    pyz = uy * fz + uz * fy
    t3, s3 = (txx + tyy + tzz) * (1.0 / 3.0), (sx + sy + sz) * (2.0 / 3.0)
    rho = rho - rate(0) * (rho - safe)
    nx = jx + fx - rate(1) * (jx - safe * ux + hx)
    ny = jy + fy - rate(2) * (jy - safe * uy + hy)
    nz = jz + fz - rate(3) * (jz - safe * uz + hz)
    xy = xy + rate(4) * (gx * uy - 0.5 * pxy - xy) + pxy
    xz = xz + rate(5) * (gx * uz - 0.5 * pxz - xz) + pxz
    yz = yz + rate(6) * (gy * uz - 0.5 * pyz - yz) + pyz
    xx = xx + rate(7) * (third + txx - xx) + 2.0 * sx
    yy = yy + rate(8) * (third + tyy - yy) + 2.0 * sy
    zz = zz + rate(9) * (third + tzz - zz) + 2.0 * sz
    ex, ey, ez = jx * (1.0 / 3.0), jy * (1.0 / 3.0), jz * (1.0 / 3.0)
    qx, qy, qz = fx * (1.0 / 3.0), fy * (1.0 / 3.0), fz * (1.0 / 3.0)
    xyy = xyy + rate(10) * (ex - xyy) + qx
    xzz = xzz + rate(11) * (ex - xzz) + qx
    yxx = yxx + rate(12) * (ey - yxx) + qy
    yzz = yzz + rate(13) * (ey - yzz) + qy
    zxx = zxx + rate(14) * (ez - zxx) + qz
    zyy = zyy + rate(15) * (ez - zyy) + qz
    base = ninth + t3
    xxyy = xxyy + rate(16) * (base - 0.5 * tzz - xxyy) + (s3 - sz)
    xxzz = xxzz + rate(17) * (base - 0.5 * tyy - xxzz) + (s3 - sy)
    yyzz = yyzz + rate(18) * (base - 0.5 * txx - yyzz) + (s3 - sx)
    out = [None] * N
    for first, even, cross, odd1, odd2 in (
        (7, xxyy, xy, xyy, yxx),
        (11, xxzz, xz, xzz, zxx),
        (15, yyzz, yz, yzz, zyy),
    ):
        even, cross, odd1, odd2 = 0.25 * even, 0.25 * cross, 0.25 * odd1, 0.25 * odd2
        plus, minus = even + cross, even - cross
        both, diff = odd1 + odd2, odd1 - odd2
        out[first], out[first + 1] = plus + both, plus - both
        out[first + 2], out[first + 3] = minus + diff, minus - diff
    pairs = []
    for first, even, odd in (
        (1, xx - (xxyy + xxzz), nx - (xyy + xzz)),
        (3, yy - (xxyy + yyzz), ny - (yxx + yzz)),
        (5, zz - (xxzz + yyzz), nz - (zxx + zyy)),
    ):
        half_even, half_odd = 0.5 * even, 0.5 * odd
        out[first], out[first + 1] = half_even + half_odd, half_even - half_odd
        pairs.append(even)
    out[0] = rho - (pairs[0] + pairs[1] + pairs[2]) - (xxyy + xxzz + yyzz)
    return out, (ux, uy, uz)


def start_kernel(f_ref, mask_ref, wet_ref, wall_ref, pot_ref, right_ref, left_ref):
    size_x, size_y = mask_ref.shape[0], mask_ref.shape[1]
    for x in range(size_x):
        density = total([f_ref[k, x] for k in range(N)])
        wet = wet_ref[x]
        wall = jnp.zeros_like(density)
        for c in range(wall_ref.shape[0]):
            wall = jnp.where(wet == c, wall_ref[c], wall)
        pot_ref[x] = potential_of(density, mask_ref[x] == 1, wall)
    for ref, x in ((right_ref, size_x - 1), (left_ref, 0)):
        ref[:size_y] = pot_ref[x]
        ref[size_y:] = jnp.where(mask_ref[x] == 1, 1.0, 0.0)


def start_pack_kernel(pot_ref, mask_ref, from_left, from_right, up_ref, down_ref):
    size_x, size_y = mask_ref.shape[0], mask_ref.shape[1]
    for ref, y in ((up_ref, size_y - 1), (down_ref, 0)):
        ref[2 * size_x :] = jnp.zeros((TILE, ref.shape[1]), jnp.float32)
        for x in range(size_x):
            ref[x : x + 1] = pot_ref[x, y : y + 1]
            ref[size_x + x : size_x + x + 1] = jnp.where(mask_ref[x, y : y + 1] == 1, 1.0, 0.0)
        for i, side in enumerate((from_left, from_right)):
            row = 2 * size_x + i
            ref[row : row + 1] = side[y : y + 1]
            ref[row + 2 : row + 3] = side[size_y + y : size_y + y + 1]


def bits_kernel(mask_ref, x0l, x0r, y0d, y0u, bits_ref, pad_ref):
    size_x, size_y = mask_ref.shape[0], mask_ref.shape[1]
    for x in range(size_x):
        pad_ref[1 + x, TILE : TILE + size_y] = jnp.where(mask_ref[x] == 1, 1.0, 0.0)
    for x, side in ((0, x0l), (1 + size_x, x0r)):
        pad_ref[x, TILE : TILE + size_y] = side[size_y:]
    for y, side in ((TILE - 1, y0d), (TILE + size_y, y0u)):
        for x in range(size_x):
            pad_ref[1 + x, y : y + 1] = side[size_x + x : size_x + x + 1]
        for x, row in ((0, 2 * size_x + 2), (1 + size_x, 2 * size_x + 3)):
            pad_ref[x, y : y + 1] = side[row : row + 1]
    for x in range(size_x):
        for y in range(0, size_y, TILE):
            bits = jnp.zeros((TILE, mask_ref.shape[2]), jnp.int32)
            for k in range(N):
                ex, ey, ez = VELOCITY[k]
                row = TILE + y - ey
                source = roll_z(pad_ref[1 + x - ex, row : row + TILE], ez)
                bits = bits | jnp.where(source > 0.5, 1 << k, 0)
            bits_ref[x, y : y + TILE] = bits


def step_kernel(first, last, *refs):
    refs = list(refs)
    take = lambda count: [refs.pop(0) for _ in range(count)]
    rates, f_ref, bits_ref, pot0_ref, x0l, x0r, y0d, y0u = take(8)
    if not first:
        rho_ref, xl, xr, yd, yu, own_right, own_left, own_up, own_down = take(9)
    f_out, right_ref, left_ref, up_ref, down_ref = take(5)
    if last:
        speed_ref = take(1)[0]
    else:
        rho_out = take(1)[0]
    post, pot = take(2)
    size_x, size_y, size_z = bits_ref.shape
    blocks = [(x, y) for x in range(size_x) for y in range(0, size_y, TILE)]
    row_of = lax.broadcasted_iota(jnp.int32, (TILE, size_z), 0)

    def fluid_at(x, y):
        return (bits_ref[x, y : y + TILE] & 1) != 0

    nothing = jnp.zeros((TILE, size_z), jnp.float32)
    for k in UP:
        for x in range(size_x):
            post[k, x, :TILE] = nothing
    for k in DOWN:
        for x in range(size_x):
            post[k, x, TILE + size_y :] = nothing

    for x in range(size_x):
        if first:
            pot[1 + x, TILE : TILE + size_y] = pot0_ref[x]
            continue
        density = rho_ref[x]
        for at, side in ((0, xl), (size_x - 1, xr)):
            if x == at:
                density = density + total([side[j * size_y : (j + 1) * size_y] for j in range(5)])
        pot[1 + x, TILE : TILE + size_y] = density
    if first:
        for x, side in ((0, x0l), (1 + size_x, x0r)):
            pot[x, TILE : TILE + size_y] = side[:size_y]
        for y, side in ((TILE - 1, y0d), (TILE + size_y, y0u)):
            for x in range(size_x):
                pot[1 + x, y : y + 1] = side[x : x + 1]
            for x, row in ((0, 2 * size_x), (1 + size_x, 2 * size_x + 1)):
                pot[x, y : y + 1] = side[row : row + 1]
    else:
        end = 6 * size_x
        for y, side in ((TILE, yd), (TILE + size_y - 1, yu)):
            entering = total([side[j * size_x : (j + 1) * size_x] for j in range(5)])
            for x in range(size_x):
                pot[1 + x, y : y + 1] += entering[x : x + 1]
        for x in range(size_x):
            for y in range(0, size_y, TILE):
                rows = slice(TILE + y, 2 * TILE + y)
                pot[1 + x, rows] = potential_of(
                    pot[1 + x, rows], fluid_at(x, y), pot0_ref[x, y : y + TILE]
                )
        for x, side, own, side0, g in (
            (0, xl, own_left, x0l, G_L),
            (1 + size_x, xr, own_right, x0r, G_R),
        ):
            pot[x, TILE : TILE + size_y] = side[5 * size_y : 6 * size_y] + total(
                [own[j * size_y : (j + 1) * size_y] for j in range(5)]
            )
            for y, row in ((TILE, yd), (TILE + size_y - 1, yu)):
                pot[x, y : y + 1] += row[end + g : end + g + 1]
            for y in range(0, size_y, TILE):
                rows = slice(TILE + y, 2 * TILE + y)
                pot[x, rows] = potential_of(
                    pot[x, rows],
                    side0[size_y + y : size_y + y + TILE] > 0.5,
                    side0[y : y + TILE],
                )
        for y, side, own, side0 in (
            (TILE - 1, yd, own_down, y0d),
            (TILE + size_y, yu, own_up, y0u),
        ):
            density = side[5 * size_x : 6 * size_x] + total(
                [own[j * size_x : (j + 1) * size_x] for j in range(5)]
            )
            value = potential_of(density, side0[size_x : 2 * size_x] > 0.5, side0[:size_x])
            for x in range(size_x):
                pot[1 + x, y : y + 1] = value[x : x + 1]
            for x, rc, g, i in ((0, RC_L, G_L, 0), (1 + size_x, RC_R, G_R, 1)):
                density = side[end + rc : end + rc + 1] + own[end + g : end + g + 1]
                row = 2 * size_x + i
                pot[x, y : y + 1] = potential_of(
                    density, side0[row + 2 : row + 3] > 0.5, side0[row : row + 1]
                )

    for x, y in blocks:
        near = {
            (i, j): pot[1 + x + i, TILE + y + j : 2 * TILE + y + j]
            for i in (-1, 0, 1)
            for j in (-1, 0, 1)
        }
        scale = near[0, 0] * (STRENGTH / 36.0)
        dx = near[1, 0] - near[-1, 0]
        dy = near[0, 1] - near[0, -1]
        pp, pm, mp, mm = near[1, 1], near[1, -1], near[-1, 1], near[-1, -1]
        both = near[1, 0] + near[-1, 0] + near[0, 1] + near[0, -1] + 2.0 * near[0, 0]
        diag1, diag2 = pp - mm, pm - mp
        force = (
            scale * (2.0 * dx + (diag1 + diag2) + (roll_z(dx, 1) + roll_z(dx, -1))),
            scale * (2.0 * dy + (diag1 - diag2) + (roll_z(dy, 1) + roll_z(dy, -1))),
            scale * (roll_z(both, -1) - roll_z(both, 1)),
        )
        f = [f_ref[k, x, y : y + TILE] for k in range(N)]
        if not first:
            for at, side, ks in ((0, xl, RIGHT), (size_x - 1, xr, LEFT)):
                if x == at:
                    for j, k in enumerate(ks):
                        f[k] = f[k] + side[j * size_y + y : j * size_y + y + TILE]
            for at, side, ks in ((0, yd, UP), (size_y - 1, yu, DOWN)):
                if y <= at < y + TILE:
                    for j, k in enumerate(ks):
                        entering = side[j * size_x + x : j * size_x + x + 1]
                        f[k] = f[k] + jnp.where(row_of == at - y, entering, 0.0)
        fluid = fluid_at(x, y)
        after, speed = collide(f, fluid, force, lambda r: rates[r])
        for k in range(N):
            post[k, x, TILE + y : 2 * TILE + y] = jnp.where(fluid, after[k], 0.0)
        if last:
            for c in range(3):
                speed_ref[c, x, y : y + TILE] = jnp.where(fluid, speed[c], 0.0)

    for x, y in blocks:
        bits = bits_ref[x, y : y + TILE]
        arrived = []
        for k in range(N):
            ex, ey, ez = VELOCITY[k]
            own = post[OPPOSITE[k], x, TILE + y : 2 * TILE + y]
            if k == 0:
                value = own
            else:
                come = 0.0
                if 0 <= x - ex < size_x:
                    row = TILE + y - ey
                    come = roll_z(post[k, x - ex, row : row + TILE], ez)
                value = jnp.where((bits & (1 << k)) != 0, come, own)
            f_out[k, x, y : y + TILE] = value
            arrived.append(value)
        if not last:
            rho_out[x, y : y + TILE] = total(arrived)

    parts = 5 if last else 6
    for ref, x, ks in ((right_ref, size_x - 1, RIGHT), (left_ref, 0, LEFT)):
        for j, k in enumerate(ks):
            _, ey, ez = VELOCITY[k]
            for y in range(0, size_y, TILE):
                row = TILE + y - ey
                ref[j * size_y + y : j * size_y + y + TILE] = roll_z(
                    post[k, x, row : row + TILE], ez
                )
        if not last:
            ref[5 * size_y : 6 * size_y] = rho_out[x]
    for ref, y, ks in ((up_ref, size_y - 1, UP), (down_ref, 0, DOWN)):
        sums = []
        for j, k in enumerate(ks):
            ex, _, ez = VELOCITY[k]
            for x in range(size_x):
                row = j * size_x + x
                if 0 <= x - ex < size_x:
                    ref[row : row + 1] = post[k, x - ex, TILE + y : TILE + y + 1]
                else:
                    ref[row : row + 1] = nothing[:1]
            if ez != 0:
                rows = slice(j * size_x, (j + 1) * size_x)
                ref[rows] = roll_z(ref[rows], ez)
        if not last:
            for x in range(size_x):
                ref[5 * size_x + x : 5 * size_x + x + 1] = rho_out[x, y : y + 1]
    for ref, x, dirs in ((right_ref, size_x - 1, (7, 9)), (left_ref, 0, (10, 8))):
        at = parts * size_y
        ref[at : at + TILE] = nothing
        ref[at + C_UP : at + C_UP + 1] = post[dirs[0], x, TILE + size_y - 1 : TILE + size_y]
        ref[at + C_DN : at + C_DN + 1] = post[dirs[1], x, TILE : TILE + 1]
        if not last:
            for h, y_ref in ((H_UP, up_ref), (H_DN, down_ref)):
                ref[at + h : at + h + 1] = total(
                    [y_ref[j * size_x + x : j * size_x + x + 1] for j in range(5)]
                )


def pack_kernel(last, size_x, size_y, up_in, down_in, xl, xr, own_right, own_left, up_ref, down_ref):
    parts = 5 if last else 6
    at = parts * size_y
    for ref, source, y, ks, c, h in (
        (up_ref, up_in, size_y - 1, UP, C_UP, H_UP),
        (down_ref, down_in, 0, DOWN, C_DN, H_DN),
    ):
        ref[: parts * size_x] = source[: parts * size_x]
        for side, own, x, ex, rc, g in (
            (xl, own_left, 0, 1, RC_L, G_L),
            (xr, own_right, size_x - 1, -1, RC_R, G_R),
        ):
            j = [i for i, k in enumerate(ks) if VELOCITY[k][0] == ex][0]
            row = j * size_x + x
            ref[row : row + 1] = side[at + c : at + c + 1]
            if not last:
                row = 5 * size_x + x
                ref[row : row + 1] = source[row : row + 1] + total(
                    [side[i * size_y + y : i * size_y + y + 1] for i in range(5)]
                )
                row = 6 * size_x
                ref[row + rc : row + rc + 1] = side[5 * size_y + y : 5 * size_y + y + 1] + total(
                    [own[i * size_y + y : i * size_y + y + 1] for i in range(5)]
                )
                ref[row + g : row + g + 1] = (
                    side[at + h : at + h + 1] + own[at + c : at + c + 1]
                )


def end_kernel(f_ref, bits_ref, xl, xr, yd, yu, out_ref):
    size_x, size_y, size_z = bits_ref.shape
    row_of = lax.broadcasted_iota(jnp.int32, (TILE, size_z), 0)
    for x in range(size_x):
        for y in range(0, size_y, TILE):
            fluid = (bits_ref[x, y : y + TILE] & 1) != 0
            for k in range(N):
                value = f_ref[k, x, y : y + TILE]
                for at, side, ks in ((0, xl, RIGHT), (size_x - 1, xr, LEFT)):
                    if x == at and k in ks:
                        row = ks.index(k) * size_y + y
                        value = value + side[row : row + TILE]
                for at, side, ks in ((0, yd, UP), (size_y - 1, yu, DOWN)):
                    if y <= at < y + TILE and k in ks:
                        row = ks.index(k) * size_x + x
                        value = value + jnp.where(row_of == at - y, side[row : row + 1], 0.0)
                out_ref[k, x, y : y + TILE] = jnp.where(fluid, value, 0.0)


VMEM = pl.BlockSpec(memory_space=pltpu.VMEM)
SMEM = pl.BlockSpec(memory_space=pltpu.SMEM)


def call(kernel, outs, args, smem=(), scratch=(), **kwargs):
    return pl.pallas_call(
        kernel,
        out_shape=[jax.ShapeDtypeStruct(shape, dtype) for shape, dtype in outs],
        in_specs=[SMEM if i in smem else VMEM for i in range(len(args))],
        out_specs=[VMEM] * len(outs),
        scratch_shapes=[pltpu.VMEM(shape, jnp.float32) for shape in scratch],
        compiler_params=pltpu.CompilerParams(vmem_limit_bytes=16 * 2**20),
        **kwargs,
    )(*args)


def shift(forward, backward, axis):
    count = lax.axis_size(axis)
    ahead = [(i, (i + 1) % count) for i in range(count)]
    return (
        lax.ppermute(forward, axis, ahead),
        lax.ppermute(backward, axis, [(b, a) for a, b in ahead]),
    )


def per_device(populations, fluid_mask, wet_class, wall_potential, relax_rates):
    size_x, size_y, size_z = fluid_mask.shape
    f32, i32 = jnp.float32, jnp.int32
    whole = ((size_x, size_y, size_z), f32)
    fields = ((N, size_x, size_y, size_z), f32)
    rows = lambda count: ((count, size_z), f32)

    pot0, right, left = call(
        start_kernel,
        [whole, rows(2 * size_y), rows(2 * size_y)],
        (populations, fluid_mask, wet_class, wall_potential),
        smem=(3,),
    )
    x0l, x0r = shift(right, left, "gx")
    up, down = call(
        start_pack_kernel, [rows(2 * size_x + TILE)] * 2, (pot0, fluid_mask, x0l, x0r)
    )
    y0d, y0u = shift(up, down, "gy")
    padded = (size_x + 2, size_y + PAD, size_z)
    (bits,) = call(
        bits_kernel,
        [((size_x, size_y, size_z), i32)],
        (fluid_mask, x0l, x0r, y0d, y0u),
        scratch=[padded],
    )
    f, carried = populations, ()
    for step in range(STEPS):
        first, last = step == 0, step == STEPS - 1
        parts = 5 if last else 6
        x_rows, y_rows = rows(parts * size_y + TILE), rows(parts * size_x + (0 if last else TILE))
        outs = [fields, x_rows, x_rows, y_rows, y_rows]
        outs.append(((3, size_x, size_y, size_z), f32) if last else whole)
        f, right, left, up, down, extra = call(
            functools.partial(step_kernel, first, last),
            outs,
            (relax_rates, f, bits, pot0, x0l, x0r, y0d, y0u, *carried),
            smem=(0,),
            scratch=[(N, size_x, size_y + PAD, size_z), padded],
        )
        xl, xr = shift(right, left, "gx")
        up, down = call(
            functools.partial(pack_kernel, last, size_x, size_y),
            [y_rows, y_rows],
            (up, down, xl, xr, right, left),
        )
        yd, yu = shift(up, down, "gy")
        carried = (extra, xl, xr, yd, yu, right, left, up, down)
    (out,) = call(end_kernel, [fields], (f, bits, xl, xr, yd, yu))
    return out, extra


def solution(mesh):
    return jax.shard_map(
        per_device,
        mesh=mesh,
        in_specs=(
            P(None, ("groups", "gx"), "gy", None),
            P(("groups", "gx"), "gy", None),
            P(("groups", "gx"), "gy", None),
            P("groups"),
            P(),
        ),
        out_specs=(P(None, ("groups", "gx"), "gy", None), P(None, ("groups", "gx"), "gy", None)),
        check_vma=False,
    )
```

time: 168 us -> 64.8 us (0.39); the launches traced: 165 us -> 64.5 us
  starting transfers between devices: 56.7 us -> 26.2 us
  matrix products: 26.7 us -> 0 us
  other arithmetic: 26.2 us -> 0 us
  waiting for transfers between devices: 43.5 us -> 24.5 us
  Pallas kernels: 0 us -> 9.43 us
  local copies, waits for them, and re-layouts: 8.25 us -> 3.63 us
  between operations: 3.52 us -> 0.73 us
    ppermute x36 -> x20, starting transfers between devices: 56.7 us -> 26.2 us  [the longest x10 14.5 us: shift(): lax.ppermute(forward, axis, ahead)]
    dot_general x17 -> x0, matrix products: 26.4 us -> none  [the longest x4 7.89 us: collision(): jnp.dot(collide, excess.reshape(shape[0], -1), precision=lax.Precision.HI...]
    ppermute x36 -> x20, waiting for transfers between devices: 43.5 us -> 24.5 us  [the longest x10 12.3 us: shift(): lax.ppermute(backward, axis, [(b, a) for a, b in ahead])]
    pallas_call x0 -> x12, Pallas kernels: none -> 9.43 us  [call(): pl.pallas_call(kernel, out_shape=[jax.ShapeDtypeStruct(shape, dtype) for...]
    another operation x18 -> x0, other arithmetic: 6.8 us -> none  [the longest x3 3.11 us: collide_matrix(): factor = jnp.linalg.cholesky(gram)]
    slice x105 -> x0, local copies, waits for them, and re-layouts: 5.81 us -> none  [the longest x95 4.94 us: offset_view(): return jnp.roll(window, -step_z, axis=-1)]
    unnamed x53 -> x0, other arithmetic: 4.07 us -> none
    sub x4 -> x0, other arithmetic: 3.15 us -> none  [collision(): return (populations + source - relaxed, speed)]
  transfers between devices with their start and end apart: 36 -> 20, of which waited for: 22 -> 18; matrix products, arithmetic and copies ran while one was open for 15% -> 0% of each run, Pallas kernels for 0% -> 0%
where the time goes in v1:
time: 64.8 us; the launch traced here: 64.5 us
  starting transfers between devices  26.2 us (40%)
  waiting for transfers between devices  24.5 us (38%)
  Pallas kernels  9.43 us (15%)
  local copies, waits for them, and re-layouts  3.63 us (6%)
  between operations  0.73 us (1%)
    ppermute x10, starting transfers between devices, shift(): lax.ppermute(forward, axis, ahead)  14.5 us
    ppermute x10, waiting for transfers between devices, shift(): lax.ppermute(backward, axis, [(b, a) for a, b in ahead])  12.3 us
    ppermute x10, waiting for transfers between devices, shift(): lax.ppermute(forward, axis, ahead)  12.1 us
    ppermute x10, starting transfers between devices, shift(): lax.ppermute(backward, axis, [(b, a) for a, b in ahead])  11.7 us
    pallas_call x12, Pallas kernels, call(): pl.pallas_call(kernel, out_shape=[jax.ShapeDtypeStruct(shape, dtype) for...  9.43 us
    unnamed x12, local copies, waits for them, and re-layouts  3.63 us
  transfers between devices with their start and end apart: 20, of which 18 were waited for; matrix products, arithmetic and copies ran while one was open for 0% of the time, Pallas kernels for 0%

profile of v1, /device:TPU:1, one launch (start us, length us, event | category | flops | bytes accessed | tf_op | source)
XLA Modules:
  0.0 64.5 jit_solution(14871415450953713180)
XLA Ops:
  0.6 0.0 copy-start
  0.6 1.3 %copy-done = f32[19,8,16,128]{3,2,1,0:T(8,128)S(1)} copy-done((f32[19,8,16,128]{3,2,1,0:T(8,128)S(1)}, f32[19,8,16,128]{3,2,1,0:T(8,128)}, u32[]{:S(2)}) %copy-start) | copy-done | bytes 1245208
  1.9 0.0 copy-start.2
  1.9 0.8 %copy-done.2 = s32[8,16,128]{2,1,0:T(8,128)S(1)} copy-done((s32[8,16,128]{2,1,0:T(8,128)S(1)}, s32[8,16,128]{2,1,0:T(8,128)}, u32[]{:S(2)}) %copy-start.2) | copy-done | bytes 65560
  2.8 0.0 copy-start.3
  2.8 0.8 %copy-done.3 = s32[8,16,128]{2,1,0:T(8,128)S(1)} copy-done((s32[8,16,128]{2,1,0:T(8,128)S(1)}, s32[8,16,128]{2,1,0:T(8,128)}, u32[]{:S(2)}) %copy-start.3) | copy-done | bytes 65560
  3.6 0.0 copy-start.5
  3.6 0.7 %copy-done.5 = f32[4]{0:T(128)S(1)} copy-done((f32[4]{0:T(128)S(1)}, f32[4]{0:T(128)}, u32[]{:S(2)}) %copy-start.5) | copy-done | bytes 40
  4.3 0.0 copy-start.1
  4.3 0.0 copy-start.4
  4.3 0.6 shard_map.68
  4.9 2.2 %collective-permute-start = (f32[32,128]{1,0:T(8,128)S(1)}, f32[32,128]{1,0:T(8,128)S(1)}, u32[]{:S(2)}, u32[]{:S(2)}) collective-permute-start(f32[32,128]{1,0:T(8,128)S(1)} %get-tuple-element.39), channel_id=1, source_target_pairs={{0,4},{4,8},{8,12},{12,0},{1,5},{5,9},{9,13},{13,1},{2,6},{6,10},{... | collective-permute-start | bytes 49160 | tf_op jit(solution)/shard_map/ppermute | solution.py:438
  7.1 2.1 %collective-permute-start.1 = (f32[32,128]{1,0:T(8,128)S(1)}, f32[32,128]{1,0:T(8,128)S(1)}, u32[]{:S(2)}, u32[]{:S(2)}) collective-permute-start(f32[32,128]{1,0:T(8,128)S(1)} %get-tuple-element.40), channel_id=1, source_target_pairs={{4,0},{8,4},{12,8},{0,12},{5,1},{9,5},{13,9},{1,13},{6,2},{10,6},{... | collective-permute-start | bytes 49160 | tf_op jit(solution)/shard_map/ppermute | solution.py:439
  9.2 1.1 %collective-permute-done.from_left.x0l.refs_4_ = f32[32,128]{1,0:T(8,128)S(1)} collective-permute-done((f32[32,128]{1,0:T(8,128)S(1)}, f32[32,128]{1,0:T(8,128)S(1)}, u32[]{:S(2)}, u32[]{:S(2)}) %collective-permute-start) | collective-permute-done | bytes 16416 | tf_op jit(solution)/shard_map/ppermute | solution.py:438
  10.2 0.0 collective-permute-done.1.from_right.x0r.refs_5_
  10.2 2.9 %collective-permute-start.2 = (f32[24,128]{1,0:T(8,128)S(1)}, f32[24,128]{1,0:T(8,128)S(1)}, u32[]{:S(2)}, u32[]{:S(2)}) collective-permute-start(f32[24,128]{1,0:T(8,128)S(1)} %get-tuple-element.42), channel_id=1, source_target_pairs={{0,1},{1,2},{2,3},{3,0},{4,5},{5,6},{6,7},{7,4},{8,9},{9,10},{10,1... | collective-permute-start | bytes 36872 | tf_op jit(solution)/shard_map/ppermute | solution.py:438
  13.1 0.0 collective-permute-start.3
  13.2 0.8 %collective-permute-done.2.y0d.refs_6_ = f32[24,128]{1,0:T(8,128)S(1)} collective-permute-done((f32[24,128]{1,0:T(8,128)S(1)}, f32[24,128]{1,0:T(8,128)S(1)}, u32[]{:S(2)}, u32[]{:S(2)}) %collective-permute-start.2) | collective-permute-done | bytes 12320 | tf_op jit(solution)/shard_map/ppermute | solution.py:438
  14.0 2.3 %collective-permute-done.3.y0u.refs_7_ = f32[24,128]{1,0:T(8,128)S(1)} collective-permute-done((f32[24,128]{1,0:T(8,128)S(1)}, f32[24,128]{1,0:T(8,128)S(1)}, u32[]{:S(2)}, u32[]{:S(2)}) %collective-permute-start.3) | collective-permute-done | bytes 12320 | tf_op jit(solution)/shard_map/ppermute | solution.py:439
  16.3 0.2 shard_map.70.refs_2_.bits_ref
  16.5 0.0 copy-done.1
  16.5 0.0 copy-done.4
  16.5 1.6 %shard_map.71 = (f32[19,8,16,128]{3,2,1,0:T(8,128)S(1)}, f32[104,128]{1,0:T(8,128)S(1)}, f32[104,128]{1,0:T(8,128)S(1)}, f32[56,128]{1,0:T(8,128)S(1)}, f32[56,1...) custom-call(f32[19]{0:T(128)S(1)} %copy-done.4, f32[19,8,16,128]{3,2,1,0:T(8,128)S(1)} %copy-done.1, ...), custom_call_target="tpu_custom_call" | custom-call | tf_op jit(solution)/shard_map/pallas_call | solution.py:423
  18.1 1.1 %collective-permute-start.4 = (f32[104,128]{1,0:T(8,128)S(1)}, f32[104,128]{1,0:T(8,128)S(1)}, u32[]{:S(2)}, u32[]{:S(2)}) collective-permute-start(f32[104,128]{1,0:T(8,128)S(1)} %get-tuple-element.46.own_right.refs_13_), channel_id=1, source_target_pairs={{0,4},{4,8},{8,12},{12,0},{1,5},{5,9},{9,13},{13,1},{2,6},{6,10},{... | collective-permute-start | bytes 159752 | tf_op jit(solution)/shard_map/ppermute | solution.py:438
  19.3 2.5 %collective-permute-start.5 = (f32[104,128]{1,0:T(8,128)S(1)}, f32[104,128]{1,0:T(8,128)S(1)}, u32[]{:S(2)}, u32[]{:S(2)}) collective-permute-start(f32[104,128]{1,0:T(8,128)S(1)} %get-tuple-element.47.own_left.refs_14_), channel_id=1, source_target_pairs={{4,0},{8,4},{12,8},{0,12},{5,1},{9,5},{13,9},{1,13},{6,2},{10,6},{... | collective-permute-start | bytes 159752 | tf_op jit(solution)/shard_map/ppermute | solution.py:439
  21.8 1.6 %collective-permute-done.4.xl.refs_9_ = f32[104,128]{1,0:T(8,128)S(1)} collective-permute-done((f32[104,128]{1,0:T(8,128)S(1)}, f32[104,128]{1,0:T(8,128)S(1)}, u32[]{:S(2)}, u32[]{:S(2)}) %collective-permute-start.4) | collective-permute-done | bytes 53280 | tf_op jit(solution)/shard_map/ppermute | solution.py:438
  23.4 0.3 collective-permute-done.5.xr.refs_10_
  23.7 1.3 %collective-permute-start.6 = (f32[56,128]{1,0:T(8,128)S(1)}, f32[56,128]{1,0:T(8,128)S(1)}, u32[]{:S(2)}, u32[]{:S(2)}) collective-permute-start(f32[56,128]{1,0:T(8,128)S(1)} %get-tuple-element.50.refs_15_), channel_id=1, source_target_pairs={{0,1},{1,2},{2,3},{3,0},{4,5},{5,6},{6,7},{7,4},{8,9},{9,10},{10,1... | collective-permute-start | bytes 86024 | tf_op jit(solution)/shard_map/ppermute | solution.py:438
  24.9 0.0 collective-permute-start.7
  24.9 1.0 %collective-permute-done.6.refs_11_ = f32[56,128]{1,0:T(8,128)S(1)} collective-permute-done((f32[56,128]{1,0:T(8,128)S(1)}, f32[56,128]{1,0:T(8,128)S(1)}, u32[]{:S(2)}, u32[]{:S(2)}) %collective-permute-start.6) | collective-permute-done | bytes 28704 | tf_op jit(solution)/shard_map/ppermute | solution.py:438
  25.9 2.3 %collective-permute-done.7.refs_12_ = f32[56,128]{1,0:T(8,128)S(1)} collective-permute-done((f32[56,128]{1,0:T(8,128)S(1)}, f32[56,128]{1,0:T(8,128)S(1)}, u32[]{:S(2)}, u32[]{:S(2)}) %collective-permute-start.7) | collective-permute-done | bytes 28704 | tf_op jit(solution)/shard_map/ppermute | solution.py:439
  28.2 1.7 %shard_map.73 = (f32[19,8,16,128]{3,2,1,0:T(8,128)S(1)}, f32[104,128]{1,0:T(8,128)S(1)}, f32[104,128]{1,0:T(8,128)S(1)}, f32[56,128]{1,0:T(8,128)S(1)}, f32[56,1...) custom-call(f32[19]{0:T(128)S(1)} %copy-done.4, f32[19,8,16,128]{3,2,1,0:T(8,128)S(1)} %get-tuple-element.44.refs_1_, ...), custom_call_target="tpu_custom_call" | custom-call | tf_op jit(solution)/shard_map/pallas_call | solution.py:423
  29.9 1.1 %collective-permute-start.8 = (f32[104,128]{1,0:T(8,128)S(1)}, f32[104,128]{1,0:T(8,128)S(1)}, u32[]{:S(2)}, u32[]{:S(2)}) collective-permute-start(f32[104,128]{1,0:T(8,128)S(1)} %get-tuple-element.54.own_right.refs_13_), channel_id=1, source_target_pairs={{0,4},{4,8},{8,12},{12,0},{1,5},{5,9},{9,13},{13,1},{2,6},{6,10},{... | collective-permute-start | bytes 159752 | tf_op jit(solution)/shard_map/ppermute | solution.py:438
  31.1 2.2 %collective-permute-start.9 = (f32[104,128]{1,0:T(8,128)S(1)}, f32[104,128]{1,0:T(8,128)S(1)}, u32[]{:S(2)}, u32[]{:S(2)}) collective-permute-start(f32[104,128]{1,0:T(8,128)S(1)} %get-tuple-element.55.own_left.refs_14_), channel_id=1, source_target_pairs={{4,0},{8,4},{12,8},{0,12},{5,1},{9,5},{13,9},{1,13},{6,2},{10,6},{... | collective-permute-start | bytes 159752 | tf_op jit(solution)/shard_map/ppermute | solution.py:439
  33.3 1.5 %collective-permute-done.8.xl.refs_9_ = f32[104,128]{1,0:T(8,128)S(1)} collective-permute-done((f32[104,128]{1,0:T(8,128)S(1)}, f32[104,128]{1,0:T(8,128)S(1)}, u32[]{:S(2)}, u32[]{:S(2)}) %collective-permute-start.8) | collective-permute-done | bytes 53280 | tf_op jit(solution)/shard_map/ppermute | solution.py:438
  34.8 0.4 collective-permute-done.9.xr.refs_10_
  35.2 1.3 %collective-permute-start.10 = (f32[56,128]{1,0:T(8,128)S(1)}, f32[56,128]{1,0:T(8,128)S(1)}, u32[]{:S(2)}, u32[]{:S(2)}) collective-permute-start(f32[56,128]{1,0:T(8,128)S(1)} %get-tuple-element.58.refs_15_), channel_id=1, source_target_pairs={{0,1},{1,2},{2,3},{3,0},{4,5},{5,6},{6,7},{7,4},{8,9},{9,10},{10,1... | collective-permute-start | bytes 86024 | tf_op jit(solution)/shard_map/ppermute | solution.py:438
  36.5 0.0 collective-permute-start.11
  36.5 1.0 %collective-permute-done.10.refs_11_ = f32[56,128]{1,0:T(8,128)S(1)} collective-permute-done((f32[56,128]{1,0:T(8,128)S(1)}, f32[56,128]{1,0:T(8,128)S(1)}, u32[]{:S(2)}, u32[]{:S(2)}) %collective-permute-start.10) | collective-permute-done | bytes 28704 | tf_op jit(solution)/shard_map/ppermute | solution.py:438
  37.5 2.3 %collective-permute-done.11.refs_12_ = f32[56,128]{1,0:T(8,128)S(1)} collective-permute-done((f32[56,128]{1,0:T(8,128)S(1)}, f32[56,128]{1,0:T(8,128)S(1)}, u32[]{:S(2)}, u32[]{:S(2)}) %collective-permute-start.11) | collective-permute-done | bytes 28704 | tf_op jit(solution)/shard_map/ppermute | solution.py:439
  39.8 1.7 %shard_map.75 = (f32[19,8,16,128]{3,2,1,0:T(8,128)S(1)}, f32[104,128]{1,0:T(8,128)S(1)}, f32[104,128]{1,0:T(8,128)S(1)}, f32[56,128]{1,0:T(8,128)S(1)}, f32[56,1...) custom-call(f32[19]{0:T(128)S(1)} %copy-done.4, f32[19,8,16,128]{3,2,1,0:T(8,128)S(1)} %get-tuple-element.52.refs_1_, ...), custom_call_target="tpu_custom_call" | custom-call | tf_op jit(solution)/shard_map/pallas_call | solution.py:423
  41.5 0.9 %collective-permute-start.12 = (f32[104,128]{1,0:T(8,128)S(1)}, f32[104,128]{1,0:T(8,128)S(1)}, u32[]{:S(2)}, u32[]{:S(2)}) collective-permute-start(f32[104,128]{1,0:T(8,128)S(1)} %get-tuple-element.62.own_right.refs_13_), channel_id=1, source_target_pairs={{0,4},{4,8},{8,12},{12,0},{1,5},{5,9},{9,13},{13,1},{2,6},{6,10},{... | collective-permute-start | bytes 159752 | tf_op jit(solution)/shard_map/ppermute | solution.py:438
  42.4 2.4 %collective-permute-start.13 = (f32[104,128]{1,0:T(8,128)S(1)}, f32[104,128]{1,0:T(8,128)S(1)}, u32[]{:S(2)}, u32[]{:S(2)}) collective-permute-start(f32[104,128]{1,0:T(8,128)S(1)} %get-tuple-element.63.own_left.refs_14_), channel_id=1, source_target_pairs={{4,0},{8,4},{12,8},{0,12},{5,1},{9,5},{13,9},{1,13},{6,2},{10,6},{... | collective-permute-start | bytes 159752 | tf_op jit(solution)/shard_map/ppermute | solution.py:439
  44.9 1.8 %collective-permute-done.12.xl.refs_9_ = f32[104,128]{1,0:T(8,128)S(1)} collective-permute-done((f32[104,128]{1,0:T(8,128)S(1)}, f32[104,128]{1,0:T(8,128)S(1)}, u32[]{:S(2)}, u32[]{:S(2)}) %collective-permute-start.12) | collective-permute-done | bytes 53280 | tf_op jit(solution)/shard_map/ppermute | solution.py:438
  46.6 0.1 collective-permute-done.13.xr.refs_10_
  46.8 1.4 %collective-permute-start.14 = (f32[56,128]{1,0:T(8,128)S(1)}, f32[56,128]{1,0:T(8,128)S(1)}, u32[]{:S(2)}, u32[]{:S(2)}) collective-permute-start(f32[56,128]{1,0:T(8,128)S(1)} %get-tuple-element.66.refs_15_), channel_id=1, source_target_pairs={{0,1},{1,2},{2,3},{3,0},{4,5},{5,6},{6,7},{7,4},{8,9},{9,10},{10,1... | collective-permute-start | bytes 86024 | tf_op jit(solution)/shard_map/ppermute | solution.py:438
  48.2 0.0 collective-permute-start.15
  48.2 1.0 %collective-permute-done.14.refs_11_ = f32[56,128]{1,0:T(8,128)S(1)} collective-permute-done((f32[56,128]{1,0:T(8,128)S(1)}, f32[56,128]{1,0:T(8,128)S(1)}, u32[]{:S(2)}, u32[]{:S(2)}) %collective-permute-start.14) | collective-permute-done | bytes 28704 | tf_op jit(solution)/shard_map/ppermute | solution.py:438
  49.2 2.3 %collective-permute-done.15.refs_12_ = f32[56,128]{1,0:T(8,128)S(1)} collective-permute-done((f32[56,128]{1,0:T(8,128)S(1)}, f32[56,128]{1,0:T(8,128)S(1)}, u32[]{:S(2)}, u32[]{:S(2)}) %collective-permute-start.15) | collective-permute-done | bytes 28704 | tf_op jit(solution)/shard_map/ppermute | solution.py:439
  51.5 2.2 %shard_map.77 = (f32[19,8,16,128]{3,2,1,0:T(8,128)S(1)}, f32[88,128]{1,0:T(8,128)S(1)}, f32[88,128]{1,0:T(8,128)S(1)}, f32[40,128]{1,0:T(8,128)S(1)}, f32[40,128]{1,0:T(8,128)S(1)}, /*index=5*/f32[3,8,16,128]{3,2,1,0:T(8,128)}) custom-call(f32[19]{0:T(128)S(1)} %copy-done.4, f32[19,8,16,128]{3,2,1,0:T(8,128)S(1)} %get-tuple-element.60.refs_1_, ...), custom_call_target="tpu_custom_call" | custom-call | tf_op jit(solution)/shard_map/pallas_call | solution.py:423
  53.8 0.8 %collective-permute-start.16 = (f32[88,128]{1,0:T(8,128)S(1)}, f32[88,128]{1,0:T(8,128)S(1)}, u32[]{:S(2)}, u32[]{:S(2)}) collective-permute-start(f32[88,128]{1,0:T(8,128)S(1)} %get-tuple-element.69.own_right), channel_id=1, source_target_pairs={{0,4},{4,8},{8,12},{12,0},{1,5},{5,9},{9,13},{13,1},{2,6},{6,10},{... | collective-permute-start | bytes 135176 | tf_op jit(solution)/shard_map/ppermute | solution.py:438
  54.6 2.5 %collective-permute-start.17 = (f32[88,128]{1,0:T(8,128)S(1)}, f32[88,128]{1,0:T(8,128)S(1)}, u32[]{:S(2)}, u32[]{:S(2)}) collective-permute-start(f32[88,128]{1,0:T(8,128)S(1)} %get-tuple-element.70.own_left), channel_id=1, source_target_pairs={{4,0},{8,4},{12,8},{0,12},{5,1},{9,5},{13,9},{1,13},{6,2},{10,6},{... | collective-permute-start | bytes 135176 | tf_op jit(solution)/shard_map/ppermute | solution.py:439
  57.0 1.5 %collective-permute-done.16.xl = f32[88,128]{1,0:T(8,128)S(1)} collective-permute-done((f32[88,128]{1,0:T(8,128)S(1)}, f32[88,128]{1,0:T(8,128)S(1)}, u32[]{:S(2)}, u32[]{:S(2)}) %collective-permute-start.16) | collective-permute-done | bytes 45088 | tf_op jit(solution)/shard_map/ppermute | solution.py:438
  58.6 0.0 collective-permute-done.17.xr
  58.6 1.5 %collective-permute-start.18 = (f32[40,128]{1,0:T(8,128)S(1)}, f32[40,128]{1,0:T(8,128)S(1)}, u32[]{:S(2)}, u32[]{:S(2)}) collective-permute-start(f32[40,128]{1,0:T(8,128)S(1)} %get-tuple-element.73), channel_id=1, source_target_pairs={{0,1},{1,2},{2,3},{3,0},{4,5},{5,6},{6,7},{7,4},{8,9},{9,10},{10,1... | collective-permute-start | bytes 61448 | tf_op jit(solution)/shard_map/ppermute | solution.py:438
  60.1 0.0 collective-permute-start.19
  60.1 0.9 %collective-permute-done.18.yd = f32[40,128]{1,0:T(8,128)S(1)} collective-permute-done((f32[40,128]{1,0:T(8,128)S(1)}, f32[40,128]{1,0:T(8,128)S(1)}, u32[]{:S(2)}, u32[]{:S(2)}) %collective-permute-start.18) | collective-permute-done | bytes 20512 | tf_op jit(solution)/shard_map/ppermute | solution.py:438
  61.0 2.3 %collective-permute-done.19.yu = f32[40,128]{1,0:T(8,128)S(1)} collective-permute-done((f32[40,128]{1,0:T(8,128)S(1)}, f32[40,128]{1,0:T(8,128)S(1)}, u32[]{:S(2)}, u32[]{:S(2)}) %collective-permute-start.19) | collective-permute-done | bytes 20512 | tf_op jit(solution)/shard_map/ppermute | solution.py:439
  63.3 1.2 %shard_map.79 = f32[19,8,16,128]{3,2,1,0:T(8,128)} custom-call(f32[19,8,16,128]{3,2,1,0:T(8,128)S(1)} %get-tuple-element.68.f_ref, s32[8,16,128]{2,1,0:T(8,128)S(1)} %shard_map.70.refs_2_.bits_ref, f32[88,128]{1,0:T(8,128)S(1)} %collective-permute-done.16.xl, f32[88,128]{1,0:T(8,128)S(1)} %collective-permute-done.17.xr, ...), custom_call_target="tpu_custom_call" | custom-call | tf_op jit(solution)/shard_map/pallas_call | solution.py:423
  (5 shorter events, 0.1 us)
Async XLA Ops:
  0.6 1.3 %copy-start = (f32[19,8,16,128]{3,2,1,0:T(8,128)S(1)}, f32[19,8,16,128]{3,2,1,0:T(8,128)}, u32[]{:S(2)}) copy-start(f32[19,8,16,128]{3,2,1,0:T(8,128)} %refs_1_.1) | copy-start | bytes 3735556
  1.9 0.8 %copy-start.2 = (s32[8,16,128]{2,1,0:T(8,128)S(1)}, s32[8,16,128]{2,1,0:T(8,128)}, u32[]{:S(2)}) copy-start(s32[8,16,128]{2,1,0:T(8,128)} %mask_ref.5) | copy-start | bytes 196612
  2.8 0.8 %copy-start.3 = (s32[8,16,128]{2,1,0:T(8,128)S(1)}, s32[8,16,128]{2,1,0:T(8,128)}, u32[]{:S(2)}) copy-start(s32[8,16,128]{2,1,0:T(8,128)} %wet_ref.1) | copy-start | bytes 196612
  3.6 0.7 %copy-start.5 = (f32[4]{0:T(128)S(1)}, f32[4]{0:T(128)}, u32[]{:S(2)}) copy-start(f32[4]{0:T(128)} %wall_ref.1) | copy-start | bytes 52
  4.3 12.2 %copy-start.1 = (f32[19,8,16,128]{3,2,1,0:T(8,128)S(1)}, f32[19,8,16,128]{3,2,1,0:T(8,128)}, u32[]{:S(2)}) copy-start(f32[19,8,16,128]{3,2,1,0:T(8,128)} %refs_1_.1) | copy-start | bytes 3735556
  4.3 12.2 %copy-start.4 = (f32[19]{0:T(128)S(1)}, f32[19]{0:T(128)}, u32[]{:S(2)}) copy-start(f32[19]{0:T(128)} %refs_0_.7) | copy-start | bytes 232
  4.9 5.3 %collective-permute-start = (f32[32,128]{1,0:T(8,128)S(1)}, f32[32,128]{1,0:T(8,128)S(1)}, u32[]{:S(2)}, u32[]{:S(2)}) collective-permute-start(f32[32,128]{1,0:T(8,128)S(1)} %get-tuple-element.39), channel_id=1, source_target_pairs={{0,4},{4,8},{8,12},{12,0},{1,5},{5,9},{9,13},{13,1},{2,6},{6,10},{... | collective-permute-start | bytes 49160 | tf_op jit(solution)/shard_map/ppermute | solution.py:438
  7.1 3.2 %collective-permute-start.1 = (f32[32,128]{1,0:T(8,128)S(1)}, f32[32,128]{1,0:T(8,128)S(1)}, u32[]{:S(2)}, u32[]{:S(2)}) collective-permute-start(f32[32,128]{1,0:T(8,128)S(1)} %get-tuple-element.40), channel_id=1, source_target_pairs={{4,0},{8,4},{12,8},{0,12},{5,1},{9,5},{13,9},{1,13},{6,2},{10,6},{... | collective-permute-start | bytes 49160 | tf_op jit(solution)/shard_map/ppermute | solution.py:439
  10.2 3.7 %collective-permute-start.2 = (f32[24,128]{1,0:T(8,128)S(1)}, f32[24,128]{1,0:T(8,128)S(1)}, u32[]{:S(2)}, u32[]{:S(2)}) collective-permute-start(f32[24,128]{1,0:T(8,128)S(1)} %get-tuple-element.42), channel_id=1, source_target_pairs={{0,1},{1,2},{2,3},{3,0},{4,5},{5,6},{6,7},{7,4},{8,9},{9,10},{10,1... | collective-permute-start | bytes 36872 | tf_op jit(solution)/shard_map/ppermute | solution.py:438
  13.1 3.1 %collective-permute-start.3 = (f32[24,128]{1,0:T(8,128)S(1)}, f32[24,128]{1,0:T(8,128)S(1)}, u32[]{:S(2)}, u32[]{:S(2)}) collective-permute-start(f32[24,128]{1,0:T(8,128)S(1)} %get-tuple-element.43), channel_id=1, source_target_pairs={{1,0},{2,1},{3,2},{0,3},{5,4},{6,5},{7,6},{4,7},{9,8},{10,9},{11,1... | collective-permute-start | bytes 36872 | tf_op jit(solution)/shard_map/ppermute | solution.py:439
  18.1 5.2 %collective-permute-start.4 = (f32[104,128]{1,0:T(8,128)S(1)}, f32[104,128]{1,0:T(8,128)S(1)}, u32[]{:S(2)}, u32[]{:S(2)}) collective-permute-start(f32[104,128]{1,0:T(8,128)S(1)} %get-tuple-element.46.own_right.refs_13_), channel_id=1, source_target_pairs={{0,4},{4,8},{8,12},{12,0},{1,5},{5,9},{9,13},{13,1},{2,6},{6,10},{... | collective-permute-start | bytes 159752 | tf_op jit(solution)/shard_map/ppermute | solution.py:438
  19.3 4.4 %collective-permute-start.5 = (f32[104,128]{1,0:T(8,128)S(1)}, f32[104,128]{1,0:T(8,128)S(1)}, u32[]{:S(2)}, u32[]{:S(2)}) collective-permute-start(f32[104,128]{1,0:T(8,128)S(1)} %get-tuple-element.47.own_left.refs_14_), channel_id=1, source_target_pairs={{4,0},{8,4},{12,8},{0,12},{5,1},{9,5},{13,9},{1,13},{6,2},{10,6},{... | collective-permute-start | bytes 159752 | tf_op jit(solution)/shard_map/ppermute | solution.py:439
  23.7 2.3 %collective-permute-start.6 = (f32[56,128]{1,0:T(8,128)S(1)}, f32[56,128]{1,0:T(8,128)S(1)}, u32[]{:S(2)}, u32[]{:S(2)}) collective-permute-start(f32[56,128]{1,0:T(8,128)S(1)} %get-tuple-element.50.refs_15_), channel_id=1, source_target_pairs={{0,1},{1,2},{2,3},{3,0},{4,5},{5,6},{6,7},{7,4},{8,9},{9,10},{10,1... | collective-permute-start | bytes 86024 | tf_op jit(solution)/shard_map/ppermute | solution.py:438
  24.9 3.3 %collective-permute-start.7 = (f32[56,128]{1,0:T(8,128)S(1)}, f32[56,128]{1,0:T(8,128)S(1)}, u32[]{:S(2)}, u32[]{:S(2)}) collective-permute-start(f32[56,128]{1,0:T(8,128)S(1)} %get-tuple-element.51.refs_16_), channel_id=1, source_target_pairs={{1,0},{2,1},{3,2},{0,3},{5,4},{6,5},{7,6},{4,7},{9,8},{10,9},{11,1... | collective-permute-start | bytes 86024 | tf_op jit(solution)/shard_map/ppermute | solution.py:439
  29.9 4.8 %collective-permute-start.8 = (f32[104,128]{1,0:T(8,128)S(1)}, f32[104,128]{1,0:T(8,128)S(1)}, u32[]{:S(2)}, u32[]{:S(2)}) collective-permute-start(f32[104,128]{1,0:T(8,128)S(1)} %get-tuple-element.54.own_right.refs_13_), channel_id=1, source_target_pairs={{0,4},{4,8},{8,12},{12,0},{1,5},{5,9},{9,13},{13,1},{2,6},{6,10},{... | collective-permute-start | bytes 159752 | tf_op jit(solution)/shard_map/ppermute | solution.py:438
  31.1 4.1 %collective-permute-start.9 = (f32[104,128]{1,0:T(8,128)S(1)}, f32[104,128]{1,0:T(8,128)S(1)}, u32[]{:S(2)}, u32[]{:S(2)}) collective-permute-start(f32[104,128]{1,0:T(8,128)S(1)} %get-tuple-element.55.own_left.refs_14_), channel_id=1, source_target_pairs={{4,0},{8,4},{12,8},{0,12},{5,1},{9,5},{13,9},{1,13},{6,2},{10,6},{... | collective-permute-start | bytes 159752 | tf_op jit(solution)/shard_map/ppermute | solution.py:439
  35.2 2.3 %collective-permute-start.10 = (f32[56,128]{1,0:T(8,128)S(1)}, f32[56,128]{1,0:T(8,128)S(1)}, u32[]{:S(2)}, u32[]{:S(2)}) collective-permute-start(f32[56,128]{1,0:T(8,128)S(1)} %get-tuple-element.58.refs_15_), channel_id=1, source_target_pairs={{0,1},{1,2},{2,3},{3,0},{4,5},{5,6},{6,7},{7,4},{8,9},{9,10},{10,1... | collective-permute-start | bytes 86024 | tf_op jit(solution)/shard_map/ppermute | solution.py:438
  36.5 3.3 %collective-permute-start.11 = (f32[56,128]{1,0:T(8,128)S(1)}, f32[56,128]{1,0:T(8,128)S(1)}, u32[]{:S(2)}, u32[]{:S(2)}) collective-permute-start(f32[56,128]{1,0:T(8,128)S(1)} %get-tuple-element.59.refs_16_), channel_id=1, source_target_pairs={{1,0},{2,1},{3,2},{0,3},{5,4},{6,5},{7,6},{4,7},{9,8},{10,9},{11,1... | collective-permute-start | bytes 86024 | tf_op jit(solution)/shard_map/ppermute | solution.py:439
  41.5 5.1 %collective-permute-start.12 = (f32[104,128]{1,0:T(8,128)S(1)}, f32[104,128]{1,0:T(8,128)S(1)}, u32[]{:S(2)}, u32[]{:S(2)}) collective-permute-start(f32[104,128]{1,0:T(8,128)S(1)} %get-tuple-element.62.own_right.refs_13_), channel_id=1, source_target_pairs={{0,4},{4,8},{8,12},{12,0},{1,5},{5,9},{9,13},{13,1},{2,6},{6,10},{... | collective-permute-start | bytes 159752 | tf_op jit(solution)/shard_map/ppermute | solution.py:438
  42.4 4.3 %collective-permute-start.13 = (f32[104,128]{1,0:T(8,128)S(1)}, f32[104,128]{1,0:T(8,128)S(1)}, u32[]{:S(2)}, u32[]{:S(2)}) collective-permute-start(f32[104,128]{1,0:T(8,128)S(1)} %get-tuple-element.63.own_left.refs_14_), channel_id=1, source_target_pairs={{4,0},{8,4},{12,8},{0,12},{5,1},{9,5},{13,9},{1,13},{6,2},{10,6},{... | collective-permute-start | bytes 159752 | tf_op jit(solution)/shard_map/ppermute | solution.py:439
  46.8 2.4 %collective-permute-start.14 = (f32[56,128]{1,0:T(8,128)S(1)}, f32[56,128]{1,0:T(8,128)S(1)}, u32[]{:S(2)}, u32[]{:S(2)}) collective-permute-start(f32[56,128]{1,0:T(8,128)S(1)} %get-tuple-element.66.refs_15_), channel_id=1, source_target_pairs={{0,1},{1,2},{2,3},{3,0},{4,5},{5,6},{6,7},{7,4},{8,9},{9,10},{10,1... | collective-permute-start | bytes 86024 | tf_op jit(solution)/shard_map/ppermute | solution.py:438
  48.2 3.3 %collective-permute-start.15 = (f32[56,128]{1,0:T(8,128)S(1)}, f32[56,128]{1,0:T(8,128)S(1)}, u32[]{:S(2)}, u32[]{:S(2)}) collective-permute-start(f32[56,128]{1,0:T(8,128)S(1)} %get-tuple-element.67.refs_16_), channel_id=1, source_target_pairs={{1,0},{2,1},{3,2},{0,3},{5,4},{6,5},{7,6},{4,7},{9,8},{10,9},{11,1... | collective-permute-start | bytes 86024 | tf_op jit(solution)/shard_map/ppermute | solution.py:439
  53.8 4.8 %collective-permute-start.16 = (f32[88,128]{1,0:T(8,128)S(1)}, f32[88,128]{1,0:T(8,128)S(1)}, u32[]{:S(2)}, u32[]{:S(2)}) collective-permute-start(f32[88,128]{1,0:T(8,128)S(1)} %get-tuple-element.69.own_right), channel_id=1, source_target_pairs={{0,4},{4,8},{8,12},{12,0},{1,5},{5,9},{9,13},{13,1},{2,6},{6,10},{... | collective-permute-start | bytes 135176 | tf_op jit(solution)/shard_map/ppermute | solution.py:438
  54.6 4.0 %collective-permute-start.17 = (f32[88,128]{1,0:T(8,128)S(1)}, f32[88,128]{1,0:T(8,128)S(1)}, u32[]{:S(2)}, u32[]{:S(2)}) collective-permute-start(f32[88,128]{1,0:T(8,128)S(1)} %get-tuple-element.70.own_left), channel_id=1, source_target_pairs={{4,0},{8,4},{12,8},{0,12},{5,1},{9,5},{13,9},{1,13},{6,2},{10,6},{... | collective-permute-start | bytes 135176 | tf_op jit(solution)/shard_map/ppermute | solution.py:439
  58.6 2.4 %collective-permute-start.18 = (f32[40,128]{1,0:T(8,128)S(1)}, f32[40,128]{1,0:T(8,128)S(1)}, u32[]{:S(2)}, u32[]{:S(2)}) collective-permute-start(f32[40,128]{1,0:T(8,128)S(1)} %get-tuple-element.73), channel_id=1, source_target_pairs={{0,1},{1,2},{2,3},{3,0},{4,5},{5,6},{6,7},{7,4},{8,9},{9,10},{10,1... | collective-permute-start | bytes 61448 | tf_op jit(solution)/shard_map/ppermute | solution.py:438
  60.1 3.2 %collective-permute-start.19 = (f32[40,128]{1,0:T(8,128)S(1)}, f32[40,128]{1,0:T(8,128)S(1)}, u32[]{:S(2)}, u32[]{:S(2)}) collective-permute-start(f32[40,128]{1,0:T(8,128)S(1)} %get-tuple-element.74), channel_id=1, source_target_pairs={{1,0},{2,1},{3,2},{0,3},{5,4},{6,5},{7,6},{4,7},{9,8},{10,9},{11,1... | collective-permute-start | bytes 61448 | tf_op jit(solution)/shard_map/ppermute | solution.py:439

commit v2 on v1

v2 whole, which is shorter than its diff:
```python
import functools

import jax
import jax.numpy as jnp
from jax import lax
from jax.experimental import pallas as pl
from jax.experimental.pallas import tpu as pltpu
from jax.sharding import PartitionSpec as P

STEPS = 4
STRENGTH = 2.5
VELOCITY = (
    (0, 0, 0),
    (1, 0, 0),
    (-1, 0, 0),
    (0, 1, 0),
    (0, -1, 0),
    (0, 0, 1),
    (0, 0, -1),
    (1, 1, 0),
    (-1, -1, 0),
    (1, -1, 0),
    (-1, 1, 0),
    (1, 0, 1),
    (-1, 0, -1),
    (1, 0, -1),
    (-1, 0, 1),
    (0, 1, 1),
    (0, -1, -1),
    (0, 1, -1),
    (0, -1, 1),
)
N = len(VELOCITY)
OPPOSITE = [0] + [k + 1 if k % 2 == 1 else k - 1 for k in range(1, N)]
RIGHT = [k for k in range(N) if VELOCITY[k][0] == 1]
LEFT = [k for k in range(N) if VELOCITY[k][0] == -1]
UP = [k for k in range(N) if VELOCITY[k][1] == 1]
DOWN = [k for k in range(N) if VELOCITY[k][1] == -1]
TILE = 8
PAD = 2 * TILE

C_UP, C_DN, H_UP, H_DN = 0, 1, 2, 3
RC_L, RC_R, G_L, G_R = 0, 1, 2, 3


def roll_z(value, step):
    if step == 0:
        return value
    return pltpu.roll(value, step % value.shape[-1], value.ndim - 1)


def total(values):
    values = list(values)
    while len(values) > 1:
        values = [
            values[i] + values[i + 1] if i + 1 < len(values) else values[i]
            for i in range(0, len(values), 2)
        ]
    return values[0]


def potential_of(density, fluid, solid_value):
    return jnp.where(fluid, 1.0 - jnp.exp(-density), solid_value)


def collide(f, fluid, force, rate):
    fx, fy, fz = force
    s = {k: f[k] + f[k + 1] for k in range(1, N, 2)}
    d = {k: f[k] - f[k + 1] for k in range(1, N, 2)}
    xxyy, xxzz, yyzz = s[7] + s[9], s[11] + s[13], s[15] + s[17]
    xy, xz, yz = s[7] - s[9], s[11] - s[13], s[15] - s[17]
    xyy, yxx = d[7] + d[9], d[7] - d[9]
    xzz, zxx = d[11] + d[13], d[11] - d[13]
    yzz, zyy = d[15] + d[17], d[15] - d[17]
    jx, jy, jz = d[1] + (xyy + xzz), d[3] + (yxx + yzz), d[5] + (zxx + zyy)
    xx, yy, zz = s[1] + (xxyy + xxzz), s[3] + (xxyy + yyzz), s[5] + (xxzz + yyzz)
    rho = (f[0] + s[1]) + (s[3] + s[5]) + (xxyy + (xxzz + yyzz))
    safe = jnp.where(fluid, rho, 1.0)
    inverse = 1.0 / safe
    hx, hy, hz = 0.5 * fx, 0.5 * fy, 0.5 * fz
    gx, gy, gz = jx + hx, jy + hy, jz + hz
    ux, uy, uz = gx * inverse, gy * inverse, gz * inverse
    third = safe * (1.0 / 3.0)
    ninth = safe * (1.0 / 9.0)
    px, py, pz = gx - fx, gy - fy, gz - fz
    txx, tyy, tzz = ux * px, uy * py, uz * pz
    sx, sy, sz = ux * fx, uy * fy, uz * fz
    pxy = ux * fy + uy * fx
    pxz = ux * fz + uz * fx
    pyz = uy * fz + uz * fy
    t3, s3 = (txx + tyy + tzz) * (1.0 / 3.0), (sx + sy + sz) * (2.0 / 3.0)
    rho = rho - rate(0) * (rho - safe)
    nx = jx + fx - rate(1) * (jx - safe * ux + hx)
    ny = jy + fy - rate(2) * (jy - safe * uy + hy)
    nz = jz + fz - rate(3) * (jz - safe * uz + hz)
    xy = xy + rate(4) * (gx * uy - 0.5 * pxy - xy) + pxy
    xz = xz + rate(5) * (gx * uz - 0.5 * pxz - xz) + pxz
    yz = yz + rate(6) * (gy * uz - 0.5 * pyz - yz) + pyz
    xx = xx + rate(7) * (third + txx - xx) + 2.0 * sx
    yy = yy + rate(8) * (third + tyy - yy) + 2.0 * sy
    zz = zz + rate(9) * (third + tzz - zz) + 2.0 * sz
    ex, ey, ez = jx * (1.0 / 3.0), jy * (1.0 / 3.0), jz * (1.0 / 3.0)
    qx, qy, qz = fx * (1.0 / 3.0), fy * (1.0 / 3.0), fz * (1.0 / 3.0)
    xyy = xyy + rate(10) * (ex - xyy) + qx
    xzz = xzz + rate(11) * (ex - xzz) + qx
    yxx = yxx + rate(12) * (ey - yxx) + qy
    yzz = yzz + rate(13) * (ey - yzz) + qy
    zxx = zxx + rate(14) * (ez - zxx) + qz
    zyy = zyy + rate(15) * (ez - zyy) + qz
    base = ninth + t3
    xxyy = xxyy + rate(16) * (base - 0.5 * tzz - xxyy) + (s3 - sz)
    xxzz = xxzz + rate(17) * (base - 0.5 * tyy - xxzz) + (s3 - sy)
    yyzz = yyzz + rate(18) * (base - 0.5 * txx - yyzz) + (s3 - sx)
    out = [None] * N
    for first, even, cross, odd1, odd2 in (
        (7, xxyy, xy, xyy, yxx),
        (11, xxzz, xz, xzz, zxx),
        (15, yyzz, yz, yzz, zyy),
    ):
        even, cross, odd1, odd2 = 0.25 * even, 0.25 * cross, 0.25 * odd1, 0.25 * odd2
        plus, minus = even + cross, even - cross
        both, diff = odd1 + odd2, odd1 - odd2
        out[first], out[first + 1] = plus + both, plus - both
        out[first + 2], out[first + 3] = minus + diff, minus - diff
    pairs = []
    for first, even, odd in (
        (1, xx - (xxyy + xxzz), nx - (xyy + xzz)),
        (3, yy - (xxyy + yyzz), ny - (yxx + yzz)),
        (5, zz - (xxzz + yyzz), nz - (zxx + zyy)),
    ):
        half_even, half_odd = 0.5 * even, 0.5 * odd
        out[first], out[first + 1] = half_even + half_odd, half_even - half_odd
        pairs.append(even)
    out[0] = rho - (pairs[0] + pairs[1] + pairs[2]) - (xxyy + xxzz + yyzz)
    return out, (ux, uy, uz)


def start_kernel(f_hbm, mask_hbm, wet_hbm, wall_hbm, f_ref, mask_ref, pot_ref, right_ref, left_ref, *scratch):
    mask_in, wet_in, wall_in, f_sems, sems = scratch
    size_x, size_y = mask_ref.shape[0], mask_ref.shape[1]
    small = [
        pltpu.make_async_copy(source, target, sems.at[i])
        for i, (source, target) in enumerate(
            ((wall_hbm, wall_in), (mask_hbm, mask_in), (wet_hbm, wet_in))
        )
    ]
    large = [pltpu.make_async_copy(f_hbm.at[k], f_ref.at[k], f_sems.at[k]) for k in range(N)]
    for copy in small + large:
        copy.start()
    for copy in small:
        copy.wait()
    for x in range(size_x):
        wet = wet_in[x]
        wall = jnp.zeros(wet.shape, jnp.float32)
        for c in range(wall_in.shape[0]):
            wall = jnp.where(wet == c, wall_in[c], wall)
        pot_ref[x] = wall
        mask_ref[x] = jnp.where(mask_in[x] == 1, 1.0, 0.0)
    for copy in large:
        copy.wait()
    for x in range(size_x):
        density = total([f_ref[k, x] for k in range(N)])
        pot_ref[x] = potential_of(density, mask_ref[x] > 0.5, pot_ref[x])
    for ref, x in ((right_ref, size_x - 1), (left_ref, 0)):
        ref[:size_y] = pot_ref[x]
        ref[size_y:] = mask_ref[x]


def start_pack_kernel(pairs, pot_ref, mask_ref, from_left, from_right, a_ref, b_ref, up_ref, down_ref):
    size_x, size_y = mask_ref.shape[0], mask_ref.shape[1]
    for ref, y in ((up_ref, size_y - 1), (down_ref, 0)):
        ref[2 * size_x :] = jnp.zeros((TILE, ref.shape[1]), jnp.float32)
        for x in range(size_x):
            ref[x : x + 1] = pot_ref[x, y : y + 1]
            ref[size_x + x : size_x + x + 1] = mask_ref[x, y : y + 1]
        for i, side in enumerate((from_left, from_right)):
            row = 2 * size_x + i
            ref[row : row + 1] = side[y : y + 1]
            ref[row + 2 : row + 3] = side[size_y + y : size_y + y + 1]
    to_pairs(pairs, up_ref, down_ref, a_ref, b_ref)


def to_pairs(pairs, up_ref, down_ref, a_ref, b_ref):
    up, down = up_ref[...], down_ref[...]
    if not pairs:
        a_ref[...], b_ref[...] = up, down
        return
    odd = lax.axis_index("gy") % 2 == 1
    a_ref[...] = jnp.where(odd, down, up)
    b_ref[...] = jnp.where(odd, up, down)


def from_pairs(pairs, a_ref, b_ref, below_ref, above_ref):
    a, b = a_ref[...], b_ref[...]
    if not pairs:
        below_ref[...], above_ref[...] = a, b
        return
    odd = lax.axis_index("gy") % 2 == 1
    below_ref[...] = jnp.where(odd, a, b)
    above_ref[...] = jnp.where(odd, b, a)


def bits_kernel(pairs, mask_ref, x0l, x0r, a_ref, b_ref, bits_ref, y0d, y0u, pad_ref):
    size_x, size_y = mask_ref.shape[0], mask_ref.shape[1]
    from_pairs(pairs, a_ref, b_ref, y0d, y0u)
    for x in range(size_x):
        pad_ref[1 + x, TILE : TILE + size_y] = mask_ref[x]
    for x, side in ((0, x0l), (1 + size_x, x0r)):
        pad_ref[x, TILE : TILE + size_y] = side[size_y:]
    for y, side in ((TILE - 1, y0d), (TILE + size_y, y0u)):
        for x in range(size_x):
            pad_ref[1 + x, y : y + 1] = side[size_x + x : size_x + x + 1]
        for x, row in ((0, 2 * size_x + 2), (1 + size_x, 2 * size_x + 3)):
            pad_ref[x, y : y + 1] = side[row : row + 1]
    for x in range(size_x):
        for y in range(0, size_y, TILE):
            bits = jnp.zeros((TILE, mask_ref.shape[2]), jnp.int32)
            for k in range(N):
                ex, ey, ez = VELOCITY[k]
                row = TILE + y - ey
                source = roll_z(pad_ref[1 + x - ex, row : row + TILE], ez)
                bits = bits | jnp.where(source > 0.5, 1 << k, 0)
            bits_ref[x, y : y + TILE] = bits


class Layers:
    def __init__(self, edge_ref, middle_ref, size_x, edge):
        self.where = {}
        middle = [x for x in range(size_x) if x not in edge]
        for ref, xs in ((edge_ref, edge), (middle_ref, middle)):
            for i, x in enumerate(xs):
                self.where[x] = (ref, i)

    def load(self, x, y, k=None):
        ref, i = self.where[x]
        return ref[i, y : y + TILE] if k is None else ref[k, i, y : y + TILE]

    def row(self, x, y, k=None):
        ref, i = self.where[x]
        return ref[i, y : y + 1] if k is None else ref[k, i, y : y + 1]

    def store(self, x, y, value, k=None):
        ref, i = self.where[x]
        if k is None:
            ref[i, y : y + TILE] = value
        else:
            ref[k, i, y : y + TILE] = value


def two_layers(size_x):
    return [0, 1, size_x - 2, size_x - 1]


def one_layer(size_x):
    return [0, size_x - 1]


def fluid_at(bits_ref, x, y):
    return (bits_ref[x, y : y + TILE] & 1) != 0


def clear_outside(post, layers, size_y):
    nothing = jnp.zeros((TILE, post.shape[-1]), jnp.float32)
    for i in range(layers):
        for k in UP:
            post[k, i, :TILE] = nothing
        for k in DOWN:
            post[k, i, TILE + size_y :] = nothing


def collide_layers(xs, rates, f, bits_ref, pot, sides, post, speed):
    size_x, size_y, size_z = bits_ref.shape
    row_of = lax.broadcasted_iota(jnp.int32, (TILE, size_z), 0)
    for x in xs:
        for y in range(0, size_y, TILE):
            near = {
                (i, j): pot[1 + x + i, TILE + y + j : 2 * TILE + y + j]
                for i in (-1, 0, 1)
                for j in (-1, 0, 1)
            }
            scale = near[0, 0] * (STRENGTH / 36.0)
            dx = near[1, 0] - near[-1, 0]
            dy = near[0, 1] - near[0, -1]
            pp, pm, mp, mm = near[1, 1], near[1, -1], near[-1, 1], near[-1, -1]
            both = near[1, 0] + near[-1, 0] + near[0, 1] + near[0, -1] + 2.0 * near[0, 0]
            diag1, diag2 = pp - mm, pm - mp
            force = (
                scale * (2.0 * dx + (diag1 + diag2) + (roll_z(dx, 1) + roll_z(dx, -1))),
                scale * (2.0 * dy + (diag1 - diag2) + (roll_z(dy, 1) + roll_z(dy, -1))),
                scale * (roll_z(both, -1) - roll_z(both, 1)),
            )
            now = [f(k, x, y) for k in range(N)]
            if sides is not None:
                xl, xr, yd, yu = sides
                for at, side, ks in ((0, xl, RIGHT), (size_x - 1, xr, LEFT)):
                    if x == at:
                        for j, k in enumerate(ks):
                            now[k] = now[k] + side[j * size_y + y : j * size_y + y + TILE]
                for at, side, ks in ((0, yd, UP), (size_y - 1, yu, DOWN)):
                    if y <= at < y + TILE:
                        for j, k in enumerate(ks):
                            entering = side[j * size_x + x : j * size_x + x + 1]
                            now[k] = now[k] + jnp.where(row_of == at - y, entering, 0.0)
            fluid = fluid_at(bits_ref, x, y)
            after, at_speed = collide(now, fluid, force, lambda r: rates[r])
            for k in range(N):
                post.store(x, TILE + y, jnp.where(fluid, after[k], 0.0), k)
            if speed is not None:
                for c in range(3):
                    speed.store(x, y, jnp.where(fluid, at_speed[c], 0.0), c)


def stream_layers(xs, bits_ref, post, f, rho):
    size_x, size_y, _ = bits_ref.shape
    for x in xs:
        for y in range(0, size_y, TILE):
            bits = bits_ref[x, y : y + TILE]
            arrived = []
            for k in range(N):
                ex, ey, ez = VELOCITY[k]
                value = post.load(x, TILE + y, OPPOSITE[k])
                if k > 0:
                    come = 0.0
                    if 0 <= x - ex < size_x:
                        come = roll_z(post.load(x - ex, TILE + y - ey, k), ez)
                    value = jnp.where((bits & (1 << k)) != 0, come, value)
                f.store(x, y, value, k)
                arrived.append(value)
            if rho is not None:
                rho.store(x, y, total(arrived))


def edge_kernel(first, last, pairs, *refs):
    refs = list(refs)
    take = lambda count: [refs.pop(0) for _ in range(count)]
    rates, bits_ref, pot0_ref, x0l, x0r, y0d, y0u = take(7)
    if first:
        f_ref = take(1)[0]
    else:
        f_edge, f_middle, rho_edge, rho_middle, xl, xr, ya, yb = take(8)
        own_right, own_left, own_a, own_b = take(4)
    pot, post_out, f_out, right_ref, left_ref = take(5)
    rest = take(1)[0]
    size_x, size_y, size_z = bits_ref.shape
    edge2, edge1 = two_layers(size_x), one_layer(size_x)
    sides = None
    if first:
        f = lambda k, x, y: f_ref[k, x, y : y + TILE]
    else:
        yd, yu, own_down, own_up = take(4)
        from_pairs(pairs, ya, yb, yd, yu)
        if pairs:
            from_pairs(pairs, own_a, own_b, own_down, own_up)
        else:
            own_down, own_up = own_b, own_a
        sides = (xl, xr, yd, yu)
        held = Layers(f_edge, f_middle, size_x, edge1)
        density_of = Layers(rho_edge, rho_middle, size_x, edge1)
        f = lambda k, x, y: held.load(x, y, k)
    clear_outside(post_out, len(edge2), size_y)

    if first:
        for x in range(size_x):
            pot[1 + x, TILE : TILE + size_y] = pot0_ref[x]
        for x, side in ((0, x0l), (1 + size_x, x0r)):
            pot[x, TILE : TILE + size_y] = side[:size_y]
        for y, side in ((TILE - 1, y0d), (TILE + size_y, y0u)):
            for x in range(size_x):
                pot[1 + x, y : y + 1] = side[x : x + 1]
            for x, row in ((0, 2 * size_x), (1 + size_x, 2 * size_x + 1)):
                pot[x, y : y + 1] = side[row : row + 1]
    else:
        end = 6 * size_x
        row_of = lax.broadcasted_iota(jnp.int32, (TILE, size_z), 0)
        entering = {
            at: total([side[j * size_x : (j + 1) * size_x] for j in range(5)])
            for at, side in ((0, yd), (size_y - 1, yu))
        }
        for x in range(size_x):
            for y in range(0, size_y, TILE):
                density = density_of.load(x, y)
                for at, side in ((0, xl), (size_x - 1, xr)):
                    if x == at:
                        density = density + total(
                            [side[j * size_y + y : j * size_y + y + TILE] for j in range(5)]
                        )
                for at, rows in entering.items():
                    if y <= at < y + TILE:
                        density = density + jnp.where(row_of == at - y, rows[x : x + 1], 0.0)
                pot[1 + x, TILE + y : 2 * TILE + y] = potential_of(
                    density, fluid_at(bits_ref, x, y), pot0_ref[x, y : y + TILE]
                )
        for x, side, own, side0, g in (
            (0, xl, own_left, x0l, G_L),
            (1 + size_x, xr, own_right, x0r, G_R),
        ):
            for y in range(0, size_y, TILE):
                density = side[5 * size_y + y : 5 * size_y + y + TILE] + total(
                    [own[j * size_y + y : j * size_y + y + TILE] for j in range(5)]
                )
                for at, row in ((0, yd), (size_y - 1, yu)):
                    if y <= at < y + TILE:
                        more = row[end + g : end + g + 1]
                        density = density + jnp.where(row_of == at - y, more, 0.0)
                pot[x, TILE + y : 2 * TILE + y] = potential_of(
                    density,
                    side0[size_y + y : size_y + y + TILE] > 0.5,
                    side0[y : y + TILE],
                )
        for y, side, own, side0 in (
            (TILE - 1, yd, own_down, y0d),
            (TILE + size_y, yu, own_up, y0u),
        ):
            density = side[5 * size_x : 6 * size_x] + total(
                [own[j * size_x : (j + 1) * size_x] for j in range(5)]
            )
            value = potential_of(density, side0[size_x : 2 * size_x] > 0.5, side0[:size_x])
            for x in range(size_x):
                pot[1 + x, y : y + 1] = value[x : x + 1]
            for x, rc, g, i in ((0, RC_L, G_L, 0), (1 + size_x, RC_R, G_R, 1)):
                density = side[end + rc : end + rc + 1] + own[end + g : end + g + 1]
                row = 2 * size_x + i
                pot[x, y : y + 1] = potential_of(
                    density, side0[row + 2 : row + 3] > 0.5, side0[row : row + 1]
                )

    post = Layers(post_out, None, size_x, edge2)
    speed = Layers(rest, None, size_x, edge2) if last else None
    collide_layers(edge2, rates, f, bits_ref, pot, sides, post, speed)
    rho = None if last else Layers(rest, None, size_x, edge1)
    stream_layers(edge1, bits_ref, post, Layers(f_out, None, size_x, edge1), rho)

    at = (5 if last else 6) * size_y
    for i, (ref, x, ks, dirs) in enumerate(
        ((left_ref, 0, LEFT, (10, 8)), (right_ref, size_x - 1, RIGHT, (7, 9)))
    ):
        for j, k in enumerate(ks):
            _, ey, ez = VELOCITY[k]
            for y in range(0, size_y, TILE):
                row = j * size_y + y
                ref[row : row + TILE] = roll_z(post.load(x, TILE + y - ey, k), ez)
        ref[at : at + TILE] = jnp.zeros((TILE, size_z), jnp.float32)
        ref[at + C_UP : at + C_UP + 1] = post.row(x, TILE + size_y - 1, dirs[0])
        ref[at + C_DN : at + C_DN + 1] = post.row(x, TILE, dirs[1])
        if not last:
            ref[5 * size_y : 6 * size_y] = rest[i]
            for h, y, leave in ((H_UP, size_y - 1, UP), (H_DN, 0, DOWN)):
                ref[at + h : at + h + 1] = total(
                    [
                        roll_z(post.row(x - VELOCITY[k][0], TILE + y, k), VELOCITY[k][2])
                        for k in leave
                        if 0 <= x - VELOCITY[k][0] < size_x
                    ]
                )


def middle_kernel(first, last, pairs, *refs):
    refs = list(refs)
    take = lambda count: [refs.pop(0) for _ in range(count)]
    rates, bits_ref, pot, post_edge, edge_rest = take(5)
    if first:
        f_ref = take(1)[0]
    else:
        f_edge, f_middle, ya, yb = take(4)
    f_out, up_ref, down_ref, rest = take(4)
    post_middle = take(1)[0]
    size_x, size_y, size_z = bits_ref.shape
    edge2, edge1 = two_layers(size_x), one_layer(size_x)
    sides = None
    if first:
        f = lambda k, x, y: f_ref[k, x, y : y + TILE]
    else:
        yd, yu = take(2)
        from_pairs(pairs, ya, yb, yd, yu)
        sides = (None, None, yd, yu)
        held = Layers(f_edge, f_middle, size_x, edge1)
        f = lambda k, x, y: held.load(x, y, k)
    clear_outside(post_middle, size_x - len(edge2), size_y)
    post = Layers(post_edge, post_middle, size_x, edge2)
    speed = None
    if last:
        speed = Layers(None, None, size_x, [])
        speed.where = {x: (rest, x) for x in range(size_x)}
        for c in range(3):
            for i, x in enumerate(edge2):
                rest[c, x] = edge_rest[c, i]
    inner = [x for x in range(size_x) if x not in edge2]
    collide_layers(inner, rates, f, bits_ref, pot, sides, post, speed)
    rho = None if last else Layers(edge_rest, rest, size_x, edge1)
    inner = [x for x in range(size_x) if x not in edge1]
    stream_layers(inner, bits_ref, post, Layers(None, f_out, size_x, edge1), rho)
    for ref, y, ks in ((up_ref, size_y - 1, UP), (down_ref, 0, DOWN)):
        for j, k in enumerate(ks):
            ex, _, ez = VELOCITY[k]
            for x in range(size_x):
                row = j * size_x + x
                if 0 <= x - ex < size_x:
                    ref[row : row + 1] = post.row(x - ex, TILE + y, k)
                else:
                    ref[row : row + 1] = jnp.zeros((1, size_z), jnp.float32)
            if ez != 0:
                rows = slice(j * size_x, (j + 1) * size_x)
                ref[rows] = roll_z(ref[rows], ez)
        if not last:
            for x in range(size_x):
                ref[5 * size_x + x : 5 * size_x + x + 1] = rho.row(x, y)


def pack_kernel(last, pairs, size_x, size_y, *refs):
    up_in, down_in, xl, xr, own_right, own_left, a_ref, b_ref, up_ref, down_ref = refs
    parts = 5 if last else 6
    at = parts * size_y
    for ref, source, y, ks, c, h in (
        (up_ref, up_in, size_y - 1, UP, C_UP, H_UP),
        (down_ref, down_in, 0, DOWN, C_DN, H_DN),
    ):
        ref[...] = jnp.zeros(ref.shape, jnp.float32)
        ref[: parts * size_x] = source[: parts * size_x]
        for side, own, x, ex, rc, g in (
            (xl, own_left, 0, 1, RC_L, G_L),
            (xr, own_right, size_x - 1, -1, RC_R, G_R),
        ):
            j = [i for i, k in enumerate(ks) if VELOCITY[k][0] == ex][0]
            row = j * size_x + x
            ref[row : row + 1] = side[at + c : at + c + 1]
            if not last:
                row = 5 * size_x + x
                ref[row : row + 1] = source[row : row + 1] + total(
                    [side[i * size_y + y : i * size_y + y + 1] for i in range(5)]
                )
                row = 6 * size_x
                ref[row + rc : row + rc + 1] = side[5 * size_y + y : 5 * size_y + y + 1] + total(
                    [own[i * size_y + y : i * size_y + y + 1] for i in range(5)]
                )
                ref[row + g : row + g + 1] = (
                    side[at + h : at + h + 1] + own[at + c : at + c + 1]
                )
    to_pairs(pairs, up_ref, down_ref, a_ref, b_ref)


def end_kernel(pairs, f_edge, f_middle, bits_ref, xl, xr, ya, yb, out_ref, yd, yu):
    size_x, size_y, size_z = bits_ref.shape
    row_of = lax.broadcasted_iota(jnp.int32, (TILE, size_z), 0)
    from_pairs(pairs, ya, yb, yd, yu)
    held = Layers(f_edge, f_middle, size_x, one_layer(size_x))
    for x in range(size_x):
        for y in range(0, size_y, TILE):
            fluid = fluid_at(bits_ref, x, y)
            for k in range(N):
                value = held.load(x, y, k)
                for at, side, ks in ((0, xl, RIGHT), (size_x - 1, xr, LEFT)):
                    if x == at and k in ks:
                        row = ks.index(k) * size_y + y
                        value = value + side[row : row + TILE]
                for at, side, ks in ((0, yd, UP), (size_y - 1, yu, DOWN)):
                    if y <= at < y + TILE and k in ks:
                        row = ks.index(k) * size_x + x
                        value = value + jnp.where(row_of == at - y, side[row : row + 1], 0.0)
                out_ref[k, x, y : y + TILE] = jnp.where(fluid, value, 0.0)


VMEM = pl.BlockSpec(memory_space=pltpu.VMEM)
SMEM = pl.BlockSpec(memory_space=pltpu.SMEM)
ANY = pl.BlockSpec(memory_space=pl.ANY)


def call(kernel, outs, args, special=None, scratch=(), cost=None):
    special = special or {}
    return pl.pallas_call(
        kernel,
        out_shape=[jax.ShapeDtypeStruct(shape, dtype) for shape, dtype in outs],
        in_specs=[special.get(i, VMEM) for i in range(len(args))],
        out_specs=[VMEM] * len(outs),
        scratch_shapes=[
            pltpu.VMEM(item, jnp.float32) if isinstance(item, tuple) else item for item in scratch
        ],
        compiler_params=pltpu.CompilerParams(vmem_limit_bytes=16 * 2**20),
        cost_estimate=cost,
    )(*args)


def shift(forward, backward, axis):
    count = lax.axis_size(axis)
    ahead = [(i, (i + 1) % count) for i in range(count)]
    return (
        lax.ppermute(forward, axis, ahead),
        lax.ppermute(backward, axis, [(b, a) for a, b in ahead]),
    )


def exchange(pairs, a, b, axis):
    if not pairs:
        return shift(a, b, axis)
    count = lax.axis_size(axis)
    partners = [
        [(i, (i + (1 if i % 2 == parity else -1)) % count) for i in range(count)]
        for parity in range(2)
    ]
    b = lax.ppermute(b, axis, partners[1])
    return lax.ppermute(a, axis, partners[0]), b


def per_device(populations, fluid_mask, wet_class, wall_potential, relax_rates):
    size_x, size_y, size_z = fluid_mask.shape
    f32, i32 = jnp.float32, jnp.int32
    pairs = lax.axis_size("gy") % 2 == 0
    whole = ((size_x, size_y, size_z), f32)
    rows = lambda count: ((count, size_z), f32)
    fields = lambda count: ((N, count, size_y, size_z), f32)
    padded = (size_x + 2, size_y + PAD, size_z)
    start_rows = rows(2 * size_x + TILE)

    f, mask, pot0, right, left = call(
        start_kernel,
        [fields(size_x), whole, whole, rows(2 * size_y), rows(2 * size_y)],
        (populations, fluid_mask, wet_class, wall_potential),
        special={i: ANY for i in range(4)},
        scratch=[
            pltpu.VMEM(fluid_mask.shape, i32),
            pltpu.VMEM(wet_class.shape, i32),
            pltpu.SMEM(wall_potential.shape, f32),
            pltpu.SemaphoreType.DMA((N,)),
            pltpu.SemaphoreType.DMA((3,)),
        ],
    )
    x0l, x0r = shift(right, left, "gx")
    a, b = call(
        functools.partial(start_pack_kernel, pairs),
        [start_rows] * 2,
        (pot0, mask, x0l, x0r),
        scratch=[start_rows[0]] * 2,
    )
    a, b = exchange(pairs, a, b, "gy")
    bits, y0d, y0u = call(
        functools.partial(bits_kernel, pairs),
        [((size_x, size_y, size_z), i32), start_rows, start_rows],
        (mask, x0l, x0r, a, b),
        scratch=[padded],
    )
    edge2, edge1 = len(two_layers(size_x)), len(one_layer(size_x))
    operations = 400 * size_x * size_y * size_z
    cost = pl.CostEstimate(flops=operations, bytes_accessed=4 * operations // 20, transcendentals=0)
    held, sent = (f,), ()
    for step in range(STEPS):
        first, last = step == 0, step == STEPS - 1
        parts = 5 if last else 6
        x_rows, y_rows = rows(parts * size_y + TILE), rows(parts * size_x + (0 if last else TILE))
        halo_rows = (6 * size_x + TILE, size_z)
        pot, post, f_edge, right, left, rest = call(
            functools.partial(edge_kernel, first, last, pairs),
            [
                (padded, f32),
                ((N, edge2, size_y + PAD, size_z), f32),
                fields(edge1),
                x_rows,
                x_rows,
                ((3, edge2, size_y, size_z) if last else (edge1, size_y, size_z), f32),
            ],
            (relax_rates, bits, pot0, x0l, x0r, y0d, y0u, *held, *sent),
            special={0: SMEM},
            scratch=[] if first else [halo_rows] * 4,
            cost=cost,
        )
        xl, xr = shift(right, left, "gx")
        f_middle, up, down, more = call(
            functools.partial(middle_kernel, first, last, pairs),
            [
                fields(size_x - edge1),
                y_rows,
                y_rows,
                ((3, *whole[0]) if last else (size_x - edge1, size_y, size_z), f32),
            ],
            (relax_rates, bits, pot, post, rest, *held[:2], *sent[2:4]),
            special={0: SMEM},
            scratch=[(N, size_x - edge2, size_y + PAD, size_z)]
            + ([] if first else [halo_rows] * 2),
            cost=cost,
        )
        a, b = call(
            functools.partial(pack_kernel, last, pairs, size_x, size_y),
            [y_rows, y_rows],
            (up, down, xl, xr, right, left),
            scratch=[y_rows[0]] * 2,
        )
        ya, yb = exchange(pairs, a, b, "gy")
        held = (f_edge, f_middle, rest, more)
        sent = (xl, xr, ya, yb, right, left, a, b)
    (out,) = call(
        functools.partial(end_kernel, pairs),
        [fields(size_x)],
        (f_edge, f_middle, bits, xl, xr, ya, yb),
        scratch=[y_rows[0]] * 2,
    )
    return out, more


def solution(mesh):
    return jax.shard_map(
        per_device,
        mesh=mesh,
        in_specs=(
            P(None, ("groups", "gx"), "gy", None),
            P(("groups", "gx"), "gy", None),
            P(("groups", "gx"), "gy", None),
            P("groups"),
            P(),
        ),
        out_specs=(P(None, ("groups", "gx"), "gy", None), P(None, ("groups", "gx"), "gy", None)),
        check_vma=False,
    )
```

time: 64.8 us -> 62.6 us (0.966)
  the two profiles are of different devices: /device:TPU:1 before, /device:TPU:0 now
where the time goes in v2:
time: 62.6 us; the launch traced here: 62.4 us
  starting transfers between devices  29.5 us (47%)
  waiting for transfers between devices  14.9 us (24%)
  Pallas kernels  13.6 us (22%)
  local copies, waits for them, and re-layouts  3.62 us (6%)
  between operations  0.76 us (1%)
    pallas_call x16, Pallas kernels, call(): pl.pallas_call(kernel, out_shape=[jax.ShapeDtypeStruct(shape, dtype) for...  13.6 us
    ppermute x5, starting transfers between devices, shift(): lax.ppermute(backward, axis, [(b, a) for a, b in ahead])  12.4 us
    ppermute x5, starting transfers between devices, exchange(): b = lax.ppermute(b, axis, partners[1])  8.44 us
    ppermute x5, starting transfers between devices, shift(): lax.ppermute(forward, axis, ahead)  8.28 us
    ppermute x5, waiting for transfers between devices, exchange(): b = lax.ppermute(b, axis, partners[1])  8.08 us
    ppermute x5, waiting for transfers between devices, shift(): lax.ppermute(forward, axis, ahead)  5.42 us
    unnamed x10, local copies, waits for them, and re-layouts  3.62 us
    ppermute x5, waiting for transfers between devices, shift(): lax.ppermute(backward, axis, [(b, a) for a, b in ahead])  1.4 us
  transfers between devices with their start and end apart: 20, of which 15 were waited for; matrix products, arithmetic and copies ran while one was open for 0% of the time, Pallas kernels for 9%

profile of v2, /device:TPU:0, one launch (start us, length us, event | category | flops | bytes accessed | tf_op | source)
XLA Modules:
  0.0 62.4 jit_solution(12902866688892085599)
XLA Ops:
  0.6 0.0 copy-start
  0.6 1.3 %copy-done = f32[19,8,16,128]{3,2,1,0:T(8,128)S(1)} copy-done((f32[19,8,16,128]{3,2,1,0:T(8,128)S(1)}, f32[19,8,16,128]{3,2,1,0:T(8,128)}, u32[]{:S(2)}) %copy-start) | copy-done | bytes 1245208
  1.9 0.0 copy-start.1
  1.9 0.8 %copy-done.1 = s32[8,16,128]{2,1,0:T(8,128)S(1)} copy-done((s32[8,16,128]{2,1,0:T(8,128)S(1)}, s32[8,16,128]{2,1,0:T(8,128)}, u32[]{:S(2)}) %copy-start.1) | copy-done | bytes 65560
  2.8 0.0 copy-start.2
  2.8 0.8 %copy-done.2 = s32[8,16,128]{2,1,0:T(8,128)S(1)} copy-done((s32[8,16,128]{2,1,0:T(8,128)S(1)}, s32[8,16,128]{2,1,0:T(8,128)}, u32[]{:S(2)}) %copy-start.2) | copy-done | bytes 65560
  3.6 0.0 copy-start.4
  3.6 0.7 %copy-done.4 = f32[4]{0:T(128)S(1)} copy-done((f32[4]{0:T(128)S(1)}, f32[4]{0:T(128)}, u32[]{:S(2)}) %copy-start.4) | copy-done | bytes 40
  4.3 0.0 copy-start.3
  4.3 2.1 %shard_map.68 = (f32[19,8,16,128]{3,2,1,0:T(8,128)S(1)}, f32[8,16,128]{2,1,0:T(8,128)S(1)}, f32[8,16,128]{2,1,0:T(8,128)S(1)}, f32[32,128]{1,0:T(8,128)S(1)}, f32[32,128]{1,0:T(8,128)S(1)}) custom-call(f32[19,8,16,128]{3,2,1,0:T(8,128)S(1)} %copy-done, s32[8,16,128]{2,1,0:T(8,128)S(1)} %copy-done.1, s32[8,16,128]{2,1,0:T(8,128)S(1)} %copy-done.2, f32[4]{0:T(128)S(1)} %copy-done.4), custom_call_target="tpu_custom_call" | custom-call | tf_op jit(solution)/shard_map/pallas_call | solution.py:569
  6.4 3.1 %collective-permute-start = (f32[32,128]{1,0:T(8,128)S(1)}, f32[32,128]{1,0:T(8,128)S(1)}, u32[]{:S(2)}, u32[]{:S(2)}) collective-permute-start(f32[32,128]{1,0:T(8,128)S(1)} %get-tuple-element.61), channel_id=1, source_target_pairs={{0,4},{4,8},{8,12},{12,0},{1,5},{5,9},{9,13},{13,1},{2,6},{6,10},{... | collective-permute-start | bytes 49160 | tf_op jit(solution)/shard_map/ppermute | solution.py:586
  9.5 2.1 %collective-permute-start.1 = (f32[32,128]{1,0:T(8,128)S(1)}, f32[32,128]{1,0:T(8,128)S(1)}, u32[]{:S(2)}, u32[]{:S(2)}) collective-permute-start(f32[32,128]{1,0:T(8,128)S(1)} %get-tuple-element.62), channel_id=1, source_target_pairs={{4,0},{8,4},{12,8},{0,12},{5,1},{9,5},{13,9},{1,13},{6,2},{10,6},{... | collective-permute-start | bytes 49160 | tf_op jit(solution)/shard_map/ppermute | solution.py:587
  11.6 1.8 %collective-permute-done.from_left.x0l.refs_3_ = f32[32,128]{1,0:T(8,128)S(1)} collective-permute-done((f32[32,128]{1,0:T(8,128)S(1)}, f32[32,128]{1,0:T(8,128)S(1)}, u32[]{:S(2)}, u32[]{:S(2)}) %collective-permute-start) | collective-permute-done | bytes 16416 | tf_op jit(solution)/shard_map/ppermute | solution.py:586
  13.3 0.1 collective-permute-done.1.from_right.x0r.refs_4_
  13.4 0.1 collective-permute-start.2
  13.5 1.6 %collective-permute-start.3 = (f32[24,128]{1,0:T(8,128)S(1)}, f32[24,128]{1,0:T(8,128)S(1)}, u32[]{:S(2)}, u32[]{:S(2)}) collective-permute-start(f32[24,128]{1,0:T(8,128)S(1)} %get-tuple-element.65), channel_id=1, source_target_pairs={{0,3},{1,2},{2,1},{3,0},{4,7},{5,6},{6,5},{7,4},{8,11},{9,10},{10,... | collective-permute-start | bytes 36872 | tf_op jit(solution)/shard_map/ppermute | solution.py:599
  15.1 0.0 collective-permute-done.2.a_ref
  15.1 1.5 %collective-permute-done.3.b_ref = f32[24,128]{1,0:T(8,128)S(1)} collective-permute-done((f32[24,128]{1,0:T(8,128)S(1)}, f32[24,128]{1,0:T(8,128)S(1)}, u32[]{:S(2)}, u32[]{:S(2)}) %collective-permute-start.3) | collective-permute-done | bytes 12320 | tf_op jit(solution)/shard_map/ppermute | solution.py:599
  16.7 0.2 shard_map.70
  16.9 0.0 copy-done.3
  16.9 1.1 %shard_map.71 = (f32[10,32,128]{2,1,0:T(8,128)S(1)}, f32[19,4,32,128]{3,2,1,0:T(8,128)S(1)}, f32[19,2,16,128]{3,2,1,0:T(8,128)S(1)}, f32[104,128]{1,0:T(8,128)S(...) custom-call(f32[19]{0:T(128)S(1)} %copy-done.3, s32[8,16,128]{2,1,0:T(8,128)S(1)} %get-tuple-element.66.refs_1_.bits_ref, ...), custom_call_target="tpu_custom_call" | custom-call | flops 6553600 | bytes 1310720 | tf_op jit(solution)/shard_map/pallas_call | solution.py:569
  18.0 1.5 %collective-permute-start.4 = (f32[104,128]{1,0:T(8,128)S(1)}, f32[104,128]{1,0:T(8,128)S(1)}, u32[]{:S(2)}, u32[]{:S(2)}) collective-permute-start(f32[104,128]{1,0:T(8,128)S(1)} %get-tuple-element.76.refs_4_.refs_15_), channel_id=1, source_target_pairs={{0,4},{4,8},{8,12},{12,0},{1,5},{5,9},{9,13},{13,1},{2,6},{6,10},{... | collective-permute-start | bytes 159752 | tf_op jit(solution)/shard_map/ppermute | solution.py:586
  19.5 2.4 %collective-permute-start.5 = (f32[104,128]{1,0:T(8,128)S(1)}, f32[104,128]{1,0:T(8,128)S(1)}, u32[]{:S(2)}, u32[]{:S(2)}) collective-permute-start(f32[104,128]{1,0:T(8,128)S(1)} %get-tuple-element.77.refs_5_.refs_16_), channel_id=1, source_target_pairs={{4,0},{8,4},{12,8},{0,12},{5,1},{9,5},{13,9},{1,13},{6,2},{10,6},{... | collective-permute-start | bytes 159752 | tf_op jit(solution)/shard_map/ppermute | solution.py:587
  21.9 1.2 %shard_map.72 = (f32[19,6,16,128]{3,2,1,0:T(8,128)S(1)}, f32[56,128]{1,0:T(8,128)S(1)}, f32[56,128]{1,0:T(8,128)S(1)}, f32[6,16,128]{2,1,0:T(8,128)S(1)}) custom-call(f32[19]{0:T(128)S(1)} %copy-done.3, s32[8,16,128]{2,1,0:T(8,128)S(1)} %get-tuple-element.66.refs_1_.bits_ref, f32[10,32,128]{2,1,0:T(8,128)S(1)} %get-tuple-element.71.refs_2_, ...), custom_call_target="tpu_custom_call" | custom-call | flops 6553600 | bytes 1310720 | tf_op jit(solution)/shard_map/pallas_call | solution.py:569
  23.1 1.2 %collective-permute-done.4.refs_2_.refs_11_ = f32[104,128]{1,0:T(8,128)S(1)} collective-permute-done((f32[104,128]{1,0:T(8,128)S(1)}, f32[104,128]{1,0:T(8,128)S(1)}, u32[]{:S(2)}, u32[]{:S(2)}) %collective-permute-start.4) | collective-permute-done | bytes 53280 | tf_op jit(solution)/shard_map/ppermute | solution.py:586
  24.3 0.4 collective-permute-done.5.refs_3_.refs_12_
  24.8 0.1 collective-permute-start.6
  24.8 1.6 %collective-permute-start.7 = (f32[56,128]{1,0:T(8,128)S(1)}, f32[56,128]{1,0:T(8,128)S(1)}, u32[]{:S(2)}, u32[]{:S(2)}) collective-permute-start(f32[56,128]{1,0:T(8,128)S(1)} %get-tuple-element.81.refs_18_), channel_id=1, source_target_pairs={{0,3},{1,2},{2,1},{3,0},{4,7},{5,6},{6,5},{7,4},{8,11},{9,10},{10,... | collective-permute-start | bytes 86024 | tf_op jit(solution)/shard_map/ppermute | solution.py:599
  26.4 0.0 collective-permute-done.6.refs_13_.refs_7_
  26.4 1.8 %collective-permute-done.7.refs_14_.refs_8_ = f32[56,128]{1,0:T(8,128)S(1)} collective-permute-done((f32[56,128]{1,0:T(8,128)S(1)}, f32[56,128]{1,0:T(8,128)S(1)}, u32[]{:S(2)}, u32[]{:S(2)}) %collective-permute-start.7) | collective-permute-done | bytes 28704 | tf_op jit(solution)/shard_map/ppermute | solution.py:599
  28.2 1.1 %shard_map.74 = (f32[10,32,128]{2,1,0:T(8,128)S(1)}, f32[19,4,32,128]{3,2,1,0:T(8,128)S(1)}, f32[19,2,16,128]{3,2,1,0:T(8,128)S(1)}, f32[104,128]{1,0:T(8,128)S(...) custom-call(f32[19]{0:T(128)S(1)} %copy-done.3, s32[8,16,128]{2,1,0:T(8,128)S(1)} %get-tuple-element.66.refs_1_.bits_ref, ...), custom_call_target="tpu_custom_call" | custom-call | flops 6553600 | bytes 1310720 | tf_op jit(solution)/shard_map/pallas_call | solution.py:569
  29.4 1.2 %collective-permute-start.8 = (f32[104,128]{1,0:T(8,128)S(1)}, f32[104,128]{1,0:T(8,128)S(1)}, u32[]{:S(2)}, u32[]{:S(2)}) collective-permute-start(f32[104,128]{1,0:T(8,128)S(1)} %get-tuple-element.88.refs_4_.refs_15_), channel_id=1, source_target_pairs={{0,4},{4,8},{8,12},{12,0},{1,5},{5,9},{9,13},{13,1},{2,6},{6,10},{... | collective-permute-start | bytes 159752 | tf_op jit(solution)/shard_map/ppermute | solution.py:586
  30.6 2.7 %collective-permute-start.9 = (f32[104,128]{1,0:T(8,128)S(1)}, f32[104,128]{1,0:T(8,128)S(1)}, u32[]{:S(2)}, u32[]{:S(2)}) collective-permute-start(f32[104,128]{1,0:T(8,128)S(1)} %get-tuple-element.89.refs_5_.refs_16_), channel_id=1, source_target_pairs={{4,0},{8,4},{12,8},{0,12},{5,1},{9,5},{13,9},{1,13},{6,2},{10,6},{... | collective-permute-start | bytes 159752 | tf_op jit(solution)/shard_map/ppermute | solution.py:587
  33.2 1.2 %shard_map.75 = (f32[19,6,16,128]{3,2,1,0:T(8,128)S(1)}, f32[56,128]{1,0:T(8,128)S(1)}, f32[56,128]{1,0:T(8,128)S(1)}, f32[6,16,128]{2,1,0:T(8,128)S(1)}) custom-call(f32[19]{0:T(128)S(1)} %copy-done.3, s32[8,16,128]{2,1,0:T(8,128)S(1)} %get-tuple-element.66.refs_1_.bits_ref, f32[10,32,128]{2,1,0:T(8,128)S(1)} %get-tuple-element.83.refs_2_, ...), custom_call_target="tpu_custom_call" | custom-call | flops 6553600 | bytes 1310720 | tf_op jit(solution)/shard_map/pallas_call | solution.py:569
  34.4 1.2 %collective-permute-done.8.refs_2_.refs_11_ = f32[104,128]{1,0:T(8,128)S(1)} collective-permute-done((f32[104,128]{1,0:T(8,128)S(1)}, f32[104,128]{1,0:T(8,128)S(1)}, u32[]{:S(2)}, u32[]{:S(2)}) %collective-permute-start.8) | collective-permute-done | bytes 53280 | tf_op jit(solution)/shard_map/ppermute | solution.py:586
  35.6 0.3 collective-permute-done.9.refs_3_.refs_12_
  35.9 0.1 collective-permute-start.10
  36.0 1.7 %collective-permute-start.11 = (f32[56,128]{1,0:T(8,128)S(1)}, f32[56,128]{1,0:T(8,128)S(1)}, u32[]{:S(2)}, u32[]{:S(2)}) collective-permute-start(f32[56,128]{1,0:T(8,128)S(1)} %get-tuple-element.93.refs_18_), channel_id=1, source_target_pairs={{0,3},{1,2},{2,1},{3,0},{4,7},{5,6},{6,5},{7,4},{8,11},{9,10},{10,... | collective-permute-start | bytes 86024 | tf_op jit(solution)/shard_map/ppermute | solution.py:599
  37.7 0.0 collective-permute-done.10.refs_13_.refs_7_
  37.7 1.6 %collective-permute-done.11.refs_14_.refs_8_ = f32[56,128]{1,0:T(8,128)S(1)} collective-permute-done((f32[56,128]{1,0:T(8,128)S(1)}, f32[56,128]{1,0:T(8,128)S(1)}, u32[]{:S(2)}, u32[]{:S(2)}) %collective-permute-start.11) | collective-permute-done | bytes 28704 | tf_op jit(solution)/shard_map/ppermute | solution.py:599
  39.3 1.1 %shard_map.77 = (f32[10,32,128]{2,1,0:T(8,128)S(1)}, f32[19,4,32,128]{3,2,1,0:T(8,128)S(1)}, f32[19,2,16,128]{3,2,1,0:T(8,128)S(1)}, f32[104,128]{1,0:T(8,128)S(...) custom-call(f32[19]{0:T(128)S(1)} %copy-done.3, s32[8,16,128]{2,1,0:T(8,128)S(1)} %get-tuple-element.66.refs_1_.bits_ref, ...), custom_call_target="tpu_custom_call" | custom-call | flops 6553600 | bytes 1310720 | tf_op jit(solution)/shard_map/pallas_call | solution.py:569
  40.5 1.1 %collective-permute-start.12 = (f32[104,128]{1,0:T(8,128)S(1)}, f32[104,128]{1,0:T(8,128)S(1)}, u32[]{:S(2)}, u32[]{:S(2)}) collective-permute-start(f32[104,128]{1,0:T(8,128)S(1)} %get-tuple-element.100.refs_4_.refs_15_), channel_id=1, source_target_pairs={{0,4},{4,8},{8,12},{12,0},{1,5},{5,9},{9,13},{13,1},{2,6},{6,10},{... | collective-permute-start | bytes 159752 | tf_op jit(solution)/shard_map/ppermute | solution.py:586
  41.6 2.8 %collective-permute-start.13 = (f32[104,128]{1,0:T(8,128)S(1)}, f32[104,128]{1,0:T(8,128)S(1)}, u32[]{:S(2)}, u32[]{:S(2)}) collective-permute-start(f32[104,128]{1,0:T(8,128)S(1)} %get-tuple-element.101.refs_5_.refs_16_), channel_id=1, source_target_pairs={{4,0},{8,4},{12,8},{0,12},{5,1},{9,5},{13,9},{1,13},{6,2},{10,6},{... | collective-permute-start | bytes 159752 | tf_op jit(solution)/shard_map/ppermute | solution.py:587
  44.3 1.2 %shard_map.78 = (f32[19,6,16,128]{3,2,1,0:T(8,128)S(1)}, f32[56,128]{1,0:T(8,128)S(1)}, f32[56,128]{1,0:T(8,128)S(1)}, f32[6,16,128]{2,1,0:T(8,128)S(1)}) custom-call(f32[19]{0:T(128)S(1)} %copy-done.3, s32[8,16,128]{2,1,0:T(8,128)S(1)} %get-tuple-element.66.refs_1_.bits_ref, f32[10,32,128]{2,1,0:T(8,128)S(1)} %get-tuple-element.95.refs_2_, ...), custom_call_target="tpu_custom_call" | custom-call | flops 6553600 | bytes 1310720 | tf_op jit(solution)/shard_map/pallas_call | solution.py:569
  45.5 1.0 %collective-permute-done.12.refs_2_.refs_11_ = f32[104,128]{1,0:T(8,128)S(1)} collective-permute-done((f32[104,128]{1,0:T(8,128)S(1)}, f32[104,128]{1,0:T(8,128)S(1)}, u32[]{:S(2)}, u32[]{:S(2)}) %collective-permute-start.12) | collective-permute-done | bytes 53280 | tf_op jit(solution)/shard_map/ppermute | solution.py:586
  46.6 0.3 collective-permute-done.13.refs_3_.refs_12_
  46.9 0.1 collective-permute-start.14
  47.0 1.7 %collective-permute-start.15 = (f32[56,128]{1,0:T(8,128)S(1)}, f32[56,128]{1,0:T(8,128)S(1)}, u32[]{:S(2)}, u32[]{:S(2)}) collective-permute-start(f32[56,128]{1,0:T(8,128)S(1)} %get-tuple-element.105.refs_18_), channel_id=1, source_target_pairs={{0,3},{1,2},{2,1},{3,0},{4,7},{5,6},{6,5},{7,4},{8,11},{9,10},{10,... | collective-permute-start | bytes 86024 | tf_op jit(solution)/shard_map/ppermute | solution.py:599
  48.7 0.0 collective-permute-done.14.refs_13_.refs_7_
  48.7 1.6 %collective-permute-done.15.refs_14_.refs_8_ = f32[56,128]{1,0:T(8,128)S(1)} collective-permute-done((f32[56,128]{1,0:T(8,128)S(1)}, f32[56,128]{1,0:T(8,128)S(1)}, u32[]{:S(2)}, u32[]{:S(2)}) %collective-permute-start.15) | collective-permute-done | bytes 28704 | tf_op jit(solution)/shard_map/ppermute | solution.py:599
  50.3 1.2 %shard_map.80 = (f32[10,32,128]{2,1,0:T(8,128)S(1)}, f32[19,4,32,128]{3,2,1,0:T(8,128)S(1)}, f32[19,2,16,128]{3,2,1,0:T(8,128)S(1)}, f32[88,128]{1,0:T(8,128)S(1...) custom-call(f32[19]{0:T(128)S(1)} %copy-done.3, s32[8,16,128]{2,1,0:T(8,128)S(1)} %get-tuple-element.66.refs_1_.bits_ref, ...), custom_call_target="tpu_custom_call" | custom-call | flops 6553600 | bytes 1310720 | tf_op jit(solution)/shard_map/pallas_call | solution.py:569
  51.5 1.4 %collective-permute-start.16 = (f32[88,128]{1,0:T(8,128)S(1)}, f32[88,128]{1,0:T(8,128)S(1)}, u32[]{:S(2)}, u32[]{:S(2)}) collective-permute-start(f32[88,128]{1,0:T(8,128)S(1)} %get-tuple-element.111.refs_4_), channel_id=1, source_target_pairs={{0,4},{4,8},{8,12},{12,0},{1,5},{5,9},{9,13},{13,1},{2,6},{6,10},{... | collective-permute-start | bytes 135176 | tf_op jit(solution)/shard_map/ppermute | solution.py:586
  52.9 2.5 %collective-permute-start.17 = (f32[88,128]{1,0:T(8,128)S(1)}, f32[88,128]{1,0:T(8,128)S(1)}, u32[]{:S(2)}, u32[]{:S(2)}) collective-permute-start(f32[88,128]{1,0:T(8,128)S(1)} %get-tuple-element.112.refs_5_), channel_id=1, source_target_pairs={{4,0},{8,4},{12,8},{0,12},{5,1},{9,5},{13,9},{1,13},{6,2},{10,6},{... | collective-permute-start | bytes 135176 | tf_op jit(solution)/shard_map/ppermute | solution.py:587
  55.4 1.8 %shard_map.81 = (f32[19,6,16,128]{3,2,1,0:T(8,128)S(1)}, f32[40,128]{1,0:T(8,128)S(1)}, f32[40,128]{1,0:T(8,128)S(1)}, f32[3,8,16,128]{3,2,1,0:T(8,128)}) custom-call(f32[19]{0:T(128)S(1)} %copy-done.3, s32[8,16,128]{2,1,0:T(8,128)S(1)} %get-tuple-element.66.refs_1_.bits_ref, f32[10,32,128]{2,1,0:T(8,128)S(1)} %get-tuple-element.107.refs_2_, ...), custom_call_target="tpu_custom_call" | custom-call | flops 6553600 | bytes 1310720 | tf_op jit(solution)/shard_map/pallas_call | solution.py:569
  57.2 0.2 collective-permute-done.16.refs_2_.xl
  57.4 0.4 collective-permute-done.17.refs_3_.xr
  57.8 0.1 collective-permute-start.18
  57.9 1.7 %collective-permute-start.19 = (f32[40,128]{1,0:T(8,128)S(1)}, f32[40,128]{1,0:T(8,128)S(1)}, u32[]{:S(2)}, u32[]{:S(2)}) collective-permute-start(f32[40,128]{1,0:T(8,128)S(1)} %get-tuple-element.116), channel_id=1, source_target_pairs={{0,3},{1,2},{2,1},{3,0},{4,7},{5,6},{6,5},{7,4},{8,11},{9,10},{10,... | collective-permute-start | bytes 61448 | tf_op jit(solution)/shard_map/ppermute | solution.py:599
  59.6 0.0 collective-permute-done.18.ya
  59.6 1.5 %collective-permute-done.19.yb = f32[40,128]{1,0:T(8,128)S(1)} collective-permute-done((f32[40,128]{1,0:T(8,128)S(1)}, f32[40,128]{1,0:T(8,128)S(1)}, u32[]{:S(2)}, u32[]{:S(2)}) %collective-permute-start.19) | collective-permute-done | bytes 20512 | tf_op jit(solution)/shard_map/ppermute | solution.py:599
  61.2 1.2 %shard_map.83 = f32[19,8,16,128]{3,2,1,0:T(8,128)} custom-call(f32[19,2,16,128]{3,2,1,0:T(8,128)S(1)} %get-tuple-element.106.f_edge, f32[19,6,16,128]{3,2,1,0:T(8,128)S(1)} %get-tuple-element.110.f_middle, s32[8,16,128]{2,1,0:T(8,128)S(1)} %get-tuple-element.66.refs_1_.bits_ref, f32[88,128]{1,0:T(8,128)S(1)} %collective-permute-done.16.refs_2_.xl, ...), custom_call_target="tpu_custom_call" | custom-call | tf_op jit(solution)/shard_map/pallas_call | solution.py:569
  (5 shorter events, 0.1 us)
Async XLA Ops:
  0.6 1.3 %copy-start = (f32[19,8,16,128]{3,2,1,0:T(8,128)S(1)}, f32[19,8,16,128]{3,2,1,0:T(8,128)}, u32[]{:S(2)}) copy-start(f32[19,8,16,128]{3,2,1,0:T(8,128)} %f_hbm.1) | copy-start | bytes 3735556
  1.9 0.8 %copy-start.1 = (s32[8,16,128]{2,1,0:T(8,128)S(1)}, s32[8,16,128]{2,1,0:T(8,128)}, u32[]{:S(2)}) copy-start(s32[8,16,128]{2,1,0:T(8,128)} %mask_hbm.1) | copy-start | bytes 196612
  2.8 0.8 %copy-start.2 = (s32[8,16,128]{2,1,0:T(8,128)S(1)}, s32[8,16,128]{2,1,0:T(8,128)}, u32[]{:S(2)}) copy-start(s32[8,16,128]{2,1,0:T(8,128)} %wet_hbm.1) | copy-start | bytes 196612
  3.6 0.7 %copy-start.4 = (f32[4]{0:T(128)S(1)}, f32[4]{0:T(128)}, u32[]{:S(2)}) copy-start(f32[4]{0:T(128)} %wall_hbm.1) | copy-start | bytes 52
  4.3 12.7 %copy-start.3 = (f32[19]{0:T(128)S(1)}, f32[19]{0:T(128)}, u32[]{:S(2)}) copy-start(f32[19]{0:T(128)} %refs_0_.15) | copy-start | bytes 232
  6.4 6.9 %collective-permute-start = (f32[32,128]{1,0:T(8,128)S(1)}, f32[32,128]{1,0:T(8,128)S(1)}, u32[]{:S(2)}, u32[]{:S(2)}) collective-permute-start(f32[32,128]{1,0:T(8,128)S(1)} %get-tuple-element.61), channel_id=1, source_target_pairs={{0,4},{4,8},{8,12},{12,0},{1,5},{5,9},{9,13},{13,1},{2,6},{6,10},{... | collective-permute-start | bytes 49160 | tf_op jit(solution)/shard_map/ppermute | solution.py:586
  9.5 3.9 %collective-permute-start.1 = (f32[32,128]{1,0:T(8,128)S(1)}, f32[32,128]{1,0:T(8,128)S(1)}, u32[]{:S(2)}, u32[]{:S(2)}) collective-permute-start(f32[32,128]{1,0:T(8,128)S(1)} %get-tuple-element.62), channel_id=1, source_target_pairs={{4,0},{8,4},{12,8},{0,12},{5,1},{9,5},{13,9},{1,13},{6,2},{10,6},{... | collective-permute-start | bytes 49160 | tf_op jit(solution)/shard_map/ppermute | solution.py:587
  13.4 1.7 %collective-permute-start.2 = (f32[24,128]{1,0:T(8,128)S(1)}, f32[24,128]{1,0:T(8,128)S(1)}, u32[]{:S(2)}, u32[]{:S(2)}) collective-permute-start(f32[24,128]{1,0:T(8,128)S(1)} %get-tuple-element.64), channel_id=1, source_target_pairs={{0,1},{1,0},{2,3},{3,2},{4,5},{5,4},{6,7},{7,6},{8,9},{9,8},{10,11... | collective-permute-start | bytes 36872 | tf_op jit(solution)/shard_map/ppermute | solution.py:600
  13.5 3.2 %collective-permute-start.3 = (f32[24,128]{1,0:T(8,128)S(1)}, f32[24,128]{1,0:T(8,128)S(1)}, u32[]{:S(2)}, u32[]{:S(2)}) collective-permute-start(f32[24,128]{1,0:T(8,128)S(1)} %get-tuple-element.65), channel_id=1, source_target_pairs={{0,3},{1,2},{2,1},{3,0},{4,7},{5,6},{6,5},{7,4},{8,11},{9,10},{10,... | collective-permute-start | bytes 36872 | tf_op jit(solution)/shard_map/ppermute | solution.py:599
  18.0 6.3 %collective-permute-start.4 = (f32[104,128]{1,0:T(8,128)S(1)}, f32[104,128]{1,0:T(8,128)S(1)}, u32[]{:S(2)}, u32[]{:S(2)}) collective-permute-start(f32[104,128]{1,0:T(8,128)S(1)} %get-tuple-element.76.refs_4_.refs_15_), channel_id=1, source_target_pairs={{0,4},{4,8},{8,12},{12,0},{1,5},{5,9},{9,13},{13,1},{2,6},{6,10},{... | collective-permute-start | bytes 159752 | tf_op jit(solution)/shard_map/ppermute | solution.py:586
  19.5 5.3 %collective-permute-start.5 = (f32[104,128]{1,0:T(8,128)S(1)}, f32[104,128]{1,0:T(8,128)S(1)}, u32[]{:S(2)}, u32[]{:S(2)}) collective-permute-start(f32[104,128]{1,0:T(8,128)S(1)} %get-tuple-element.77.refs_5_.refs_16_), channel_id=1, source_target_pairs={{4,0},{8,4},{12,8},{0,12},{5,1},{9,5},{13,9},{1,13},{6,2},{10,6},{... | collective-permute-start | bytes 159752 | tf_op jit(solution)/shard_map/ppermute | solution.py:587
  24.8 1.7 %collective-permute-start.6 = (f32[56,128]{1,0:T(8,128)S(1)}, f32[56,128]{1,0:T(8,128)S(1)}, u32[]{:S(2)}, u32[]{:S(2)}) collective-permute-start(f32[56,128]{1,0:T(8,128)S(1)} %get-tuple-element.80.refs_17_), channel_id=1, source_target_pairs={{0,1},{1,0},{2,3},{3,2},{4,5},{5,4},{6,7},{7,6},{8,9},{9,8},{10,11... | collective-permute-start | bytes 86024 | tf_op jit(solution)/shard_map/ppermute | solution.py:600
  24.8 3.4 %collective-permute-start.7 = (f32[56,128]{1,0:T(8,128)S(1)}, f32[56,128]{1,0:T(8,128)S(1)}, u32[]{:S(2)}, u32[]{:S(2)}) collective-permute-start(f32[56,128]{1,0:T(8,128)S(1)} %get-tuple-element.81.refs_18_), channel_id=1, source_target_pairs={{0,3},{1,2},{2,1},{3,0},{4,7},{5,6},{6,5},{7,4},{8,11},{9,10},{10,... | collective-permute-start | bytes 86024 | tf_op jit(solution)/shard_map/ppermute | solution.py:599
  29.4 6.2 %collective-permute-start.8 = (f32[104,128]{1,0:T(8,128)S(1)}, f32[104,128]{1,0:T(8,128)S(1)}, u32[]{:S(2)}, u32[]{:S(2)}) collective-permute-start(f32[104,128]{1,0:T(8,128)S(1)} %get-tuple-element.88.refs_4_.refs_15_), channel_id=1, source_target_pairs={{0,4},{4,8},{8,12},{12,0},{1,5},{5,9},{9,13},{13,1},{2,6},{6,10},{... | collective-permute-start | bytes 159752 | tf_op jit(solution)/shard_map/ppermute | solution.py:586
  30.6 5.3 %collective-permute-start.9 = (f32[104,128]{1,0:T(8,128)S(1)}, f32[104,128]{1,0:T(8,128)S(1)}, u32[]{:S(2)}, u32[]{:S(2)}) collective-permute-start(f32[104,128]{1,0:T(8,128)S(1)} %get-tuple-element.89.refs_5_.refs_16_), channel_id=1, source_target_pairs={{4,0},{8,4},{12,8},{0,12},{5,1},{9,5},{13,9},{1,13},{6,2},{10,6},{... | collective-permute-start | bytes 159752 | tf_op jit(solution)/shard_map/ppermute | solution.py:587
  35.9 1.8 %collective-permute-start.10 = (f32[56,128]{1,0:T(8,128)S(1)}, f32[56,128]{1,0:T(8,128)S(1)}, u32[]{:S(2)}, u32[]{:S(2)}) collective-permute-start(f32[56,128]{1,0:T(8,128)S(1)} %get-tuple-element.92.refs_17_), channel_id=1, source_target_pairs={{0,1},{1,0},{2,3},{3,2},{4,5},{5,4},{6,7},{7,6},{8,9},{9,8},{10,11... | collective-permute-start | bytes 86024 | tf_op jit(solution)/shard_map/ppermute | solution.py:600
  36.0 3.4 %collective-permute-start.11 = (f32[56,128]{1,0:T(8,128)S(1)}, f32[56,128]{1,0:T(8,128)S(1)}, u32[]{:S(2)}, u32[]{:S(2)}) collective-permute-start(f32[56,128]{1,0:T(8,128)S(1)} %get-tuple-element.93.refs_18_), channel_id=1, source_target_pairs={{0,3},{1,2},{2,1},{3,0},{4,7},{5,6},{6,5},{7,4},{8,11},{9,10},{10,... | collective-permute-start | bytes 86024 | tf_op jit(solution)/shard_map/ppermute | solution.py:599
  40.5 6.1 %collective-permute-start.12 = (f32[104,128]{1,0:T(8,128)S(1)}, f32[104,128]{1,0:T(8,128)S(1)}, u32[]{:S(2)}, u32[]{:S(2)}) collective-permute-start(f32[104,128]{1,0:T(8,128)S(1)} %get-tuple-element.100.refs_4_.refs_15_), channel_id=1, source_target_pairs={{0,4},{4,8},{8,12},{12,0},{1,5},{5,9},{9,13},{13,1},{2,6},{6,10},{... | collective-permute-start | bytes 159752 | tf_op jit(solution)/shard_map/ppermute | solution.py:586
  41.6 5.3 %collective-permute-start.13 = (f32[104,128]{1,0:T(8,128)S(1)}, f32[104,128]{1,0:T(8,128)S(1)}, u32[]{:S(2)}, u32[]{:S(2)}) collective-permute-start(f32[104,128]{1,0:T(8,128)S(1)} %get-tuple-element.101.refs_5_.refs_16_), channel_id=1, source_target_pairs={{4,0},{8,4},{12,8},{0,12},{5,1},{9,5},{13,9},{1,13},{6,2},{10,6},{... | collective-permute-start | bytes 159752 | tf_op jit(solution)/shard_map/ppermute | solution.py:587
  46.9 1.8 %collective-permute-start.14 = (f32[56,128]{1,0:T(8,128)S(1)}, f32[56,128]{1,0:T(8,128)S(1)}, u32[]{:S(2)}, u32[]{:S(2)}) collective-permute-start(f32[56,128]{1,0:T(8,128)S(1)} %get-tuple-element.104.refs_17_), channel_id=1, source_target_pairs={{0,1},{1,0},{2,3},{3,2},{4,5},{5,4},{6,7},{7,6},{8,9},{9,8},{10,11... | collective-permute-start | bytes 86024 | tf_op jit(solution)/shard_map/ppermute | solution.py:600
  47.0 3.4 %collective-permute-start.15 = (f32[56,128]{1,0:T(8,128)S(1)}, f32[56,128]{1,0:T(8,128)S(1)}, u32[]{:S(2)}, u32[]{:S(2)}) collective-permute-start(f32[56,128]{1,0:T(8,128)S(1)} %get-tuple-element.105.refs_18_), channel_id=1, source_target_pairs={{0,3},{1,2},{2,1},{3,0},{4,7},{5,6},{6,5},{7,4},{8,11},{9,10},{10,... | collective-permute-start | bytes 86024 | tf_op jit(solution)/shard_map/ppermute | solution.py:599
  51.5 5.9 %collective-permute-start.16 = (f32[88,128]{1,0:T(8,128)S(1)}, f32[88,128]{1,0:T(8,128)S(1)}, u32[]{:S(2)}, u32[]{:S(2)}) collective-permute-start(f32[88,128]{1,0:T(8,128)S(1)} %get-tuple-element.111.refs_4_), channel_id=1, source_target_pairs={{0,4},{4,8},{8,12},{12,0},{1,5},{5,9},{9,13},{13,1},{2,6},{6,10},{... | collective-permute-start | bytes 135176 | tf_op jit(solution)/shard_map/ppermute | solution.py:586
  52.9 4.9 %collective-permute-start.17 = (f32[88,128]{1,0:T(8,128)S(1)}, f32[88,128]{1,0:T(8,128)S(1)}, u32[]{:S(2)}, u32[]{:S(2)}) collective-permute-start(f32[88,128]{1,0:T(8,128)S(1)} %get-tuple-element.112.refs_5_), channel_id=1, source_target_pairs={{4,0},{8,4},{12,8},{0,12},{5,1},{9,5},{13,9},{1,13},{6,2},{10,6},{... | collective-permute-start | bytes 135176 | tf_op jit(solution)/shard_map/ppermute | solution.py:587
  57.8 1.8 %collective-permute-start.18 = (f32[40,128]{1,0:T(8,128)S(1)}, f32[40,128]{1,0:T(8,128)S(1)}, u32[]{:S(2)}, u32[]{:S(2)}) collective-permute-start(f32[40,128]{1,0:T(8,128)S(1)} %get-tuple-element.115), channel_id=1, source_target_pairs={{0,1},{1,0},{2,3},{3,2},{4,5},{5,4},{6,7},{7,6},{8,9},{9,8},{10,11... | collective-permute-start | bytes 61448 | tf_op jit(solution)/shard_map/ppermute | solution.py:600
  57.9 3.3 %collective-permute-start.19 = (f32[40,128]{1,0:T(8,128)S(1)}, f32[40,128]{1,0:T(8,128)S(1)}, u32[]{:S(2)}, u32[]{:S(2)}) collective-permute-start(f32[40,128]{1,0:T(8,128)S(1)} %get-tuple-element.116), channel_id=1, source_target_pairs={{0,3},{1,2},{2,1},{3,0},{4,7},{5,6},{6,5},{7,4},{8,11},{9,10},{10,... | collective-permute-start | bytes 61448 | tf_op jit(solution)/shard_map/ppermute | solution.py:599

commit v3 on v2

--- a/solution.py
+++ b/solution.py
@@ -561,7 +561,7 @@
 
 VMEM = pl.BlockSpec(memory_space=pltpu.VMEM)
 SMEM = pl.BlockSpec(memory_space=pltpu.SMEM)
-ANY = pl.BlockSpec(memory_space=pl.ANY)
+HBM = pl.BlockSpec(memory_space=pltpu.HBM)
 
 
 def call(kernel, outs, args, special=None, scratch=(), cost=None):
@@ -613,8 +613,11 @@
     f, mask, pot0, right, left = call(
         start_kernel,
         [fields(size_x), whole, whole, rows(2 * size_y), rows(2 * size_y)],
-        (populations, fluid_mask, wet_class, wall_potential),
-        special={i: ANY for i in range(4)},
+        [
+            pltpu.with_memory_space_constraint(item, pltpu.HBM)
+            for item in (populations, fluid_mask, wet_class, wall_potential)
+        ],
+        special={i: HBM for i in range(4)},
         scratch=[
             pltpu.VMEM(fluid_mask.shape, i32),
             pltpu.VMEM(wet_class.shape, i32),

time: 62.6 us -> 58.5 us (0.935)
  local copies, waits for them, and re-layouts: 3.62 us -> 0.01 us
    unnamed x10 -> x2, local copies, waits for them, and re-layouts: 3.62 us -> 0.01 us
where the time goes in v3:
time: 58.5 us; the launch traced here: 58.3 us
  starting transfers between devices  29.5 us (50%)
  waiting for transfers between devices  14.9 us (25%)
  Pallas kernels  13.2 us (23%)
  between operations  0.75 us (1%)
    pallas_call x16, Pallas kernels, call(): pl.pallas_call(kernel, out_shape=[jax.ShapeDtypeStruct(shape, dtype) for...  13.2 us
    ppermute x5, starting transfers between devices, shift(): lax.ppermute(backward, axis, [(b, a) for a, b in ahead])  12.4 us
    ppermute x5, starting transfers between devices, exchange(): b = lax.ppermute(b, axis, partners[1])  8.44 us
    ppermute x5, starting transfers between devices, shift(): lax.ppermute(forward, axis, ahead)  8.28 us
    ppermute x5, waiting for transfers between devices, exchange(): b = lax.ppermute(b, axis, partners[1])  8.08 us
    ppermute x5, waiting for transfers between devices, shift(): lax.ppermute(forward, axis, ahead)  5.41 us
    ppermute x5, waiting for transfers between devices, shift(): lax.ppermute(backward, axis, [(b, a) for a, b in ahead])  1.4 us
  transfers between devices with their start and end apart: 20, of which 15 were waited for; matrix products, arithmetic and copies ran while one was open for 0% of the time, Pallas kernels for 9%

profile of v3, /device:TPU:0, one launch (start us, length us, event | category | flops | bytes accessed | tf_op | source)
XLA Modules:
  0.0 58.3 jit_solution(16625203052031318453)
XLA Ops:
  0.6 0.0 copy-start
  0.6 1.6 %shard_map.68 = (f32[19,8,16,128]{3,2,1,0:T(8,128)S(1)}, f32[8,16,128]{2,1,0:T(8,128)S(1)}, f32[8,16,128]{2,1,0:T(8,128)S(1)}, f32[32,128]{1,0:T(8,128)S(1)}, f32[32,128]{1,0:T(8,128)S(1)}) custom-call(f32[19,8,16,128]{3,2,1,0:T(8,128)} %f_hbm.1, s32[8,16,128]{2,1,0:T(8,128)} %mask_hbm.1, s32[8,16,128]{2,1,0:T(8,128)} %wet_hbm.1, f32[4]{0:T(128)} %wall_hbm.1), custom_call_target="tpu_custom_call" | custom-call | tf_op jit(solution)/shard_map/pallas_call | solution.py:569
  2.3 3.1 %collective-permute-start = (f32[32,128]{1,0:T(8,128)S(1)}, f32[32,128]{1,0:T(8,128)S(1)}, u32[]{:S(2)}, u32[]{:S(2)}) collective-permute-start(f32[32,128]{1,0:T(8,128)S(1)} %get-tuple-element.61), channel_id=1, source_target_pairs={{0,4},{4,8},{8,12},{12,0},{1,5},{5,9},{9,13},{13,1},{2,6},{6,10},{... | collective-permute-start | bytes 49160 | tf_op jit(solution)/shard_map/ppermute | solution.py:586
  5.4 2.1 %collective-permute-start.1 = (f32[32,128]{1,0:T(8,128)S(1)}, f32[32,128]{1,0:T(8,128)S(1)}, u32[]{:S(2)}, u32[]{:S(2)}) collective-permute-start(f32[32,128]{1,0:T(8,128)S(1)} %get-tuple-element.62), channel_id=1, source_target_pairs={{4,0},{8,4},{12,8},{0,12},{5,1},{9,5},{13,9},{1,13},{6,2},{10,6},{... | collective-permute-start | bytes 49160 | tf_op jit(solution)/shard_map/ppermute | solution.py:587
  7.5 1.8 %collective-permute-done.from_left.x0l.refs_3_ = f32[32,128]{1,0:T(8,128)S(1)} collective-permute-done((f32[32,128]{1,0:T(8,128)S(1)}, f32[32,128]{1,0:T(8,128)S(1)}, u32[]{:S(2)}, u32[]{:S(2)}) %collective-permute-start) | collective-permute-done | bytes 16416 | tf_op jit(solution)/shard_map/ppermute | solution.py:586
  9.2 0.1 collective-permute-done.1.from_right.x0r.refs_4_
  9.3 0.1 collective-permute-start.2
  9.4 1.6 %collective-permute-start.3 = (f32[24,128]{1,0:T(8,128)S(1)}, f32[24,128]{1,0:T(8,128)S(1)}, u32[]{:S(2)}, u32[]{:S(2)}) collective-permute-start(f32[24,128]{1,0:T(8,128)S(1)} %get-tuple-element.65), channel_id=1, source_target_pairs={{0,3},{1,2},{2,1},{3,0},{4,7},{5,6},{6,5},{7,4},{8,11},{9,10},{10,... | collective-permute-start | bytes 36872 | tf_op jit(solution)/shard_map/ppermute | solution.py:599
  11.1 0.0 collective-permute-done.2.a_ref
  11.1 1.5 %collective-permute-done.3.b_ref = f32[24,128]{1,0:T(8,128)S(1)} collective-permute-done((f32[24,128]{1,0:T(8,128)S(1)}, f32[24,128]{1,0:T(8,128)S(1)}, u32[]{:S(2)}, u32[]{:S(2)}) %collective-permute-start.3) | collective-permute-done | bytes 12320 | tf_op jit(solution)/shard_map/ppermute | solution.py:599
  12.6 0.2 shard_map.70
  12.9 0.0 copy-done
  12.9 1.1 %shard_map.71 = (f32[10,32,128]{2,1,0:T(8,128)S(1)}, f32[19,4,32,128]{3,2,1,0:T(8,128)S(1)}, f32[19,2,16,128]{3,2,1,0:T(8,128)S(1)}, f32[104,128]{1,0:T(8,128)S(...) custom-call(f32[19]{0:T(128)S(1)} %copy-done, s32[8,16,128]{2,1,0:T(8,128)S(1)} %get-tuple-element.66.refs_1_.bits_ref, ...), custom_call_target="tpu_custom_call" | custom-call | flops 6553600 | bytes 1310720 | tf_op jit(solution)/shard_map/pallas_call | solution.py:569
  14.0 1.5 %collective-permute-start.4 = (f32[104,128]{1,0:T(8,128)S(1)}, f32[104,128]{1,0:T(8,128)S(1)}, u32[]{:S(2)}, u32[]{:S(2)}) collective-permute-start(f32[104,128]{1,0:T(8,128)S(1)} %get-tuple-element.76.refs_4_.refs_15_), channel_id=1, source_target_pairs={{0,4},{4,8},{8,12},{12,0},{1,5},{5,9},{9,13},{13,1},{2,6},{6,10},{... | collective-permute-start | bytes 159752 | tf_op jit(solution)/shard_map/ppermute | solution.py:586
  15.4 2.4 %collective-permute-start.5 = (f32[104,128]{1,0:T(8,128)S(1)}, f32[104,128]{1,0:T(8,128)S(1)}, u32[]{:S(2)}, u32[]{:S(2)}) collective-permute-start(f32[104,128]{1,0:T(8,128)S(1)} %get-tuple-element.77.refs_5_.refs_16_), channel_id=1, source_target_pairs={{4,0},{8,4},{12,8},{0,12},{5,1},{9,5},{13,9},{1,13},{6,2},{10,6},{... | collective-permute-start | bytes 159752 | tf_op jit(solution)/shard_map/ppermute | solution.py:587
  17.8 1.2 %shard_map.72 = (f32[19,6,16,128]{3,2,1,0:T(8,128)S(1)}, f32[56,128]{1,0:T(8,128)S(1)}, f32[56,128]{1,0:T(8,128)S(1)}, f32[6,16,128]{2,1,0:T(8,128)S(1)}) custom-call(f32[19]{0:T(128)S(1)} %copy-done, s32[8,16,128]{2,1,0:T(8,128)S(1)} %get-tuple-element.66.refs_1_.bits_ref, f32[10,32,128]{2,1,0:T(8,128)S(1)} %get-tuple-element.71.refs_2_, ...), custom_call_target="tpu_custom_call" | custom-call | flops 6553600 | bytes 1310720 | tf_op jit(solution)/shard_map/pallas_call | solution.py:569
  19.0 1.2 %collective-permute-done.4.refs_2_.refs_11_ = f32[104,128]{1,0:T(8,128)S(1)} collective-permute-done((f32[104,128]{1,0:T(8,128)S(1)}, f32[104,128]{1,0:T(8,128)S(1)}, u32[]{:S(2)}, u32[]{:S(2)}) %collective-permute-start.4) | collective-permute-done | bytes 53280 | tf_op jit(solution)/shard_map/ppermute | solution.py:586
  20.2 0.4 collective-permute-done.5.refs_3_.refs_12_
  20.7 0.1 collective-permute-start.6
  20.8 1.6 %collective-permute-start.7 = (f32[56,128]{1,0:T(8,128)S(1)}, f32[56,128]{1,0:T(8,128)S(1)}, u32[]{:S(2)}, u32[]{:S(2)}) collective-permute-start(f32[56,128]{1,0:T(8,128)S(1)} %get-tuple-element.81.refs_18_), channel_id=1, source_target_pairs={{0,3},{1,2},{2,1},{3,0},{4,7},{5,6},{6,5},{7,4},{8,11},{9,10},{10,... | collective-permute-start | bytes 86024 | tf_op jit(solution)/shard_map/ppermute | solution.py:599
  22.4 0.0 collective-permute-done.6.refs_13_.refs_7_
  22.4 1.8 %collective-permute-done.7.refs_14_.refs_8_ = f32[56,128]{1,0:T(8,128)S(1)} collective-permute-done((f32[56,128]{1,0:T(8,128)S(1)}, f32[56,128]{1,0:T(8,128)S(1)}, u32[]{:S(2)}, u32[]{:S(2)}) %collective-permute-start.7) | collective-permute-done | bytes 28704 | tf_op jit(solution)/shard_map/ppermute | solution.py:599
  24.2 1.1 %shard_map.74 = (f32[10,32,128]{2,1,0:T(8,128)S(1)}, f32[19,4,32,128]{3,2,1,0:T(8,128)S(1)}, f32[19,2,16,128]{3,2,1,0:T(8,128)S(1)}, f32[104,128]{1,0:T(8,128)S(...) custom-call(f32[19]{0:T(128)S(1)} %copy-done, s32[8,16,128]{2,1,0:T(8,128)S(1)} %get-tuple-element.66.refs_1_.bits_ref, ...), custom_call_target="tpu_custom_call" | custom-call | flops 6553600 | bytes 1310720 | tf_op jit(solution)/shard_map/pallas_call | solution.py:569
  25.3 1.2 %collective-permute-start.8 = (f32[104,128]{1,0:T(8,128)S(1)}, f32[104,128]{1,0:T(8,128)S(1)}, u32[]{:S(2)}, u32[]{:S(2)}) collective-permute-start(f32[104,128]{1,0:T(8,128)S(1)} %get-tuple-element.88.refs_4_.refs_15_), channel_id=1, source_target_pairs={{0,4},{4,8},{8,12},{12,0},{1,5},{5,9},{9,13},{13,1},{2,6},{6,10},{... | collective-permute-start | bytes 159752 | tf_op jit(solution)/shard_map/ppermute | solution.py:586
  26.5 2.7 %collective-permute-start.9 = (f32[104,128]{1,0:T(8,128)S(1)}, f32[104,128]{1,0:T(8,128)S(1)}, u32[]{:S(2)}, u32[]{:S(2)}) collective-permute-start(f32[104,128]{1,0:T(8,128)S(1)} %get-tuple-element.89.refs_5_.refs_16_), channel_id=1, source_target_pairs={{4,0},{8,4},{12,8},{0,12},{5,1},{9,5},{13,9},{1,13},{6,2},{10,6},{... | collective-permute-start | bytes 159752 | tf_op jit(solution)/shard_map/ppermute | solution.py:587
  29.2 1.2 %shard_map.75 = (f32[19,6,16,128]{3,2,1,0:T(8,128)S(1)}, f32[56,128]{1,0:T(8,128)S(1)}, f32[56,128]{1,0:T(8,128)S(1)}, f32[6,16,128]{2,1,0:T(8,128)S(1)}) custom-call(f32[19]{0:T(128)S(1)} %copy-done, s32[8,16,128]{2,1,0:T(8,128)S(1)} %get-tuple-element.66.refs_1_.bits_ref, f32[10,32,128]{2,1,0:T(8,128)S(1)} %get-tuple-element.83.refs_2_, ...), custom_call_target="tpu_custom_call" | custom-call | flops 6553600 | bytes 1310720 | tf_op jit(solution)/shard_map/pallas_call | solution.py:569
  30.4 1.2 %collective-permute-done.8.refs_2_.refs_11_ = f32[104,128]{1,0:T(8,128)S(1)} collective-permute-done((f32[104,128]{1,0:T(8,128)S(1)}, f32[104,128]{1,0:T(8,128)S(1)}, u32[]{:S(2)}, u32[]{:S(2)}) %collective-permute-start.8) | collective-permute-done | bytes 53280 | tf_op jit(solution)/shard_map/ppermute | solution.py:586
  31.5 0.3 collective-permute-done.9.refs_3_.refs_12_
  31.8 0.1 collective-permute-start.10
  31.9 1.7 %collective-permute-start.11 = (f32[56,128]{1,0:T(8,128)S(1)}, f32[56,128]{1,0:T(8,128)S(1)}, u32[]{:S(2)}, u32[]{:S(2)}) collective-permute-start(f32[56,128]{1,0:T(8,128)S(1)} %get-tuple-element.93.refs_18_), channel_id=1, source_target_pairs={{0,3},{1,2},{2,1},{3,0},{4,7},{5,6},{6,5},{7,4},{8,11},{9,10},{10,... | collective-permute-start | bytes 86024 | tf_op jit(solution)/shard_map/ppermute | solution.py:599
  33.6 0.0 collective-permute-done.10.refs_13_.refs_7_
  33.7 1.6 %collective-permute-done.11.refs_14_.refs_8_ = f32[56,128]{1,0:T(8,128)S(1)} collective-permute-done((f32[56,128]{1,0:T(8,128)S(1)}, f32[56,128]{1,0:T(8,128)S(1)}, u32[]{:S(2)}, u32[]{:S(2)}) %collective-permute-start.11) | collective-permute-done | bytes 28704 | tf_op jit(solution)/shard_map/ppermute | solution.py:599
  35.3 1.1 %shard_map.77 = (f32[10,32,128]{2,1,0:T(8,128)S(1)}, f32[19,4,32,128]{3,2,1,0:T(8,128)S(1)}, f32[19,2,16,128]{3,2,1,0:T(8,128)S(1)}, f32[104,128]{1,0:T(8,128)S(...) custom-call(f32[19]{0:T(128)S(1)} %copy-done, s32[8,16,128]{2,1,0:T(8,128)S(1)} %get-tuple-element.66.refs_1_.bits_ref, ...), custom_call_target="tpu_custom_call" | custom-call | flops 6553600 | bytes 1310720 | tf_op jit(solution)/shard_map/pallas_call | solution.py:569
  36.4 1.1 %collective-permute-start.12 = (f32[104,128]{1,0:T(8,128)S(1)}, f32[104,128]{1,0:T(8,128)S(1)}, u32[]{:S(2)}, u32[]{:S(2)}) collective-permute-start(f32[104,128]{1,0:T(8,128)S(1)} %get-tuple-element.100.refs_4_.refs_15_), channel_id=1, source_target_pairs={{0,4},{4,8},{8,12},{12,0},{1,5},{5,9},{9,13},{13,1},{2,6},{6,10},{... | collective-permute-start | bytes 159752 | tf_op jit(solution)/shard_map/ppermute | solution.py:586
  37.5 2.8 %collective-permute-start.13 = (f32[104,128]{1,0:T(8,128)S(1)}, f32[104,128]{1,0:T(8,128)S(1)}, u32[]{:S(2)}, u32[]{:S(2)}) collective-permute-start(f32[104,128]{1,0:T(8,128)S(1)} %get-tuple-element.101.refs_5_.refs_16_), channel_id=1, source_target_pairs={{4,0},{8,4},{12,8},{0,12},{5,1},{9,5},{13,9},{1,13},{6,2},{10,6},{... | collective-permute-start | bytes 159752 | tf_op jit(solution)/shard_map/ppermute | solution.py:587
  40.3 1.2 %shard_map.78 = (f32[19,6,16,128]{3,2,1,0:T(8,128)S(1)}, f32[56,128]{1,0:T(8,128)S(1)}, f32[56,128]{1,0:T(8,128)S(1)}, f32[6,16,128]{2,1,0:T(8,128)S(1)}) custom-call(f32[19]{0:T(128)S(1)} %copy-done, s32[8,16,128]{2,1,0:T(8,128)S(1)} %get-tuple-element.66.refs_1_.bits_ref, f32[10,32,128]{2,1,0:T(8,128)S(1)} %get-tuple-element.95.refs_2_, ...), custom_call_target="tpu_custom_call" | custom-call | flops 6553600 | bytes 1310720 | tf_op jit(solution)/shard_map/pallas_call | solution.py:569
  41.5 1.0 %collective-permute-done.12.refs_2_.refs_11_ = f32[104,128]{1,0:T(8,128)S(1)} collective-permute-done((f32[104,128]{1,0:T(8,128)S(1)}, f32[104,128]{1,0:T(8,128)S(1)}, u32[]{:S(2)}, u32[]{:S(2)}) %collective-permute-start.12) | collective-permute-done | bytes 53280 | tf_op jit(solution)/shard_map/ppermute | solution.py:586
  42.5 0.3 collective-permute-done.13.refs_3_.refs_12_
  42.8 0.1 collective-permute-start.14
  42.9 1.7 %collective-permute-start.15 = (f32[56,128]{1,0:T(8,128)S(1)}, f32[56,128]{1,0:T(8,128)S(1)}, u32[]{:S(2)}, u32[]{:S(2)}) collective-permute-start(f32[56,128]{1,0:T(8,128)S(1)} %get-tuple-element.105.refs_18_), channel_id=1, source_target_pairs={{0,3},{1,2},{2,1},{3,0},{4,7},{5,6},{6,5},{7,4},{8,11},{9,10},{10,... | collective-permute-start | bytes 86024 | tf_op jit(solution)/shard_map/ppermute | solution.py:599
  44.6 0.0 collective-permute-done.14.refs_13_.refs_7_
  44.6 1.6 %collective-permute-done.15.refs_14_.refs_8_ = f32[56,128]{1,0:T(8,128)S(1)} collective-permute-done((f32[56,128]{1,0:T(8,128)S(1)}, f32[56,128]{1,0:T(8,128)S(1)}, u32[]{:S(2)}, u32[]{:S(2)}) %collective-permute-start.15) | collective-permute-done | bytes 28704 | tf_op jit(solution)/shard_map/ppermute | solution.py:599
  46.3 1.2 %shard_map.80 = (f32[10,32,128]{2,1,0:T(8,128)S(1)}, f32[19,4,32,128]{3,2,1,0:T(8,128)S(1)}, f32[19,2,16,128]{3,2,1,0:T(8,128)S(1)}, f32[88,128]{1,0:T(8,128)S(1...) custom-call(f32[19]{0:T(128)S(1)} %copy-done, s32[8,16,128]{2,1,0:T(8,128)S(1)} %get-tuple-element.66.refs_1_.bits_ref, ...), custom_call_target="tpu_custom_call" | custom-call | flops 6553600 | bytes 1310720 | tf_op jit(solution)/shard_map/pallas_call | solution.py:569
  47.4 1.4 %collective-permute-start.16 = (f32[88,128]{1,0:T(8,128)S(1)}, f32[88,128]{1,0:T(8,128)S(1)}, u32[]{:S(2)}, u32[]{:S(2)}) collective-permute-start(f32[88,128]{1,0:T(8,128)S(1)} %get-tuple-element.111.refs_4_), channel_id=1, source_target_pairs={{0,4},{4,8},{8,12},{12,0},{1,5},{5,9},{9,13},{13,1},{2,6},{6,10},{... | collective-permute-start | bytes 135176 | tf_op jit(solution)/shard_map/ppermute | solution.py:586
  48.8 2.5 %collective-permute-start.17 = (f32[88,128]{1,0:T(8,128)S(1)}, f32[88,128]{1,0:T(8,128)S(1)}, u32[]{:S(2)}, u32[]{:S(2)}) collective-permute-start(f32[88,128]{1,0:T(8,128)S(1)} %get-tuple-element.112.refs_5_), channel_id=1, source_target_pairs={{4,0},{8,4},{12,8},{0,12},{5,1},{9,5},{13,9},{1,13},{6,2},{10,6},{... | collective-permute-start | bytes 135176 | tf_op jit(solution)/shard_map/ppermute | solution.py:587
  51.3 1.8 %shard_map.81 = (f32[19,6,16,128]{3,2,1,0:T(8,128)S(1)}, f32[40,128]{1,0:T(8,128)S(1)}, f32[40,128]{1,0:T(8,128)S(1)}, f32[3,8,16,128]{3,2,1,0:T(8,128)}) custom-call(f32[19]{0:T(128)S(1)} %copy-done, s32[8,16,128]{2,1,0:T(8,128)S(1)} %get-tuple-element.66.refs_1_.bits_ref, f32[10,32,128]{2,1,0:T(8,128)S(1)} %get-tuple-element.107.refs_2_, ...), custom_call_target="tpu_custom_call" | custom-call | flops 6553600 | bytes 1310720 | tf_op jit(solution)/shard_map/pallas_call | solution.py:569
  53.2 0.2 collective-permute-done.16.refs_2_.xl
  53.4 0.4 collective-permute-done.17.refs_3_.xr
  53.8 0.1 collective-permute-start.18
  53.9 1.7 %collective-permute-start.19 = (f32[40,128]{1,0:T(8,128)S(1)}, f32[40,128]{1,0:T(8,128)S(1)}, u32[]{:S(2)}, u32[]{:S(2)}) collective-permute-start(f32[40,128]{1,0:T(8,128)S(1)} %get-tuple-element.116), channel_id=1, source_target_pairs={{0,3},{1,2},{2,1},{3,0},{4,7},{5,6},{6,5},{7,4},{8,11},{9,10},{10,... | collective-permute-start | bytes 61448 | tf_op jit(solution)/shard_map/ppermute | solution.py:599
  55.6 0.0 collective-permute-done.18.ya
  55.6 1.5 %collective-permute-done.19.yb = f32[40,128]{1,0:T(8,128)S(1)} collective-permute-done((f32[40,128]{1,0:T(8,128)S(1)}, f32[40,128]{1,0:T(8,128)S(1)}, u32[]{:S(2)}, u32[]{:S(2)}) %collective-permute-start.19) | collective-permute-done | bytes 20512 | tf_op jit(solution)/shard_map/ppermute | solution.py:599
  57.1 1.2 %shard_map.83 = f32[19,8,16,128]{3,2,1,0:T(8,128)} custom-call(f32[19,2,16,128]{3,2,1,0:T(8,128)S(1)} %get-tuple-element.106.f_edge, f32[19,6,16,128]{3,2,1,0:T(8,128)S(1)} %get-tuple-element.110.f_middle, s32[8,16,128]{2,1,0:T(8,128)S(1)} %get-tuple-element.66.refs_1_.bits_ref, f32[88,128]{1,0:T(8,128)S(1)} %collective-permute-done.16.refs_2_.xl, ...), custom_call_target="tpu_custom_call" | custom-call | tf_op jit(solution)/shard_map/pallas_call | solution.py:569
  (5 shorter events, 0.1 us)
Async XLA Ops:
  0.6 12.2 %copy-start = (f32[19]{0:T(128)S(1)}, f32[19]{0:T(128)}, u32[]{:S(2)}) copy-start(f32[19]{0:T(128)} %refs_0_.15) | copy-start | bytes 232
  2.3 6.9 %collective-permute-start = (f32[32,128]{1,0:T(8,128)S(1)}, f32[32,128]{1,0:T(8,128)S(1)}, u32[]{:S(2)}, u32[]{:S(2)}) collective-permute-start(f32[32,128]{1,0:T(8,128)S(1)} %get-tuple-element.61), channel_id=1, source_target_pairs={{0,4},{4,8},{8,12},{12,0},{1,5},{5,9},{9,13},{13,1},{2,6},{6,10},{... | collective-permute-start | bytes 49160 | tf_op jit(solution)/shard_map/ppermute | solution.py:586
  5.4 3.9 %collective-permute-start.1 = (f32[32,128]{1,0:T(8,128)S(1)}, f32[32,128]{1,0:T(8,128)S(1)}, u32[]{:S(2)}, u32[]{:S(2)}) collective-permute-start(f32[32,128]{1,0:T(8,128)S(1)} %get-tuple-element.62), channel_id=1, source_target_pairs={{4,0},{8,4},{12,8},{0,12},{5,1},{9,5},{13,9},{1,13},{6,2},{10,6},{... | collective-permute-start | bytes 49160 | tf_op jit(solution)/shard_map/ppermute | solution.py:587
  9.3 1.7 %collective-permute-start.2 = (f32[24,128]{1,0:T(8,128)S(1)}, f32[24,128]{1,0:T(8,128)S(1)}, u32[]{:S(2)}, u32[]{:S(2)}) collective-permute-start(f32[24,128]{1,0:T(8,128)S(1)} %get-tuple-element.64), channel_id=1, source_target_pairs={{0,1},{1,0},{2,3},{3,2},{4,5},{5,4},{6,7},{7,6},{8,9},{9,8},{10,11... | collective-permute-start | bytes 36872 | tf_op jit(solution)/shard_map/ppermute | solution.py:600
  9.4 3.2 %collective-permute-start.3 = (f32[24,128]{1,0:T(8,128)S(1)}, f32[24,128]{1,0:T(8,128)S(1)}, u32[]{:S(2)}, u32[]{:S(2)}) collective-permute-start(f32[24,128]{1,0:T(8,128)S(1)} %get-tuple-element.65), channel_id=1, source_target_pairs={{0,3},{1,2},{2,1},{3,0},{4,7},{5,6},{6,5},{7,4},{8,11},{9,10},{10,... | collective-permute-start | bytes 36872 | tf_op jit(solution)/shard_map/ppermute | solution.py:599
  14.0 6.3 %collective-permute-start.4 = (f32[104,128]{1,0:T(8,128)S(1)}, f32[104,128]{1,0:T(8,128)S(1)}, u32[]{:S(2)}, u32[]{:S(2)}) collective-permute-start(f32[104,128]{1,0:T(8,128)S(1)} %get-tuple-element.76.refs_4_.refs_15_), channel_id=1, source_target_pairs={{0,4},{4,8},{8,12},{12,0},{1,5},{5,9},{9,13},{13,1},{2,6},{6,10},{... | collective-permute-start | bytes 159752 | tf_op jit(solution)/shard_map/ppermute | solution.py:586
  15.4 5.3 %collective-permute-start.5 = (f32[104,128]{1,0:T(8,128)S(1)}, f32[104,128]{1,0:T(8,128)S(1)}, u32[]{:S(2)}, u32[]{:S(2)}) collective-permute-start(f32[104,128]{1,0:T(8,128)S(1)} %get-tuple-element.77.refs_5_.refs_16_), channel_id=1, source_target_pairs={{4,0},{8,4},{12,8},{0,12},{5,1},{9,5},{13,9},{1,13},{6,2},{10,6},{... | collective-permute-start | bytes 159752 | tf_op jit(solution)/shard_map/ppermute | solution.py:587
  20.7 1.7 %collective-permute-start.6 = (f32[56,128]{1,0:T(8,128)S(1)}, f32[56,128]{1,0:T(8,128)S(1)}, u32[]{:S(2)}, u32[]{:S(2)}) collective-permute-start(f32[56,128]{1,0:T(8,128)S(1)} %get-tuple-element.80.refs_17_), channel_id=1, source_target_pairs={{0,1},{1,0},{2,3},{3,2},{4,5},{5,4},{6,7},{7,6},{8,9},{9,8},{10,11... | collective-permute-start | bytes 86024 | tf_op jit(solution)/shard_map/ppermute | solution.py:600
  20.8 3.4 %collective-permute-start.7 = (f32[56,128]{1,0:T(8,128)S(1)}, f32[56,128]{1,0:T(8,128)S(1)}, u32[]{:S(2)}, u32[]{:S(2)}) collective-permute-start(f32[56,128]{1,0:T(8,128)S(1)} %get-tuple-element.81.refs_18_), channel_id=1, source_target_pairs={{0,3},{1,2},{2,1},{3,0},{4,7},{5,6},{6,5},{7,4},{8,11},{9,10},{10,... | collective-permute-start | bytes 86024 | tf_op jit(solution)/shard_map/ppermute | solution.py:599
  25.3 6.2 %collective-permute-start.8 = (f32[104,128]{1,0:T(8,128)S(1)}, f32[104,128]{1,0:T(8,128)S(1)}, u32[]{:S(2)}, u32[]{:S(2)}) collective-permute-start(f32[104,128]{1,0:T(8,128)S(1)} %get-tuple-element.88.refs_4_.refs_15_), channel_id=1, source_target_pairs={{0,4},{4,8},{8,12},{12,0},{1,5},{5,9},{9,13},{13,1},{2,6},{6,10},{... | collective-permute-start | bytes 159752 | tf_op jit(solution)/shard_map/ppermute | solution.py:586
  26.5 5.3 %collective-permute-start.9 = (f32[104,128]{1,0:T(8,128)S(1)}, f32[104,128]{1,0:T(8,128)S(1)}, u32[]{:S(2)}, u32[]{:S(2)}) collective-permute-start(f32[104,128]{1,0:T(8,128)S(1)} %get-tuple-element.89.refs_5_.refs_16_), channel_id=1, source_target_pairs={{4,0},{8,4},{12,8},{0,12},{5,1},{9,5},{13,9},{1,13},{6,2},{10,6},{... | collective-permute-start | bytes 159752 | tf_op jit(solution)/shard_map/ppermute | solution.py:587
  31.8 1.8 %collective-permute-start.10 = (f32[56,128]{1,0:T(8,128)S(1)}, f32[56,128]{1,0:T(8,128)S(1)}, u32[]{:S(2)}, u32[]{:S(2)}) collective-permute-start(f32[56,128]{1,0:T(8,128)S(1)} %get-tuple-element.92.refs_17_), channel_id=1, source_target_pairs={{0,1},{1,0},{2,3},{3,2},{4,5},{5,4},{6,7},{7,6},{8,9},{9,8},{10,11... | collective-permute-start | bytes 86024 | tf_op jit(solution)/shard_map/ppermute | solution.py:600
  31.9 3.4 %collective-permute-start.11 = (f32[56,128]{1,0:T(8,128)S(1)}, f32[56,128]{1,0:T(8,128)S(1)}, u32[]{:S(2)}, u32[]{:S(2)}) collective-permute-start(f32[56,128]{1,0:T(8,128)S(1)} %get-tuple-element.93.refs_18_), channel_id=1, source_target_pairs={{0,3},{1,2},{2,1},{3,0},{4,7},{5,6},{6,5},{7,4},{8,11},{9,10},{10,... | collective-permute-start | bytes 86024 | tf_op jit(solution)/shard_map/ppermute | solution.py:599
  36.4 6.1 %collective-permute-start.12 = (f32[104,128]{1,0:T(8,128)S(1)}, f32[104,128]{1,0:T(8,128)S(1)}, u32[]{:S(2)}, u32[]{:S(2)}) collective-permute-start(f32[104,128]{1,0:T(8,128)S(1)} %get-tuple-element.100.refs_4_.refs_15_), channel_id=1, source_target_pairs={{0,4},{4,8},{8,12},{12,0},{1,5},{5,9},{9,13},{13,1},{2,6},{6,10},{... | collective-permute-start | bytes 159752 | tf_op jit(solution)/shard_map/ppermute | solution.py:586
  37.5 5.3 %collective-permute-start.13 = (f32[104,128]{1,0:T(8,128)S(1)}, f32[104,128]{1,0:T(8,128)S(1)}, u32[]{:S(2)}, u32[]{:S(2)}) collective-permute-start(f32[104,128]{1,0:T(8,128)S(1)} %get-tuple-element.101.refs_5_.refs_16_), channel_id=1, source_target_pairs={{4,0},{8,4},{12,8},{0,12},{5,1},{9,5},{13,9},{1,13},{6,2},{10,6},{... | collective-permute-start | bytes 159752 | tf_op jit(solution)/shard_map/ppermute | solution.py:587
  42.8 1.8 %collective-permute-start.14 = (f32[56,128]{1,0:T(8,128)S(1)}, f32[56,128]{1,0:T(8,128)S(1)}, u32[]{:S(2)}, u32[]{:S(2)}) collective-permute-start(f32[56,128]{1,0:T(8,128)S(1)} %get-tuple-element.104.refs_17_), channel_id=1, source_target_pairs={{0,1},{1,0},{2,3},{3,2},{4,5},{5,4},{6,7},{7,6},{8,9},{9,8},{10,11... | collective-permute-start | bytes 86024 | tf_op jit(solution)/shard_map/ppermute | solution.py:600
  42.9 3.4 %collective-permute-start.15 = (f32[56,128]{1,0:T(8,128)S(1)}, f32[56,128]{1,0:T(8,128)S(1)}, u32[]{:S(2)}, u32[]{:S(2)}) collective-permute-start(f32[56,128]{1,0:T(8,128)S(1)} %get-tuple-element.105.refs_18_), channel_id=1, source_target_pairs={{0,3},{1,2},{2,1},{3,0},{4,7},{5,6},{6,5},{7,4},{8,11},{9,10},{10,... | collective-permute-start | bytes 86024 | tf_op jit(solution)/shard_map/ppermute | solution.py:599
  47.4 5.9 %collective-permute-start.16 = (f32[88,128]{1,0:T(8,128)S(1)}, f32[88,128]{1,0:T(8,128)S(1)}, u32[]{:S(2)}, u32[]{:S(2)}) collective-permute-start(f32[88,128]{1,0:T(8,128)S(1)} %get-tuple-element.111.refs_4_), channel_id=1, source_target_pairs={{0,4},{4,8},{8,12},{12,0},{1,5},{5,9},{9,13},{13,1},{2,6},{6,10},{... | collective-permute-start | bytes 135176 | tf_op jit(solution)/shard_map/ppermute | solution.py:586
  48.8 4.9 %collective-permute-start.17 = (f32[88,128]{1,0:T(8,128)S(1)}, f32[88,128]{1,0:T(8,128)S(1)}, u32[]{:S(2)}, u32[]{:S(2)}) collective-permute-start(f32[88,128]{1,0:T(8,128)S(1)} %get-tuple-element.112.refs_5_), channel_id=1, source_target_pairs={{4,0},{8,4},{12,8},{0,12},{5,1},{9,5},{13,9},{1,13},{6,2},{10,6},{... | collective-permute-start | bytes 135176 | tf_op jit(solution)/shard_map/ppermute | solution.py:587
  53.8 1.8 %collective-permute-start.18 = (f32[40,128]{1,0:T(8,128)S(1)}, f32[40,128]{1,0:T(8,128)S(1)}, u32[]{:S(2)}, u32[]{:S(2)}) collective-permute-start(f32[40,128]{1,0:T(8,128)S(1)} %get-tuple-element.115), channel_id=1, source_target_pairs={{0,1},{1,0},{2,3},{3,2},{4,5},{5,4},{6,7},{7,6},{8,9},{9,8},{10,11... | collective-permute-start | bytes 61448 | tf_op jit(solution)/shard_map/ppermute | solution.py:600
  53.9 3.3 %collective-permute-start.19 = (f32[40,128]{1,0:T(8,128)S(1)}, f32[40,128]{1,0:T(8,128)S(1)}, u32[]{:S(2)}, u32[]{:S(2)}) collective-permute-start(f32[40,128]{1,0:T(8,128)S(1)} %get-tuple-element.116), channel_id=1, source_target_pairs={{0,3},{1,2},{2,1},{3,0},{4,7},{5,6},{6,5},{7,4},{8,11},{9,10},{10,... | collective-permute-start | bytes 61448 | tf_op jit(solution)/shard_map/ppermute | solution.py:599

commit v4 on v3

--- a/solution.py
+++ b/solution.py
@@ -32,10 +32,11 @@
 )
 N = len(VELOCITY)
 OPPOSITE = [0] + [k + 1 if k % 2 == 1 else k - 1 for k in range(1, N)]
-RIGHT = [k for k in range(N) if VELOCITY[k][0] == 1]
-LEFT = [k for k in range(N) if VELOCITY[k][0] == -1]
-UP = [k for k in range(N) if VELOCITY[k][1] == 1]
-DOWN = [k for k in range(N) if VELOCITY[k][1] == -1]
+SHIFT = [(y, x, z) for x, y, z in VELOCITY]
+RIGHT = [k for k in range(N) if SHIFT[k][0] == 1]
+LEFT = [k for k in range(N) if SHIFT[k][0] == -1]
+UP = [k for k in range(N) if SHIFT[k][1] == 1]
+DOWN = [k for k in range(N) if SHIFT[k][1] == -1]
 TILE = 8
 PAD = 2 * TILE
 
@@ -135,38 +136,53 @@
     return out, (ux, uy, uz)
 
 
-def start_kernel(f_hbm, mask_hbm, wet_hbm, wall_hbm, f_ref, mask_ref, pot_ref, right_ref, left_ref, *scratch):
+def corner_pops(side):
+    return SHIFT.index((side, 1, 0)), SHIFT.index((side, -1, 0))
+
+
+def start_kernel(f_hbm, mask_hbm, wet_hbm, wall_hbm, raw_ref, flat_ref, mask_ref, pot_ref, right_ref, left_ref, *scratch):
     mask_in, wet_in, wall_in, f_sems, sems = scratch
-    size_x, size_y = mask_ref.shape[0], mask_ref.shape[1]
+    layers, rows = mask_ref.shape[0], mask_ref.shape[1]
     small = [
         pltpu.make_async_copy(source, target, sems.at[i])
         for i, (source, target) in enumerate(
             ((wall_hbm, wall_in), (mask_hbm, mask_in), (wet_hbm, wet_in))
         )
     ]
-    large = [pltpu.make_async_copy(f_hbm.at[k], f_ref.at[k], f_sems.at[k]) for k in range(N)]
+    large = [pltpu.make_async_copy(f_hbm.at[k], raw_ref.at[k], f_sems.at[k]) for k in range(N)]
     for copy in small + large:
         copy.start()
     for copy in small:
         copy.wait()
-    for x in range(size_x):
-        wet = wet_in[x]
+    blocks = [slice(i, i + TILE) for i in range(0, layers * rows, TILE)]
+    for at in blocks:
+        wet = wet_in[at]
         wall = jnp.zeros(wet.shape, jnp.float32)
         for c in range(wall_in.shape[0]):
             wall = jnp.where(wet == c, wall_in[c], wall)
-        pot_ref[x] = wall
-        mask_ref[x] = jnp.where(mask_in[x] == 1, 1.0, 0.0)
+        flat_ref[1, at] = wall
+        flat_ref[0, at] = jnp.where(mask_in[at] == 1, 1.0, 0.0)
     for copy in large:
         copy.wait()
-    for x in range(size_x):
-        density = total([f_ref[k, x] for k in range(N)])
-        pot_ref[x] = potential_of(density, mask_ref[x] > 0.5, pot_ref[x])
-    for ref, x in ((right_ref, size_x - 1), (left_ref, 0)):
-        ref[:size_y] = pot_ref[x]
-        ref[size_y:] = mask_ref[x]
-
-
-def start_pack_kernel(pairs, pot_ref, mask_ref, from_left, from_right, a_ref, b_ref, up_ref, down_ref):
+    for at in blocks:
+        density = total([raw_ref[k, at] for k in range(N)])
+        flat_ref[1, at] = potential_of(density, flat_ref[0, at] > 0.5, flat_ref[1, at])
+    for i in range(layers):
+        mask_ref[i] = flat_ref[0, pl.ds(i, rows, stride=layers)]
+        pot_ref[i] = flat_ref[1, pl.ds(i, rows, stride=layers)]
+    for ref, i in ((right_ref, layers - 1), (left_ref, 0)):
+        ref[:rows] = pot_ref[i]
+        ref[rows:] = mask_ref[i]
+
+
+def turn_kernel(raw_ref, f_ref):
+    layers, rows = f_ref.shape[1], f_ref.shape[2]
+    for k in range(N):
+        for i in range(layers):
+            f_ref[k, i] = raw_ref[k, pl.ds(i, rows, stride=layers)]
+
+
+def start_pack_kernel(pot_ref, mask_ref, from_left, from_right, up_ref, down_ref):
     size_x, size_y = mask_ref.shape[0], mask_ref.shape[1]
     for ref, y in ((up_ref, size_y - 1), (down_ref, 0)):
         ref[2 * size_x :] = jnp.zeros((TILE, ref.shape[1]), jnp.float32)
@@ -177,32 +193,10 @@
             row = 2 * size_x + i
             ref[row : row + 1] = side[y : y + 1]
             ref[row + 2 : row + 3] = side[size_y + y : size_y + y + 1]
-    to_pairs(pairs, up_ref, down_ref, a_ref, b_ref)
-
-
-def to_pairs(pairs, up_ref, down_ref, a_ref, b_ref):
-    up, down = up_ref[...], down_ref[...]
-    if not pairs:
-        a_ref[...], b_ref[...] = up, down
-        return
-    odd = lax.axis_index("gy") % 2 == 1
-    a_ref[...] = jnp.where(odd, down, up)
-    b_ref[...] = jnp.where(odd, up, down)
-
-
-def from_pairs(pairs, a_ref, b_ref, below_ref, above_ref):
-    a, b = a_ref[...], b_ref[...]
-    if not pairs:
-        below_ref[...], above_ref[...] = a, b
-        return
-    odd = lax.axis_index("gy") % 2 == 1
-    below_ref[...] = jnp.where(odd, a, b)
-    above_ref[...] = jnp.where(odd, b, a)
-
-
-def bits_kernel(pairs, mask_ref, x0l, x0r, a_ref, b_ref, bits_ref, y0d, y0u, pad_ref):
+
+
+def bits_kernel(mask_ref, x0l, x0r, y0d, y0u, bits_ref, pad_ref):
     size_x, size_y = mask_ref.shape[0], mask_ref.shape[1]
-    from_pairs(pairs, a_ref, b_ref, y0d, y0u)
     for x in range(size_x):
         pad_ref[1 + x, TILE : TILE + size_y] = mask_ref[x]
     for x, side in ((0, x0l), (1 + size_x, x0r)):
@@ -216,7 +210,7 @@
         for y in range(0, size_y, TILE):
             bits = jnp.zeros((TILE, mask_ref.shape[2]), jnp.int32)
             for k in range(N):
-                ex, ey, ez = VELOCITY[k]
+                ex, ey, ez = SHIFT[k]
                 row = TILE + y - ey
                 source = roll_z(pad_ref[1 + x - ex, row : row + TILE], ez)
                 bits = bits | jnp.where(source > 0.5, 1 << k, 0)
@@ -285,8 +279,8 @@
             both = near[1, 0] + near[-1, 0] + near[0, 1] + near[0, -1] + 2.0 * near[0, 0]
             diag1, diag2 = pp - mm, pm - mp
             force = (
+                scale * (2.0 * dy + (diag1 - diag2) + (roll_z(dy, 1) + roll_z(dy, -1))),
                 scale * (2.0 * dx + (diag1 + diag2) + (roll_z(dx, 1) + roll_z(dx, -1))),
-                scale * (2.0 * dy + (diag1 - diag2) + (roll_z(dy, 1) + roll_z(dy, -1))),
                 scale * (roll_z(both, -1) - roll_z(both, 1)),
             )
             now = [f(k, x, y) for k in range(N)]
@@ -317,7 +311,7 @@
             bits = bits_ref[x, y : y + TILE]
             arrived = []
             for k in range(N):
-                ex, ey, ez = VELOCITY[k]
+                ex, ey, ez = SHIFT[k]
                 value = post.load(x, TILE + y, OPPOSITE[k])
                 if k > 0:
                     come = 0.0
@@ -330,15 +324,15 @@
                 rho.store(x, y, total(arrived))
 
 
-def edge_kernel(first, last, pairs, *refs):
+def edge_kernel(first, last, *refs):
     refs = list(refs)
     take = lambda count: [refs.pop(0) for _ in range(count)]
     rates, bits_ref, pot0_ref, x0l, x0r, y0d, y0u = take(7)
     if first:
         f_ref = take(1)[0]
     else:
-        f_edge, f_middle, rho_edge, rho_middle, xl, xr, ya, yb = take(8)
-        own_right, own_left, own_a, own_b = take(4)
+        f_edge, f_middle, rho_edge, rho_middle, xl, xr, yd, yu = take(8)
+        own_right, own_left, own_up, own_down = take(4)
     pot, post_out, f_out, right_ref, left_ref = take(5)
     rest = take(1)[0]
     size_x, size_y, size_z = bits_ref.shape
@@ -347,12 +341,6 @@
     if first:
         f = lambda k, x, y: f_ref[k, x, y : y + TILE]
     else:
-        yd, yu, own_down, own_up = take(4)
-        from_pairs(pairs, ya, yb, yd, yu)
-        if pairs:
-            from_pairs(pairs, own_a, own_b, own_down, own_up)
-        else:
-            own_down, own_up = own_b, own_a
         sides = (xl, xr, yd, yu)
         held = Layers(f_edge, f_middle, size_x, edge1)
         density_of = Layers(rho_edge, rho_middle, size_x, edge1)
@@ -432,10 +420,10 @@
 
     at = (5 if last else 6) * size_y
     for i, (ref, x, ks, dirs) in enumerate(
-        ((left_ref, 0, LEFT, (10, 8)), (right_ref, size_x - 1, RIGHT, (7, 9)))
+        ((left_ref, 0, LEFT, corner_pops(-1)), (right_ref, size_x - 1, RIGHT, corner_pops(1)))
     ):
         for j, k in enumerate(ks):
-            _, ey, ez = VELOCITY[k]
+            _, ey, ez = SHIFT[k]
             for y in range(0, size_y, TILE):
                 row = j * size_y + y
                 ref[row : row + TILE] = roll_z(post.load(x, TILE + y - ey, k), ez)
@@ -447,21 +435,21 @@
             for h, y, leave in ((H_UP, size_y - 1, UP), (H_DN, 0, DOWN)):
                 ref[at + h : at + h + 1] = total(
                     [
-                        roll_z(post.row(x - VELOCITY[k][0], TILE + y, k), VELOCITY[k][2])
+                        roll_z(post.row(x - SHIFT[k][0], TILE + y, k), SHIFT[k][2])
                         for k in leave
-                        if 0 <= x - VELOCITY[k][0] < size_x
+                        if 0 <= x - SHIFT[k][0] < size_x
                     ]
                 )
 
 
-def middle_kernel(first, last, pairs, *refs):
+def middle_kernel(first, last, *refs):
     refs = list(refs)
     take = lambda count: [refs.pop(0) for _ in range(count)]
     rates, bits_ref, pot, post_edge, edge_rest = take(5)
     if first:
         f_ref = take(1)[0]
     else:
-        f_edge, f_middle, ya, yb = take(4)
+        f_edge, f_middle, yd, yu = take(4)
     f_out, up_ref, down_ref, rest = take(4)
     post_middle = take(1)[0]
     size_x, size_y, size_z = bits_ref.shape
@@ -470,8 +458,6 @@
     if first:
         f = lambda k, x, y: f_ref[k, x, y : y + TILE]
     else:
-        yd, yu = take(2)
-        from_pairs(pairs, ya, yb, yd, yu)
         sides = (None, None, yd, yu)
         held = Layers(f_edge, f_middle, size_x, edge1)
         f = lambda k, x, y: held.load(x, y, k)
@@ -480,10 +466,11 @@
     speed = None
     if last:
         speed = Layers(None, None, size_x, [])
-        speed.where = {x: (rest, x) for x in range(size_x)}
+        speed.store = lambda x, y, value, c: rest.__setitem__((c, turned(x, y, size_x)), value)
         for c in range(3):
             for i, x in enumerate(edge2):
-                rest[c, x] = edge_rest[c, i]
+                for y in range(0, size_y, TILE):
+                    rest[c, turned(x, y, size_x)] = edge_rest[c, i, y : y + TILE]
     inner = [x for x in range(size_x) if x not in edge2]
     collide_layers(inner, rates, f, bits_ref, pot, sides, post, speed)
     rho = None if last else Layers(edge_rest, rest, size_x, edge1)
@@ -491,7 +478,7 @@
     stream_layers(inner, bits_ref, post, Layers(None, f_out, size_x, edge1), rho)
     for ref, y, ks in ((up_ref, size_y - 1, UP), (down_ref, 0, DOWN)):
         for j, k in enumerate(ks):
-            ex, _, ez = VELOCITY[k]
+            ex, _, ez = SHIFT[k]
             for x in range(size_x):
                 row = j * size_x + x
                 if 0 <= x - ex < size_x:
@@ -506,8 +493,8 @@
                 ref[5 * size_x + x : 5 * size_x + x + 1] = rho.row(x, y)
 
 
-def pack_kernel(last, pairs, size_x, size_y, *refs):
-    up_in, down_in, xl, xr, own_right, own_left, a_ref, b_ref, up_ref, down_ref = refs
+def pack_kernel(last, size_x, size_y, *refs):
+    up_in, down_in, xl, xr, own_right, own_left, up_ref, down_ref = refs
     parts = 5 if last else 6
     at = parts * size_y
     for ref, source, y, ks, c, h in (
@@ -520,7 +507,7 @@
             (xl, own_left, 0, 1, RC_L, G_L),
             (xr, own_right, size_x - 1, -1, RC_R, G_R),
         ):
-            j = [i for i, k in enumerate(ks) if VELOCITY[k][0] == ex][0]
+            j = [i for i, k in enumerate(ks) if SHIFT[k][0] == ex][0]
             row = j * size_x + x
             ref[row : row + 1] = side[at + c : at + c + 1]
             if not last:
@@ -535,28 +522,48 @@
                 ref[row + g : row + g + 1] = (
                     side[at + h : at + h + 1] + own[at + c : at + c + 1]
                 )
-    to_pairs(pairs, up_ref, down_ref, a_ref, b_ref)
-
-
-def end_kernel(pairs, f_edge, f_middle, bits_ref, xl, xr, ya, yb, out_ref, yd, yu):
-    size_x, size_y, size_z = bits_ref.shape
-    row_of = lax.broadcasted_iota(jnp.int32, (TILE, size_z), 0)
-    from_pairs(pairs, ya, yb, yd, yu)
+
+
+def turned(layer, row, layers):
+    return pl.ds(layer + row * layers, TILE, stride=layers)
+
+
+def write_kernel(f_edge, f_middle, bits_ref, xl, xr, out_hbm, flat_ref, sems):
+    size_x, size_y, _ = bits_ref.shape
     held = Layers(f_edge, f_middle, size_x, one_layer(size_x))
-    for x in range(size_x):
-        for y in range(0, size_y, TILE):
-            fluid = fluid_at(bits_ref, x, y)
-            for k in range(N):
+    copies = []
+    for k in range(N):
+        for x in range(size_x):
+            for y in range(0, size_y, TILE):
                 value = held.load(x, y, k)
                 for at, side, ks in ((0, xl, RIGHT), (size_x - 1, xr, LEFT)):
                     if x == at and k in ks:
                         row = ks.index(k) * size_y + y
                         value = value + side[row : row + TILE]
-                for at, side, ks in ((0, yd, UP), (size_y - 1, yu, DOWN)):
-                    if y <= at < y + TILE and k in ks:
-                        row = ks.index(k) * size_x + x
-                        value = value + jnp.where(row_of == at - y, side[row : row + 1], 0.0)
-                out_ref[k, x, y : y + TILE] = jnp.where(fluid, value, 0.0)
+                value = jnp.where(fluid_at(bits_ref, x, y), value, 0.0)
+                flat_ref[k, turned(x, y, size_x)] = value
+        copies.append(pltpu.make_async_copy(flat_ref.at[k], out_hbm.at[k], sems.at[k]))
+        copies[-1].start()
+    for copy in copies:
+        copy.wait()
+
+
+def end_kernel(out_in, flat_ref, mask_ref, yd, yu, out_hbm, planes, sems):
+    del out_in
+    layers = planes.shape[1]
+    last = flat_ref.shape[1] - layers
+    copies = []
+    for at, side, ks in ((0, yd, UP), (last, yu, DOWN)):
+        for j, k in enumerate(ks):
+            i = len(copies)
+            entering = side[j * layers : (j + 1) * layers]
+            fluid = mask_ref[0, at : at + layers] > 0.5
+            planes[i] = jnp.where(fluid, flat_ref[k, at : at + layers] + entering, 0.0)
+            target = out_hbm.at[k, pl.ds(at, layers)]
+            copies.append(pltpu.make_async_copy(planes.at[i], target, sems.at[i]))
+            copies[-1].start()
+    for copy in copies:
+        copy.wait()
 
 
 VMEM = pl.BlockSpec(memory_space=pltpu.VMEM)
@@ -564,18 +571,19 @@
 HBM = pl.BlockSpec(memory_space=pltpu.HBM)
 
 
-def call(kernel, outs, args, special=None, scratch=(), cost=None):
-    special = special or {}
+def call(kernel, outs, args, special=None, special_out=None, scratch=(), cost=None, **kwargs):
+    special, special_out = special or {}, special_out or {}
     return pl.pallas_call(
         kernel,
         out_shape=[jax.ShapeDtypeStruct(shape, dtype) for shape, dtype in outs],
         in_specs=[special.get(i, VMEM) for i in range(len(args))],
-        out_specs=[VMEM] * len(outs),
+        out_specs=[special_out.get(i, VMEM) for i in range(len(outs))],
         scratch_shapes=[
             pltpu.VMEM(item, jnp.float32) if isinstance(item, tuple) else item for item in scratch
         ],
         compiler_params=pltpu.CompilerParams(vmem_limit_bytes=16 * 2**20),
         cost_estimate=cost,
+        **kwargs,
     )(*args)
 
 
@@ -588,69 +596,59 @@
     )
 
 
-def exchange(pairs, a, b, axis):
-    if not pairs:
-        return shift(a, b, axis)
-    count = lax.axis_size(axis)
-    partners = [
-        [(i, (i + (1 if i % 2 == parity else -1)) % count) for i in range(count)]
-        for parity in range(2)
-    ]
-    b = lax.ppermute(b, axis, partners[1])
-    return lax.ppermute(a, axis, partners[0]), b
-
-
 def per_device(populations, fluid_mask, wet_class, wall_potential, relax_rates):
-    size_x, size_y, size_z = fluid_mask.shape
+    rows_x, rows_y, size_z = fluid_mask.shape
+    size_x, size_y = rows_y, rows_x
+    cells = size_x * size_y
     f32, i32 = jnp.float32, jnp.int32
-    pairs = lax.axis_size("gy") % 2 == 0
     whole = ((size_x, size_y, size_z), f32)
     rows = lambda count: ((count, size_z), f32)
     fields = lambda count: ((N, count, size_y, size_z), f32)
+    flat = lambda count: ((count, cells, size_z), f32)
     padded = (size_x + 2, size_y + PAD, size_z)
-    start_rows = rows(2 * size_x + TILE)
-
-    f, mask, pot0, right, left = call(
+    operations = 400 * cells * size_z
+    cost = pl.CostEstimate(flops=operations, bytes_accessed=4 * operations // 20, transcendentals=0)
+
+    operands = [
+        pltpu.with_memory_space_constraint(item, pltpu.HBM)
+        for item in (
+            populations.reshape(N, cells, size_z),
+            fluid_mask.reshape(cells, size_z),
+            wet_class.reshape(cells, size_z),
+            wall_potential,
+        )
+    ]
+    raw, flat_mask, mask, pot0, right, left = call(
         start_kernel,
-        [fields(size_x), whole, whole, rows(2 * size_y), rows(2 * size_y)],
-        [
-            pltpu.with_memory_space_constraint(item, pltpu.HBM)
-            for item in (populations, fluid_mask, wet_class, wall_potential)
-        ],
+        [flat(N), flat(2), whole, whole, rows(2 * size_y), rows(2 * size_y)],
+        operands,
         special={i: HBM for i in range(4)},
         scratch=[
-            pltpu.VMEM(fluid_mask.shape, i32),
-            pltpu.VMEM(wet_class.shape, i32),
+            pltpu.VMEM((cells, size_z), i32),
+            pltpu.VMEM((cells, size_z), i32),
             pltpu.SMEM(wall_potential.shape, f32),
             pltpu.SemaphoreType.DMA((N,)),
             pltpu.SemaphoreType.DMA((3,)),
         ],
     )
-    x0l, x0r = shift(right, left, "gx")
-    a, b = call(
-        functools.partial(start_pack_kernel, pairs),
-        [start_rows] * 2,
-        (pot0, mask, x0l, x0r),
-        scratch=[start_rows[0]] * 2,
-    )
-    a, b = exchange(pairs, a, b, "gy")
-    bits, y0d, y0u = call(
-        functools.partial(bits_kernel, pairs),
-        [((size_x, size_y, size_z), i32), start_rows, start_rows],
-        (mask, x0l, x0r, a, b),
+    x0l, x0r = shift(right, left, "gy")
+    (f,) = call(turn_kernel, [fields(size_x)], (raw,), cost=cost)
+    up, down = call(start_pack_kernel, [rows(2 * size_x + TILE)] * 2, (pot0, mask, x0l, x0r))
+    y0d, y0u = shift(up, down, "gx")
+    (bits,) = call(
+        bits_kernel,
+        [((size_x, size_y, size_z), i32)],
+        (mask, x0l, x0r, y0d, y0u),
         scratch=[padded],
     )
     edge2, edge1 = len(two_layers(size_x)), len(one_layer(size_x))
-    operations = 400 * size_x * size_y * size_z
-    cost = pl.CostEstimate(flops=operations, bytes_accessed=4 * operations // 20, transcendentals=0)
     held, sent = (f,), ()
     for step in range(STEPS):
         first, last = step == 0, step == STEPS - 1
         parts = 5 if last else 6
         x_rows, y_rows = rows(parts * size_y + TILE), rows(parts * size_x + (0 if last else TILE))
-        halo_rows = (6 * size_x + TILE, size_z)
         pot, post, f_edge, right, left, rest = call(
-            functools.partial(edge_kernel, first, last, pairs),
+            functools.partial(edge_kernel, first, last),
             [
                 (padded, f32),
                 ((N, edge2, size_y + PAD, size_z), f32),
@@ -661,40 +659,49 @@
             ],
             (relax_rates, bits, pot0, x0l, x0r, y0d, y0u, *held, *sent),
             special={0: SMEM},
-            scratch=[] if first else [halo_rows] * 4,
             cost=cost,
         )
-        xl, xr = shift(right, left, "gx")
+        xl, xr = shift(right, left, "gy")
         f_middle, up, down, more = call(
-            functools.partial(middle_kernel, first, last, pairs),
+            functools.partial(middle_kernel, first, last),
             [
                 fields(size_x - edge1),
                 y_rows,
                 y_rows,
-                ((3, *whole[0]) if last else (size_x - edge1, size_y, size_z), f32),
+                flat(3) if last else ((size_x - edge1, size_y, size_z), f32),
             ],
             (relax_rates, bits, pot, post, rest, *held[:2], *sent[2:4]),
             special={0: SMEM},
-            scratch=[(N, size_x - edge2, size_y + PAD, size_z)]
-            + ([] if first else [halo_rows] * 2),
+            scratch=[(N, size_x - edge2, size_y + PAD, size_z)],
             cost=cost,
         )
-        a, b = call(
-            functools.partial(pack_kernel, last, pairs, size_x, size_y),
+        up, down = call(
+            functools.partial(pack_kernel, last, size_x, size_y),
             [y_rows, y_rows],
             (up, down, xl, xr, right, left),
-            scratch=[y_rows[0]] * 2,
         )
-        ya, yb = exchange(pairs, a, b, "gy")
+        yd, yu = shift(up, down, "gx")
         held = (f_edge, f_middle, rest, more)
-        sent = (xl, xr, ya, yb, right, left, a, b)
+        sent = (xl, xr, yd, yu, right, left, up, down)
+    out, flat_f = call(
+        write_kernel,
+        [flat(N), flat(N)],
+        (f_edge, f_middle, bits, xl, xr),
+        special_out={0: HBM},
+        scratch=[pltpu.SemaphoreType.DMA((N,))],
+        cost=cost,
+    )
     (out,) = call(
-        functools.partial(end_kernel, pairs),
-        [fields(size_x)],
-        (f_edge, f_middle, bits, xl, xr, ya, yb),
-        scratch=[y_rows[0]] * 2,
+        end_kernel,
+        [flat(N)],
+        (out, flat_f, flat_mask, yd, yu),
+        special={0: HBM},
+        special_out={0: HBM},
+        scratch=[(10, size_x, size_z), pltpu.SemaphoreType.DMA((10,))],
+        input_output_aliases={0: 0},
     )
-    return out, more
+    shape = (rows_x, rows_y, size_z)
+    return out.reshape(N, *shape), more.reshape(3, *shape)
 
 
 def solution(mesh):

time: 58.5 us -> 58.3 us (level)
  waiting for transfers between devices: 14.9 us -> 12.8 us
  Pallas kernels: 13.2 us -> 14.4 us
  starting transfers between devices: 29.5 us -> 30.3 us
    ppermute x10 -> x0, starting transfers between devices: 8.8 us -> none  [the longest x5 8.44 us: exchange(): b = lax.ppermute(b, axis, partners[1])]
    ppermute x10 -> x0, waiting for transfers between devices: 8.09 us -> none  [the longest x5 8.08 us: exchange(): b = lax.ppermute(b, axis, partners[1])]
    ppermute x5 -> x10, starting transfers between devices: 12.4 us -> 20.4 us  [shift(): lax.ppermute(backward, axis, [(b, a) for a, b in ahead])]
    ppermute x5 -> x10, waiting for transfers between devices: 5.41 us -> 11.2 us  [shift(): lax.ppermute(forward, axis, ahead)]
    ppermute x5 -> x10, starting transfers between devices: 8.28 us -> 9.84 us  [shift(): lax.ppermute(forward, axis, ahead)]
    pallas_call x16 -> x18, Pallas kernels: 13.2 us -> 14.4 us  [call(): pl.pallas_call(kernel, out_shape=[jax.ShapeDtypeStruct(shape, dtype) for...]
    ppermute x5 -> x10, waiting for transfers between devices: 1.4 us -> 1.52 us  [shift(): lax.ppermute(backward, axis, [(b, a) for a, b in ahead])]
  transfers between devices with their start and end apart: 20 -> 20, of which waited for: 15 -> 13; matrix products, arithmetic and copies ran while one was open for 0% -> 0% of each run, Pallas kernels for 9% -> 14%
where the time goes in v4:
time: 58.3 us; the launch traced here: 58.1 us
  starting transfers between devices  30.3 us (52%)
  Pallas kernels  14.4 us (25%)
  waiting for transfers between devices  12.8 us (22%)
  between operations  0.73 us (1%)
    ppermute x10, starting transfers between devices, shift(): lax.ppermute(backward, axis, [(b, a) for a, b in ahead])  20.4 us
    pallas_call x18, Pallas kernels, call(): pl.pallas_call(kernel, out_shape=[jax.ShapeDtypeStruct(shape, dtype) for...  14.4 us
    ppermute x10, waiting for transfers between devices, shift(): lax.ppermute(forward, axis, ahead)  11.2 us
    ppermute x10, starting transfers between devices, shift(): lax.ppermute(forward, axis, ahead)  9.84 us
    ppermute x10, waiting for transfers between devices, shift(): lax.ppermute(backward, axis, [(b, a) for a, b in ahead])  1.52 us
  transfers between devices with their start and end apart: 20, of which 13 were waited for; matrix products, arithmetic and copies ran while one was open for 0% of the time, Pallas kernels for 14%

profile of v4, /device:TPU:0, one launch (start us, length us, event | category | flops | bytes accessed | tf_op | source)
XLA Modules:
  0.0 58.1 jit_solution(18212872535996668548)
XLA Ops:
  0.6 1.7 %shard_map.68 = (f32[19,128,128]{2,1,0:T(8,128)S(1)}, f32[2,128,128]{2,1,0:T(8,128)S(1)}, f32[16,8,128]{2,1,0:T(8,128)S(1)}, f32[16,8,128]{2,1,0:T(8,128)S(1)}, ...) custom-call(f32[19,128,128]{2,1,0:T(8,128)} %bitcast.5, s32[128,128]{1,0:T(8,128)} %bitcast.7, s32[128,128]{1,0:T(8,128)} %bitcast.8, ...), custom_call_target="tpu_custom_call" | custom-call | tf_op jit(solution)/shard_map/pallas_call | solution.py:576
  2.3 0.5 collective-permute-start
  2.9 2.0 %collective-permute-start.1 = (f32[16,128]{1,0:T(8,128)S(1)}, f32[16,128]{1,0:T(8,128)S(1)}, u32[]{:S(2)}, u32[]{:S(2)}) collective-permute-start(f32[16,128]{1,0:T(8,128)S(1)} %get-tuple-element.62), channel_id=1, source_target_pairs={{1,0},{2,1},{3,2},{0,3},{5,4},{6,5},{7,6},{4,7},{9,8},{10,9},{11,1... | collective-permute-start | bytes 24584 | tf_op jit(solution)/shard_map/ppermute | solution.py:595
  4.8 1.3 %collective-permute-done.from_left.x0l.refs_3_ = f32[16,128]{1,0:T(8,128)S(1)} collective-permute-done((f32[16,128]{1,0:T(8,128)S(1)}, f32[16,128]{1,0:T(8,128)S(1)}, u32[]{:S(2)}, u32[]{:S(2)}) %collective-permute-start) | collective-permute-done | bytes 8224 | tf_op jit(solution)/shard_map/ppermute | solution.py:594
  6.1 0.1 collective-permute-done.1.from_right.x0r.refs_4_
  6.2 2.4 %collective-permute-start.2 = (f32[40,128]{1,0:T(8,128)S(1)}, f32[40,128]{1,0:T(8,128)S(1)}, u32[]{:S(2)}, u32[]{:S(2)}) collective-permute-start(f32[40,128]{1,0:T(8,128)S(1)} %get-tuple-element.64), channel_id=1, source_target_pairs={{0,4},{4,8},{8,12},{12,0},{1,5},{5,9},{9,13},{13,1},{2,6},{6,10},{... | collective-permute-start | bytes 61448 | tf_op jit(solution)/shard_map/ppermute | solution.py:594
  8.6 2.1 %collective-permute-start.3 = (f32[40,128]{1,0:T(8,128)S(1)}, f32[40,128]{1,0:T(8,128)S(1)}, u32[]{:S(2)}, u32[]{:S(2)}) collective-permute-start(f32[40,128]{1,0:T(8,128)S(1)} %get-tuple-element.65), channel_id=1, source_target_pairs={{4,0},{8,4},{12,8},{0,12},{5,1},{9,5},{13,9},{1,13},{6,2},{10,6},{... | collective-permute-start | bytes 61448 | tf_op jit(solution)/shard_map/ppermute | solution.py:595
  10.7 0.0 copy-start
  10.7 0.4 shard_map.71.refs_7_.refs_5_
  11.1 1.4 %collective-permute-done.2.y0d.refs_5_ = f32[40,128]{1,0:T(8,128)S(1)} collective-permute-done((f32[40,128]{1,0:T(8,128)S(1)}, f32[40,128]{1,0:T(8,128)S(1)}, u32[]{:S(2)}, u32[]{:S(2)}) %collective-permute-start.2) | collective-permute-done | bytes 20512 | tf_op jit(solution)/shard_map/ppermute | solution.py:594
  12.5 0.2 collective-permute-done.3.y0u.refs_6_
  12.7 0.2 shard_map.70.refs_1_.bits_ref
  13.0 0.0 copy-done
  13.0 0.9 %shard_map.72 = (f32[18,24,128]{2,1,0:T(8,128)S(1)}, f32[19,4,24,128]{3,2,1,0:T(8,128)S(1)}, f32[19,2,8,128]{3,2,1,0:T(8,128)S(1)}, f32[56,128]{1,0:T(8,128)S(1)...) custom-call(f32[19]{0:T(128)S(1)} %copy-done, s32[16,8,128]{2,1,0:T(8,128)S(1)} %shard_map.70.refs_1_.bits_ref, ...), custom_call_target="tpu_custom_call" | custom-call | flops 6553600 | bytes 1310720 | tf_op jit(solution)/shard_map/pallas_call | solution.py:576
  13.9 0.4 collective-permute-start.4
  14.3 1.4 %collective-permute-start.5 = (f32[56,128]{1,0:T(8,128)S(1)}, f32[56,128]{1,0:T(8,128)S(1)}, u32[]{:S(2)}, u32[]{:S(2)}) collective-permute-start(f32[56,128]{1,0:T(8,128)S(1)} %get-tuple-element.74.refs_5_.refs_16_), channel_id=1, source_target_pairs={{1,0},{2,1},{3,2},{0,3},{5,4},{6,5},{7,6},{4,7},{9,8},{10,9},{11,1... | collective-permute-start | bytes 86024 | tf_op jit(solution)/shard_map/ppermute | solution.py:595
  15.7 1.4 %shard_map.73 = (f32[19,14,8,128]{3,2,1,0:T(8,128)S(1)}, f32[104,128]{1,0:T(8,128)S(1)}, f32[104,128]{1,0:T(8,128)S(1)}, f32[14,8,128]{2,1,0:T(8,128)S(1)}) custom-call(f32[19]{0:T(128)S(1)} %copy-done, s32[16,8,128]{2,1,0:T(8,128)S(1)} %shard_map.70.refs_1_.bits_ref, f32[18,24,128]{2,1,0:T(8,128)S(1)} %get-tuple-element.68.refs_2_, ...), custom_call_target="tpu_custom_call" | custom-call | flops 6553600 | bytes 1310720 | tf_op jit(solution)/shard_map/pallas_call | solution.py:576
  17.1 0.1 collective-permute-done.4.refs_2_.refs_11_
  17.2 0.0 collective-permute-done.5.refs_3_.refs_12_
  17.2 1.4 %collective-permute-start.6 = (f32[104,128]{1,0:T(8,128)S(1)}, f32[104,128]{1,0:T(8,128)S(1)}, u32[]{:S(2)}, u32[]{:S(2)}) collective-permute-start(f32[104,128]{1,0:T(8,128)S(1)} %get-tuple-element.77.refs_17_), channel_id=1, source_target_pairs={{0,4},{4,8},{8,12},{12,0},{1,5},{5,9},{9,13},{13,1},{2,6},{6,10},{... | collective-permute-start | bytes 159752 | tf_op jit(solution)/shard_map/ppermute | solution.py:594
  18.6 2.5 %collective-permute-start.7 = (f32[104,128]{1,0:T(8,128)S(1)}, f32[104,128]{1,0:T(8,128)S(1)}, u32[]{:S(2)}, u32[]{:S(2)}) collective-permute-start(f32[104,128]{1,0:T(8,128)S(1)} %get-tuple-element.78.refs_18_), channel_id=1, source_target_pairs={{4,0},{8,4},{12,8},{0,12},{5,1},{9,5},{13,9},{1,13},{6,2},{10,6},{... | collective-permute-start | bytes 159752 | tf_op jit(solution)/shard_map/ppermute | solution.py:595
  21.1 2.2 %collective-permute-done.6.refs_13_.refs_7_ = f32[104,128]{1,0:T(8,128)S(1)} collective-permute-done((f32[104,128]{1,0:T(8,128)S(1)}, f32[104,128]{1,0:T(8,128)S(1)}, u32[]{:S(2)}, u32[]{:S(2)}) %collective-permute-start.6) | collective-permute-done | bytes 53280 | tf_op jit(solution)/shard_map/ppermute | solution.py:594
  23.3 0.9 %collective-permute-done.7.refs_14_.refs_8_ = f32[104,128]{1,0:T(8,128)S(1)} collective-permute-done((f32[104,128]{1,0:T(8,128)S(1)}, f32[104,128]{1,0:T(8,128)S(1)}, u32[]{:S(2)}, u32[]{:S(2)}) %collective-permute-start.7) | collective-permute-done | bytes 53280 | tf_op jit(solution)/shard_map/ppermute | solution.py:595
  24.2 0.9 %shard_map.75 = (f32[18,24,128]{2,1,0:T(8,128)S(1)}, f32[19,4,24,128]{3,2,1,0:T(8,128)S(1)}, f32[19,2,8,128]{3,2,1,0:T(8,128)S(1)}, f32[56,128]{1,0:T(8,128)S(1)...) custom-call(f32[19]{0:T(128)S(1)} %copy-done, s32[16,8,128]{2,1,0:T(8,128)S(1)} %shard_map.70.refs_1_.bits_ref, ...), custom_call_target="tpu_custom_call" | custom-call | flops 6553600 | bytes 1310720 | tf_op jit(solution)/shard_map/pallas_call | solution.py:576
  25.1 0.2 collective-permute-start.8
  25.3 1.6 %collective-permute-start.9 = (f32[56,128]{1,0:T(8,128)S(1)}, f32[56,128]{1,0:T(8,128)S(1)}, u32[]{:S(2)}, u32[]{:S(2)}) collective-permute-start(f32[56,128]{1,0:T(8,128)S(1)} %get-tuple-element.86.refs_5_.refs_16_), channel_id=1, source_target_pairs={{1,0},{2,1},{3,2},{0,3},{5,4},{6,5},{7,6},{4,7},{9,8},{10,9},{11,1... | collective-permute-start | bytes 86024 | tf_op jit(solution)/shard_map/ppermute | solution.py:595
  26.9 1.4 %shard_map.76 = (f32[19,14,8,128]{3,2,1,0:T(8,128)S(1)}, f32[104,128]{1,0:T(8,128)S(1)}, f32[104,128]{1,0:T(8,128)S(1)}, f32[14,8,128]{2,1,0:T(8,128)S(1)}) custom-call(f32[19]{0:T(128)S(1)} %copy-done, s32[16,8,128]{2,1,0:T(8,128)S(1)} %shard_map.70.refs_1_.bits_ref, f32[18,24,128]{2,1,0:T(8,128)S(1)} %get-tuple-element.80.refs_2_, ...), custom_call_target="tpu_custom_call" | custom-call | flops 6553600 | bytes 1310720 | tf_op jit(solution)/shard_map/pallas_call | solution.py:576
  28.4 0.1 collective-permute-done.8.refs_2_.refs_11_
  28.5 0.0 collective-permute-done.9.refs_3_.refs_12_
  28.5 1.1 %collective-permute-start.10 = (f32[104,128]{1,0:T(8,128)S(1)}, f32[104,128]{1,0:T(8,128)S(1)}, u32[]{:S(2)}, u32[]{:S(2)}) collective-permute-start(f32[104,128]{1,0:T(8,128)S(1)} %get-tuple-element.89.refs_17_), channel_id=1, source_target_pairs={{0,4},{4,8},{8,12},{12,0},{1,5},{5,9},{9,13},{13,1},{2,6},{6,10},{... | collective-permute-start | bytes 159752 | tf_op jit(solution)/shard_map/ppermute | solution.py:594
  29.6 2.8 %collective-permute-start.11 = (f32[104,128]{1,0:T(8,128)S(1)}, f32[104,128]{1,0:T(8,128)S(1)}, u32[]{:S(2)}, u32[]{:S(2)}) collective-permute-start(f32[104,128]{1,0:T(8,128)S(1)} %get-tuple-element.90.refs_18_), channel_id=1, source_target_pairs={{4,0},{8,4},{12,8},{0,12},{5,1},{9,5},{13,9},{1,13},{6,2},{10,6},{... | collective-permute-start | bytes 159752 | tf_op jit(solution)/shard_map/ppermute | solution.py:595
  32.4 2.5 %collective-permute-done.10.refs_13_.refs_7_ = f32[104,128]{1,0:T(8,128)S(1)} collective-permute-done((f32[104,128]{1,0:T(8,128)S(1)}, f32[104,128]{1,0:T(8,128)S(1)}, u32[]{:S(2)}, u32[]{:S(2)}) %collective-permute-start.10) | collective-permute-done | bytes 53280 | tf_op jit(solution)/shard_map/ppermute | solution.py:594
  34.9 0.0 collective-permute-done.11.refs_14_.refs_8_
  34.9 0.9 %shard_map.78 = (f32[18,24,128]{2,1,0:T(8,128)S(1)}, f32[19,4,24,128]{3,2,1,0:T(8,128)S(1)}, f32[19,2,8,128]{3,2,1,0:T(8,128)S(1)}, f32[56,128]{1,0:T(8,128)S(1)...) custom-call(f32[19]{0:T(128)S(1)} %copy-done, s32[16,8,128]{2,1,0:T(8,128)S(1)} %shard_map.70.refs_1_.bits_ref, ...), custom_call_target="tpu_custom_call" | custom-call | flops 6553600 | bytes 1310720 | tf_op jit(solution)/shard_map/pallas_call | solution.py:576
  35.8 0.4 collective-permute-start.12
  36.2 1.4 %collective-permute-start.13 = (f32[56,128]{1,0:T(8,128)S(1)}, f32[56,128]{1,0:T(8,128)S(1)}, u32[]{:S(2)}, u32[]{:S(2)}) collective-permute-start(f32[56,128]{1,0:T(8,128)S(1)} %get-tuple-element.98.refs_5_.refs_16_), channel_id=1, source_target_pairs={{1,0},{2,1},{3,2},{0,3},{5,4},{6,5},{7,6},{4,7},{9,8},{10,9},{11,1... | collective-permute-start | bytes 86024 | tf_op jit(solution)/shard_map/ppermute | solution.py:595
  37.6 1.4 %shard_map.79 = (f32[19,14,8,128]{3,2,1,0:T(8,128)S(1)}, f32[104,128]{1,0:T(8,128)S(1)}, f32[104,128]{1,0:T(8,128)S(1)}, f32[14,8,128]{2,1,0:T(8,128)S(1)}) custom-call(f32[19]{0:T(128)S(1)} %copy-done, s32[16,8,128]{2,1,0:T(8,128)S(1)} %shard_map.70.refs_1_.bits_ref, f32[18,24,128]{2,1,0:T(8,128)S(1)} %get-tuple-element.92.refs_2_, ...), custom_call_target="tpu_custom_call" | custom-call | flops 6553600 | bytes 1310720 | tf_op jit(solution)/shard_map/pallas_call | solution.py:576
  39.1 0.1 collective-permute-done.12.refs_2_.refs_11_
  39.2 0.0 collective-permute-done.13.refs_3_.refs_12_
  39.2 1.0 %collective-permute-start.14 = (f32[104,128]{1,0:T(8,128)S(1)}, f32[104,128]{1,0:T(8,128)S(1)}, u32[]{:S(2)}, u32[]{:S(2)}) collective-permute-start(f32[104,128]{1,0:T(8,128)S(1)} %get-tuple-element.101.refs_17_), channel_id=1, source_target_pairs={{0,4},{4,8},{8,12},{12,0},{1,5},{5,9},{9,13},{13,1},{2,6},{6,10},{... | collective-permute-start | bytes 159752 | tf_op jit(solution)/shard_map/ppermute | solution.py:594
  40.2 3.1 %collective-permute-start.15 = (f32[104,128]{1,0:T(8,128)S(1)}, f32[104,128]{1,0:T(8,128)S(1)}, u32[]{:S(2)}, u32[]{:S(2)}) collective-permute-start(f32[104,128]{1,0:T(8,128)S(1)} %get-tuple-element.102.refs_18_), channel_id=1, source_target_pairs={{4,0},{8,4},{12,8},{0,12},{5,1},{9,5},{13,9},{1,13},{6,2},{10,6},{... | collective-permute-start | bytes 159752 | tf_op jit(solution)/shard_map/ppermute | solution.py:595
  43.3 2.3 %collective-permute-done.14.refs_13_.refs_7_ = f32[104,128]{1,0:T(8,128)S(1)} collective-permute-done((f32[104,128]{1,0:T(8,128)S(1)}, f32[104,128]{1,0:T(8,128)S(1)}, u32[]{:S(2)}, u32[]{:S(2)}) %collective-permute-start.14) | collective-permute-done | bytes 53280 | tf_op jit(solution)/shard_map/ppermute | solution.py:594
  45.6 0.0 collective-permute-done.15.refs_14_.refs_8_
  45.6 0.9 %shard_map.81 = (f32[18,24,128]{2,1,0:T(8,128)S(1)}, f32[19,4,24,128]{3,2,1,0:T(8,128)S(1)}, f32[19,2,8,128]{3,2,1,0:T(8,128)S(1)}, f32[48,128]{1,0:T(8,128)S(1)...) custom-call(f32[19]{0:T(128)S(1)} %copy-done, s32[16,8,128]{2,1,0:T(8,128)S(1)} %shard_map.70.refs_1_.bits_ref, ...), custom_call_target="tpu_custom_call" | custom-call | flops 6553600 | bytes 1310720 | tf_op jit(solution)/shard_map/pallas_call | solution.py:576
  46.5 0.3 collective-permute-start.16
  46.9 1.5 %collective-permute-start.17 = (f32[48,128]{1,0:T(8,128)S(1)}, f32[48,128]{1,0:T(8,128)S(1)}, u32[]{:S(2)}, u32[]{:S(2)}) collective-permute-start(f32[48,128]{1,0:T(8,128)S(1)} %get-tuple-element.109.refs_5_), channel_id=1, source_target_pairs={{1,0},{2,1},{3,2},{0,3},{5,4},{6,5},{7,6},{4,7},{9,8},{10,9},{11,1... | collective-permute-start | bytes 73736 | tf_op jit(solution)/shard_map/ppermute | solution.py:595
  48.3 2.1 %shard_map.82 = (f32[19,14,8,128]{3,2,1,0:T(8,128)S(1)}, f32[80,128]{1,0:T(8,128)S(1)}, f32[80,128]{1,0:T(8,128)S(1)}, f32[3,128,128]{2,1,0:T(8,128)}) custom-call(f32[19]{0:T(128)S(1)} %copy-done, s32[16,8,128]{2,1,0:T(8,128)S(1)} %shard_map.70.refs_1_.bits_ref, f32[18,24,128]{2,1,0:T(8,128)S(1)} %get-tuple-element.104.refs_2_, ...), custom_call_target="tpu_custom_call" | custom-call | flops 6553600 | bytes 1310720 | tf_op jit(solution)/shard_map/pallas_call | solution.py:576
  50.4 0.0 collective-permute-done.16.xl.refs_2_
  50.4 0.0 collective-permute-done.17.xr.refs_3_
  50.5 2.1 %collective-permute-start.18 = (f32[80,128]{1,0:T(8,128)S(1)}, f32[80,128]{1,0:T(8,128)S(1)}, u32[]{:S(2)}, u32[]{:S(2)}) collective-permute-start(f32[80,128]{1,0:T(8,128)S(1)} %get-tuple-element.115), channel_id=1, source_target_pairs={{0,4},{4,8},{8,12},{12,0},{1,5},{5,9},{9,13},{13,1},{2,6},{6,10},{... | collective-permute-start | bytes 122888 | tf_op jit(solution)/shard_map/ppermute | solution.py:594
  52.5 2.2 %collective-permute-start.19 = (f32[80,128]{1,0:T(8,128)S(1)}, f32[80,128]{1,0:T(8,128)S(1)}, u32[]{:S(2)}, u32[]{:S(2)}) collective-permute-start(f32[80,128]{1,0:T(8,128)S(1)} %get-tuple-element.116), channel_id=1, source_target_pairs={{4,0},{8,4},{12,8},{0,12},{5,1},{9,5},{13,9},{1,13},{6,2},{10,6},{... | collective-permute-start | bytes 122888 | tf_op jit(solution)/shard_map/ppermute | solution.py:595
  54.7 1.2 %shard_map.83 = (f32[19,128,128]{2,1,0:T(8,128)}, f32[19,128,128]{2,1,0:T(8,128)S(1)}) custom-call(f32[19,2,8,128]{3,2,1,0:T(8,128)S(1)} %get-tuple-element.103.f_edge, f32[19,14,8,128]{3,2,1,0:T(8,128)S(1)} %get-tuple-element.107.f_middle, s32[16,8,128]{2,1,0:T(8,128)S(1)} %shard_map.70.refs_1_.bits_ref, f32[48,128]{1,0:T(8,128)S(1)} %collective-permute-done.16.xl.refs_2_, ...), custom_call_target="tpu_custom_call" | custom-call | flops 6553600 | bytes 1310720 | tf_op jit(solution)/shard_map/pallas_call | solution.py:576
  55.9 1.2 %collective-permute-done.18.yd = f32[80,128]{1,0:T(8,128)S(1)} collective-permute-done((f32[80,128]{1,0:T(8,128)S(1)}, f32[80,128]{1,0:T(8,128)S(1)}, u32[]{:S(2)}, u32[]{:S(2)}) %collective-permute-start.18) | collective-permute-done | bytes 40992 | tf_op jit(solution)/shard_map/ppermute | solution.py:594
  57.1 0.3 collective-permute-done.19.yu
  57.4 0.7 %shard_map.85 = f32[19,128,128]{2,1,0:T(8,128)} custom-call(f32[19,128,128]{2,1,0:T(8,128)} %get-tuple-element.110.out_in, f32[19,128,128]{2,1,0:T(8,128)S(1)} %get-tuple-element.111.flat_ref, f32[2,128,128]{2,1,0:T(8,128)S(1)} %get-tuple-element.112.mask_ref, f32[80,128]{1,0:T(8,128)S(1)} %collective-permute-done.18.yd, ...), custom_call_target="tpu_custom_call", output_to_operand_aliasing={{}: (0, {})} | custom-call | tf_op jit(solution)/shard_map/pallas_call | solution.py:576
  (5 shorter events, 0.1 us)
Async XLA Ops:
  2.3 3.8 %collective-permute-start = (f32[16,128]{1,0:T(8,128)S(1)}, f32[16,128]{1,0:T(8,128)S(1)}, u32[]{:S(2)}, u32[]{:S(2)}) collective-permute-start(f32[16,128]{1,0:T(8,128)S(1)} %get-tuple-element.61), channel_id=1, source_target_pairs={{0,1},{1,2},{2,3},{3,0},{4,5},{5,6},{6,7},{7,4},{8,9},{9,10},{10,1... | collective-permute-start | bytes 24584 | tf_op jit(solution)/shard_map/ppermute | solution.py:594
  2.9 3.3 %collective-permute-start.1 = (f32[16,128]{1,0:T(8,128)S(1)}, f32[16,128]{1,0:T(8,128)S(1)}, u32[]{:S(2)}, u32[]{:S(2)}) collective-permute-start(f32[16,128]{1,0:T(8,128)S(1)} %get-tuple-element.62), channel_id=1, source_target_pairs={{1,0},{2,1},{3,2},{0,3},{5,4},{6,5},{7,6},{4,7},{9,8},{10,9},{11,1... | collective-permute-start | bytes 24584 | tf_op jit(solution)/shard_map/ppermute | solution.py:595
  6.2 6.3 %collective-permute-start.2 = (f32[40,128]{1,0:T(8,128)S(1)}, f32[40,128]{1,0:T(8,128)S(1)}, u32[]{:S(2)}, u32[]{:S(2)}) collective-permute-start(f32[40,128]{1,0:T(8,128)S(1)} %get-tuple-element.64), channel_id=1, source_target_pairs={{0,4},{4,8},{8,12},{12,0},{1,5},{5,9},{9,13},{13,1},{2,6},{6,10},{... | collective-permute-start | bytes 61448 | tf_op jit(solution)/shard_map/ppermute | solution.py:594
  8.6 4.1 %collective-permute-start.3 = (f32[40,128]{1,0:T(8,128)S(1)}, f32[40,128]{1,0:T(8,128)S(1)}, u32[]{:S(2)}, u32[]{:S(2)}) collective-permute-start(f32[40,128]{1,0:T(8,128)S(1)} %get-tuple-element.65), channel_id=1, source_target_pairs={{4,0},{8,4},{12,8},{0,12},{5,1},{9,5},{13,9},{1,13},{6,2},{10,6},{... | collective-permute-start | bytes 61448 | tf_op jit(solution)/shard_map/ppermute | solution.py:595
  10.7 2.3 %copy-start = (f32[19]{0:T(128)S(1)}, f32[19]{0:T(128)}, u32[]{:S(2)}) copy-start(f32[19]{0:T(128)} %refs_0_.15) | copy-start | bytes 232
  13.9 3.3 %collective-permute-start.4 = (f32[56,128]{1,0:T(8,128)S(1)}, f32[56,128]{1,0:T(8,128)S(1)}, u32[]{:S(2)}, u32[]{:S(2)}) collective-permute-start(f32[56,128]{1,0:T(8,128)S(1)} %get-tuple-element.73.refs_4_.refs_15_), channel_id=1, source_target_pairs={{0,1},{1,2},{2,3},{3,0},{4,5},{5,6},{6,7},{7,4},{8,9},{9,10},{10,1... | collective-permute-start | bytes 86024 | tf_op jit(solution)/shard_map/ppermute | solution.py:594
  14.3 2.9 %collective-permute-start.5 = (f32[56,128]{1,0:T(8,128)S(1)}, f32[56,128]{1,0:T(8,128)S(1)}, u32[]{:S(2)}, u32[]{:S(2)}) collective-permute-start(f32[56,128]{1,0:T(8,128)S(1)} %get-tuple-element.74.refs_5_.refs_16_), channel_id=1, source_target_pairs={{1,0},{2,1},{3,2},{0,3},{5,4},{6,5},{7,6},{4,7},{9,8},{10,9},{11,1... | collective-permute-start | bytes 86024 | tf_op jit(solution)/shard_map/ppermute | solution.py:595
  17.2 6.1 %collective-permute-start.6 = (f32[104,128]{1,0:T(8,128)S(1)}, f32[104,128]{1,0:T(8,128)S(1)}, u32[]{:S(2)}, u32[]{:S(2)}) collective-permute-start(f32[104,128]{1,0:T(8,128)S(1)} %get-tuple-element.77.refs_17_), channel_id=1, source_target_pairs={{0,4},{4,8},{8,12},{12,0},{1,5},{5,9},{9,13},{13,1},{2,6},{6,10},{... | collective-permute-start | bytes 159752 | tf_op jit(solution)/shard_map/ppermute | solution.py:594
  18.6 5.6 %collective-permute-start.7 = (f32[104,128]{1,0:T(8,128)S(1)}, f32[104,128]{1,0:T(8,128)S(1)}, u32[]{:S(2)}, u32[]{:S(2)}) collective-permute-start(f32[104,128]{1,0:T(8,128)S(1)} %get-tuple-element.78.refs_18_), channel_id=1, source_target_pairs={{4,0},{8,4},{12,8},{0,12},{5,1},{9,5},{13,9},{1,13},{6,2},{10,6},{... | collective-permute-start | bytes 159752 | tf_op jit(solution)/shard_map/ppermute | solution.py:595
  25.1 3.3 %collective-permute-start.8 = (f32[56,128]{1,0:T(8,128)S(1)}, f32[56,128]{1,0:T(8,128)S(1)}, u32[]{:S(2)}, u32[]{:S(2)}) collective-permute-start(f32[56,128]{1,0:T(8,128)S(1)} %get-tuple-element.85.refs_4_.refs_15_), channel_id=1, source_target_pairs={{0,1},{1,2},{2,3},{3,0},{4,5},{5,6},{6,7},{7,4},{8,9},{9,10},{10,1... | collective-permute-start | bytes 86024 | tf_op jit(solution)/shard_map/ppermute | solution.py:594
  25.3 3.2 %collective-permute-start.9 = (f32[56,128]{1,0:T(8,128)S(1)}, f32[56,128]{1,0:T(8,128)S(1)}, u32[]{:S(2)}, u32[]{:S(2)}) collective-permute-start(f32[56,128]{1,0:T(8,128)S(1)} %get-tuple-element.86.refs_5_.refs_16_), channel_id=1, source_target_pairs={{1,0},{2,1},{3,2},{0,3},{5,4},{6,5},{7,6},{4,7},{9,8},{10,9},{11,1... | collective-permute-start | bytes 86024 | tf_op jit(solution)/shard_map/ppermute | solution.py:595
  28.5 6.4 %collective-permute-start.10 = (f32[104,128]{1,0:T(8,128)S(1)}, f32[104,128]{1,0:T(8,128)S(1)}, u32[]{:S(2)}, u32[]{:S(2)}) collective-permute-start(f32[104,128]{1,0:T(8,128)S(1)} %get-tuple-element.89.refs_17_), channel_id=1, source_target_pairs={{0,4},{4,8},{8,12},{12,0},{1,5},{5,9},{9,13},{13,1},{2,6},{6,10},{... | collective-permute-start | bytes 159752 | tf_op jit(solution)/shard_map/ppermute | solution.py:594
  29.6 5.3 %collective-permute-start.11 = (f32[104,128]{1,0:T(8,128)S(1)}, f32[104,128]{1,0:T(8,128)S(1)}, u32[]{:S(2)}, u32[]{:S(2)}) collective-permute-start(f32[104,128]{1,0:T(8,128)S(1)} %get-tuple-element.90.refs_18_), channel_id=1, source_target_pairs={{4,0},{8,4},{12,8},{0,12},{5,1},{9,5},{13,9},{1,13},{6,2},{10,6},{... | collective-permute-start | bytes 159752 | tf_op jit(solution)/shard_map/ppermute | solution.py:595
  35.8 3.3 %collective-permute-start.12 = (f32[56,128]{1,0:T(8,128)S(1)}, f32[56,128]{1,0:T(8,128)S(1)}, u32[]{:S(2)}, u32[]{:S(2)}) collective-permute-start(f32[56,128]{1,0:T(8,128)S(1)} %get-tuple-element.97.refs_4_.refs_15_), channel_id=1, source_target_pairs={{0,1},{1,2},{2,3},{3,0},{4,5},{5,6},{6,7},{7,4},{8,9},{9,10},{10,1... | collective-permute-start | bytes 86024 | tf_op jit(solution)/shard_map/ppermute | solution.py:594
  36.2 2.9 %collective-permute-start.13 = (f32[56,128]{1,0:T(8,128)S(1)}, f32[56,128]{1,0:T(8,128)S(1)}, u32[]{:S(2)}, u32[]{:S(2)}) collective-permute-start(f32[56,128]{1,0:T(8,128)S(1)} %get-tuple-element.98.refs_5_.refs_16_), channel_id=1, source_target_pairs={{1,0},{2,1},{3,2},{0,3},{5,4},{6,5},{7,6},{4,7},{9,8},{10,9},{11,1... | collective-permute-start | bytes 86024 | tf_op jit(solution)/shard_map/ppermute | solution.py:595
  39.2 6.4 %collective-permute-start.14 = (f32[104,128]{1,0:T(8,128)S(1)}, f32[104,128]{1,0:T(8,128)S(1)}, u32[]{:S(2)}, u32[]{:S(2)}) collective-permute-start(f32[104,128]{1,0:T(8,128)S(1)} %get-tuple-element.101.refs_17_), channel_id=1, source_target_pairs={{0,4},{4,8},{8,12},{12,0},{1,5},{5,9},{9,13},{13,1},{2,6},{6,10},{... | collective-permute-start | bytes 159752 | tf_op jit(solution)/shard_map/ppermute | solution.py:594
  40.2 5.4 %collective-permute-start.15 = (f32[104,128]{1,0:T(8,128)S(1)}, f32[104,128]{1,0:T(8,128)S(1)}, u32[]{:S(2)}, u32[]{:S(2)}) collective-permute-start(f32[104,128]{1,0:T(8,128)S(1)} %get-tuple-element.102.refs_18_), channel_id=1, source_target_pairs={{4,0},{8,4},{12,8},{0,12},{5,1},{9,5},{13,9},{1,13},{6,2},{10,6},{... | collective-permute-start | bytes 159752 | tf_op jit(solution)/shard_map/ppermute | solution.py:595
  46.5 3.9 %collective-permute-start.16 = (f32[48,128]{1,0:T(8,128)S(1)}, f32[48,128]{1,0:T(8,128)S(1)}, u32[]{:S(2)}, u32[]{:S(2)}) collective-permute-start(f32[48,128]{1,0:T(8,128)S(1)} %get-tuple-element.108.refs_4_), channel_id=1, source_target_pairs={{0,1},{1,2},{2,3},{3,0},{4,5},{5,6},{6,7},{7,4},{8,9},{9,10},{10,1... | collective-permute-start | bytes 73736 | tf_op jit(solution)/shard_map/ppermute | solution.py:594
  46.9 3.6 %collective-permute-start.17 = (f32[48,128]{1,0:T(8,128)S(1)}, f32[48,128]{1,0:T(8,128)S(1)}, u32[]{:S(2)}, u32[]{:S(2)}) collective-permute-start(f32[48,128]{1,0:T(8,128)S(1)} %get-tuple-element.109.refs_5_), channel_id=1, source_target_pairs={{1,0},{2,1},{3,2},{0,3},{5,4},{6,5},{7,6},{4,7},{9,8},{10,9},{11,1... | collective-permute-start | bytes 73736 | tf_op jit(solution)/shard_map/ppermute | solution.py:595
  50.5 6.7 %collective-permute-start.18 = (f32[80,128]{1,0:T(8,128)S(1)}, f32[80,128]{1,0:T(8,128)S(1)}, u32[]{:S(2)}, u32[]{:S(2)}) collective-permute-start(f32[80,128]{1,0:T(8,128)S(1)} %get-tuple-element.115), channel_id=1, source_target_pairs={{0,4},{4,8},{8,12},{12,0},{1,5},{5,9},{9,13},{13,1},{2,6},{6,10},{... | collective-permute-start | bytes 122888 | tf_op jit(solution)/shard_map/ppermute | solution.py:594
  52.5 4.9 %collective-permute-start.19 = (f32[80,128]{1,0:T(8,128)S(1)}, f32[80,128]{1,0:T(8,128)S(1)}, u32[]{:S(2)}, u32[]{:S(2)}) collective-permute-start(f32[80,128]{1,0:T(8,128)S(1)} %get-tuple-element.116), channel_id=1, source_target_pairs={{4,0},{8,4},{12,8},{0,12},{5,1},{9,5},{13,9},{1,13},{6,2},{10,6},{... | collective-permute-start | bytes 122888 | tf_op jit(solution)/shard_map/ppermute | solution.py:595

commit v5 on v4

--- a/solution.py
+++ b/solution.py
@@ -162,11 +162,13 @@
             wall = jnp.where(wet == c, wall_in[c], wall)
         flat_ref[1, at] = wall
         flat_ref[0, at] = jnp.where(mask_in[at] == 1, 1.0, 0.0)
-    for copy in large:
+    density = None
+    for k, copy in enumerate(large):
         copy.wait()
-    for at in blocks:
-        density = total([raw_ref[k, at] for k in range(N)])
-        flat_ref[1, at] = potential_of(density, flat_ref[0, at] > 0.5, flat_ref[1, at])
+        here = [raw_ref[k, at] for at in blocks]
+        density = here if density is None else [a + b for a, b in zip(density, here)]
+    for at, value in zip(blocks, density):
+        flat_ref[1, at] = potential_of(value, flat_ref[0, at] > 0.5, flat_ref[1, at])
     for i in range(layers):
         mask_ref[i] = flat_ref[0, pl.ds(i, rows, stride=layers)]
         pot_ref[i] = flat_ref[1, pl.ds(i, rows, stride=layers)]
@@ -195,25 +197,47 @@
             ref[row + 2 : row + 3] = side[size_y + y : size_y + y + 1]
 
 
-def bits_kernel(mask_ref, x0l, x0r, y0d, y0u, bits_ref, pad_ref):
-    size_x, size_y = mask_ref.shape[0], mask_ref.shape[1]
+def bits_kernel(mask_ref, x0l, x0r, bits_ref, pad_ref):
+    size_x, size_y, size_z = mask_ref.shape
+    nothing = jnp.zeros((TILE, size_z), jnp.float32)
+    for x in range(size_x + 2):
+        pad_ref[x, :TILE] = nothing
+        pad_ref[x, TILE + size_y :] = nothing
     for x in range(size_x):
         pad_ref[1 + x, TILE : TILE + size_y] = mask_ref[x]
     for x, side in ((0, x0l), (1 + size_x, x0r)):
         pad_ref[x, TILE : TILE + size_y] = side[size_y:]
-    for y, side in ((TILE - 1, y0d), (TILE + size_y, y0u)):
-        for x in range(size_x):
-            pad_ref[1 + x, y : y + 1] = side[size_x + x : size_x + x + 1]
-        for x, row in ((0, 2 * size_x + 2), (1 + size_x, 2 * size_x + 3)):
-            pad_ref[x, y : y + 1] = side[row : row + 1]
     for x in range(size_x):
         for y in range(0, size_y, TILE):
-            bits = jnp.zeros((TILE, mask_ref.shape[2]), jnp.int32)
+            bits = jnp.zeros((TILE, size_z), jnp.int32)
             for k in range(N):
                 ex, ey, ez = SHIFT[k]
                 row = TILE + y - ey
                 source = roll_z(pad_ref[1 + x - ex, row : row + TILE], ez)
                 bits = bits | jnp.where(source > 0.5, 1 << k, 0)
+            bits_ref[x, y : y + TILE] = bits
+
+
+def more_bits_kernel(bits_in, y0d, y0u, bits_ref, pad_ref):
+    size_x, size_y, size_z = bits_ref.shape
+    row_of = lax.broadcasted_iota(jnp.int32, (TILE, size_z), 0)
+    found = []
+    for i, (side, ks) in enumerate(((y0d, UP), (y0u, DOWN))):
+        pad_ref[i, TILE : TILE + size_x] = side[size_x : 2 * size_x]
+        for row, x in ((TILE - 1, 2 * size_x + 2), (TILE + size_x, 2 * size_x + 3)):
+            pad_ref[i, row : row + 1] = side[x : x + 1]
+        bits = jnp.zeros((size_x, size_z), jnp.int32)
+        for k in ks:
+            ex, _, ez = SHIFT[k]
+            source = roll_z(pad_ref[i, TILE - ex : TILE - ex + size_x], ez)
+            bits = bits | jnp.where(source > 0.5, 1 << k, 0)
+        found.append(bits)
+    for x in range(size_x):
+        for y in range(0, size_y, TILE):
+            bits = bits_in[x, y : y + TILE]
+            for at, more in ((0, found[0]), (size_y - 1, found[1])):
+                if y <= at < y + TILE:
+                    bits = bits | jnp.where(row_of == at - y, more[x : x + 1], 0)
             bits_ref[x, y : y + TILE] = bits
 
 
@@ -528,10 +552,11 @@
     return pl.ds(layer + row * layers, TILE, stride=layers)
 
 
-def write_kernel(f_edge, f_middle, bits_ref, xl, xr, out_hbm, flat_ref, sems):
+def write_kernel(f_edge, f_middle, bits_ref, xl, xr, speed_ref, out_hbm, flat_ref, speed_hbm, sems, speed_sem):
     size_x, size_y, _ = bits_ref.shape
     held = Layers(f_edge, f_middle, size_x, one_layer(size_x))
-    copies = []
+    copies = [pltpu.make_async_copy(speed_ref, speed_hbm, speed_sem)]
+    copies[0].start()
     for k in range(N):
         for x in range(size_x):
             for y in range(0, size_y, TILE):
@@ -567,7 +592,6 @@
 
 
 VMEM = pl.BlockSpec(memory_space=pltpu.VMEM)
-SMEM = pl.BlockSpec(memory_space=pltpu.SMEM)
 HBM = pl.BlockSpec(memory_space=pltpu.HBM)
 
 
@@ -633,13 +657,13 @@
     )
     x0l, x0r = shift(right, left, "gy")
     (f,) = call(turn_kernel, [fields(size_x)], (raw,), cost=cost)
+    rates = jnp.broadcast_to(relax_rates[:, None, None], (N, TILE, size_z))
     up, down = call(start_pack_kernel, [rows(2 * size_x + TILE)] * 2, (pot0, mask, x0l, x0r))
     y0d, y0u = shift(up, down, "gx")
+    whole_bits = [((size_x, size_y, size_z), i32)]
+    (bits,) = call(bits_kernel, whole_bits, (mask, x0l, x0r), scratch=[padded], cost=cost)
     (bits,) = call(
-        bits_kernel,
-        [((size_x, size_y, size_z), i32)],
-        (mask, x0l, x0r, y0d, y0u),
-        scratch=[padded],
+        more_bits_kernel, whole_bits, (bits, y0d, y0u), scratch=[(2, size_x + PAD, size_z)]
     )
     edge2, edge1 = len(two_layers(size_x)), len(one_layer(size_x))
     held, sent = (f,), ()
@@ -657,8 +681,7 @@
                 x_rows,
                 ((3, edge2, size_y, size_z) if last else (edge1, size_y, size_z), f32),
             ],
-            (relax_rates, bits, pot0, x0l, x0r, y0d, y0u, *held, *sent),
-            special={0: SMEM},
+            (rates, bits, pot0, x0l, x0r, y0d, y0u, *held, *sent),
             cost=cost,
         )
         xl, xr = shift(right, left, "gy")
@@ -670,8 +693,7 @@
                 y_rows,
                 flat(3) if last else ((size_x - edge1, size_y, size_z), f32),
             ],
-            (relax_rates, bits, pot, post, rest, *held[:2], *sent[2:4]),
-            special={0: SMEM},
+            (rates, bits, pot, post, rest, *held[:2], *sent[2:4]),
             scratch=[(N, size_x - edge2, size_y + PAD, size_z)],
             cost=cost,
         )
@@ -683,12 +705,12 @@
         yd, yu = shift(up, down, "gx")
         held = (f_edge, f_middle, rest, more)
         sent = (xl, xr, yd, yu, right, left, up, down)
-    out, flat_f = call(
+    out, flat_f, speed = call(
         write_kernel,
-        [flat(N), flat(N)],
-        (f_edge, f_middle, bits, xl, xr),
-        special_out={0: HBM},
-        scratch=[pltpu.SemaphoreType.DMA((N,))],
+        [flat(N), flat(N), flat(3)],
+        (f_edge, f_middle, bits, xl, xr, more),
+        special_out={0: HBM, 2: HBM},
+        scratch=[pltpu.SemaphoreType.DMA((N,)), pltpu.SemaphoreType.DMA(())],
         cost=cost,
     )
     (out,) = call(
@@ -701,7 +723,7 @@
         input_output_aliases={0: 0},
     )
     shape = (rows_x, rows_y, size_z)
-    return out.reshape(N, *shape), more.reshape(3, *shape)
+    return out.reshape(N, *shape), speed.reshape(3, *shape)
 
 
 def solution(mesh):

time: 58.3 us -> 55.8 us (0.957)
  Pallas kernels: 14.4 us -> 9.54 us
  waiting for transfers between devices: 12.8 us -> 15 us
    pallas_call x18 -> x19, Pallas kernels: 14.4 us -> 9.54 us  [call(): pl.pallas_call(kernel, out_shape=[jax.ShapeDtypeStruct(shape, dtype) for...]
    ppermute x10, waiting for transfers between devices: 11.2 us -> 12.7 us  [shift(): lax.ppermute(forward, axis, ahead)]
    ppermute x10, waiting for transfers between devices: 1.52 us -> 2.27 us  [shift(): lax.ppermute(backward, axis, [(b, a) for a, b in ahead])]
  transfers between devices with their start and end apart: 20 -> 20, of which waited for: 13 -> 14; matrix products, arithmetic and copies ran while one was open for 0% -> 0% of each run, Pallas kernels for 14% -> 10%
where the time goes in v5:
time: 55.8 us; the launch traced here: 55.6 us
  starting transfers between devices  30.3 us (54%)
  waiting for transfers between devices  15 us (27%)
  Pallas kernels  9.54 us (17%)
  between operations  0.74 us (1%)
    ppermute x10, starting transfers between devices, shift(): lax.ppermute(backward, axis, [(b, a) for a, b in ahead])  20.4 us
    ppermute x10, waiting for transfers between devices, shift(): lax.ppermute(forward, axis, ahead)  12.7 us
    ppermute x10, starting transfers between devices, shift(): lax.ppermute(forward, axis, ahead)  9.84 us
    pallas_call x19, Pallas kernels, call(): pl.pallas_call(kernel, out_shape=[jax.ShapeDtypeStruct(shape, dtype) for...  9.54 us
    ppermute x10, waiting for transfers between devices, shift(): lax.ppermute(backward, axis, [(b, a) for a, b in ahead])  2.27 us
  transfers between devices with their start and end apart: 20, of which 14 were waited for; matrix products, arithmetic and copies ran while one was open for 0% of the time, Pallas kernels for 10%

profile of v5, /device:TPU:0, one launch (start us, length us, event | category | flops | bytes accessed | tf_op | source)
XLA Modules:
  0.0 55.6 jit_solution(13380828452026753502)
XLA Ops:
  0.6 1.7 %shard_map.68 = (f32[19,128,128]{2,1,0:T(8,128)S(1)}, f32[2,128,128]{2,1,0:T(8,128)S(1)}, f32[16,8,128]{2,1,0:T(8,128)S(1)}, f32[16,8,128]{2,1,0:T(8,128)S(1)}, ...) custom-call(f32[19,128,128]{2,1,0:T(8,128)} %bitcast.5, s32[128,128]{1,0:T(8,128)} %bitcast.7, s32[128,128]{1,0:T(8,128)} %bitcast.8, ...), custom_call_target="tpu_custom_call" | custom-call | tf_op jit(solution)/shard_map/pallas_call | solution.py:600
  2.3 0.5 collective-permute-start
  2.9 2.0 %collective-permute-start.1 = (f32[16,128]{1,0:T(8,128)S(1)}, f32[16,128]{1,0:T(8,128)S(1)}, u32[]{:S(2)}, u32[]{:S(2)}) collective-permute-start(f32[16,128]{1,0:T(8,128)S(1)} %get-tuple-element.63), channel_id=1, source_target_pairs={{1,0},{2,1},{3,2},{0,3},{5,4},{6,5},{7,6},{4,7},{9,8},{10,9},{11,1... | collective-permute-start | bytes 24584 | tf_op jit(solution)/shard_map/ppermute | solution.py:619
  4.8 1.3 %collective-permute-done.x0l.from_left.refs_3_ = f32[16,128]{1,0:T(8,128)S(1)} collective-permute-done((f32[16,128]{1,0:T(8,128)S(1)}, f32[16,128]{1,0:T(8,128)S(1)}, u32[]{:S(2)}, u32[]{:S(2)}) %collective-permute-start) | collective-permute-done | bytes 8224 | tf_op jit(solution)/shard_map/ppermute | solution.py:618
  6.1 0.1 collective-permute-done.1.x0r.from_right.refs_4_
  6.2 2.4 %collective-permute-start.2 = (f32[40,128]{1,0:T(8,128)S(1)}, f32[40,128]{1,0:T(8,128)S(1)}, u32[]{:S(2)}, u32[]{:S(2)}) collective-permute-start(f32[40,128]{1,0:T(8,128)S(1)} %get-tuple-element.65), channel_id=1, source_target_pairs={{0,4},{4,8},{8,12},{12,0},{1,5},{5,9},{9,13},{13,1},{2,6},{6,10},{... | collective-permute-start | bytes 61448 | tf_op jit(solution)/shard_map/ppermute | solution.py:618
  8.6 2.1 %collective-permute-start.3 = (f32[40,128]{1,0:T(8,128)S(1)}, f32[40,128]{1,0:T(8,128)S(1)}, u32[]{:S(2)}, u32[]{:S(2)}) collective-permute-start(f32[40,128]{1,0:T(8,128)S(1)} %get-tuple-element.66), channel_id=1, source_target_pairs={{4,0},{8,4},{12,8},{0,12},{5,1},{9,5},{13,9},{1,13},{6,2},{10,6},{... | collective-permute-start | bytes 61448 | tf_op jit(solution)/shard_map/ppermute | solution.py:619
  10.7 0.0 copy-start
  10.7 0.4 shard_map.72.refs_7_.refs_5_
  11.1 0.2 shard_map.69.bits_in
  11.4 1.1 %collective-permute-done.2.y0d.refs_5_ = f32[40,128]{1,0:T(8,128)S(1)} collective-permute-done((f32[40,128]{1,0:T(8,128)S(1)}, f32[40,128]{1,0:T(8,128)S(1)}, u32[]{:S(2)}, u32[]{:S(2)}) %collective-permute-start.2) | collective-permute-done | bytes 20512 | tf_op jit(solution)/shard_map/ppermute | solution.py:618
  12.5 0.2 collective-permute-done.3.y0u.refs_6_
  12.7 0.1 shard_map.71.refs_1_.bits_ref
  12.8 0.0 copy-done
  12.8 0.1 broadcast_in_dim.2.refs_0_
  12.9 0.3 shard_map.73
  13.2 0.4 collective-permute-start.4
  13.7 1.4 %collective-permute-start.5 = (f32[56,128]{1,0:T(8,128)S(1)}, f32[56,128]{1,0:T(8,128)S(1)}, u32[]{:S(2)}, u32[]{:S(2)}) collective-permute-start(f32[56,128]{1,0:T(8,128)S(1)} %get-tuple-element.75.refs_5_.refs_16_), channel_id=1, source_target_pairs={{1,0},{2,1},{3,2},{0,3},{5,4},{6,5},{7,6},{4,7},{9,8},{10,9},{11,1... | collective-permute-start | bytes 86024 | tf_op jit(solution)/shard_map/ppermute | solution.py:619
  15.0 0.9 %shard_map.74 = (f32[19,14,8,128]{3,2,1,0:T(8,128)S(1)}, f32[104,128]{1,0:T(8,128)S(1)}, f32[104,128]{1,0:T(8,128)S(1)}, f32[14,8,128]{2,1,0:T(8,128)S(1)}) custom-call(f32[19,8,128]{2,1,0:T(8,128)S(1)} %broadcast_in_dim.2.refs_0_, s32[16,8,128]{2,1,0:T(8,128)S(1)} %shard_map.71.refs_1_.bits_ref, f32[18,24,128]{2,1,0:T(8,128)S(1)} %get-tuple-element.69.refs_2_, ...), custom_call_target="tpu_custom_call" | custom-call | flops 6553600 | bytes 1310720 | tf_op jit(solution)/shard_map/pallas_call | solution.py:600
  15.9 0.7 %collective-permute-done.4.refs_2_.refs_11_ = f32[56,128]{1,0:T(8,128)S(1)} collective-permute-done((f32[56,128]{1,0:T(8,128)S(1)}, f32[56,128]{1,0:T(8,128)S(1)}, u32[]{:S(2)}, u32[]{:S(2)}) %collective-permute-start.4) | collective-permute-done | bytes 28704 | tf_op jit(solution)/shard_map/ppermute | solution.py:618
  16.6 0.0 collective-permute-done.5.refs_3_.refs_12_
  16.6 1.4 %collective-permute-start.6 = (f32[104,128]{1,0:T(8,128)S(1)}, f32[104,128]{1,0:T(8,128)S(1)}, u32[]{:S(2)}, u32[]{:S(2)}) collective-permute-start(f32[104,128]{1,0:T(8,128)S(1)} %get-tuple-element.78.refs_17_), channel_id=1, source_target_pairs={{0,4},{4,8},{8,12},{12,0},{1,5},{5,9},{9,13},{13,1},{2,6},{6,10},{... | collective-permute-start | bytes 159752 | tf_op jit(solution)/shard_map/ppermute | solution.py:618
  18.0 2.5 %collective-permute-start.7 = (f32[104,128]{1,0:T(8,128)S(1)}, f32[104,128]{1,0:T(8,128)S(1)}, u32[]{:S(2)}, u32[]{:S(2)}) collective-permute-start(f32[104,128]{1,0:T(8,128)S(1)} %get-tuple-element.79.refs_18_), channel_id=1, source_target_pairs={{4,0},{8,4},{12,8},{0,12},{5,1},{9,5},{13,9},{1,13},{6,2},{10,6},{... | collective-permute-start | bytes 159752 | tf_op jit(solution)/shard_map/ppermute | solution.py:619
  20.5 2.2 %collective-permute-done.6.refs_13_.refs_7_ = f32[104,128]{1,0:T(8,128)S(1)} collective-permute-done((f32[104,128]{1,0:T(8,128)S(1)}, f32[104,128]{1,0:T(8,128)S(1)}, u32[]{:S(2)}, u32[]{:S(2)}) %collective-permute-start.6) | collective-permute-done | bytes 53280 | tf_op jit(solution)/shard_map/ppermute | solution.py:618
  22.7 0.9 %collective-permute-done.7.refs_14_.refs_8_ = f32[104,128]{1,0:T(8,128)S(1)} collective-permute-done((f32[104,128]{1,0:T(8,128)S(1)}, f32[104,128]{1,0:T(8,128)S(1)}, u32[]{:S(2)}, u32[]{:S(2)}) %collective-permute-start.7) | collective-permute-done | bytes 53280 | tf_op jit(solution)/shard_map/ppermute | solution.py:619
  23.6 0.4 shard_map.76
  24.0 0.2 collective-permute-start.8
  24.2 1.6 %collective-permute-start.9 = (f32[56,128]{1,0:T(8,128)S(1)}, f32[56,128]{1,0:T(8,128)S(1)}, u32[]{:S(2)}, u32[]{:S(2)}) collective-permute-start(f32[56,128]{1,0:T(8,128)S(1)} %get-tuple-element.87.refs_5_.refs_16_), channel_id=1, source_target_pairs={{1,0},{2,1},{3,2},{0,3},{5,4},{6,5},{7,6},{4,7},{9,8},{10,9},{11,1... | collective-permute-start | bytes 86024 | tf_op jit(solution)/shard_map/ppermute | solution.py:619
  25.8 0.9 %shard_map.77 = (f32[19,14,8,128]{3,2,1,0:T(8,128)S(1)}, f32[104,128]{1,0:T(8,128)S(1)}, f32[104,128]{1,0:T(8,128)S(1)}, f32[14,8,128]{2,1,0:T(8,128)S(1)}) custom-call(f32[19,8,128]{2,1,0:T(8,128)S(1)} %broadcast_in_dim.2.refs_0_, s32[16,8,128]{2,1,0:T(8,128)S(1)} %shard_map.71.refs_1_.bits_ref, f32[18,24,128]{2,1,0:T(8,128)S(1)} %get-tuple-element.81.refs_2_, ...), custom_call_target="tpu_custom_call" | custom-call | flops 6553600 | bytes 1310720 | tf_op jit(solution)/shard_map/pallas_call | solution.py:600
  26.7 0.7 %collective-permute-done.8.refs_2_.refs_11_ = f32[56,128]{1,0:T(8,128)S(1)} collective-permute-done((f32[56,128]{1,0:T(8,128)S(1)}, f32[56,128]{1,0:T(8,128)S(1)}, u32[]{:S(2)}, u32[]{:S(2)}) %collective-permute-start.8) | collective-permute-done | bytes 28704 | tf_op jit(solution)/shard_map/ppermute | solution.py:618
  27.3 0.0 collective-permute-done.9.refs_3_.refs_12_
  27.4 1.1 %collective-permute-start.10 = (f32[104,128]{1,0:T(8,128)S(1)}, f32[104,128]{1,0:T(8,128)S(1)}, u32[]{:S(2)}, u32[]{:S(2)}) collective-permute-start(f32[104,128]{1,0:T(8,128)S(1)} %get-tuple-element.90.refs_17_), channel_id=1, source_target_pairs={{0,4},{4,8},{8,12},{12,0},{1,5},{5,9},{9,13},{13,1},{2,6},{6,10},{... | collective-permute-start | bytes 159752 | tf_op jit(solution)/shard_map/ppermute | solution.py:618
  28.5 2.8 %collective-permute-start.11 = (f32[104,128]{1,0:T(8,128)S(1)}, f32[104,128]{1,0:T(8,128)S(1)}, u32[]{:S(2)}, u32[]{:S(2)}) collective-permute-start(f32[104,128]{1,0:T(8,128)S(1)} %get-tuple-element.91.refs_18_), channel_id=1, source_target_pairs={{4,0},{8,4},{12,8},{0,12},{5,1},{9,5},{13,9},{1,13},{6,2},{10,6},{... | collective-permute-start | bytes 159752 | tf_op jit(solution)/shard_map/ppermute | solution.py:619
  31.3 2.5 %collective-permute-done.10.refs_13_.refs_7_ = f32[104,128]{1,0:T(8,128)S(1)} collective-permute-done((f32[104,128]{1,0:T(8,128)S(1)}, f32[104,128]{1,0:T(8,128)S(1)}, u32[]{:S(2)}, u32[]{:S(2)}) %collective-permute-start.10) | collective-permute-done | bytes 53280 | tf_op jit(solution)/shard_map/ppermute | solution.py:618
  33.8 0.0 collective-permute-done.11.refs_14_.refs_8_
  33.8 0.4 shard_map.79
  34.2 0.4 collective-permute-start.12
  34.6 1.4 %collective-permute-start.13 = (f32[56,128]{1,0:T(8,128)S(1)}, f32[56,128]{1,0:T(8,128)S(1)}, u32[]{:S(2)}, u32[]{:S(2)}) collective-permute-start(f32[56,128]{1,0:T(8,128)S(1)} %get-tuple-element.99.refs_5_.refs_16_), channel_id=1, source_target_pairs={{1,0},{2,1},{3,2},{0,3},{5,4},{6,5},{7,6},{4,7},{9,8},{10,9},{11,1... | collective-permute-start | bytes 86024 | tf_op jit(solution)/shard_map/ppermute | solution.py:619
  36.0 0.9 %shard_map.80 = (f32[19,14,8,128]{3,2,1,0:T(8,128)S(1)}, f32[104,128]{1,0:T(8,128)S(1)}, f32[104,128]{1,0:T(8,128)S(1)}, f32[14,8,128]{2,1,0:T(8,128)S(1)}) custom-call(f32[19,8,128]{2,1,0:T(8,128)S(1)} %broadcast_in_dim.2.refs_0_, s32[16,8,128]{2,1,0:T(8,128)S(1)} %shard_map.71.refs_1_.bits_ref, f32[18,24,128]{2,1,0:T(8,128)S(1)} %get-tuple-element.93.refs_2_, ...), custom_call_target="tpu_custom_call" | custom-call | flops 6553600 | bytes 1310720 | tf_op jit(solution)/shard_map/pallas_call | solution.py:600
  36.8 0.7 %collective-permute-done.12.refs_2_.refs_11_ = f32[56,128]{1,0:T(8,128)S(1)} collective-permute-done((f32[56,128]{1,0:T(8,128)S(1)}, f32[56,128]{1,0:T(8,128)S(1)}, u32[]{:S(2)}, u32[]{:S(2)}) %collective-permute-start.12) | collective-permute-done | bytes 28704 | tf_op jit(solution)/shard_map/ppermute | solution.py:618
  37.5 0.0 collective-permute-done.13.refs_3_.refs_12_
  37.5 1.0 %collective-permute-start.14 = (f32[104,128]{1,0:T(8,128)S(1)}, f32[104,128]{1,0:T(8,128)S(1)}, u32[]{:S(2)}, u32[]{:S(2)}) collective-permute-start(f32[104,128]{1,0:T(8,128)S(1)} %get-tuple-element.102.refs_17_), channel_id=1, source_target_pairs={{0,4},{4,8},{8,12},{12,0},{1,5},{5,9},{9,13},{13,1},{2,6},{6,10},{... | collective-permute-start | bytes 159752 | tf_op jit(solution)/shard_map/ppermute | solution.py:618
  38.6 3.1 %collective-permute-start.15 = (f32[104,128]{1,0:T(8,128)S(1)}, f32[104,128]{1,0:T(8,128)S(1)}, u32[]{:S(2)}, u32[]{:S(2)}) collective-permute-start(f32[104,128]{1,0:T(8,128)S(1)} %get-tuple-element.103.refs_18_), channel_id=1, source_target_pairs={{4,0},{8,4},{12,8},{0,12},{5,1},{9,5},{13,9},{1,13},{6,2},{10,6},{... | collective-permute-start | bytes 159752 | tf_op jit(solution)/shard_map/ppermute | solution.py:619
  41.6 2.3 %collective-permute-done.14.refs_13_.refs_7_ = f32[104,128]{1,0:T(8,128)S(1)} collective-permute-done((f32[104,128]{1,0:T(8,128)S(1)}, f32[104,128]{1,0:T(8,128)S(1)}, u32[]{:S(2)}, u32[]{:S(2)}) %collective-permute-start.14) | collective-permute-done | bytes 53280 | tf_op jit(solution)/shard_map/ppermute | solution.py:618
  44.0 0.0 collective-permute-done.15.refs_14_.refs_8_
  44.0 0.4 shard_map.82
  44.3 0.3 collective-permute-start.16
  44.7 1.5 %collective-permute-start.17 = (f32[48,128]{1,0:T(8,128)S(1)}, f32[48,128]{1,0:T(8,128)S(1)}, u32[]{:S(2)}, u32[]{:S(2)}) collective-permute-start(f32[48,128]{1,0:T(8,128)S(1)} %get-tuple-element.110.refs_5_), channel_id=1, source_target_pairs={{1,0},{2,1},{3,2},{0,3},{5,4},{6,5},{7,6},{4,7},{9,8},{10,9},{11,1... | collective-permute-start | bytes 73736 | tf_op jit(solution)/shard_map/ppermute | solution.py:619
  46.1 0.9 %shard_map.83 = (f32[19,14,8,128]{3,2,1,0:T(8,128)S(1)}, f32[80,128]{1,0:T(8,128)S(1)}, f32[80,128]{1,0:T(8,128)S(1)}, f32[3,128,128]{2,1,0:T(8,128)S(1)}) custom-call(f32[19,8,128]{2,1,0:T(8,128)S(1)} %broadcast_in_dim.2.refs_0_, s32[16,8,128]{2,1,0:T(8,128)S(1)} %shard_map.71.refs_1_.bits_ref, f32[18,24,128]{2,1,0:T(8,128)S(1)} %get-tuple-element.105.refs_2_, ...), custom_call_target="tpu_custom_call" | custom-call | flops 6553600 | bytes 1310720 | tf_op jit(solution)/shard_map/pallas_call | solution.py:600
  47.1 0.6 %collective-permute-done.16.xl.refs_2_ = f32[48,128]{1,0:T(8,128)S(1)} collective-permute-done((f32[48,128]{1,0:T(8,128)S(1)}, f32[48,128]{1,0:T(8,128)S(1)}, u32[]{:S(2)}, u32[]{:S(2)}) %collective-permute-start.16) | collective-permute-done | bytes 24608 | tf_op jit(solution)/shard_map/ppermute | solution.py:618
  47.6 0.0 collective-permute-done.17.xr.refs_3_
  47.7 2.0 %collective-permute-start.18 = (f32[80,128]{1,0:T(8,128)S(1)}, f32[80,128]{1,0:T(8,128)S(1)}, u32[]{:S(2)}, u32[]{:S(2)}) collective-permute-start(f32[80,128]{1,0:T(8,128)S(1)} %get-tuple-element.117), channel_id=1, source_target_pairs={{0,4},{4,8},{8,12},{12,0},{1,5},{5,9},{9,13},{13,1},{2,6},{6,10},{... | collective-permute-start | bytes 122888 | tf_op jit(solution)/shard_map/ppermute | solution.py:618
  49.7 2.2 %collective-permute-start.19 = (f32[80,128]{1,0:T(8,128)S(1)}, f32[80,128]{1,0:T(8,128)S(1)}, u32[]{:S(2)}, u32[]{:S(2)}) collective-permute-start(f32[80,128]{1,0:T(8,128)S(1)} %get-tuple-element.118), channel_id=1, source_target_pairs={{4,0},{8,4},{12,8},{0,12},{5,1},{9,5},{13,9},{1,13},{6,2},{10,6},{... | collective-permute-start | bytes 122888 | tf_op jit(solution)/shard_map/ppermute | solution.py:619
  51.9 1.3 %shard_map.84 = (f32[19,128,128]{2,1,0:T(8,128)}, f32[19,128,128]{2,1,0:T(8,128)S(1)}, f32[3,128,128]{2,1,0:T(8,128)}) custom-call(f32[19,2,8,128]{3,2,1,0:T(8,128)S(1)} %get-tuple-element.104.f_edge, f32[19,14,8,128]{3,2,1,0:T(8,128)S(1)} %get-tuple-element.108.f_middle, s32[16,8,128]{2,1,0:T(8,128)S(1)} %shard_map.71.refs_1_.bits_ref, ...), custom_call_target="tpu_custom_call" | custom-call | flops 6553600 | bytes 1310720 | tf_op jit(solution)/shard_map/pallas_call | solution.py:600
  53.2 0.7 %collective-permute-done.18.yd = f32[80,128]{1,0:T(8,128)S(1)} collective-permute-done((f32[80,128]{1,0:T(8,128)S(1)}, f32[80,128]{1,0:T(8,128)S(1)}, u32[]{:S(2)}, u32[]{:S(2)}) %collective-permute-start.18) | collective-permute-done | bytes 40992 | tf_op jit(solution)/shard_map/ppermute | solution.py:618
  53.9 1.0 %collective-permute-done.19.yu = f32[80,128]{1,0:T(8,128)S(1)} collective-permute-done((f32[80,128]{1,0:T(8,128)S(1)}, f32[80,128]{1,0:T(8,128)S(1)}, u32[]{:S(2)}, u32[]{:S(2)}) %collective-permute-start.19) | collective-permute-done | bytes 40992 | tf_op jit(solution)/shard_map/ppermute | solution.py:619
  54.9 0.7 %shard_map.86 = f32[19,128,128]{2,1,0:T(8,128)} custom-call(f32[19,128,128]{2,1,0:T(8,128)} %get-tuple-element.112.out_in, f32[19,128,128]{2,1,0:T(8,128)S(1)} %get-tuple-element.113.flat_ref, f32[2,128,128]{2,1,0:T(8,128)S(1)} %get-tuple-element.114.mask_ref, f32[80,128]{1,0:T(8,128)S(1)} %collective-permute-done.18.yd, ...), custom_call_target="tpu_custom_call", output_to_operand_aliasing={{}: (0, {})} | custom-call | tf_op jit(solution)/shard_map/pallas_call | solution.py:600
  (5 shorter events, 0.1 us)
Async XLA Ops:
  2.3 3.8 %collective-permute-start = (f32[16,128]{1,0:T(8,128)S(1)}, f32[16,128]{1,0:T(8,128)S(1)}, u32[]{:S(2)}, u32[]{:S(2)}) collective-permute-start(f32[16,128]{1,0:T(8,128)S(1)} %get-tuple-element.62), channel_id=1, source_target_pairs={{0,1},{1,2},{2,3},{3,0},{4,5},{5,6},{6,7},{7,4},{8,9},{9,10},{10,1... | collective-permute-start | bytes 24584 | tf_op jit(solution)/shard_map/ppermute | solution.py:618
  2.9 3.3 %collective-permute-start.1 = (f32[16,128]{1,0:T(8,128)S(1)}, f32[16,128]{1,0:T(8,128)S(1)}, u32[]{:S(2)}, u32[]{:S(2)}) collective-permute-start(f32[16,128]{1,0:T(8,128)S(1)} %get-tuple-element.63), channel_id=1, source_target_pairs={{1,0},{2,1},{3,2},{0,3},{5,4},{6,5},{7,6},{4,7},{9,8},{10,9},{11,1... | collective-permute-start | bytes 24584 | tf_op jit(solution)/shard_map/ppermute | solution.py:619
  6.2 6.3 %collective-permute-start.2 = (f32[40,128]{1,0:T(8,128)S(1)}, f32[40,128]{1,0:T(8,128)S(1)}, u32[]{:S(2)}, u32[]{:S(2)}) collective-permute-start(f32[40,128]{1,0:T(8,128)S(1)} %get-tuple-element.65), channel_id=1, source_target_pairs={{0,4},{4,8},{8,12},{12,0},{1,5},{5,9},{9,13},{13,1},{2,6},{6,10},{... | collective-permute-start | bytes 61448 | tf_op jit(solution)/shard_map/ppermute | solution.py:618
  8.6 4.1 %collective-permute-start.3 = (f32[40,128]{1,0:T(8,128)S(1)}, f32[40,128]{1,0:T(8,128)S(1)}, u32[]{:S(2)}, u32[]{:S(2)}) collective-permute-start(f32[40,128]{1,0:T(8,128)S(1)} %get-tuple-element.66), channel_id=1, source_target_pairs={{4,0},{8,4},{12,8},{0,12},{5,1},{9,5},{13,9},{1,13},{6,2},{10,6},{... | collective-permute-start | bytes 61448 | tf_op jit(solution)/shard_map/ppermute | solution.py:619
  10.7 2.1 %copy-start = (f32[19]{0:T(128)S(1)}, f32[19]{0:T(128)}, u32[]{:S(2)}) copy-start(f32[19]{0:T(128)} %param.9) | copy-start | bytes 232
  13.2 3.3 %collective-permute-start.4 = (f32[56,128]{1,0:T(8,128)S(1)}, f32[56,128]{1,0:T(8,128)S(1)}, u32[]{:S(2)}, u32[]{:S(2)}) collective-permute-start(f32[56,128]{1,0:T(8,128)S(1)} %get-tuple-element.74.refs_4_.refs_15_), channel_id=1, source_target_pairs={{0,1},{1,2},{2,3},{3,0},{4,5},{5,6},{6,7},{7,4},{8,9},{9,10},{10,1... | collective-permute-start | bytes 86024 | tf_op jit(solution)/shard_map/ppermute | solution.py:618
  13.7 2.9 %collective-permute-start.5 = (f32[56,128]{1,0:T(8,128)S(1)}, f32[56,128]{1,0:T(8,128)S(1)}, u32[]{:S(2)}, u32[]{:S(2)}) collective-permute-start(f32[56,128]{1,0:T(8,128)S(1)} %get-tuple-element.75.refs_5_.refs_16_), channel_id=1, source_target_pairs={{1,0},{2,1},{3,2},{0,3},{5,4},{6,5},{7,6},{4,7},{9,8},{10,9},{11,1... | collective-permute-start | bytes 86024 | tf_op jit(solution)/shard_map/ppermute | solution.py:619
  16.6 6.1 %collective-permute-start.6 = (f32[104,128]{1,0:T(8,128)S(1)}, f32[104,128]{1,0:T(8,128)S(1)}, u32[]{:S(2)}, u32[]{:S(2)}) collective-permute-start(f32[104,128]{1,0:T(8,128)S(1)} %get-tuple-element.78.refs_17_), channel_id=1, source_target_pairs={{0,4},{4,8},{8,12},{12,0},{1,5},{5,9},{9,13},{13,1},{2,6},{6,10},{... | collective-permute-start | bytes 159752 | tf_op jit(solution)/shard_map/ppermute | solution.py:618
  18.0 5.6 %collective-permute-start.7 = (f32[104,128]{1,0:T(8,128)S(1)}, f32[104,128]{1,0:T(8,128)S(1)}, u32[]{:S(2)}, u32[]{:S(2)}) collective-permute-start(f32[104,128]{1,0:T(8,128)S(1)} %get-tuple-element.79.refs_18_), channel_id=1, source_target_pairs={{4,0},{8,4},{12,8},{0,12},{5,1},{9,5},{13,9},{1,13},{6,2},{10,6},{... | collective-permute-start | bytes 159752 | tf_op jit(solution)/shard_map/ppermute | solution.py:619
  24.0 3.3 %collective-permute-start.8 = (f32[56,128]{1,0:T(8,128)S(1)}, f32[56,128]{1,0:T(8,128)S(1)}, u32[]{:S(2)}, u32[]{:S(2)}) collective-permute-start(f32[56,128]{1,0:T(8,128)S(1)} %get-tuple-element.86.refs_4_.refs_15_), channel_id=1, source_target_pairs={{0,1},{1,2},{2,3},{3,0},{4,5},{5,6},{6,7},{7,4},{8,9},{9,10},{10,1... | collective-permute-start | bytes 86024 | tf_op jit(solution)/shard_map/ppermute | solution.py:618
  24.2 3.2 %collective-permute-start.9 = (f32[56,128]{1,0:T(8,128)S(1)}, f32[56,128]{1,0:T(8,128)S(1)}, u32[]{:S(2)}, u32[]{:S(2)}) collective-permute-start(f32[56,128]{1,0:T(8,128)S(1)} %get-tuple-element.87.refs_5_.refs_16_), channel_id=1, source_target_pairs={{1,0},{2,1},{3,2},{0,3},{5,4},{6,5},{7,6},{4,7},{9,8},{10,9},{11,1... | collective-permute-start | bytes 86024 | tf_op jit(solution)/shard_map/ppermute | solution.py:619
  27.4 6.4 %collective-permute-start.10 = (f32[104,128]{1,0:T(8,128)S(1)}, f32[104,128]{1,0:T(8,128)S(1)}, u32[]{:S(2)}, u32[]{:S(2)}) collective-permute-start(f32[104,128]{1,0:T(8,128)S(1)} %get-tuple-element.90.refs_17_), channel_id=1, source_target_pairs={{0,4},{4,8},{8,12},{12,0},{1,5},{5,9},{9,13},{13,1},{2,6},{6,10},{... | collective-permute-start | bytes 159752 | tf_op jit(solution)/shard_map/ppermute | solution.py:618
  28.5 5.3 %collective-permute-start.11 = (f32[104,128]{1,0:T(8,128)S(1)}, f32[104,128]{1,0:T(8,128)S(1)}, u32[]{:S(2)}, u32[]{:S(2)}) collective-permute-start(f32[104,128]{1,0:T(8,128)S(1)} %get-tuple-element.91.refs_18_), channel_id=1, source_target_pairs={{4,0},{8,4},{12,8},{0,12},{5,1},{9,5},{13,9},{1,13},{6,2},{10,6},{... | collective-permute-start | bytes 159752 | tf_op jit(solution)/shard_map/ppermute | solution.py:619
  34.2 3.3 %collective-permute-start.12 = (f32[56,128]{1,0:T(8,128)S(1)}, f32[56,128]{1,0:T(8,128)S(1)}, u32[]{:S(2)}, u32[]{:S(2)}) collective-permute-start(f32[56,128]{1,0:T(8,128)S(1)} %get-tuple-element.98.refs_4_.refs_15_), channel_id=1, source_target_pairs={{0,1},{1,2},{2,3},{3,0},{4,5},{5,6},{6,7},{7,4},{8,9},{9,10},{10,1... | collective-permute-start | bytes 86024 | tf_op jit(solution)/shard_map/ppermute | solution.py:618
  34.6 2.9 %collective-permute-start.13 = (f32[56,128]{1,0:T(8,128)S(1)}, f32[56,128]{1,0:T(8,128)S(1)}, u32[]{:S(2)}, u32[]{:S(2)}) collective-permute-start(f32[56,128]{1,0:T(8,128)S(1)} %get-tuple-element.99.refs_5_.refs_16_), channel_id=1, source_target_pairs={{1,0},{2,1},{3,2},{0,3},{5,4},{6,5},{7,6},{4,7},{9,8},{10,9},{11,1... | collective-permute-start | bytes 86024 | tf_op jit(solution)/shard_map/ppermute | solution.py:619
  37.5 6.4 %collective-permute-start.14 = (f32[104,128]{1,0:T(8,128)S(1)}, f32[104,128]{1,0:T(8,128)S(1)}, u32[]{:S(2)}, u32[]{:S(2)}) collective-permute-start(f32[104,128]{1,0:T(8,128)S(1)} %get-tuple-element.102.refs_17_), channel_id=1, source_target_pairs={{0,4},{4,8},{8,12},{12,0},{1,5},{5,9},{9,13},{13,1},{2,6},{6,10},{... | collective-permute-start | bytes 159752 | tf_op jit(solution)/shard_map/ppermute | solution.py:618
  38.6 5.4 %collective-permute-start.15 = (f32[104,128]{1,0:T(8,128)S(1)}, f32[104,128]{1,0:T(8,128)S(1)}, u32[]{:S(2)}, u32[]{:S(2)}) collective-permute-start(f32[104,128]{1,0:T(8,128)S(1)} %get-tuple-element.103.refs_18_), channel_id=1, source_target_pairs={{4,0},{8,4},{12,8},{0,12},{5,1},{9,5},{13,9},{1,13},{6,2},{10,6},{... | collective-permute-start | bytes 159752 | tf_op jit(solution)/shard_map/ppermute | solution.py:619
  44.3 3.3 %collective-permute-start.16 = (f32[48,128]{1,0:T(8,128)S(1)}, f32[48,128]{1,0:T(8,128)S(1)}, u32[]{:S(2)}, u32[]{:S(2)}) collective-permute-start(f32[48,128]{1,0:T(8,128)S(1)} %get-tuple-element.109.refs_4_), channel_id=1, source_target_pairs={{0,1},{1,2},{2,3},{3,0},{4,5},{5,6},{6,7},{7,4},{8,9},{9,10},{10,1... | collective-permute-start | bytes 73736 | tf_op jit(solution)/shard_map/ppermute | solution.py:618
  44.7 3.0 %collective-permute-start.17 = (f32[48,128]{1,0:T(8,128)S(1)}, f32[48,128]{1,0:T(8,128)S(1)}, u32[]{:S(2)}, u32[]{:S(2)}) collective-permute-start(f32[48,128]{1,0:T(8,128)S(1)} %get-tuple-element.110.refs_5_), channel_id=1, source_target_pairs={{1,0},{2,1},{3,2},{0,3},{5,4},{6,5},{7,6},{4,7},{9,8},{10,9},{11,1... | collective-permute-start | bytes 73736 | tf_op jit(solution)/shard_map/ppermute | solution.py:619
  47.7 6.3 %collective-permute-start.18 = (f32[80,128]{1,0:T(8,128)S(1)}, f32[80,128]{1,0:T(8,128)S(1)}, u32[]{:S(2)}, u32[]{:S(2)}) collective-permute-start(f32[80,128]{1,0:T(8,128)S(1)} %get-tuple-element.117), channel_id=1, source_target_pairs={{0,4},{4,8},{8,12},{12,0},{1,5},{5,9},{9,13},{13,1},{2,6},{6,10},{... | collective-permute-start | bytes 122888 | tf_op jit(solution)/shard_map/ppermute | solution.py:618
  49.7 5.2 %collective-permute-start.19 = (f32[80,128]{1,0:T(8,128)S(1)}, f32[80,128]{1,0:T(8,128)S(1)}, u32[]{:S(2)}, u32[]{:S(2)}) collective-permute-start(f32[80,128]{1,0:T(8,128)S(1)} %get-tuple-element.118), channel_id=1, source_target_pairs={{4,0},{8,4},{12,8},{0,12},{5,1},{9,5},{13,9},{1,13},{6,2},{10,6},{... | collective-permute-start | bytes 122888 | tf_op jit(solution)/shard_map/ppermute | solution.py:619

commit v6 on v5

--- a/solution.py
+++ b/solution.py
@@ -140,7 +140,21 @@
     return SHIFT.index((side, 1, 0)), SHIFT.index((side, -1, 0))
 
 
-def start_kernel(f_hbm, mask_hbm, wet_hbm, wall_hbm, raw_ref, flat_ref, mask_ref, pot_ref, right_ref, left_ref, *scratch):
+def in_swap_order(pairs, right, left):
+    if not pairs:
+        return right, left
+    odd = lax.axis_index("gy") % 2 == 1
+    return jnp.where(odd, left, right), jnp.where(odd, right, left)
+
+
+def sort_received(pairs, a_ref, b_ref, xl_ref, xr_ref):
+    if pairs:
+        xr_ref[...], xl_ref[...] = in_swap_order(pairs, a_ref[...], b_ref[...])
+    else:
+        xl_ref[...], xr_ref[...] = a_ref[...], b_ref[...]
+
+
+def start_kernel(pairs, f_hbm, mask_hbm, wet_hbm, wall_hbm, raw_ref, flat_ref, mask_ref, pot_ref, a_ref, b_ref, *scratch):
     mask_in, wet_in, wall_in, f_sems, sems = scratch
     layers, rows = mask_ref.shape[0], mask_ref.shape[1]
     small = [
@@ -172,9 +186,9 @@
     for i in range(layers):
         mask_ref[i] = flat_ref[0, pl.ds(i, rows, stride=layers)]
         pot_ref[i] = flat_ref[1, pl.ds(i, rows, stride=layers)]
-    for ref, i in ((right_ref, layers - 1), (left_ref, 0)):
-        ref[:rows] = pot_ref[i]
-        ref[rows:] = mask_ref[i]
+    for ref in (pot_ref, mask_ref):
+        at = slice(0, rows) if ref is pot_ref else slice(rows, 2 * rows)
+        a_ref[at], b_ref[at] = in_swap_order(pairs, ref[layers - 1], ref[0])
 
 
 def turn_kernel(raw_ref, f_ref):
@@ -184,8 +198,9 @@
             f_ref[k, i] = raw_ref[k, pl.ds(i, rows, stride=layers)]
 
 
-def start_pack_kernel(pot_ref, mask_ref, from_left, from_right, up_ref, down_ref):
+def start_pack_kernel(pairs, pot_ref, mask_ref, a_ref, b_ref, up_ref, down_ref, from_left, from_right):
     size_x, size_y = mask_ref.shape[0], mask_ref.shape[1]
+    sort_received(pairs, a_ref, b_ref, from_left, from_right)
     for ref, y in ((up_ref, size_y - 1), (down_ref, 0)):
         ref[2 * size_x :] = jnp.zeros((TILE, ref.shape[1]), jnp.float32)
         for x in range(size_x):
@@ -348,7 +363,7 @@
                 rho.store(x, y, total(arrived))
 
 
-def edge_kernel(first, last, *refs):
+def edge_kernel(first, last, pairs, *refs):
     refs = list(refs)
     take = lambda count: [refs.pop(0) for _ in range(count)]
     rates, bits_ref, pot0_ref, x0l, x0r, y0d, y0u = take(7)
@@ -357,8 +372,7 @@
     else:
         f_edge, f_middle, rho_edge, rho_middle, xl, xr, yd, yu = take(8)
         own_right, own_left, own_up, own_down = take(4)
-    pot, post_out, f_out, right_ref, left_ref = take(5)
-    rest = take(1)[0]
+    pot, post_out, f_out, right_ref, left_ref, a_ref, b_ref, rest = take(8)
     size_x, size_y, size_z = bits_ref.shape
     edge2, edge1 = two_layers(size_x), one_layer(size_x)
     sides = None
@@ -464,6 +478,7 @@
                         if 0 <= x - SHIFT[k][0] < size_x
                     ]
                 )
+    a_ref[...], b_ref[...] = in_swap_order(pairs, right_ref[...], left_ref[...])
 
 
 def middle_kernel(first, last, *refs):
@@ -517,8 +532,9 @@
                 ref[5 * size_x + x : 5 * size_x + x + 1] = rho.row(x, y)
 
 
-def pack_kernel(last, size_x, size_y, *refs):
-    up_in, down_in, xl, xr, own_right, own_left, up_ref, down_ref = refs
+def pack_kernel(last, pairs, size_x, size_y, *refs):
+    up_in, down_in, a_ref, b_ref, own_right, own_left, up_ref, down_ref, xl, xr = refs
+    sort_received(pairs, a_ref, b_ref, xl, xr)
     parts = 5 if last else 6
     at = parts * size_y
     for ref, source, y, ks, c, h in (
@@ -620,8 +636,20 @@
     )
 
 
+def swap(a, b, axis):
+    count = lax.axis_size(axis)
+    partners = [
+        [(i, (i + (1 if i % 2 == parity else -1)) % count) for i in range(count)]
+        for parity in range(2)
+    ]
+    b = lax.ppermute(b, axis, partners[1])
+    return lax.ppermute(a, axis, partners[0]), b
+
+
 def per_device(populations, fluid_mask, wet_class, wall_potential, relax_rates):
     rows_x, rows_y, size_z = fluid_mask.shape
+    pairs = lax.axis_size("gy") % 2 == 0
+    exchange = swap if pairs else shift
     size_x, size_y = rows_y, rows_x
     cells = size_x * size_y
     f32, i32 = jnp.float32, jnp.int32
@@ -642,8 +670,8 @@
             wall_potential,
         )
     ]
-    raw, flat_mask, mask, pot0, right, left = call(
-        start_kernel,
+    raw, flat_mask, mask, pot0, a, b = call(
+        functools.partial(start_kernel, pairs),
         [flat(N), flat(2), whole, whole, rows(2 * size_y), rows(2 * size_y)],
         operands,
         special={i: HBM for i in range(4)},
@@ -655,10 +683,14 @@
             pltpu.SemaphoreType.DMA((3,)),
         ],
     )
-    x0l, x0r = shift(right, left, "gy")
+    a, b = exchange(a, b, "gy")
     (f,) = call(turn_kernel, [fields(size_x)], (raw,), cost=cost)
     rates = jnp.broadcast_to(relax_rates[:, None, None], (N, TILE, size_z))
-    up, down = call(start_pack_kernel, [rows(2 * size_x + TILE)] * 2, (pot0, mask, x0l, x0r))
+    up, down, x0l, x0r = call(
+        functools.partial(start_pack_kernel, pairs),
+        [rows(2 * size_x + TILE)] * 2 + [rows(2 * size_y)] * 2,
+        (pot0, mask, a, b),
+    )
     y0d, y0u = shift(up, down, "gx")
     whole_bits = [((size_x, size_y, size_z), i32)]
     (bits,) = call(bits_kernel, whole_bits, (mask, x0l, x0r), scratch=[padded], cost=cost)
@@ -671,12 +703,14 @@
         first, last = step == 0, step == STEPS - 1
         parts = 5 if last else 6
         x_rows, y_rows = rows(parts * size_y + TILE), rows(parts * size_x + (0 if last else TILE))
-        pot, post, f_edge, right, left, rest = call(
-            functools.partial(edge_kernel, first, last),
+        pot, post, f_edge, right, left, a, b, rest = call(
+            functools.partial(edge_kernel, first, last, pairs),
             [
                 (padded, f32),
                 ((N, edge2, size_y + PAD, size_z), f32),
                 fields(edge1),
+                x_rows,
+                x_rows,
                 x_rows,
                 x_rows,
                 ((3, edge2, size_y, size_z) if last else (edge1, size_y, size_z), f32),
@@ -684,7 +718,7 @@
             (rates, bits, pot0, x0l, x0r, y0d, y0u, *held, *sent),
             cost=cost,
         )
-        xl, xr = shift(right, left, "gy")
+        a, b = exchange(a, b, "gy")
         f_middle, up, down, more = call(
             functools.partial(middle_kernel, first, last),
             [
@@ -697,10 +731,10 @@
             scratch=[(N, size_x - edge2, size_y + PAD, size_z)],
             cost=cost,
         )
-        up, down = call(
-            functools.partial(pack_kernel, last, size_x, size_y),
-            [y_rows, y_rows],
-            (up, down, xl, xr, right, left),
+        up, down, xl, xr = call(
+            functools.partial(pack_kernel, last, pairs, size_x, size_y),
+            [y_rows, y_rows, x_rows, x_rows],
+            (up, down, a, b, right, left),
         )
         yd, yu = shift(up, down, "gx")
         held = (f_edge, f_middle, rest, more)

time: 55.8 us -> 54.9 us (0.984)
  starting transfers between devices: 30.3 us -> 29.6 us
    ppermute x0 -> x10, starting transfers between devices: none -> 10.2 us  [the longest x5 9.32 us: swap(): b = lax.ppermute(b, axis, partners[1])]
    ppermute x10 -> x5, starting transfers between devices: 20.4 us -> 12.5 us  [shift(): lax.ppermute(backward, axis, [(b, a) for a, b in ahead])]
    ppermute x0 -> x10, waiting for transfers between devices: none -> 4.47 us  [the longest x5 4.46 us: swap(): b = lax.ppermute(b, axis, partners[1])]
    ppermute x10 -> x5, waiting for transfers between devices: 12.7 us -> 8.79 us  [shift(): lax.ppermute(forward, axis, ahead)]
    ppermute x10 -> x5, starting transfers between devices: 9.84 us -> 6.94 us  [shift(): lax.ppermute(forward, axis, ahead)]
    ppermute x10 -> x5, waiting for transfers between devices: 2.27 us -> 1.44 us  [shift(): lax.ppermute(backward, axis, [(b, a) for a, b in ahead])]
  transfers between devices with their start and end apart: 20 -> 20, of which waited for: 14 -> 15; matrix products, arithmetic and copies ran while one was open for 0% -> 0% of each run, Pallas kernels for 10% -> 10%
where the time goes in v6:
time: 54.9 us; the launch traced here: 54.7 us
  starting transfers between devices  29.6 us (54%)
  waiting for transfers between devices  14.7 us (27%)
  Pallas kernels  9.58 us (17%)
  between operations  0.81 us (1%)
    ppermute x5, starting transfers between devices, shift(): lax.ppermute(backward, axis, [(b, a) for a, b in ahead])  12.5 us
    pallas_call x19, Pallas kernels, call(): pl.pallas_call(kernel, out_shape=[jax.ShapeDtypeStruct(shape, dtype) for...  9.58 us
    ppermute x5, starting transfers between devices, swap(): b = lax.ppermute(b, axis, partners[1])  9.32 us
    ppermute x5, waiting for transfers between devices, shift(): lax.ppermute(forward, axis, ahead)  8.79 us
    ppermute x5, starting transfers between devices, shift(): lax.ppermute(forward, axis, ahead)  6.94 us
    ppermute x5, waiting for transfers between devices, swap(): b = lax.ppermute(b, axis, partners[1])  4.46 us
    ppermute x5, waiting for transfers between devices, shift(): lax.ppermute(backward, axis, [(b, a) for a, b in ahead])  1.44 us
  transfers between devices with their start and end apart: 20, of which 15 were waited for; matrix products, arithmetic and copies ran while one was open for 0% of the time, Pallas kernels for 10%

profile of v6, /device:TPU:0, one launch (start us, length us, event | category | flops | bytes accessed | tf_op | source)
XLA Modules:
  0.0 54.7 jit_solution(3475054685450314455)
XLA Ops:
  0.6 1.7 %shard_map.68 = (f32[19,128,128]{2,1,0:T(8,128)S(1)}, f32[2,128,128]{2,1,0:T(8,128)S(1)}, f32[16,8,128]{2,1,0:T(8,128)S(1)}, f32[16,8,128]{2,1,0:T(8,128)S(1)}, ...) custom-call(f32[19,128,128]{2,1,0:T(8,128)} %bitcast.5, s32[128,128]{1,0:T(8,128)} %bitcast.7, s32[128,128]{1,0:T(8,128)} %bitcast.8, ...), custom_call_target="tpu_custom_call" | custom-call | tf_op jit(solution)/shard_map/pallas_call | solution.py:616
  2.3 0.6 %collective-permute-start = (f32[16,128]{1,0:T(8,128)S(1)}, f32[16,128]{1,0:T(8,128)S(1)}, u32[]{:S(2)}, u32[]{:S(2)}) collective-permute-start(f32[16,128]{1,0:T(8,128)S(1)} %get-tuple-element.81), channel_id=1, source_target_pairs={{0,1},{1,0},{2,3},{3,2},{4,5},{5,4},{6,7},{7,6},{8,9},{9,8},{10,11... | collective-permute-start | bytes 24584 | tf_op jit(solution)/shard_map/ppermute | solution.py:646
  2.9 2.6 %collective-permute-start.1 = (f32[16,128]{1,0:T(8,128)S(1)}, f32[16,128]{1,0:T(8,128)S(1)}, u32[]{:S(2)}, u32[]{:S(2)}) collective-permute-start(f32[16,128]{1,0:T(8,128)S(1)} %get-tuple-element.82), channel_id=1, source_target_pairs={{0,3},{1,2},{2,1},{3,0},{4,7},{5,6},{6,5},{7,4},{8,11},{9,10},{10,... | collective-permute-start | bytes 24584 | tf_op jit(solution)/shard_map/ppermute | solution.py:645
  5.5 0.0 collective-permute-done.a_ref
  5.5 1.4 %collective-permute-done.1.b_ref = f32[16,128]{1,0:T(8,128)S(1)} collective-permute-done((f32[16,128]{1,0:T(8,128)S(1)}, f32[16,128]{1,0:T(8,128)S(1)}, u32[]{:S(2)}, u32[]{:S(2)}) %collective-permute-start.1) | collective-permute-done | bytes 8224 | tf_op jit(solution)/shard_map/ppermute | solution.py:645
  6.9 1.8 %collective-permute-start.2 = (f32[40,128]{1,0:T(8,128)S(1)}, f32[40,128]{1,0:T(8,128)S(1)}, u32[]{:S(2)}, u32[]{:S(2)}) collective-permute-start(f32[40,128]{1,0:T(8,128)S(1)} %get-tuple-element.85), channel_id=1, source_target_pairs={{0,4},{4,8},{8,12},{12,0},{1,5},{5,9},{9,13},{13,1},{2,6},{6,10},{... | collective-permute-start | bytes 61448 | tf_op jit(solution)/shard_map/ppermute | solution.py:634
  8.7 2.1 %collective-permute-start.3 = (f32[40,128]{1,0:T(8,128)S(1)}, f32[40,128]{1,0:T(8,128)S(1)}, u32[]{:S(2)}, u32[]{:S(2)}) collective-permute-start(f32[40,128]{1,0:T(8,128)S(1)} %get-tuple-element.86), channel_id=1, source_target_pairs={{4,0},{8,4},{12,8},{0,12},{5,1},{9,5},{13,9},{1,13},{6,2},{10,6},{... | collective-permute-start | bytes 61448 | tf_op jit(solution)/shard_map/ppermute | solution.py:635
  10.8 0.0 copy-start
  10.8 0.4 shard_map.72.refs_7_.refs_5_
  11.2 0.2 shard_map.70.bits_in
  11.4 1.2 %collective-permute-done.2.y0d.refs_5_ = f32[40,128]{1,0:T(8,128)S(1)} collective-permute-done((f32[40,128]{1,0:T(8,128)S(1)}, f32[40,128]{1,0:T(8,128)S(1)}, u32[]{:S(2)}, u32[]{:S(2)}) %collective-permute-start.2) | collective-permute-done | bytes 20512 | tf_op jit(solution)/shard_map/ppermute | solution.py:634
  12.6 0.1 collective-permute-done.3.y0u.refs_6_
  12.7 0.1 shard_map.71.refs_1_.bits_ref
  12.8 0.0 copy-done
  12.8 0.1 broadcast_in_dim.2.refs_0_
  12.9 0.3 shard_map.73
  13.2 0.1 collective-permute-start.4
  13.3 1.7 %collective-permute-start.5 = (f32[56,128]{1,0:T(8,128)S(1)}, f32[56,128]{1,0:T(8,128)S(1)}, u32[]{:S(2)}, u32[]{:S(2)}) collective-permute-start(f32[56,128]{1,0:T(8,128)S(1)} %get-tuple-element.97), channel_id=1, source_target_pairs={{0,3},{1,2},{2,1},{3,0},{4,7},{5,6},{6,5},{7,4},{8,11},{9,10},{10,... | collective-permute-start | bytes 86024 | tf_op jit(solution)/shard_map/ppermute | solution.py:645
  15.0 0.9 %shard_map.74 = (f32[19,14,8,128]{3,2,1,0:T(8,128)S(1)}, f32[104,128]{1,0:T(8,128)S(1)}, f32[104,128]{1,0:T(8,128)S(1)}, f32[14,8,128]{2,1,0:T(8,128)S(1)}) custom-call(f32[19,8,128]{2,1,0:T(8,128)S(1)} %broadcast_in_dim.2.refs_0_, s32[16,8,128]{2,1,0:T(8,128)S(1)} %shard_map.71.refs_1_.bits_ref, f32[18,24,128]{2,1,0:T(8,128)S(1)} %get-tuple-element.89.refs_2_, ...), custom_call_target="tpu_custom_call" | custom-call | flops 6553600 | bytes 1310720 | tf_op jit(solution)/shard_map/pallas_call | solution.py:616
  15.8 0.0 collective-permute-done.4.refs_2_
  15.8 0.8 %collective-permute-done.5.refs_3_ = f32[56,128]{1,0:T(8,128)S(1)} collective-permute-done((f32[56,128]{1,0:T(8,128)S(1)}, f32[56,128]{1,0:T(8,128)S(1)}, u32[]{:S(2)}, u32[]{:S(2)}) %collective-permute-start.5) | collective-permute-done | bytes 28704 | tf_op jit(solution)/shard_map/ppermute | solution.py:645
  16.7 1.4 %collective-permute-start.6 = (f32[104,128]{1,0:T(8,128)S(1)}, f32[104,128]{1,0:T(8,128)S(1)}, u32[]{:S(2)}, u32[]{:S(2)}) collective-permute-start(f32[104,128]{1,0:T(8,128)S(1)} %get-tuple-element.102.refs_17_), channel_id=1, source_target_pairs={{0,4},{4,8},{8,12},{12,0},{1,5},{5,9},{9,13},{13,1},{2,6},{6,10},{... | collective-permute-start | bytes 159752 | tf_op jit(solution)/shard_map/ppermute | solution.py:634
  18.1 2.5 %collective-permute-start.7 = (f32[104,128]{1,0:T(8,128)S(1)}, f32[104,128]{1,0:T(8,128)S(1)}, u32[]{:S(2)}, u32[]{:S(2)}) collective-permute-start(f32[104,128]{1,0:T(8,128)S(1)} %get-tuple-element.103.refs_18_), channel_id=1, source_target_pairs={{4,0},{8,4},{12,8},{0,12},{5,1},{9,5},{13,9},{1,13},{6,2},{10,6},{... | collective-permute-start | bytes 159752 | tf_op jit(solution)/shard_map/ppermute | solution.py:635
  20.6 2.4 %collective-permute-done.6.refs_13_.refs_7_ = f32[104,128]{1,0:T(8,128)S(1)} collective-permute-done((f32[104,128]{1,0:T(8,128)S(1)}, f32[104,128]{1,0:T(8,128)S(1)}, u32[]{:S(2)}, u32[]{:S(2)}) %collective-permute-start.6) | collective-permute-done | bytes 53280 | tf_op jit(solution)/shard_map/ppermute | solution.py:634
  22.9 0.4 collective-permute-done.7.refs_14_.refs_8_
  23.4 0.4 shard_map.76
  23.7 0.1 collective-permute-start.8
  23.8 1.6 %collective-permute-start.9 = (f32[56,128]{1,0:T(8,128)S(1)}, f32[56,128]{1,0:T(8,128)S(1)}, u32[]{:S(2)}, u32[]{:S(2)}) collective-permute-start(f32[56,128]{1,0:T(8,128)S(1)} %get-tuple-element.113), channel_id=1, source_target_pairs={{0,3},{1,2},{2,1},{3,0},{4,7},{5,6},{6,5},{7,4},{8,11},{9,10},{10,... | collective-permute-start | bytes 86024 | tf_op jit(solution)/shard_map/ppermute | solution.py:645
  25.4 0.9 %shard_map.77 = (f32[19,14,8,128]{3,2,1,0:T(8,128)S(1)}, f32[104,128]{1,0:T(8,128)S(1)}, f32[104,128]{1,0:T(8,128)S(1)}, f32[14,8,128]{2,1,0:T(8,128)S(1)}) custom-call(f32[19,8,128]{2,1,0:T(8,128)S(1)} %broadcast_in_dim.2.refs_0_, s32[16,8,128]{2,1,0:T(8,128)S(1)} %shard_map.71.refs_1_.bits_ref, f32[18,24,128]{2,1,0:T(8,128)S(1)} %get-tuple-element.105.refs_2_, ...), custom_call_target="tpu_custom_call" | custom-call | flops 6553600 | bytes 1310720 | tf_op jit(solution)/shard_map/pallas_call | solution.py:616
  26.3 0.0 collective-permute-done.8.refs_2_
  26.3 0.9 %collective-permute-done.9.refs_3_ = f32[56,128]{1,0:T(8,128)S(1)} collective-permute-done((f32[56,128]{1,0:T(8,128)S(1)}, f32[56,128]{1,0:T(8,128)S(1)}, u32[]{:S(2)}, u32[]{:S(2)}) %collective-permute-start.9) | collective-permute-done | bytes 28704 | tf_op jit(solution)/shard_map/ppermute | solution.py:645
  27.2 1.2 %collective-permute-start.10 = (f32[104,128]{1,0:T(8,128)S(1)}, f32[104,128]{1,0:T(8,128)S(1)}, u32[]{:S(2)}, u32[]{:S(2)}) collective-permute-start(f32[104,128]{1,0:T(8,128)S(1)} %get-tuple-element.118.refs_17_), channel_id=1, source_target_pairs={{0,4},{4,8},{8,12},{12,0},{1,5},{5,9},{9,13},{13,1},{2,6},{6,10},{... | collective-permute-start | bytes 159752 | tf_op jit(solution)/shard_map/ppermute | solution.py:634
  28.4 2.7 %collective-permute-start.11 = (f32[104,128]{1,0:T(8,128)S(1)}, f32[104,128]{1,0:T(8,128)S(1)}, u32[]{:S(2)}, u32[]{:S(2)}) collective-permute-start(f32[104,128]{1,0:T(8,128)S(1)} %get-tuple-element.119.refs_18_), channel_id=1, source_target_pairs={{4,0},{8,4},{12,8},{0,12},{5,1},{9,5},{13,9},{1,13},{6,2},{10,6},{... | collective-permute-start | bytes 159752 | tf_op jit(solution)/shard_map/ppermute | solution.py:635
  31.1 2.3 %collective-permute-done.10.refs_13_.refs_7_ = f32[104,128]{1,0:T(8,128)S(1)} collective-permute-done((f32[104,128]{1,0:T(8,128)S(1)}, f32[104,128]{1,0:T(8,128)S(1)}, u32[]{:S(2)}, u32[]{:S(2)}) %collective-permute-start.10) | collective-permute-done | bytes 53280 | tf_op jit(solution)/shard_map/ppermute | solution.py:634
  33.4 0.3 collective-permute-done.11.refs_14_.refs_8_
  33.7 0.4 shard_map.79
  34.1 0.1 collective-permute-start.12
  34.2 1.7 %collective-permute-start.13 = (f32[56,128]{1,0:T(8,128)S(1)}, f32[56,128]{1,0:T(8,128)S(1)}, u32[]{:S(2)}, u32[]{:S(2)}) collective-permute-start(f32[56,128]{1,0:T(8,128)S(1)} %get-tuple-element.129), channel_id=1, source_target_pairs={{0,3},{1,2},{2,1},{3,0},{4,7},{5,6},{6,5},{7,4},{8,11},{9,10},{10,... | collective-permute-start | bytes 86024 | tf_op jit(solution)/shard_map/ppermute | solution.py:645
  35.9 0.9 %shard_map.80 = (f32[19,14,8,128]{3,2,1,0:T(8,128)S(1)}, f32[104,128]{1,0:T(8,128)S(1)}, f32[104,128]{1,0:T(8,128)S(1)}, f32[14,8,128]{2,1,0:T(8,128)S(1)}) custom-call(f32[19,8,128]{2,1,0:T(8,128)S(1)} %broadcast_in_dim.2.refs_0_, s32[16,8,128]{2,1,0:T(8,128)S(1)} %shard_map.71.refs_1_.bits_ref, f32[18,24,128]{2,1,0:T(8,128)S(1)} %get-tuple-element.121.refs_2_, ...), custom_call_target="tpu_custom_call" | custom-call | flops 6553600 | bytes 1310720 | tf_op jit(solution)/shard_map/pallas_call | solution.py:616
  36.8 0.0 collective-permute-done.12.refs_2_
  36.8 0.7 %collective-permute-done.13.refs_3_ = f32[56,128]{1,0:T(8,128)S(1)} collective-permute-done((f32[56,128]{1,0:T(8,128)S(1)}, f32[56,128]{1,0:T(8,128)S(1)}, u32[]{:S(2)}, u32[]{:S(2)}) %collective-permute-start.13) | collective-permute-done | bytes 28704 | tf_op jit(solution)/shard_map/ppermute | solution.py:645
  37.6 1.1 %collective-permute-start.14 = (f32[104,128]{1,0:T(8,128)S(1)}, f32[104,128]{1,0:T(8,128)S(1)}, u32[]{:S(2)}, u32[]{:S(2)}) collective-permute-start(f32[104,128]{1,0:T(8,128)S(1)} %get-tuple-element.134.refs_17_), channel_id=1, source_target_pairs={{0,4},{4,8},{8,12},{12,0},{1,5},{5,9},{9,13},{13,1},{2,6},{6,10},{... | collective-permute-start | bytes 159752 | tf_op jit(solution)/shard_map/ppermute | solution.py:634
  38.7 2.7 %collective-permute-start.15 = (f32[104,128]{1,0:T(8,128)S(1)}, f32[104,128]{1,0:T(8,128)S(1)}, u32[]{:S(2)}, u32[]{:S(2)}) collective-permute-start(f32[104,128]{1,0:T(8,128)S(1)} %get-tuple-element.135.refs_18_), channel_id=1, source_target_pairs={{4,0},{8,4},{12,8},{0,12},{5,1},{9,5},{13,9},{1,13},{6,2},{10,6},{... | collective-permute-start | bytes 159752 | tf_op jit(solution)/shard_map/ppermute | solution.py:635
  41.5 2.2 %collective-permute-done.14.refs_13_.refs_7_ = f32[104,128]{1,0:T(8,128)S(1)} collective-permute-done((f32[104,128]{1,0:T(8,128)S(1)}, f32[104,128]{1,0:T(8,128)S(1)}, u32[]{:S(2)}, u32[]{:S(2)}) %collective-permute-start.14) | collective-permute-done | bytes 53280 | tf_op jit(solution)/shard_map/ppermute | solution.py:634
  43.7 0.3 collective-permute-done.15.refs_14_.refs_8_
  44.0 0.4 shard_map.82
  44.4 0.1 collective-permute-start.16
  44.5 1.7 %collective-permute-start.17 = (f32[48,128]{1,0:T(8,128)S(1)}, f32[48,128]{1,0:T(8,128)S(1)}, u32[]{:S(2)}, u32[]{:S(2)}) collective-permute-start(f32[48,128]{1,0:T(8,128)S(1)} %get-tuple-element.144), channel_id=1, source_target_pairs={{0,3},{1,2},{2,1},{3,0},{4,7},{5,6},{6,5},{7,4},{8,11},{9,10},{10,... | collective-permute-start | bytes 73736 | tf_op jit(solution)/shard_map/ppermute | solution.py:645
  46.2 0.9 %shard_map.83 = (f32[19,14,8,128]{3,2,1,0:T(8,128)S(1)}, f32[80,128]{1,0:T(8,128)S(1)}, f32[80,128]{1,0:T(8,128)S(1)}, f32[3,128,128]{2,1,0:T(8,128)S(1)}) custom-call(f32[19,8,128]{2,1,0:T(8,128)S(1)} %broadcast_in_dim.2.refs_0_, s32[16,8,128]{2,1,0:T(8,128)S(1)} %shard_map.71.refs_1_.bits_ref, f32[18,24,128]{2,1,0:T(8,128)S(1)} %get-tuple-element.137.refs_2_, ...), custom_call_target="tpu_custom_call" | custom-call | flops 6553600 | bytes 1310720 | tf_op jit(solution)/shard_map/pallas_call | solution.py:616
  47.1 0.0 collective-permute-done.16.refs_2_
  47.1 0.7 %collective-permute-done.17.refs_3_ = f32[48,128]{1,0:T(8,128)S(1)} collective-permute-done((f32[48,128]{1,0:T(8,128)S(1)}, f32[48,128]{1,0:T(8,128)S(1)}, u32[]{:S(2)}, u32[]{:S(2)}) %collective-permute-start.17) | collective-permute-done | bytes 24608 | tf_op jit(solution)/shard_map/ppermute | solution.py:645
  47.8 1.4 %collective-permute-start.18 = (f32[80,128]{1,0:T(8,128)S(1)}, f32[80,128]{1,0:T(8,128)S(1)}, u32[]{:S(2)}, u32[]{:S(2)}) collective-permute-start(f32[80,128]{1,0:T(8,128)S(1)} %get-tuple-element.153), channel_id=1, source_target_pairs={{0,4},{4,8},{8,12},{12,0},{1,5},{5,9},{9,13},{13,1},{2,6},{6,10},{... | collective-permute-start | bytes 122888 | tf_op jit(solution)/shard_map/ppermute | solution.py:634
  49.2 2.5 %collective-permute-start.19 = (f32[80,128]{1,0:T(8,128)S(1)}, f32[80,128]{1,0:T(8,128)S(1)}, u32[]{:S(2)}, u32[]{:S(2)}) collective-permute-start(f32[80,128]{1,0:T(8,128)S(1)} %get-tuple-element.154), channel_id=1, source_target_pairs={{4,0},{8,4},{12,8},{0,12},{5,1},{9,5},{13,9},{1,13},{6,2},{10,6},{... | collective-permute-start | bytes 122888 | tf_op jit(solution)/shard_map/ppermute | solution.py:635
  51.7 1.3 %shard_map.85 = (f32[19,128,128]{2,1,0:T(8,128)}, f32[19,128,128]{2,1,0:T(8,128)S(1)}, f32[3,128,128]{2,1,0:T(8,128)}) custom-call(f32[19,2,8,128]{3,2,1,0:T(8,128)S(1)} %get-tuple-element.136.f_edge, f32[19,14,8,128]{3,2,1,0:T(8,128)S(1)} %get-tuple-element.140.f_middle, s32[16,8,128]{2,1,0:T(8,128)S(1)} %shard_map.71.refs_1_.bits_ref, ...), custom_call_target="tpu_custom_call" | custom-call | flops 6553600 | bytes 1310720 | tf_op jit(solution)/shard_map/pallas_call | solution.py:616
  53.0 0.7 %collective-permute-done.18.yd = f32[80,128]{1,0:T(8,128)S(1)} collective-permute-done((f32[80,128]{1,0:T(8,128)S(1)}, f32[80,128]{1,0:T(8,128)S(1)}, u32[]{:S(2)}, u32[]{:S(2)}) %collective-permute-start.18) | collective-permute-done | bytes 40992 | tf_op jit(solution)/shard_map/ppermute | solution.py:634
  53.7 0.3 collective-permute-done.19.yu
  54.0 0.7 %shard_map.86 = f32[19,128,128]{2,1,0:T(8,128)} custom-call(f32[19,128,128]{2,1,0:T(8,128)} %get-tuple-element.150.out_in, f32[19,128,128]{2,1,0:T(8,128)S(1)} %get-tuple-element.151.flat_ref, f32[2,128,128]{2,1,0:T(8,128)S(1)} %get-tuple-element.152.mask_ref, f32[80,128]{1,0:T(8,128)S(1)} %collective-permute-done.18.yd, ...), custom_call_target="tpu_custom_call", output_to_operand_aliasing={{}: (0, {})} | custom-call | tf_op jit(solution)/shard_map/pallas_call | solution.py:616
  (5 shorter events, 0.2 us)
Async XLA Ops:
  2.3 3.2 %collective-permute-start = (f32[16,128]{1,0:T(8,128)S(1)}, f32[16,128]{1,0:T(8,128)S(1)}, u32[]{:S(2)}, u32[]{:S(2)}) collective-permute-start(f32[16,128]{1,0:T(8,128)S(1)} %get-tuple-element.81), channel_id=1, source_target_pairs={{0,1},{1,0},{2,3},{3,2},{4,5},{5,4},{6,7},{7,6},{8,9},{9,8},{10,11... | collective-permute-start | bytes 24584 | tf_op jit(solution)/shard_map/ppermute | solution.py:646
  2.9 4.0 %collective-permute-start.1 = (f32[16,128]{1,0:T(8,128)S(1)}, f32[16,128]{1,0:T(8,128)S(1)}, u32[]{:S(2)}, u32[]{:S(2)}) collective-permute-start(f32[16,128]{1,0:T(8,128)S(1)} %get-tuple-element.82), channel_id=1, source_target_pairs={{0,3},{1,2},{2,1},{3,0},{4,7},{5,6},{6,5},{7,4},{8,11},{9,10},{10,... | collective-permute-start | bytes 24584 | tf_op jit(solution)/shard_map/ppermute | solution.py:645
  6.9 5.7 %collective-permute-start.2 = (f32[40,128]{1,0:T(8,128)S(1)}, f32[40,128]{1,0:T(8,128)S(1)}, u32[]{:S(2)}, u32[]{:S(2)}) collective-permute-start(f32[40,128]{1,0:T(8,128)S(1)} %get-tuple-element.85), channel_id=1, source_target_pairs={{0,4},{4,8},{8,12},{12,0},{1,5},{5,9},{9,13},{13,1},{2,6},{6,10},{... | collective-permute-start | bytes 61448 | tf_op jit(solution)/shard_map/ppermute | solution.py:634
  8.7 4.0 %collective-permute-start.3 = (f32[40,128]{1,0:T(8,128)S(1)}, f32[40,128]{1,0:T(8,128)S(1)}, u32[]{:S(2)}, u32[]{:S(2)}) collective-permute-start(f32[40,128]{1,0:T(8,128)S(1)} %get-tuple-element.86), channel_id=1, source_target_pairs={{4,0},{8,4},{12,8},{0,12},{5,1},{9,5},{13,9},{1,13},{6,2},{10,6},{... | collective-permute-start | bytes 61448 | tf_op jit(solution)/shard_map/ppermute | solution.py:635
  10.8 2.0 %copy-start = (f32[19]{0:T(128)S(1)}, f32[19]{0:T(128)}, u32[]{:S(2)}) copy-start(f32[19]{0:T(128)} %param.9) | copy-start | bytes 232
  13.2 2.6 %collective-permute-start.4 = (f32[56,128]{1,0:T(8,128)S(1)}, f32[56,128]{1,0:T(8,128)S(1)}, u32[]{:S(2)}, u32[]{:S(2)}) collective-permute-start(f32[56,128]{1,0:T(8,128)S(1)} %get-tuple-element.96), channel_id=1, source_target_pairs={{0,1},{1,0},{2,3},{3,2},{4,5},{5,4},{6,7},{7,6},{8,9},{9,8},{10,11... | collective-permute-start | bytes 86024 | tf_op jit(solution)/shard_map/ppermute | solution.py:646
  13.3 3.4 %collective-permute-start.5 = (f32[56,128]{1,0:T(8,128)S(1)}, f32[56,128]{1,0:T(8,128)S(1)}, u32[]{:S(2)}, u32[]{:S(2)}) collective-permute-start(f32[56,128]{1,0:T(8,128)S(1)} %get-tuple-element.97), channel_id=1, source_target_pairs={{0,3},{1,2},{2,1},{3,0},{4,7},{5,6},{6,5},{7,4},{8,11},{9,10},{10,... | collective-permute-start | bytes 86024 | tf_op jit(solution)/shard_map/ppermute | solution.py:645
  16.7 6.3 %collective-permute-start.6 = (f32[104,128]{1,0:T(8,128)S(1)}, f32[104,128]{1,0:T(8,128)S(1)}, u32[]{:S(2)}, u32[]{:S(2)}) collective-permute-start(f32[104,128]{1,0:T(8,128)S(1)} %get-tuple-element.102.refs_17_), channel_id=1, source_target_pairs={{0,4},{4,8},{8,12},{12,0},{1,5},{5,9},{9,13},{13,1},{2,6},{6,10},{... | collective-permute-start | bytes 159752 | tf_op jit(solution)/shard_map/ppermute | solution.py:634
  18.1 5.3 %collective-permute-start.7 = (f32[104,128]{1,0:T(8,128)S(1)}, f32[104,128]{1,0:T(8,128)S(1)}, u32[]{:S(2)}, u32[]{:S(2)}) collective-permute-start(f32[104,128]{1,0:T(8,128)S(1)} %get-tuple-element.103.refs_18_), channel_id=1, source_target_pairs={{4,0},{8,4},{12,8},{0,12},{5,1},{9,5},{13,9},{1,13},{6,2},{10,6},{... | collective-permute-start | bytes 159752 | tf_op jit(solution)/shard_map/ppermute | solution.py:635
  23.7 2.5 %collective-permute-start.8 = (f32[56,128]{1,0:T(8,128)S(1)}, f32[56,128]{1,0:T(8,128)S(1)}, u32[]{:S(2)}, u32[]{:S(2)}) collective-permute-start(f32[56,128]{1,0:T(8,128)S(1)} %get-tuple-element.112), channel_id=1, source_target_pairs={{0,1},{1,0},{2,3},{3,2},{4,5},{5,4},{6,7},{7,6},{8,9},{9,8},{10,11... | collective-permute-start | bytes 86024 | tf_op jit(solution)/shard_map/ppermute | solution.py:646
  23.8 3.4 %collective-permute-start.9 = (f32[56,128]{1,0:T(8,128)S(1)}, f32[56,128]{1,0:T(8,128)S(1)}, u32[]{:S(2)}, u32[]{:S(2)}) collective-permute-start(f32[56,128]{1,0:T(8,128)S(1)} %get-tuple-element.113), channel_id=1, source_target_pairs={{0,3},{1,2},{2,1},{3,0},{4,7},{5,6},{6,5},{7,4},{8,11},{9,10},{10,... | collective-permute-start | bytes 86024 | tf_op jit(solution)/shard_map/ppermute | solution.py:645
  27.2 6.2 %collective-permute-start.10 = (f32[104,128]{1,0:T(8,128)S(1)}, f32[104,128]{1,0:T(8,128)S(1)}, u32[]{:S(2)}, u32[]{:S(2)}) collective-permute-start(f32[104,128]{1,0:T(8,128)S(1)} %get-tuple-element.118.refs_17_), channel_id=1, source_target_pairs={{0,4},{4,8},{8,12},{12,0},{1,5},{5,9},{9,13},{13,1},{2,6},{6,10},{... | collective-permute-start | bytes 159752 | tf_op jit(solution)/shard_map/ppermute | solution.py:634
  28.4 5.3 %collective-permute-start.11 = (f32[104,128]{1,0:T(8,128)S(1)}, f32[104,128]{1,0:T(8,128)S(1)}, u32[]{:S(2)}, u32[]{:S(2)}) collective-permute-start(f32[104,128]{1,0:T(8,128)S(1)} %get-tuple-element.119.refs_18_), channel_id=1, source_target_pairs={{4,0},{8,4},{12,8},{0,12},{5,1},{9,5},{13,9},{1,13},{6,2},{10,6},{... | collective-permute-start | bytes 159752 | tf_op jit(solution)/shard_map/ppermute | solution.py:635
  34.1 2.7 %collective-permute-start.12 = (f32[56,128]{1,0:T(8,128)S(1)}, f32[56,128]{1,0:T(8,128)S(1)}, u32[]{:S(2)}, u32[]{:S(2)}) collective-permute-start(f32[56,128]{1,0:T(8,128)S(1)} %get-tuple-element.128), channel_id=1, source_target_pairs={{0,1},{1,0},{2,3},{3,2},{4,5},{5,4},{6,7},{7,6},{8,9},{9,8},{10,11... | collective-permute-start | bytes 86024 | tf_op jit(solution)/shard_map/ppermute | solution.py:646
  34.2 3.4 %collective-permute-start.13 = (f32[56,128]{1,0:T(8,128)S(1)}, f32[56,128]{1,0:T(8,128)S(1)}, u32[]{:S(2)}, u32[]{:S(2)}) collective-permute-start(f32[56,128]{1,0:T(8,128)S(1)} %get-tuple-element.129), channel_id=1, source_target_pairs={{0,3},{1,2},{2,1},{3,0},{4,7},{5,6},{6,5},{7,4},{8,11},{9,10},{10,... | collective-permute-start | bytes 86024 | tf_op jit(solution)/shard_map/ppermute | solution.py:645
  37.6 6.1 %collective-permute-start.14 = (f32[104,128]{1,0:T(8,128)S(1)}, f32[104,128]{1,0:T(8,128)S(1)}, u32[]{:S(2)}, u32[]{:S(2)}) collective-permute-start(f32[104,128]{1,0:T(8,128)S(1)} %get-tuple-element.134.refs_17_), channel_id=1, source_target_pairs={{0,4},{4,8},{8,12},{12,0},{1,5},{5,9},{9,13},{13,1},{2,6},{6,10},{... | collective-permute-start | bytes 159752 | tf_op jit(solution)/shard_map/ppermute | solution.py:634
  38.7 5.3 %collective-permute-start.15 = (f32[104,128]{1,0:T(8,128)S(1)}, f32[104,128]{1,0:T(8,128)S(1)}, u32[]{:S(2)}, u32[]{:S(2)}) collective-permute-start(f32[104,128]{1,0:T(8,128)S(1)} %get-tuple-element.135.refs_18_), channel_id=1, source_target_pairs={{4,0},{8,4},{12,8},{0,12},{5,1},{9,5},{13,9},{1,13},{6,2},{10,6},{... | collective-permute-start | bytes 159752 | tf_op jit(solution)/shard_map/ppermute | solution.py:635
  44.4 2.7 %collective-permute-start.16 = (f32[48,128]{1,0:T(8,128)S(1)}, f32[48,128]{1,0:T(8,128)S(1)}, u32[]{:S(2)}, u32[]{:S(2)}) collective-permute-start(f32[48,128]{1,0:T(8,128)S(1)} %get-tuple-element.143), channel_id=1, source_target_pairs={{0,1},{1,0},{2,3},{3,2},{4,5},{5,4},{6,7},{7,6},{8,9},{9,8},{10,11... | collective-permute-start | bytes 73736 | tf_op jit(solution)/shard_map/ppermute | solution.py:646
  44.5 3.3 %collective-permute-start.17 = (f32[48,128]{1,0:T(8,128)S(1)}, f32[48,128]{1,0:T(8,128)S(1)}, u32[]{:S(2)}, u32[]{:S(2)}) collective-permute-start(f32[48,128]{1,0:T(8,128)S(1)} %get-tuple-element.144), channel_id=1, source_target_pairs={{0,3},{1,2},{2,1},{3,0},{4,7},{5,6},{6,5},{7,4},{8,11},{9,10},{10,... | collective-permute-start | bytes 73736 | tf_op jit(solution)/shard_map/ppermute | solution.py:645
  47.8 5.9 %collective-permute-start.18 = (f32[80,128]{1,0:T(8,128)S(1)}, f32[80,128]{1,0:T(8,128)S(1)}, u32[]{:S(2)}, u32[]{:S(2)}) collective-permute-start(f32[80,128]{1,0:T(8,128)S(1)} %get-tuple-element.153), channel_id=1, source_target_pairs={{0,4},{4,8},{8,12},{12,0},{1,5},{5,9},{9,13},{13,1},{2,6},{6,10},{... | collective-permute-start | bytes 122888 | tf_op jit(solution)/shard_map/ppermute | solution.py:634
  49.2 4.8 %collective-permute-start.19 = (f32[80,128]{1,0:T(8,128)S(1)}, f32[80,128]{1,0:T(8,128)S(1)}, u32[]{:S(2)}, u32[]{:S(2)}) collective-permute-start(f32[80,128]{1,0:T(8,128)S(1)} %get-tuple-element.154), channel_id=1, source_target_pairs={{4,0},{8,4},{12,8},{0,12},{5,1},{9,5},{13,9},{1,13},{6,2},{10,6},{... | collective-permute-start | bytes 122888 | tf_op jit(solution)/shard_map/ppermute | solution.py:635

commit v7 on v6

--- a/solution.py
+++ b/solution.py
@@ -154,58 +154,78 @@
         xl_ref[...], xr_ref[...] = a_ref[...], b_ref[...]
 
 
-def start_kernel(pairs, f_hbm, mask_hbm, wet_hbm, wall_hbm, raw_ref, flat_ref, mask_ref, pot_ref, a_ref, b_ref, *scratch):
-    mask_in, wet_in, wall_in, f_sems, sems = scratch
-    layers, rows = mask_ref.shape[0], mask_ref.shape[1]
+def wall_of(wet, wall_ref):
+    wall = jnp.zeros(wet.shape, jnp.float32)
+    for c in range(wall_ref.shape[0]):
+        wall = jnp.where(wet == c, wall_ref[c], wall)
+    return wall
+
+
+def face_kernel(pairs, f_hbm, mask_hbm, wet_hbm, wall_hbm, a_ref, b_ref, rows_ref, *scratch):
+    layer_in, row_in, mask_in, wet_in, wall_in, layer_sems, row_sems, sems = scratch
+    layers, rows = row_in.shape[2], layer_in.shape[2]
     small = [
         pltpu.make_async_copy(source, target, sems.at[i])
         for i, (source, target) in enumerate(
             ((wall_hbm, wall_in), (mask_hbm, mask_in), (wet_hbm, wet_in))
         )
     ]
-    large = [pltpu.make_async_copy(f_hbm.at[k], raw_ref.at[k], f_sems.at[k]) for k in range(N)]
+    large = []
+    for s, layer in enumerate((0, layers - 1)):
+        for row in range(rows):
+            source = f_hbm.at[:, pl.ds(row * layers + layer, 1)]
+            target = layer_in.at[s, :, pl.ds(row, 1)]
+            large.append(pltpu.make_async_copy(source, target, layer_sems.at[s, row]))
+    for s, row in enumerate((0, rows - 1)):
+        source = f_hbm.at[:, pl.ds(row * layers, layers)]
+        large.append(pltpu.make_async_copy(source, row_in.at[s], row_sems.at[s]))
     for copy in small + large:
         copy.start()
-    for copy in small:
+    for copy in small + large:
         copy.wait()
-    blocks = [slice(i, i + TILE) for i in range(0, layers * rows, TILE)]
-    for at in blocks:
-        wet = wet_in[at]
-        wall = jnp.zeros(wet.shape, jnp.float32)
-        for c in range(wall_in.shape[0]):
-            wall = jnp.where(wet == c, wall_in[c], wall)
-        flat_ref[1, at] = wall
-        flat_ref[0, at] = jnp.where(mask_in[at] == 1, 1.0, 0.0)
-    density = None
-    for k, copy in enumerate(large):
-        copy.wait()
-        here = [raw_ref[k, at] for at in blocks]
-        density = here if density is None else [a + b for a, b in zip(density, here)]
-    for at, value in zip(blocks, density):
-        flat_ref[1, at] = potential_of(value, flat_ref[0, at] > 0.5, flat_ref[1, at])
+    faces = []
+    for s, layer in enumerate((0, layers - 1)):
+        at = pl.ds(layer, rows, stride=layers)
+        pore = mask_in[at] == 1
+        density = total([layer_in[s, k] for k in range(N)])
+        pot = potential_of(density, pore, wall_of(wet_in[at], wall_in))
+        faces.append((pot, jnp.where(pore, 1.0, 0.0)))
+    for i in range(2):
+        at = slice(i * rows, (i + 1) * rows)
+        a_ref[at], b_ref[at] = in_swap_order(pairs, faces[1][i], faces[0][i])
+    for s, row in enumerate((0, rows - 1)):
+        at = slice(row * layers, (row + 1) * layers)
+        pore = mask_in[at] == 1
+        density = total([row_in[s, k] for k in range(N)])
+        rows_ref[s, :layers] = potential_of(density, pore, wall_of(wet_in[at], wall_in))
+        rows_ref[s, layers:] = jnp.where(pore, 1.0, 0.0)
+
+
+def turn_kernel(raw_ref, mask_in, wet_in, wall_ref, rate_ref, f_ref, rates_ref, flat_ref, mask_ref, pot_ref):
+    layers, rows = f_ref.shape[1], f_ref.shape[2]
+    for k in range(N):
+        rates_ref[k] = jnp.full(rates_ref.shape[1:], rate_ref[k], jnp.float32)
+    for i in range(0, layers * rows, TILE):
+        at = slice(i, i + TILE)
+        pore = mask_in[at] == 1
+        density = total([raw_ref[k, at] for k in range(N)])
+        flat_ref[0, at] = jnp.where(pore, 1.0, 0.0)
+        flat_ref[1, at] = potential_of(density, pore, wall_of(wet_in[at], wall_ref))
     for i in range(layers):
         mask_ref[i] = flat_ref[0, pl.ds(i, rows, stride=layers)]
         pot_ref[i] = flat_ref[1, pl.ds(i, rows, stride=layers)]
-    for ref in (pot_ref, mask_ref):
-        at = slice(0, rows) if ref is pot_ref else slice(rows, 2 * rows)
-        a_ref[at], b_ref[at] = in_swap_order(pairs, ref[layers - 1], ref[0])
-
-
-def turn_kernel(raw_ref, f_ref):
-    layers, rows = f_ref.shape[1], f_ref.shape[2]
     for k in range(N):
         for i in range(layers):
             f_ref[k, i] = raw_ref[k, pl.ds(i, rows, stride=layers)]
 
 
-def start_pack_kernel(pairs, pot_ref, mask_ref, a_ref, b_ref, up_ref, down_ref, from_left, from_right):
-    size_x, size_y = mask_ref.shape[0], mask_ref.shape[1]
+def start_pack_kernel(pairs, rows_ref, a_ref, b_ref, up_ref, down_ref, from_left, from_right):
+    size_x = rows_ref.shape[1] // 2
+    size_y = a_ref.shape[0] // 2
     sort_received(pairs, a_ref, b_ref, from_left, from_right)
-    for ref, y in ((up_ref, size_y - 1), (down_ref, 0)):
+    for s, ref, y in ((1, up_ref, size_y - 1), (0, down_ref, 0)):
+        ref[: 2 * size_x] = rows_ref[s]
         ref[2 * size_x :] = jnp.zeros((TILE, ref.shape[1]), jnp.float32)
-        for x in range(size_x):
-            ref[x : x + 1] = pot_ref[x, y : y + 1]
-            ref[size_x + x : size_x + x + 1] = mask_ref[x, y : y + 1]
         for i, side in enumerate((from_left, from_right)):
             row = 2 * size_x + i
             ref[row : row + 1] = side[y : y + 1]
@@ -608,6 +628,7 @@
 
 
 VMEM = pl.BlockSpec(memory_space=pltpu.VMEM)
+SMEM = pl.BlockSpec(memory_space=pltpu.SMEM)
 HBM = pl.BlockSpec(memory_space=pltpu.HBM)
 
 
@@ -661,35 +682,41 @@
     operations = 400 * cells * size_z
     cost = pl.CostEstimate(flops=operations, bytes_accessed=4 * operations // 20, transcendentals=0)
 
-    operands = [
-        pltpu.with_memory_space_constraint(item, pltpu.HBM)
-        for item in (
-            populations.reshape(N, cells, size_z),
-            fluid_mask.reshape(cells, size_z),
-            wet_class.reshape(cells, size_z),
-            wall_potential,
-        )
-    ]
-    raw, flat_mask, mask, pot0, a, b = call(
-        functools.partial(start_kernel, pairs),
-        [flat(N), flat(2), whole, whole, rows(2 * size_y), rows(2 * size_y)],
-        operands,
+    operands = (
+        populations.reshape(N, cells, size_z),
+        fluid_mask.reshape(cells, size_z),
+        wet_class.reshape(cells, size_z),
+        wall_potential,
+    )
+    start_rows = rows(2 * size_x + TILE)
+    a, b, row_faces = call(
+        functools.partial(face_kernel, pairs),
+        [rows(2 * size_y), rows(2 * size_y), ((2, 2 * size_x, size_z), f32)],
+        [pltpu.with_memory_space_constraint(item, pltpu.HBM) for item in operands],
         special={i: HBM for i in range(4)},
         scratch=[
+            (2, N, size_y, size_z),
+            (2, N, size_x, size_z),
             pltpu.VMEM((cells, size_z), i32),
             pltpu.VMEM((cells, size_z), i32),
             pltpu.SMEM(wall_potential.shape, f32),
-            pltpu.SemaphoreType.DMA((N,)),
+            pltpu.SemaphoreType.DMA((2, size_y)),
+            pltpu.SemaphoreType.DMA((2,)),
             pltpu.SemaphoreType.DMA((3,)),
         ],
     )
     a, b = exchange(a, b, "gy")
-    (f,) = call(turn_kernel, [fields(size_x)], (raw,), cost=cost)
-    rates = jnp.broadcast_to(relax_rates[:, None, None], (N, TILE, size_z))
     up, down, x0l, x0r = call(
         functools.partial(start_pack_kernel, pairs),
-        [rows(2 * size_x + TILE)] * 2 + [rows(2 * size_y)] * 2,
-        (pot0, mask, a, b),
+        [start_rows, start_rows, rows(2 * size_y), rows(2 * size_y)],
+        (row_faces, a, b),
+    )
+    f, rates, flat_mask, mask, pot0 = call(
+        turn_kernel,
+        [fields(size_x), ((N, TILE, size_z), f32), flat(2), whole, whole],
+        (*operands, relax_rates),
+        special={3: SMEM, 4: SMEM},
+        cost=cost,
     )
     y0d, y0u = shift(up, down, "gx")
     whole_bits = [((size_x, size_y, size_z), i32)]

time: 54.9 us -> 54.7 us (level)
  waiting for transfers between devices: 14.7 us -> 14 us
    ppermute x5, waiting for transfers between devices: 8.79 us -> 8.13 us  [shift(): lax.ppermute(forward, axis, ahead)]
  transfers between devices with their start and end apart: 20 -> 20, of which waited for: 15 -> 15; matrix products, arithmetic and copies ran while one was open for 0% -> 0% of each run, Pallas kernels for 10% -> 11%
where the time goes in v7:
time: 54.7 us; the launch traced here: 54.5 us
  starting transfers between devices  29.6 us (54%)
  waiting for transfers between devices  14 us (26%)
  Pallas kernels  10.1 us (18%)
  between operations  0.84 us (2%)
    ppermute x5, starting transfers between devices, shift(): lax.ppermute(backward, axis, [(b, a) for a, b in ahead])  12.5 us
    pallas_call x19, Pallas kernels, call(): pl.pallas_call(kernel, out_shape=[jax.ShapeDtypeStruct(shape, dtype) for...  10.1 us
    ppermute x5, starting transfers between devices, swap(): b = lax.ppermute(b, axis, partners[1])  9.32 us
    ppermute x5, waiting for transfers between devices, shift(): lax.ppermute(forward, axis, ahead)  8.13 us
    ppermute x5, starting transfers between devices, shift(): lax.ppermute(forward, axis, ahead)  6.94 us
    ppermute x5, waiting for transfers between devices, swap(): b = lax.ppermute(b, axis, partners[1])  4.41 us
    ppermute x5, waiting for transfers between devices, shift(): lax.ppermute(backward, axis, [(b, a) for a, b in ahead])  1.44 us
  transfers between devices with their start and end apart: 20, of which 15 were waited for; matrix products, arithmetic and copies ran while one was open for 0% of the time, Pallas kernels for 11%

profile of v7, /device:TPU:0, one launch (start us, length us, event | category | flops | bytes accessed | tf_op | source)
XLA Modules:
  0.0 54.5 jit_solution(13637430085745709827)
XLA Ops:
  0.6 0.0 copy-start.3
  0.6 0.0 copy-start.2
  0.7 0.0 copy-start.1
  0.7 0.0 copy-start
  0.7 0.0 copy-start.4
  0.7 1.5 %shard_map.69 = (f32[16,128]{1,0:T(8,128)S(1)}, f32[16,128]{1,0:T(8,128)S(1)}, f32[2,32,128]{2,1,0:T(8,128)S(1)}) custom-call(f32[19,128,128]{2,1,0:T(8,128)} %bitcast.5, s32[128,128]{1,0:T(8,128)} %bitcast.7, s32[128,128]{1,0:T(8,128)} %bitcast.9, f32[4]{0:T(128)} %wall_hbm.1), custom_call_target="tpu_custom_call" | custom-call | tf_op jit(solution)/shard_map/pallas_call | solution.py:637
  2.2 0.6 %collective-permute-start = (f32[16,128]{1,0:T(8,128)S(1)}, f32[16,128]{1,0:T(8,128)S(1)}, u32[]{:S(2)}, u32[]{:S(2)}) collective-permute-start(f32[16,128]{1,0:T(8,128)S(1)} %get-tuple-element.84), channel_id=1, source_target_pairs={{0,1},{1,0},{2,3},{3,2},{4,5},{5,4},{6,7},{7,6},{8,9},{9,8},{10,11... | collective-permute-start | bytes 24584 | tf_op jit(solution)/shard_map/ppermute | solution.py:667
  2.8 2.6 %collective-permute-start.1 = (f32[16,128]{1,0:T(8,128)S(1)}, f32[16,128]{1,0:T(8,128)S(1)}, u32[]{:S(2)}, u32[]{:S(2)}) collective-permute-start(f32[16,128]{1,0:T(8,128)S(1)} %get-tuple-element.85), channel_id=1, source_target_pairs={{0,3},{1,2},{2,1},{3,0},{4,7},{5,6},{6,5},{7,4},{8,11},{9,10},{10,... | collective-permute-start | bytes 24584 | tf_op jit(solution)/shard_map/ppermute | solution.py:666
  5.3 0.0 collective-permute-done.a_ref
  5.4 1.4 %collective-permute-done.1.b_ref = f32[16,128]{1,0:T(8,128)S(1)} collective-permute-done((f32[16,128]{1,0:T(8,128)S(1)}, f32[16,128]{1,0:T(8,128)S(1)}, u32[]{:S(2)}, u32[]{:S(2)}) %collective-permute-start.1) | collective-permute-done | bytes 8224 | tf_op jit(solution)/shard_map/ppermute | solution.py:666
  6.7 1.8 %collective-permute-start.2 = (f32[40,128]{1,0:T(8,128)S(1)}, f32[40,128]{1,0:T(8,128)S(1)}, u32[]{:S(2)}, u32[]{:S(2)}) collective-permute-start(f32[40,128]{1,0:T(8,128)S(1)} %get-tuple-element.88), channel_id=1, source_target_pairs={{0,4},{4,8},{8,12},{12,0},{1,5},{5,9},{9,13},{13,1},{2,6},{6,10},{... | collective-permute-start | bytes 61448 | tf_op jit(solution)/shard_map/ppermute | solution.py:655
  8.5 2.1 %collective-permute-start.3 = (f32[40,128]{1,0:T(8,128)S(1)}, f32[40,128]{1,0:T(8,128)S(1)}, u32[]{:S(2)}, u32[]{:S(2)}) collective-permute-start(f32[40,128]{1,0:T(8,128)S(1)} %get-tuple-element.89), channel_id=1, source_target_pairs={{4,0},{8,4},{12,8},{0,12},{5,1},{9,5},{13,9},{1,13},{6,2},{10,6},{... | collective-permute-start | bytes 61448 | tf_op jit(solution)/shard_map/ppermute | solution.py:656
  10.6 0.0 copy-done.3
  10.6 0.0 copy-done.2
  10.6 0.0 copy-done.1
  10.6 0.0 copy-done
  10.6 0.0 copy-done.4
  10.7 1.1 %shard_map.68 = (f32[19,16,8,128]{3,2,1,0:T(8,128)S(1)}, f32[19,8,128]{2,1,0:T(8,128)S(1)}, f32[2,128,128]{2,1,0:T(8,128)S(1)}, f32[16,8,128]{2,1,0:T(8,128)S(1)}, f32[16,8,128]{2,1,0:T(8,128)S(1)}) custom-call(f32[19,128,128]{2,1,0:T(8,128)S(1)} %bitcast.6, s32[128,128]{1,0:T(8,128)S(1)} %bitcast.8, s32[128,128]{1,0:T(8,128)S(1)} %bitcast.10, ...), custom_call_target="tpu_custom_call" | custom-call | flops 6553600 | bytes 1310720 | tf_op jit(solution)/shard_map/pallas_call | solution.py:637
  11.7 0.2 shard_map.71.bits_in
  12.0 0.5 collective-permute-done.2.y0d.refs_5_
  12.5 0.1 collective-permute-done.3.y0u.refs_6_
  12.5 0.1 shard_map.72.refs_1_.bits_ref
  12.6 0.3 shard_map.73
  13.0 0.1 collective-permute-start.4
  13.0 1.7 %collective-permute-start.5 = (f32[56,128]{1,0:T(8,128)S(1)}, f32[56,128]{1,0:T(8,128)S(1)}, u32[]{:S(2)}, u32[]{:S(2)}) collective-permute-start(f32[56,128]{1,0:T(8,128)S(1)} %get-tuple-element.101), channel_id=1, source_target_pairs={{0,3},{1,2},{2,1},{3,0},{4,7},{5,6},{6,5},{7,4},{8,11},{9,10},{10,... | collective-permute-start | bytes 86024 | tf_op jit(solution)/shard_map/ppermute | solution.py:666
  14.7 0.8 %shard_map.74 = (f32[19,14,8,128]{3,2,1,0:T(8,128)S(1)}, f32[104,128]{1,0:T(8,128)S(1)}, f32[104,128]{1,0:T(8,128)S(1)}, f32[14,8,128]{2,1,0:T(8,128)S(1)}) custom-call(f32[19,8,128]{2,1,0:T(8,128)S(1)} %get-tuple-element.81.refs_0_, s32[16,8,128]{2,1,0:T(8,128)S(1)} %shard_map.72.refs_1_.bits_ref, f32[18,24,128]{2,1,0:T(8,128)S(1)} %get-tuple-element.93.refs_2_, ...), custom_call_target="tpu_custom_call" | custom-call | flops 6553600 | bytes 1310720 | tf_op jit(solution)/shard_map/pallas_call | solution.py:637
  15.6 0.0 collective-permute-done.4.refs_2_
  15.6 0.8 %collective-permute-done.5.refs_3_ = f32[56,128]{1,0:T(8,128)S(1)} collective-permute-done((f32[56,128]{1,0:T(8,128)S(1)}, f32[56,128]{1,0:T(8,128)S(1)}, u32[]{:S(2)}, u32[]{:S(2)}) %collective-permute-start.5) | collective-permute-done | bytes 28704 | tf_op jit(solution)/shard_map/ppermute | solution.py:666
  16.4 1.4 %collective-permute-start.6 = (f32[104,128]{1,0:T(8,128)S(1)}, f32[104,128]{1,0:T(8,128)S(1)}, u32[]{:S(2)}, u32[]{:S(2)}) collective-permute-start(f32[104,128]{1,0:T(8,128)S(1)} %get-tuple-element.106.refs_17_), channel_id=1, source_target_pairs={{0,4},{4,8},{8,12},{12,0},{1,5},{5,9},{9,13},{13,1},{2,6},{6,10},{... | collective-permute-start | bytes 159752 | tf_op jit(solution)/shard_map/ppermute | solution.py:655
  17.9 2.5 %collective-permute-start.7 = (f32[104,128]{1,0:T(8,128)S(1)}, f32[104,128]{1,0:T(8,128)S(1)}, u32[]{:S(2)}, u32[]{:S(2)}) collective-permute-start(f32[104,128]{1,0:T(8,128)S(1)} %get-tuple-element.107.refs_18_), channel_id=1, source_target_pairs={{4,0},{8,4},{12,8},{0,12},{5,1},{9,5},{13,9},{1,13},{6,2},{10,6},{... | collective-permute-start | bytes 159752 | tf_op jit(solution)/shard_map/ppermute | solution.py:656
  20.3 2.4 %collective-permute-done.6.refs_13_.refs_7_ = f32[104,128]{1,0:T(8,128)S(1)} collective-permute-done((f32[104,128]{1,0:T(8,128)S(1)}, f32[104,128]{1,0:T(8,128)S(1)}, u32[]{:S(2)}, u32[]{:S(2)}) %collective-permute-start.6) | collective-permute-done | bytes 53280 | tf_op jit(solution)/shard_map/ppermute | solution.py:655
  22.7 0.4 collective-permute-done.7.refs_14_.refs_8_
  23.1 0.4 shard_map.76
  23.5 0.1 collective-permute-start.8
  23.6 1.6 %collective-permute-start.9 = (f32[56,128]{1,0:T(8,128)S(1)}, f32[56,128]{1,0:T(8,128)S(1)}, u32[]{:S(2)}, u32[]{:S(2)}) collective-permute-start(f32[56,128]{1,0:T(8,128)S(1)} %get-tuple-element.117), channel_id=1, source_target_pairs={{0,3},{1,2},{2,1},{3,0},{4,7},{5,6},{6,5},{7,4},{8,11},{9,10},{10,... | collective-permute-start | bytes 86024 | tf_op jit(solution)/shard_map/ppermute | solution.py:666
  25.2 0.9 %shard_map.77 = (f32[19,14,8,128]{3,2,1,0:T(8,128)S(1)}, f32[104,128]{1,0:T(8,128)S(1)}, f32[104,128]{1,0:T(8,128)S(1)}, f32[14,8,128]{2,1,0:T(8,128)S(1)}) custom-call(f32[19,8,128]{2,1,0:T(8,128)S(1)} %get-tuple-element.81.refs_0_, s32[16,8,128]{2,1,0:T(8,128)S(1)} %shard_map.72.refs_1_.bits_ref, f32[18,24,128]{2,1,0:T(8,128)S(1)} %get-tuple-element.109.refs_2_, ...), custom_call_target="tpu_custom_call" | custom-call | flops 6553600 | bytes 1310720 | tf_op jit(solution)/shard_map/pallas_call | solution.py:637
  26.1 0.0 collective-permute-done.8.refs_2_
  26.1 0.9 %collective-permute-done.9.refs_3_ = f32[56,128]{1,0:T(8,128)S(1)} collective-permute-done((f32[56,128]{1,0:T(8,128)S(1)}, f32[56,128]{1,0:T(8,128)S(1)}, u32[]{:S(2)}, u32[]{:S(2)}) %collective-permute-start.9) | collective-permute-done | bytes 28704 | tf_op jit(solution)/shard_map/ppermute | solution.py:666
  27.0 1.2 %collective-permute-start.10 = (f32[104,128]{1,0:T(8,128)S(1)}, f32[104,128]{1,0:T(8,128)S(1)}, u32[]{:S(2)}, u32[]{:S(2)}) collective-permute-start(f32[104,128]{1,0:T(8,128)S(1)} %get-tuple-element.122.refs_17_), channel_id=1, source_target_pairs={{0,4},{4,8},{8,12},{12,0},{1,5},{5,9},{9,13},{13,1},{2,6},{6,10},{... | collective-permute-start | bytes 159752 | tf_op jit(solution)/shard_map/ppermute | solution.py:655
  28.2 2.7 %collective-permute-start.11 = (f32[104,128]{1,0:T(8,128)S(1)}, f32[104,128]{1,0:T(8,128)S(1)}, u32[]{:S(2)}, u32[]{:S(2)}) collective-permute-start(f32[104,128]{1,0:T(8,128)S(1)} %get-tuple-element.123.refs_18_), channel_id=1, source_target_pairs={{4,0},{8,4},{12,8},{0,12},{5,1},{9,5},{13,9},{1,13},{6,2},{10,6},{... | collective-permute-start | bytes 159752 | tf_op jit(solution)/shard_map/ppermute | solution.py:656
  30.9 2.3 %collective-permute-done.10.refs_13_.refs_7_ = f32[104,128]{1,0:T(8,128)S(1)} collective-permute-done((f32[104,128]{1,0:T(8,128)S(1)}, f32[104,128]{1,0:T(8,128)S(1)}, u32[]{:S(2)}, u32[]{:S(2)}) %collective-permute-start.10) | collective-permute-done | bytes 53280 | tf_op jit(solution)/shard_map/ppermute | solution.py:655
  33.2 0.3 collective-permute-done.11.refs_14_.refs_8_
  33.5 0.4 shard_map.79
  33.9 0.1 collective-permute-start.12
  34.0 1.7 %collective-permute-start.13 = (f32[56,128]{1,0:T(8,128)S(1)}, f32[56,128]{1,0:T(8,128)S(1)}, u32[]{:S(2)}, u32[]{:S(2)}) collective-permute-start(f32[56,128]{1,0:T(8,128)S(1)} %get-tuple-element.133), channel_id=1, source_target_pairs={{0,3},{1,2},{2,1},{3,0},{4,7},{5,6},{6,5},{7,4},{8,11},{9,10},{10,... | collective-permute-start | bytes 86024 | tf_op jit(solution)/shard_map/ppermute | solution.py:666
  35.7 0.9 %shard_map.80 = (f32[19,14,8,128]{3,2,1,0:T(8,128)S(1)}, f32[104,128]{1,0:T(8,128)S(1)}, f32[104,128]{1,0:T(8,128)S(1)}, f32[14,8,128]{2,1,0:T(8,128)S(1)}) custom-call(f32[19,8,128]{2,1,0:T(8,128)S(1)} %get-tuple-element.81.refs_0_, s32[16,8,128]{2,1,0:T(8,128)S(1)} %shard_map.72.refs_1_.bits_ref, f32[18,24,128]{2,1,0:T(8,128)S(1)} %get-tuple-element.125.refs_2_, ...), custom_call_target="tpu_custom_call" | custom-call | flops 6553600 | bytes 1310720 | tf_op jit(solution)/shard_map/pallas_call | solution.py:637
  36.6 0.0 collective-permute-done.12.refs_2_
  36.6 0.7 %collective-permute-done.13.refs_3_ = f32[56,128]{1,0:T(8,128)S(1)} collective-permute-done((f32[56,128]{1,0:T(8,128)S(1)}, f32[56,128]{1,0:T(8,128)S(1)}, u32[]{:S(2)}, u32[]{:S(2)}) %collective-permute-start.13) | collective-permute-done | bytes 28704 | tf_op jit(solution)/shard_map/ppermute | solution.py:666
  37.4 1.1 %collective-permute-start.14 = (f32[104,128]{1,0:T(8,128)S(1)}, f32[104,128]{1,0:T(8,128)S(1)}, u32[]{:S(2)}, u32[]{:S(2)}) collective-permute-start(f32[104,128]{1,0:T(8,128)S(1)} %get-tuple-element.138.refs_17_), channel_id=1, source_target_pairs={{0,4},{4,8},{8,12},{12,0},{1,5},{5,9},{9,13},{13,1},{2,6},{6,10},{... | collective-permute-start | bytes 159752 | tf_op jit(solution)/shard_map/ppermute | solution.py:655
  38.5 2.7 %collective-permute-start.15 = (f32[104,128]{1,0:T(8,128)S(1)}, f32[104,128]{1,0:T(8,128)S(1)}, u32[]{:S(2)}, u32[]{:S(2)}) collective-permute-start(f32[104,128]{1,0:T(8,128)S(1)} %get-tuple-element.139.refs_18_), channel_id=1, source_target_pairs={{4,0},{8,4},{12,8},{0,12},{5,1},{9,5},{13,9},{1,13},{6,2},{10,6},{... | collective-permute-start | bytes 159752 | tf_op jit(solution)/shard_map/ppermute | solution.py:656
  41.2 2.2 %collective-permute-done.14.refs_13_.refs_7_ = f32[104,128]{1,0:T(8,128)S(1)} collective-permute-done((f32[104,128]{1,0:T(8,128)S(1)}, f32[104,128]{1,0:T(8,128)S(1)}, u32[]{:S(2)}, u32[]{:S(2)}) %collective-permute-start.14) | collective-permute-done | bytes 53280 | tf_op jit(solution)/shard_map/ppermute | solution.py:655
  43.5 0.3 collective-permute-done.15.refs_14_.refs_8_
  43.8 0.4 shard_map.82
  44.2 0.1 collective-permute-start.16
  44.2 1.7 %collective-permute-start.17 = (f32[48,128]{1,0:T(8,128)S(1)}, f32[48,128]{1,0:T(8,128)S(1)}, u32[]{:S(2)}, u32[]{:S(2)}) collective-permute-start(f32[48,128]{1,0:T(8,128)S(1)} %get-tuple-element.148), channel_id=1, source_target_pairs={{0,3},{1,2},{2,1},{3,0},{4,7},{5,6},{6,5},{7,4},{8,11},{9,10},{10,... | collective-permute-start | bytes 73736 | tf_op jit(solution)/shard_map/ppermute | solution.py:666
  45.9 0.9 %shard_map.83 = (f32[19,14,8,128]{3,2,1,0:T(8,128)S(1)}, f32[80,128]{1,0:T(8,128)S(1)}, f32[80,128]{1,0:T(8,128)S(1)}, f32[3,128,128]{2,1,0:T(8,128)S(1)}) custom-call(f32[19,8,128]{2,1,0:T(8,128)S(1)} %get-tuple-element.81.refs_0_, s32[16,8,128]{2,1,0:T(8,128)S(1)} %shard_map.72.refs_1_.bits_ref, f32[18,24,128]{2,1,0:T(8,128)S(1)} %get-tuple-element.141.refs_2_, ...), custom_call_target="tpu_custom_call" | custom-call | flops 6553600 | bytes 1310720 | tf_op jit(solution)/shard_map/pallas_call | solution.py:637
  46.9 0.0 collective-permute-done.16.refs_2_
  46.9 0.7 %collective-permute-done.17.refs_3_ = f32[48,128]{1,0:T(8,128)S(1)} collective-permute-done((f32[48,128]{1,0:T(8,128)S(1)}, f32[48,128]{1,0:T(8,128)S(1)}, u32[]{:S(2)}, u32[]{:S(2)}) %collective-permute-start.17) | collective-permute-done | bytes 24608 | tf_op jit(solution)/shard_map/ppermute | solution.py:666
  47.6 1.4 %collective-permute-start.18 = (f32[80,128]{1,0:T(8,128)S(1)}, f32[80,128]{1,0:T(8,128)S(1)}, u32[]{:S(2)}, u32[]{:S(2)}) collective-permute-start(f32[80,128]{1,0:T(8,128)S(1)} %get-tuple-element.157), channel_id=1, source_target_pairs={{0,4},{4,8},{8,12},{12,0},{1,5},{5,9},{9,13},{13,1},{2,6},{6,10},{... | collective-permute-start | bytes 122888 | tf_op jit(solution)/shard_map/ppermute | solution.py:655
  48.9 2.5 %collective-permute-start.19 = (f32[80,128]{1,0:T(8,128)S(1)}, f32[80,128]{1,0:T(8,128)S(1)}, u32[]{:S(2)}, u32[]{:S(2)}) collective-permute-start(f32[80,128]{1,0:T(8,128)S(1)} %get-tuple-element.158), channel_id=1, source_target_pairs={{4,0},{8,4},{12,8},{0,12},{5,1},{9,5},{13,9},{1,13},{6,2},{10,6},{... | collective-permute-start | bytes 122888 | tf_op jit(solution)/shard_map/ppermute | solution.py:656
  51.5 1.3 %shard_map.85 = (f32[19,128,128]{2,1,0:T(8,128)}, f32[19,128,128]{2,1,0:T(8,128)S(1)}, f32[3,128,128]{2,1,0:T(8,128)}) custom-call(f32[19,2,8,128]{3,2,1,0:T(8,128)S(1)} %get-tuple-element.140.f_edge, f32[19,14,8,128]{3,2,1,0:T(8,128)S(1)} %get-tuple-element.144.f_middle, s32[16,8,128]{2,1,0:T(8,128)S(1)} %shard_map.72.refs_1_.bits_ref, ...), custom_call_target="tpu_custom_call" | custom-call | flops 6553600 | bytes 1310720 | tf_op jit(solution)/shard_map/pallas_call | solution.py:637
  52.7 0.7 %collective-permute-done.18.yd = f32[80,128]{1,0:T(8,128)S(1)} collective-permute-done((f32[80,128]{1,0:T(8,128)S(1)}, f32[80,128]{1,0:T(8,128)S(1)}, u32[]{:S(2)}, u32[]{:S(2)}) %collective-permute-start.18) | collective-permute-done | bytes 40992 | tf_op jit(solution)/shard_map/ppermute | solution.py:655
  53.4 0.3 collective-permute-done.19.yu
  53.8 0.7 %shard_map.86 = f32[19,128,128]{2,1,0:T(8,128)} custom-call(f32[19,128,128]{2,1,0:T(8,128)} %get-tuple-element.154.out_in, f32[19,128,128]{2,1,0:T(8,128)S(1)} %get-tuple-element.155.flat_ref, f32[2,128,128]{2,1,0:T(8,128)S(1)} %get-tuple-element.156.mask_ref, f32[80,128]{1,0:T(8,128)S(1)} %collective-permute-done.18.yd, ...), custom_call_target="tpu_custom_call", output_to_operand_aliasing={{}: (0, {})} | custom-call | tf_op jit(solution)/shard_map/pallas_call | solution.py:637
  (5 shorter events, 0.1 us)
Async XLA Ops:
  0.6 10.0 %copy-start.3 = (f32[4]{0:T(128)S(1)}, f32[4]{0:T(128)}, u32[]{:S(2)}) copy-start(f32[4]{0:T(128)} %wall_hbm.1) | copy-start | bytes 52
  0.6 10.0 %copy-start.2 = (s32[8,16,128]{2,1,0:T(8,128)S(1)}, s32[8,16,128]{2,1,0:T(8,128)}, u32[]{:S(2)}) copy-start(s32[8,16,128]{2,1,0:T(8,128)} %param.7) | copy-start | bytes 196612
  0.7 10.0 %copy-start.1 = (s32[8,16,128]{2,1,0:T(8,128)S(1)}, s32[8,16,128]{2,1,0:T(8,128)}, u32[]{:S(2)}) copy-start(s32[8,16,128]{2,1,0:T(8,128)} %param.6) | copy-start | bytes 196612
  0.7 10.0 %copy-start = (f32[19,8,16,128]{3,2,1,0:T(8,128)S(1)}, f32[19,8,16,128]{3,2,1,0:T(8,128)}, u32[]{:S(2)}) copy-start(f32[19,8,16,128]{3,2,1,0:T(8,128)} %param.5) | copy-start | bytes 3735556
  0.7 10.0 %copy-start.4 = (f32[19]{0:T(128)S(1)}, f32[19]{0:T(128)}, u32[]{:S(2)}) copy-start(f32[19]{0:T(128)} %rate_ref.1) | copy-start | bytes 232
  2.2 3.2 %collective-permute-start = (f32[16,128]{1,0:T(8,128)S(1)}, f32[16,128]{1,0:T(8,128)S(1)}, u32[]{:S(2)}, u32[]{:S(2)}) collective-permute-start(f32[16,128]{1,0:T(8,128)S(1)} %get-tuple-element.84), channel_id=1, source_target_pairs={{0,1},{1,0},{2,3},{3,2},{4,5},{5,4},{6,7},{7,6},{8,9},{9,8},{10,11... | collective-permute-start | bytes 24584 | tf_op jit(solution)/shard_map/ppermute | solution.py:667
  2.8 4.0 %collective-permute-start.1 = (f32[16,128]{1,0:T(8,128)S(1)}, f32[16,128]{1,0:T(8,128)S(1)}, u32[]{:S(2)}, u32[]{:S(2)}) collective-permute-start(f32[16,128]{1,0:T(8,128)S(1)} %get-tuple-element.85), channel_id=1, source_target_pairs={{0,3},{1,2},{2,1},{3,0},{4,7},{5,6},{6,5},{7,4},{8,11},{9,10},{10,... | collective-permute-start | bytes 24584 | tf_op jit(solution)/shard_map/ppermute | solution.py:666
  6.7 5.7 %collective-permute-start.2 = (f32[40,128]{1,0:T(8,128)S(1)}, f32[40,128]{1,0:T(8,128)S(1)}, u32[]{:S(2)}, u32[]{:S(2)}) collective-permute-start(f32[40,128]{1,0:T(8,128)S(1)} %get-tuple-element.88), channel_id=1, source_target_pairs={{0,4},{4,8},{8,12},{12,0},{1,5},{5,9},{9,13},{13,1},{2,6},{6,10},{... | collective-permute-start | bytes 61448 | tf_op jit(solution)/shard_map/ppermute | solution.py:655
  8.5 4.0 %collective-permute-start.3 = (f32[40,128]{1,0:T(8,128)S(1)}, f32[40,128]{1,0:T(8,128)S(1)}, u32[]{:S(2)}, u32[]{:S(2)}) collective-permute-start(f32[40,128]{1,0:T(8,128)S(1)} %get-tuple-element.89), channel_id=1, source_target_pairs={{4,0},{8,4},{12,8},{0,12},{5,1},{9,5},{13,9},{1,13},{6,2},{10,6},{... | collective-permute-start | bytes 61448 | tf_op jit(solution)/shard_map/ppermute | solution.py:656
  13.0 2.6 %collective-permute-start.4 = (f32[56,128]{1,0:T(8,128)S(1)}, f32[56,128]{1,0:T(8,128)S(1)}, u32[]{:S(2)}, u32[]{:S(2)}) collective-permute-start(f32[56,128]{1,0:T(8,128)S(1)} %get-tuple-element.100), channel_id=1, source_target_pairs={{0,1},{1,0},{2,3},{3,2},{4,5},{5,4},{6,7},{7,6},{8,9},{9,8},{10,11... | collective-permute-start | bytes 86024 | tf_op jit(solution)/shard_map/ppermute | solution.py:667
  13.0 3.4 %collective-permute-start.5 = (f32[56,128]{1,0:T(8,128)S(1)}, f32[56,128]{1,0:T(8,128)S(1)}, u32[]{:S(2)}, u32[]{:S(2)}) collective-permute-start(f32[56,128]{1,0:T(8,128)S(1)} %get-tuple-element.101), channel_id=1, source_target_pairs={{0,3},{1,2},{2,1},{3,0},{4,7},{5,6},{6,5},{7,4},{8,11},{9,10},{10,... | collective-permute-start | bytes 86024 | tf_op jit(solution)/shard_map/ppermute | solution.py:666
  16.4 6.3 %collective-permute-start.6 = (f32[104,128]{1,0:T(8,128)S(1)}, f32[104,128]{1,0:T(8,128)S(1)}, u32[]{:S(2)}, u32[]{:S(2)}) collective-permute-start(f32[104,128]{1,0:T(8,128)S(1)} %get-tuple-element.106.refs_17_), channel_id=1, source_target_pairs={{0,4},{4,8},{8,12},{12,0},{1,5},{5,9},{9,13},{13,1},{2,6},{6,10},{... | collective-permute-start | bytes 159752 | tf_op jit(solution)/shard_map/ppermute | solution.py:655
  17.9 5.3 %collective-permute-start.7 = (f32[104,128]{1,0:T(8,128)S(1)}, f32[104,128]{1,0:T(8,128)S(1)}, u32[]{:S(2)}, u32[]{:S(2)}) collective-permute-start(f32[104,128]{1,0:T(8,128)S(1)} %get-tuple-element.107.refs_18_), channel_id=1, source_target_pairs={{4,0},{8,4},{12,8},{0,12},{5,1},{9,5},{13,9},{1,13},{6,2},{10,6},{... | collective-permute-start | bytes 159752 | tf_op jit(solution)/shard_map/ppermute | solution.py:656
  23.5 2.6 %collective-permute-start.8 = (f32[56,128]{1,0:T(8,128)S(1)}, f32[56,128]{1,0:T(8,128)S(1)}, u32[]{:S(2)}, u32[]{:S(2)}) collective-permute-start(f32[56,128]{1,0:T(8,128)S(1)} %get-tuple-element.116), channel_id=1, source_target_pairs={{0,1},{1,0},{2,3},{3,2},{4,5},{5,4},{6,7},{7,6},{8,9},{9,8},{10,11... | collective-permute-start | bytes 86024 | tf_op jit(solution)/shard_map/ppermute | solution.py:667
  23.6 3.4 %collective-permute-start.9 = (f32[56,128]{1,0:T(8,128)S(1)}, f32[56,128]{1,0:T(8,128)S(1)}, u32[]{:S(2)}, u32[]{:S(2)}) collective-permute-start(f32[56,128]{1,0:T(8,128)S(1)} %get-tuple-element.117), channel_id=1, source_target_pairs={{0,3},{1,2},{2,1},{3,0},{4,7},{5,6},{6,5},{7,4},{8,11},{9,10},{10,... | collective-permute-start | bytes 86024 | tf_op jit(solution)/shard_map/ppermute | solution.py:666
  27.0 6.2 %collective-permute-start.10 = (f32[104,128]{1,0:T(8,128)S(1)}, f32[104,128]{1,0:T(8,128)S(1)}, u32[]{:S(2)}, u32[]{:S(2)}) collective-permute-start(f32[104,128]{1,0:T(8,128)S(1)} %get-tuple-element.122.refs_17_), channel_id=1, source_target_pairs={{0,4},{4,8},{8,12},{12,0},{1,5},{5,9},{9,13},{13,1},{2,6},{6,10},{... | collective-permute-start | bytes 159752 | tf_op jit(solution)/shard_map/ppermute | solution.py:655
  28.2 5.3 %collective-permute-start.11 = (f32[104,128]{1,0:T(8,128)S(1)}, f32[104,128]{1,0:T(8,128)S(1)}, u32[]{:S(2)}, u32[]{:S(2)}) collective-permute-start(f32[104,128]{1,0:T(8,128)S(1)} %get-tuple-element.123.refs_18_), channel_id=1, source_target_pairs={{4,0},{8,4},{12,8},{0,12},{5,1},{9,5},{13,9},{1,13},{6,2},{10,6},{... | collective-permute-start | bytes 159752 | tf_op jit(solution)/shard_map/ppermute | solution.py:656
  33.9 2.7 %collective-permute-start.12 = (f32[56,128]{1,0:T(8,128)S(1)}, f32[56,128]{1,0:T(8,128)S(1)}, u32[]{:S(2)}, u32[]{:S(2)}) collective-permute-start(f32[56,128]{1,0:T(8,128)S(1)} %get-tuple-element.132), channel_id=1, source_target_pairs={{0,1},{1,0},{2,3},{3,2},{4,5},{5,4},{6,7},{7,6},{8,9},{9,8},{10,11... | collective-permute-start | bytes 86024 | tf_op jit(solution)/shard_map/ppermute | solution.py:667
  34.0 3.4 %collective-permute-start.13 = (f32[56,128]{1,0:T(8,128)S(1)}, f32[56,128]{1,0:T(8,128)S(1)}, u32[]{:S(2)}, u32[]{:S(2)}) collective-permute-start(f32[56,128]{1,0:T(8,128)S(1)} %get-tuple-element.133), channel_id=1, source_target_pairs={{0,3},{1,2},{2,1},{3,0},{4,7},{5,6},{6,5},{7,4},{8,11},{9,10},{10,... | collective-permute-start | bytes 86024 | tf_op jit(solution)/shard_map/ppermute | solution.py:666
  37.4 6.1 %collective-permute-start.14 = (f32[104,128]{1,0:T(8,128)S(1)}, f32[104,128]{1,0:T(8,128)S(1)}, u32[]{:S(2)}, u32[]{:S(2)}) collective-permute-start(f32[104,128]{1,0:T(8,128)S(1)} %get-tuple-element.138.refs_17_), channel_id=1, source_target_pairs={{0,4},{4,8},{8,12},{12,0},{1,5},{5,9},{9,13},{13,1},{2,6},{6,10},{... | collective-permute-start | bytes 159752 | tf_op jit(solution)/shard_map/ppermute | solution.py:655
  38.5 5.3 %collective-permute-start.15 = (f32[104,128]{1,0:T(8,128)S(1)}, f32[104,128]{1,0:T(8,128)S(1)}, u32[]{:S(2)}, u32[]{:S(2)}) collective-permute-start(f32[104,128]{1,0:T(8,128)S(1)} %get-tuple-element.139.refs_18_), channel_id=1, source_target_pairs={{4,0},{8,4},{12,8},{0,12},{5,1},{9,5},{13,9},{1,13},{6,2},{10,6},{... | collective-permute-start | bytes 159752 | tf_op jit(solution)/shard_map/ppermute | solution.py:656
  44.2 2.7 %collective-permute-start.16 = (f32[48,128]{1,0:T(8,128)S(1)}, f32[48,128]{1,0:T(8,128)S(1)}, u32[]{:S(2)}, u32[]{:S(2)}) collective-permute-start(f32[48,128]{1,0:T(8,128)S(1)} %get-tuple-element.147), channel_id=1, source_target_pairs={{0,1},{1,0},{2,3},{3,2},{4,5},{5,4},{6,7},{7,6},{8,9},{9,8},{10,11... | collective-permute-start | bytes 73736 | tf_op jit(solution)/shard_map/ppermute | solution.py:667
  44.2 3.3 %collective-permute-start.17 = (f32[48,128]{1,0:T(8,128)S(1)}, f32[48,128]{1,0:T(8,128)S(1)}, u32[]{:S(2)}, u32[]{:S(2)}) collective-permute-start(f32[48,128]{1,0:T(8,128)S(1)} %get-tuple-element.148), channel_id=1, source_target_pairs={{0,3},{1,2},{2,1},{3,0},{4,7},{5,6},{6,5},{7,4},{8,11},{9,10},{10,... | collective-permute-start | bytes 73736 | tf_op jit(solution)/shard_map/ppermute | solution.py:666
  47.6 5.9 %collective-permute-start.18 = (f32[80,128]{1,0:T(8,128)S(1)}, f32[80,128]{1,0:T(8,128)S(1)}, u32[]{:S(2)}, u32[]{:S(2)}) collective-permute-start(f32[80,128]{1,0:T(8,128)S(1)} %get-tuple-element.157), channel_id=1, source_target_pairs={{0,4},{4,8},{8,12},{12,0},{1,5},{5,9},{9,13},{13,1},{2,6},{6,10},{... | collective-permute-start | bytes 122888 | tf_op jit(solution)/shard_map/ppermute | solution.py:655
  48.9 4.8 %collective-permute-start.19 = (f32[80,128]{1,0:T(8,128)S(1)}, f32[80,128]{1,0:T(8,128)S(1)}, u32[]{:S(2)}, u32[]{:S(2)}) collective-permute-start(f32[80,128]{1,0:T(8,128)S(1)} %get-tuple-element.158), channel_id=1, source_target_pairs={{4,0},{8,4},{12,8},{0,12},{5,1},{9,5},{13,9},{1,13},{6,2},{10,6},{... | collective-permute-start | bytes 122888 | tf_op jit(solution)/shard_map/ppermute | solution.py:656

commit v8 on v7

--- a/solution.py
+++ b/solution.py
@@ -201,6 +201,17 @@
         rows_ref[s, layers:] = jnp.where(pore, 1.0, 0.0)
 
 
+def load_kernel(f_hbm, mask_hbm, wet_hbm, after_ref, f_ref, mask_ref, wet_ref, f_sems, sems):
+    del after_ref
+    copies = [pltpu.make_async_copy(f_hbm.at[k], f_ref.at[k], f_sems.at[k]) for k in range(N)]
+    copies.append(pltpu.make_async_copy(mask_hbm, mask_ref, sems.at[0]))
+    copies.append(pltpu.make_async_copy(wet_hbm, wet_ref, sems.at[1]))
+    for copy in copies:
+        copy.start()
+    for copy in copies:
+        copy.wait()
+
+
 def turn_kernel(raw_ref, mask_in, wet_in, wall_ref, rate_ref, f_ref, rates_ref, flat_ref, mask_ref, pot_ref):
     layers, rows = f_ref.shape[1], f_ref.shape[2]
     for k in range(N):
@@ -688,11 +699,12 @@
         wet_class.reshape(cells, size_z),
         wall_potential,
     )
+    operands = [pltpu.with_memory_space_constraint(item, pltpu.HBM) for item in operands]
     start_rows = rows(2 * size_x + TILE)
     a, b, row_faces = call(
         functools.partial(face_kernel, pairs),
         [rows(2 * size_y), rows(2 * size_y), ((2, 2 * size_x, size_z), f32)],
-        [pltpu.with_memory_space_constraint(item, pltpu.HBM) for item in operands],
+        operands,
         special={i: HBM for i in range(4)},
         scratch=[
             (2, N, size_y, size_z),
@@ -705,6 +717,14 @@
             pltpu.SemaphoreType.DMA((3,)),
         ],
     )
+    tile = call(
+        load_kernel,
+        [flat(N), ((cells, size_z), i32), ((cells, size_z), i32)],
+        (*operands[:3], a),
+        special={i: HBM for i in range(3)},
+        scratch=[pltpu.SemaphoreType.DMA((N,)), pltpu.SemaphoreType.DMA((2,))],
+        cost=cost,
+    )
     a, b = exchange(a, b, "gy")
     up, down, x0l, x0r = call(
         functools.partial(start_pack_kernel, pairs),
@@ -714,7 +734,7 @@
     f, rates, flat_mask, mask, pot0 = call(
         turn_kernel,
         [fields(size_x), ((N, TILE, size_z), f32), flat(2), whole, whole],
-        (*operands, relax_rates),
+        (*tile, wall_potential, relax_rates),
         special={3: SMEM, 4: SMEM},
         cost=cost,
     )

time: 54.7 us -> 55.2 us (level)
  waiting for transfers between devices: 14 us -> 12.2 us
  Pallas kernels: 10.1 us -> 11.5 us
  starting transfers between devices: 29.6 us -> 30.5 us
    pallas_call x19 -> x20, Pallas kernels: 10.1 us -> 11.5 us  [call(): pl.pallas_call(kernel, out_shape=[jax.ShapeDtypeStruct(shape, dtype) for...]
    ppermute x5, starting transfers between devices: 12.5 us -> 13.6 us  [shift(): lax.ppermute(backward, axis, [(b, a) for a, b in ahead])]
    ppermute x5, waiting for transfers between devices: 4.41 us -> 3.34 us  [swap(): b = lax.ppermute(b, axis, partners[1])]
    ppermute x5, waiting for transfers between devices: 1.44 us -> 0.69 us  [shift(): lax.ppermute(backward, axis, [(b, a) for a, b in ahead])]
    ppermute x5, starting transfers between devices: 6.94 us -> 6.27 us  [shift(): lax.ppermute(forward, axis, ahead)]
  transfers between devices with their start and end apart: 20 -> 20, of which waited for: 15 -> 12; matrix products, arithmetic and copies ran while one was open for 0% -> 0% of each run, Pallas kernels for 11% -> 14%
where the time goes in v8:
time: 55.2 us; the launch traced here: 55 us
  starting transfers between devices  30.5 us (55%)
  waiting for transfers between devices  12.2 us (22%)
  Pallas kernels  11.5 us (21%)
  between operations  0.84 us (2%)
    ppermute x5, starting transfers between devices, shift(): lax.ppermute(backward, axis, [(b, a) for a, b in ahead])  13.6 us
    pallas_call x20, Pallas kernels, call(): pl.pallas_call(kernel, out_shape=[jax.ShapeDtypeStruct(shape, dtype) for...  11.5 us
    ppermute x5, starting transfers between devices, swap(): b = lax.ppermute(b, axis, partners[1])  9.6 us
    ppermute x5, waiting for transfers between devices, shift(): lax.ppermute(forward, axis, ahead)  7.98 us
    ppermute x5, starting transfers between devices, shift(): lax.ppermute(forward, axis, ahead)  6.27 us
    ppermute x5, waiting for transfers between devices, swap(): b = lax.ppermute(b, axis, partners[1])  3.34 us
  transfers between devices with their start and end apart: 20, of which 12 were waited for; matrix products, arithmetic and copies ran while one was open for 0% of the time, Pallas kernels for 14%

profile of v8, /device:TPU:0, one launch (start us, length us, event | category | flops | bytes accessed | tf_op | source)
XLA Modules:
  0.0 55.0 jit_solution(12262519035003879532)
XLA Ops:
  0.6 0.0 copy-start
  0.6 0.0 copy-start.1
  0.6 1.5 %shard_map.68 = (f32[16,128]{1,0:T(8,128)S(1)}, f32[16,128]{1,0:T(8,128)S(1)}, f32[2,32,128]{2,1,0:T(8,128)S(1)}) custom-call(f32[19,128,128]{2,1,0:T(8,128)} %bitcast.5, s32[128,128]{1,0:T(8,128)} %bitcast.8, s32[128,128]{1,0:T(8,128)} %bitcast.10, f32[4]{0:T(128)} %wall_ref.1), custom_call_target="tpu_custom_call" | custom-call | tf_op jit(solution)/shard_map/pallas_call | solution.py:648
  2.1 2.5 %collective-permute-start.1 = (f32[16,128]{1,0:T(8,128)S(1)}, f32[16,128]{1,0:T(8,128)S(1)}, u32[]{:S(2)}, u32[]{:S(2)}) collective-permute-start(f32[16,128]{1,0:T(8,128)S(1)} %get-tuple-element.91), channel_id=1, source_target_pairs={{0,3},{1,2},{2,1},{3,0},{4,7},{5,6},{6,5},{7,4},{8,11},{9,10},{10,... | collective-permute-start | bytes 24584 | tf_op jit(solution)/shard_map/ppermute | solution.py:677
  4.6 0.7 %collective-permute-start = (f32[16,128]{1,0:T(8,128)S(1)}, f32[16,128]{1,0:T(8,128)S(1)}, u32[]{:S(2)}, u32[]{:S(2)}) collective-permute-start(f32[16,128]{1,0:T(8,128)S(1)} %get-tuple-element.84.after_ref), channel_id=1, source_target_pairs={{0,1},{1,0},{2,3},{3,2},{4,5},{5,4},{6,7},{7,6},{8,9},{9,8},{10,11... | collective-permute-start | bytes 24584 | tf_op jit(solution)/shard_map/ppermute | solution.py:678
  5.3 0.7 %collective-permute-done.1.b_ref = f32[16,128]{1,0:T(8,128)S(1)} collective-permute-done((f32[16,128]{1,0:T(8,128)S(1)}, f32[16,128]{1,0:T(8,128)S(1)}, u32[]{:S(2)}, u32[]{:S(2)}) %collective-permute-start.1) | collective-permute-done | bytes 8224 | tf_op jit(solution)/shard_map/ppermute | solution.py:677
  6.0 0.1 collective-permute-done.a_ref
  6.1 2.3 %collective-permute-start.2 = (f32[40,128]{1,0:T(8,128)S(1)}, f32[40,128]{1,0:T(8,128)S(1)}, u32[]{:S(2)}, u32[]{:S(2)}) collective-permute-start(f32[40,128]{1,0:T(8,128)S(1)} %get-tuple-element.94), channel_id=1, source_target_pairs={{0,4},{4,8},{8,12},{12,0},{1,5},{5,9},{9,13},{13,1},{2,6},{6,10},{... | collective-permute-start | bytes 61448 | tf_op jit(solution)/shard_map/ppermute | solution.py:666
  8.4 2.1 %collective-permute-start.3 = (f32[40,128]{1,0:T(8,128)S(1)}, f32[40,128]{1,0:T(8,128)S(1)}, u32[]{:S(2)}, u32[]{:S(2)}) collective-permute-start(f32[40,128]{1,0:T(8,128)S(1)} %get-tuple-element.95), channel_id=1, source_target_pairs={{4,0},{8,4},{12,8},{0,12},{5,1},{9,5},{13,9},{1,13},{6,2},{10,6},{... | collective-permute-start | bytes 61448 | tf_op jit(solution)/shard_map/ppermute | solution.py:667
  10.5 1.5 %shard_map.69 = (f32[19,128,128]{2,1,0:T(8,128)S(1)}, s32[128,128]{1,0:T(8,128)S(1)}, s32[128,128]{1,0:T(8,128)S(1)}) custom-call(f32[19,128,128]{2,1,0:T(8,128)} %bitcast.6, s32[128,128]{1,0:T(8,128)} %bitcast.9, s32[128,128]{1,0:T(8,128)} %bitcast.11, f32[16,128]{1,0:T(8,128)S(1)} %get-tuple-element.84.after_ref), custom_call_target="tpu_custom_call" | custom-call | flops 6553600 | bytes 1310720 | tf_op jit(solution)/shard_map/pallas_call | solution.py:648
  12.0 0.0 copy-done
  12.0 0.0 copy-done.1
  12.1 1.1 %shard_map.70 = (f32[19,16,8,128]{3,2,1,0:T(8,128)S(1)}, f32[19,8,128]{2,1,0:T(8,128)S(1)}, f32[2,128,128]{2,1,0:T(8,128)S(1)}, f32[16,8,128]{2,1,0:T(8,128)S(1)}, f32[16,8,128]{2,1,0:T(8,128)S(1)}) custom-call(f32[19,128,128]{2,1,0:T(8,128)S(1)} %get-tuple-element.85.raw_ref, s32[128,128]{1,0:T(8,128)S(1)} %get-tuple-element.86.mask_in, ...), custom_call_target="tpu_custom_call" | custom-call | flops 6553600 | bytes 1310720 | tf_op jit(solution)/shard_map/pallas_call | solution.py:648
  13.1 0.2 shard_map.72.bits_in
  13.4 0.0 collective-permute-done.2.y0d.refs_5_
  13.4 0.0 collective-permute-done.3.y0u.refs_6_
  13.4 0.1 shard_map.73.refs_1_.bits_ref
  13.5 0.3 shard_map.74
  13.8 0.1 collective-permute-start.4
  13.9 1.8 %collective-permute-start.5 = (f32[56,128]{1,0:T(8,128)S(1)}, f32[56,128]{1,0:T(8,128)S(1)}, u32[]{:S(2)}, u32[]{:S(2)}) collective-permute-start(f32[56,128]{1,0:T(8,128)S(1)} %get-tuple-element.107), channel_id=1, source_target_pairs={{0,3},{1,2},{2,1},{3,0},{4,7},{5,6},{6,5},{7,4},{8,11},{9,10},{10,... | collective-permute-start | bytes 86024 | tf_op jit(solution)/shard_map/ppermute | solution.py:677
  15.7 0.8 %shard_map.75 = (f32[19,14,8,128]{3,2,1,0:T(8,128)S(1)}, f32[104,128]{1,0:T(8,128)S(1)}, f32[104,128]{1,0:T(8,128)S(1)}, f32[14,8,128]{2,1,0:T(8,128)S(1)}) custom-call(f32[19,8,128]{2,1,0:T(8,128)S(1)} %get-tuple-element.88.refs_0_, s32[16,8,128]{2,1,0:T(8,128)S(1)} %shard_map.73.refs_1_.bits_ref, f32[18,24,128]{2,1,0:T(8,128)S(1)} %get-tuple-element.99.refs_2_, ...), custom_call_target="tpu_custom_call" | custom-call | flops 6553600 | bytes 1310720 | tf_op jit(solution)/shard_map/pallas_call | solution.py:648
  16.5 0.0 collective-permute-done.4.refs_2_
  16.5 0.7 %collective-permute-done.5.refs_3_ = f32[56,128]{1,0:T(8,128)S(1)} collective-permute-done((f32[56,128]{1,0:T(8,128)S(1)}, f32[56,128]{1,0:T(8,128)S(1)}, u32[]{:S(2)}, u32[]{:S(2)}) %collective-permute-start.5) | collective-permute-done | bytes 28704 | tf_op jit(solution)/shard_map/ppermute | solution.py:677
  17.3 0.4 collective-permute-start.6
  17.7 3.4 %collective-permute-start.7 = (f32[104,128]{1,0:T(8,128)S(1)}, f32[104,128]{1,0:T(8,128)S(1)}, u32[]{:S(2)}, u32[]{:S(2)}) collective-permute-start(f32[104,128]{1,0:T(8,128)S(1)} %get-tuple-element.113.refs_18_), channel_id=1, source_target_pairs={{4,0},{8,4},{12,8},{0,12},{5,1},{9,5},{13,9},{1,13},{6,2},{10,6},{... | collective-permute-start | bytes 159752 | tf_op jit(solution)/shard_map/ppermute | solution.py:667
  21.2 2.7 %collective-permute-done.6.refs_13_.refs_7_ = f32[104,128]{1,0:T(8,128)S(1)} collective-permute-done((f32[104,128]{1,0:T(8,128)S(1)}, f32[104,128]{1,0:T(8,128)S(1)}, u32[]{:S(2)}, u32[]{:S(2)}) %collective-permute-start.6) | collective-permute-done | bytes 53280 | tf_op jit(solution)/shard_map/ppermute | solution.py:666
  23.8 0.0 collective-permute-done.7.refs_14_.refs_8_
  23.8 0.4 shard_map.77
  24.2 0.1 collective-permute-start.8
  24.3 1.8 %collective-permute-start.9 = (f32[56,128]{1,0:T(8,128)S(1)}, f32[56,128]{1,0:T(8,128)S(1)}, u32[]{:S(2)}, u32[]{:S(2)}) collective-permute-start(f32[56,128]{1,0:T(8,128)S(1)} %get-tuple-element.123), channel_id=1, source_target_pairs={{0,3},{1,2},{2,1},{3,0},{4,7},{5,6},{6,5},{7,4},{8,11},{9,10},{10,... | collective-permute-start | bytes 86024 | tf_op jit(solution)/shard_map/ppermute | solution.py:677
  26.1 0.9 %shard_map.78 = (f32[19,14,8,128]{3,2,1,0:T(8,128)S(1)}, f32[104,128]{1,0:T(8,128)S(1)}, f32[104,128]{1,0:T(8,128)S(1)}, f32[14,8,128]{2,1,0:T(8,128)S(1)}) custom-call(f32[19,8,128]{2,1,0:T(8,128)S(1)} %get-tuple-element.88.refs_0_, s32[16,8,128]{2,1,0:T(8,128)S(1)} %shard_map.73.refs_1_.bits_ref, f32[18,24,128]{2,1,0:T(8,128)S(1)} %get-tuple-element.115.refs_2_, ...), custom_call_target="tpu_custom_call" | custom-call | flops 6553600 | bytes 1310720 | tf_op jit(solution)/shard_map/pallas_call | solution.py:648
  27.0 0.0 collective-permute-done.8.refs_2_
  27.0 0.7 %collective-permute-done.9.refs_3_ = f32[56,128]{1,0:T(8,128)S(1)} collective-permute-done((f32[56,128]{1,0:T(8,128)S(1)}, f32[56,128]{1,0:T(8,128)S(1)}, u32[]{:S(2)}, u32[]{:S(2)}) %collective-permute-start.9) | collective-permute-done | bytes 28704 | tf_op jit(solution)/shard_map/ppermute | solution.py:677
  27.7 0.7 %collective-permute-start.10 = (f32[104,128]{1,0:T(8,128)S(1)}, f32[104,128]{1,0:T(8,128)S(1)}, u32[]{:S(2)}, u32[]{:S(2)}) collective-permute-start(f32[104,128]{1,0:T(8,128)S(1)} %get-tuple-element.128.refs_17_), channel_id=1, source_target_pairs={{0,4},{4,8},{8,12},{12,0},{1,5},{5,9},{9,13},{13,1},{2,6},{6,10},{... | collective-permute-start | bytes 159752 | tf_op jit(solution)/shard_map/ppermute | solution.py:666
  28.4 3.2 %collective-permute-start.11 = (f32[104,128]{1,0:T(8,128)S(1)}, f32[104,128]{1,0:T(8,128)S(1)}, u32[]{:S(2)}, u32[]{:S(2)}) collective-permute-start(f32[104,128]{1,0:T(8,128)S(1)} %get-tuple-element.129.refs_18_), channel_id=1, source_target_pairs={{4,0},{8,4},{12,8},{0,12},{5,1},{9,5},{13,9},{1,13},{6,2},{10,6},{... | collective-permute-start | bytes 159752 | tf_op jit(solution)/shard_map/ppermute | solution.py:667
  31.6 2.2 %collective-permute-done.10.refs_13_.refs_7_ = f32[104,128]{1,0:T(8,128)S(1)} collective-permute-done((f32[104,128]{1,0:T(8,128)S(1)}, f32[104,128]{1,0:T(8,128)S(1)}, u32[]{:S(2)}, u32[]{:S(2)}) %collective-permute-start.10) | collective-permute-done | bytes 53280 | tf_op jit(solution)/shard_map/ppermute | solution.py:666
  33.8 0.0 collective-permute-done.11.refs_14_.refs_8_
  33.8 0.4 shard_map.80
  34.2 0.1 collective-permute-start.12
  34.3 1.8 %collective-permute-start.13 = (f32[56,128]{1,0:T(8,128)S(1)}, f32[56,128]{1,0:T(8,128)S(1)}, u32[]{:S(2)}, u32[]{:S(2)}) collective-permute-start(f32[56,128]{1,0:T(8,128)S(1)} %get-tuple-element.139), channel_id=1, source_target_pairs={{0,3},{1,2},{2,1},{3,0},{4,7},{5,6},{6,5},{7,4},{8,11},{9,10},{10,... | collective-permute-start | bytes 86024 | tf_op jit(solution)/shard_map/ppermute | solution.py:677
  36.1 0.9 %shard_map.81 = (f32[19,14,8,128]{3,2,1,0:T(8,128)S(1)}, f32[104,128]{1,0:T(8,128)S(1)}, f32[104,128]{1,0:T(8,128)S(1)}, f32[14,8,128]{2,1,0:T(8,128)S(1)}) custom-call(f32[19,8,128]{2,1,0:T(8,128)S(1)} %get-tuple-element.88.refs_0_, s32[16,8,128]{2,1,0:T(8,128)S(1)} %shard_map.73.refs_1_.bits_ref, f32[18,24,128]{2,1,0:T(8,128)S(1)} %get-tuple-element.131.refs_2_, ...), custom_call_target="tpu_custom_call" | custom-call | flops 6553600 | bytes 1310720 | tf_op jit(solution)/shard_map/pallas_call | solution.py:648
  36.9 0.0 collective-permute-done.12.refs_2_
  37.0 0.7 %collective-permute-done.13.refs_3_ = f32[56,128]{1,0:T(8,128)S(1)} collective-permute-done((f32[56,128]{1,0:T(8,128)S(1)}, f32[56,128]{1,0:T(8,128)S(1)}, u32[]{:S(2)}, u32[]{:S(2)}) %collective-permute-start.13) | collective-permute-done | bytes 28704 | tf_op jit(solution)/shard_map/ppermute | solution.py:677
  37.7 1.7 %collective-permute-start.14 = (f32[104,128]{1,0:T(8,128)S(1)}, f32[104,128]{1,0:T(8,128)S(1)}, u32[]{:S(2)}, u32[]{:S(2)}) collective-permute-start(f32[104,128]{1,0:T(8,128)S(1)} %get-tuple-element.144.refs_17_), channel_id=1, source_target_pairs={{0,4},{4,8},{8,12},{12,0},{1,5},{5,9},{9,13},{13,1},{2,6},{6,10},{... | collective-permute-start | bytes 159752 | tf_op jit(solution)/shard_map/ppermute | solution.py:666
  39.3 2.2 %collective-permute-start.15 = (f32[104,128]{1,0:T(8,128)S(1)}, f32[104,128]{1,0:T(8,128)S(1)}, u32[]{:S(2)}, u32[]{:S(2)}) collective-permute-start(f32[104,128]{1,0:T(8,128)S(1)} %get-tuple-element.145.refs_18_), channel_id=1, source_target_pairs={{4,0},{8,4},{12,8},{0,12},{5,1},{9,5},{13,9},{1,13},{6,2},{10,6},{... | collective-permute-start | bytes 159752 | tf_op jit(solution)/shard_map/ppermute | solution.py:667
  41.6 2.4 %collective-permute-done.14.refs_13_.refs_7_ = f32[104,128]{1,0:T(8,128)S(1)} collective-permute-done((f32[104,128]{1,0:T(8,128)S(1)}, f32[104,128]{1,0:T(8,128)S(1)}, u32[]{:S(2)}, u32[]{:S(2)}) %collective-permute-start.14) | collective-permute-done | bytes 53280 | tf_op jit(solution)/shard_map/ppermute | solution.py:666
  44.0 0.5 collective-permute-done.15.refs_14_.refs_8_
  44.4 0.4 shard_map.83
  44.8 0.1 collective-permute-start.16
  44.9 1.8 %collective-permute-start.17 = (f32[48,128]{1,0:T(8,128)S(1)}, f32[48,128]{1,0:T(8,128)S(1)}, u32[]{:S(2)}, u32[]{:S(2)}) collective-permute-start(f32[48,128]{1,0:T(8,128)S(1)} %get-tuple-element.154), channel_id=1, source_target_pairs={{0,3},{1,2},{2,1},{3,0},{4,7},{5,6},{6,5},{7,4},{8,11},{9,10},{10,... | collective-permute-start | bytes 73736 | tf_op jit(solution)/shard_map/ppermute | solution.py:677
  46.7 0.9 %shard_map.84 = (f32[19,14,8,128]{3,2,1,0:T(8,128)S(1)}, f32[80,128]{1,0:T(8,128)S(1)}, f32[80,128]{1,0:T(8,128)S(1)}, f32[3,128,128]{2,1,0:T(8,128)S(1)}) custom-call(f32[19,8,128]{2,1,0:T(8,128)S(1)} %get-tuple-element.88.refs_0_, s32[16,8,128]{2,1,0:T(8,128)S(1)} %shard_map.73.refs_1_.bits_ref, f32[18,24,128]{2,1,0:T(8,128)S(1)} %get-tuple-element.147.refs_2_, ...), custom_call_target="tpu_custom_call" | custom-call | flops 6553600 | bytes 1310720 | tf_op jit(solution)/shard_map/pallas_call | solution.py:648
  47.6 0.0 collective-permute-done.16.refs_2_
  47.6 0.6 %collective-permute-done.17.refs_3_ = f32[48,128]{1,0:T(8,128)S(1)} collective-permute-done((f32[48,128]{1,0:T(8,128)S(1)}, f32[48,128]{1,0:T(8,128)S(1)}, u32[]{:S(2)}, u32[]{:S(2)}) %collective-permute-start.17) | collective-permute-done | bytes 24608 | tf_op jit(solution)/shard_map/ppermute | solution.py:677
  48.2 1.2 %collective-permute-start.18 = (f32[80,128]{1,0:T(8,128)S(1)}, f32[80,128]{1,0:T(8,128)S(1)}, u32[]{:S(2)}, u32[]{:S(2)}) collective-permute-start(f32[80,128]{1,0:T(8,128)S(1)} %get-tuple-element.163), channel_id=1, source_target_pairs={{0,4},{4,8},{8,12},{12,0},{1,5},{5,9},{9,13},{13,1},{2,6},{6,10},{... | collective-permute-start | bytes 122888 | tf_op jit(solution)/shard_map/ppermute | solution.py:666
  49.4 2.7 %collective-permute-start.19 = (f32[80,128]{1,0:T(8,128)S(1)}, f32[80,128]{1,0:T(8,128)S(1)}, u32[]{:S(2)}, u32[]{:S(2)}) collective-permute-start(f32[80,128]{1,0:T(8,128)S(1)} %get-tuple-element.164), channel_id=1, source_target_pairs={{4,0},{8,4},{12,8},{0,12},{5,1},{9,5},{13,9},{1,13},{6,2},{10,6},{... | collective-permute-start | bytes 122888 | tf_op jit(solution)/shard_map/ppermute | solution.py:667
  52.1 1.3 %shard_map.86 = (f32[19,128,128]{2,1,0:T(8,128)}, f32[19,128,128]{2,1,0:T(8,128)S(1)}, f32[3,128,128]{2,1,0:T(8,128)}) custom-call(f32[19,2,8,128]{3,2,1,0:T(8,128)S(1)} %get-tuple-element.146.f_edge, f32[19,14,8,128]{3,2,1,0:T(8,128)S(1)} %get-tuple-element.150.f_middle, s32[16,8,128]{2,1,0:T(8,128)S(1)} %shard_map.73.refs_1_.bits_ref, ...), custom_call_target="tpu_custom_call" | custom-call | flops 6553600 | bytes 1310720 | tf_op jit(solution)/shard_map/pallas_call | solution.py:648
  53.4 0.7 %collective-permute-done.18.yd = f32[80,128]{1,0:T(8,128)S(1)} collective-permute-done((f32[80,128]{1,0:T(8,128)S(1)}, f32[80,128]{1,0:T(8,128)S(1)}, u32[]{:S(2)}, u32[]{:S(2)}) %collective-permute-start.18) | collective-permute-done | bytes 40992 | tf_op jit(solution)/shard_map/ppermute | solution.py:666
  54.1 0.2 collective-permute-done.19.yu
  54.3 0.7 %shard_map.87 = f32[19,128,128]{2,1,0:T(8,128)} custom-call(f32[19,128,128]{2,1,0:T(8,128)} %get-tuple-element.160.out_in, f32[19,128,128]{2,1,0:T(8,128)S(1)} %get-tuple-element.161.flat_ref, f32[2,128,128]{2,1,0:T(8,128)S(1)} %get-tuple-element.162.mask_ref, f32[80,128]{1,0:T(8,128)S(1)} %collective-permute-done.18.yd, ...), custom_call_target="tpu_custom_call", output_to_operand_aliasing={{}: (0, {})} | custom-call | tf_op jit(solution)/shard_map/pallas_call | solution.py:648
  (5 shorter events, 0.1 us)
Async XLA Ops:
  0.6 11.4 %copy-start = (f32[4]{0:T(128)S(1)}, f32[4]{0:T(128)}, u32[]{:S(2)}) copy-start(f32[4]{0:T(128)} %wall_ref.1) | copy-start | bytes 52
  0.6 11.4 %copy-start.1 = (f32[19]{0:T(128)S(1)}, f32[19]{0:T(128)}, u32[]{:S(2)}) copy-start(f32[19]{0:T(128)} %rate_ref.1) | copy-start | bytes 232
  2.1 3.8 %collective-permute-start.1 = (f32[16,128]{1,0:T(8,128)S(1)}, f32[16,128]{1,0:T(8,128)S(1)}, u32[]{:S(2)}, u32[]{:S(2)}) collective-permute-start(f32[16,128]{1,0:T(8,128)S(1)} %get-tuple-element.91), channel_id=1, source_target_pairs={{0,3},{1,2},{2,1},{3,0},{4,7},{5,6},{6,5},{7,4},{8,11},{9,10},{10,... | collective-permute-start | bytes 24584 | tf_op jit(solution)/shard_map/ppermute | solution.py:677
  4.6 1.5 %collective-permute-start = (f32[16,128]{1,0:T(8,128)S(1)}, f32[16,128]{1,0:T(8,128)S(1)}, u32[]{:S(2)}, u32[]{:S(2)}) collective-permute-start(f32[16,128]{1,0:T(8,128)S(1)} %get-tuple-element.84.after_ref), channel_id=1, source_target_pairs={{0,1},{1,0},{2,3},{3,2},{4,5},{5,4},{6,7},{7,6},{8,9},{9,8},{10,11... | collective-permute-start | bytes 24584 | tf_op jit(solution)/shard_map/ppermute | solution.py:678
  6.1 7.3 %collective-permute-start.2 = (f32[40,128]{1,0:T(8,128)S(1)}, f32[40,128]{1,0:T(8,128)S(1)}, u32[]{:S(2)}, u32[]{:S(2)}) collective-permute-start(f32[40,128]{1,0:T(8,128)S(1)} %get-tuple-element.94), channel_id=1, source_target_pairs={{0,4},{4,8},{8,12},{12,0},{1,5},{5,9},{9,13},{13,1},{2,6},{6,10},{... | collective-permute-start | bytes 61448 | tf_op jit(solution)/shard_map/ppermute | solution.py:666
  8.4 5.0 %collective-permute-start.3 = (f32[40,128]{1,0:T(8,128)S(1)}, f32[40,128]{1,0:T(8,128)S(1)}, u32[]{:S(2)}, u32[]{:S(2)}) collective-permute-start(f32[40,128]{1,0:T(8,128)S(1)} %get-tuple-element.95), channel_id=1, source_target_pairs={{4,0},{8,4},{12,8},{0,12},{5,1},{9,5},{13,9},{1,13},{6,2},{10,6},{... | collective-permute-start | bytes 61448 | tf_op jit(solution)/shard_map/ppermute | solution.py:667
  13.8 2.7 %collective-permute-start.4 = (f32[56,128]{1,0:T(8,128)S(1)}, f32[56,128]{1,0:T(8,128)S(1)}, u32[]{:S(2)}, u32[]{:S(2)}) collective-permute-start(f32[56,128]{1,0:T(8,128)S(1)} %get-tuple-element.106), channel_id=1, source_target_pairs={{0,1},{1,0},{2,3},{3,2},{4,5},{5,4},{6,7},{7,6},{8,9},{9,8},{10,11... | collective-permute-start | bytes 86024 | tf_op jit(solution)/shard_map/ppermute | solution.py:678
  13.9 3.4 %collective-permute-start.5 = (f32[56,128]{1,0:T(8,128)S(1)}, f32[56,128]{1,0:T(8,128)S(1)}, u32[]{:S(2)}, u32[]{:S(2)}) collective-permute-start(f32[56,128]{1,0:T(8,128)S(1)} %get-tuple-element.107), channel_id=1, source_target_pairs={{0,3},{1,2},{2,1},{3,0},{4,7},{5,6},{6,5},{7,4},{8,11},{9,10},{10,... | collective-permute-start | bytes 86024 | tf_op jit(solution)/shard_map/ppermute | solution.py:677
  17.3 6.5 %collective-permute-start.6 = (f32[104,128]{1,0:T(8,128)S(1)}, f32[104,128]{1,0:T(8,128)S(1)}, u32[]{:S(2)}, u32[]{:S(2)}) collective-permute-start(f32[104,128]{1,0:T(8,128)S(1)} %get-tuple-element.112.refs_17_), channel_id=1, source_target_pairs={{0,4},{4,8},{8,12},{12,0},{1,5},{5,9},{9,13},{13,1},{2,6},{6,10},{... | collective-permute-start | bytes 159752 | tf_op jit(solution)/shard_map/ppermute | solution.py:666
  17.7 6.1 %collective-permute-start.7 = (f32[104,128]{1,0:T(8,128)S(1)}, f32[104,128]{1,0:T(8,128)S(1)}, u32[]{:S(2)}, u32[]{:S(2)}) collective-permute-start(f32[104,128]{1,0:T(8,128)S(1)} %get-tuple-element.113.refs_18_), channel_id=1, source_target_pairs={{4,0},{8,4},{12,8},{0,12},{5,1},{9,5},{13,9},{1,13},{6,2},{10,6},{... | collective-permute-start | bytes 159752 | tf_op jit(solution)/shard_map/ppermute | solution.py:667
  24.2 2.8 %collective-permute-start.8 = (f32[56,128]{1,0:T(8,128)S(1)}, f32[56,128]{1,0:T(8,128)S(1)}, u32[]{:S(2)}, u32[]{:S(2)}) collective-permute-start(f32[56,128]{1,0:T(8,128)S(1)} %get-tuple-element.122), channel_id=1, source_target_pairs={{0,1},{1,0},{2,3},{3,2},{4,5},{5,4},{6,7},{7,6},{8,9},{9,8},{10,11... | collective-permute-start | bytes 86024 | tf_op jit(solution)/shard_map/ppermute | solution.py:678
  24.3 3.4 %collective-permute-start.9 = (f32[56,128]{1,0:T(8,128)S(1)}, f32[56,128]{1,0:T(8,128)S(1)}, u32[]{:S(2)}, u32[]{:S(2)}) collective-permute-start(f32[56,128]{1,0:T(8,128)S(1)} %get-tuple-element.123), channel_id=1, source_target_pairs={{0,3},{1,2},{2,1},{3,0},{4,7},{5,6},{6,5},{7,4},{8,11},{9,10},{10,... | collective-permute-start | bytes 86024 | tf_op jit(solution)/shard_map/ppermute | solution.py:677
  27.7 6.1 %collective-permute-start.10 = (f32[104,128]{1,0:T(8,128)S(1)}, f32[104,128]{1,0:T(8,128)S(1)}, u32[]{:S(2)}, u32[]{:S(2)}) collective-permute-start(f32[104,128]{1,0:T(8,128)S(1)} %get-tuple-element.128.refs_17_), channel_id=1, source_target_pairs={{0,4},{4,8},{8,12},{12,0},{1,5},{5,9},{9,13},{13,1},{2,6},{6,10},{... | collective-permute-start | bytes 159752 | tf_op jit(solution)/shard_map/ppermute | solution.py:666
  28.4 5.4 %collective-permute-start.11 = (f32[104,128]{1,0:T(8,128)S(1)}, f32[104,128]{1,0:T(8,128)S(1)}, u32[]{:S(2)}, u32[]{:S(2)}) collective-permute-start(f32[104,128]{1,0:T(8,128)S(1)} %get-tuple-element.129.refs_18_), channel_id=1, source_target_pairs={{4,0},{8,4},{12,8},{0,12},{5,1},{9,5},{13,9},{1,13},{6,2},{10,6},{... | collective-permute-start | bytes 159752 | tf_op jit(solution)/shard_map/ppermute | solution.py:667
  34.2 2.7 %collective-permute-start.12 = (f32[56,128]{1,0:T(8,128)S(1)}, f32[56,128]{1,0:T(8,128)S(1)}, u32[]{:S(2)}, u32[]{:S(2)}) collective-permute-start(f32[56,128]{1,0:T(8,128)S(1)} %get-tuple-element.138), channel_id=1, source_target_pairs={{0,1},{1,0},{2,3},{3,2},{4,5},{5,4},{6,7},{7,6},{8,9},{9,8},{10,11... | collective-permute-start | bytes 86024 | tf_op jit(solution)/shard_map/ppermute | solution.py:678
  34.3 3.4 %collective-permute-start.13 = (f32[56,128]{1,0:T(8,128)S(1)}, f32[56,128]{1,0:T(8,128)S(1)}, u32[]{:S(2)}, u32[]{:S(2)}) collective-permute-start(f32[56,128]{1,0:T(8,128)S(1)} %get-tuple-element.139), channel_id=1, source_target_pairs={{0,3},{1,2},{2,1},{3,0},{4,7},{5,6},{6,5},{7,4},{8,11},{9,10},{10,... | collective-permute-start | bytes 86024 | tf_op jit(solution)/shard_map/ppermute | solution.py:677
  37.7 6.3 %collective-permute-start.14 = (f32[104,128]{1,0:T(8,128)S(1)}, f32[104,128]{1,0:T(8,128)S(1)}, u32[]{:S(2)}, u32[]{:S(2)}) collective-permute-start(f32[104,128]{1,0:T(8,128)S(1)} %get-tuple-element.144.refs_17_), channel_id=1, source_target_pairs={{0,4},{4,8},{8,12},{12,0},{1,5},{5,9},{9,13},{13,1},{2,6},{6,10},{... | collective-permute-start | bytes 159752 | tf_op jit(solution)/shard_map/ppermute | solution.py:666
  39.3 5.1 %collective-permute-start.15 = (f32[104,128]{1,0:T(8,128)S(1)}, f32[104,128]{1,0:T(8,128)S(1)}, u32[]{:S(2)}, u32[]{:S(2)}) collective-permute-start(f32[104,128]{1,0:T(8,128)S(1)} %get-tuple-element.145.refs_18_), channel_id=1, source_target_pairs={{4,0},{8,4},{12,8},{0,12},{5,1},{9,5},{13,9},{1,13},{6,2},{10,6},{... | collective-permute-start | bytes 159752 | tf_op jit(solution)/shard_map/ppermute | solution.py:667
  44.8 2.8 %collective-permute-start.16 = (f32[48,128]{1,0:T(8,128)S(1)}, f32[48,128]{1,0:T(8,128)S(1)}, u32[]{:S(2)}, u32[]{:S(2)}) collective-permute-start(f32[48,128]{1,0:T(8,128)S(1)} %get-tuple-element.153), channel_id=1, source_target_pairs={{0,1},{1,0},{2,3},{3,2},{4,5},{5,4},{6,7},{7,6},{8,9},{9,8},{10,11... | collective-permute-start | bytes 73736 | tf_op jit(solution)/shard_map/ppermute | solution.py:678
  44.9 3.3 %collective-permute-start.17 = (f32[48,128]{1,0:T(8,128)S(1)}, f32[48,128]{1,0:T(8,128)S(1)}, u32[]{:S(2)}, u32[]{:S(2)}) collective-permute-start(f32[48,128]{1,0:T(8,128)S(1)} %get-tuple-element.154), channel_id=1, source_target_pairs={{0,3},{1,2},{2,1},{3,0},{4,7},{5,6},{6,5},{7,4},{8,11},{9,10},{10,... | collective-permute-start | bytes 73736 | tf_op jit(solution)/shard_map/ppermute | solution.py:677
  48.2 5.9 %collective-permute-start.18 = (f32[80,128]{1,0:T(8,128)S(1)}, f32[80,128]{1,0:T(8,128)S(1)}, u32[]{:S(2)}, u32[]{:S(2)}) collective-permute-start(f32[80,128]{1,0:T(8,128)S(1)} %get-tuple-element.163), channel_id=1, source_target_pairs={{0,4},{4,8},{8,12},{12,0},{1,5},{5,9},{9,13},{13,1},{2,6},{6,10},{... | collective-permute-start | bytes 122888 | tf_op jit(solution)/shard_map/ppermute | solution.py:666
  49.4 4.9 %collective-permute-start.19 = (f32[80,128]{1,0:T(8,128)S(1)}, f32[80,128]{1,0:T(8,128)S(1)}, u32[]{:S(2)}, u32[]{:S(2)}) collective-permute-start(f32[80,128]{1,0:T(8,128)S(1)} %get-tuple-element.164), channel_id=1, source_target_pairs={{4,0},{8,4},{12,8},{0,12},{5,1},{9,5},{13,9},{1,13},{6,2},{10,6},{... | collective-permute-start | bytes 122888 | tf_op jit(solution)/shard_map/ppermute | solution.py:667

commit v9 on v7

--- a/solution.py
+++ b/solution.py
@@ -161,44 +161,30 @@
     return wall
 
 
-def face_kernel(pairs, f_hbm, mask_hbm, wet_hbm, wall_hbm, a_ref, b_ref, rows_ref, *scratch):
-    layer_in, row_in, mask_in, wet_in, wall_in, layer_sems, row_sems, sems = scratch
-    layers, rows = row_in.shape[2], layer_in.shape[2]
-    small = [
-        pltpu.make_async_copy(source, target, sems.at[i])
-        for i, (source, target) in enumerate(
-            ((wall_hbm, wall_in), (mask_hbm, mask_in), (wet_hbm, wet_in))
+def face_kernel(f_hbm, mask_hbm, wet_hbm, wall_hbm, up_ref, down_ref, *scratch):
+    row_in, mask_in, wet_in, wall_in, sems = scratch
+    layers = row_in.shape[2]
+    sides = ((0, down_ref, 0), (1, up_ref, f_hbm.shape[1] - layers))
+    copies = [pltpu.make_async_copy(wall_hbm, wall_in, sems.at[0])]
+    for s, _, at in sides:
+        for i, (source, target) in enumerate(((mask_hbm, mask_in), (wet_hbm, wet_in))):
+            sem = sems.at[1 + 2 * s + i]
+            copies.append(
+                pltpu.make_async_copy(source.at[pl.ds(at, layers)], target.at[s], sem)
+            )
+        sem = sems.at[5 + s]
+        copies.append(
+            pltpu.make_async_copy(f_hbm.at[:, pl.ds(at, layers)], row_in.at[s], sem)
         )
-    ]
-    large = []
-    for s, layer in enumerate((0, layers - 1)):
-        for row in range(rows):
-            source = f_hbm.at[:, pl.ds(row * layers + layer, 1)]
-            target = layer_in.at[s, :, pl.ds(row, 1)]
-            large.append(pltpu.make_async_copy(source, target, layer_sems.at[s, row]))
-    for s, row in enumerate((0, rows - 1)):
-        source = f_hbm.at[:, pl.ds(row * layers, layers)]
-        large.append(pltpu.make_async_copy(source, row_in.at[s], row_sems.at[s]))
-    for copy in small + large:
+    for copy in copies:
         copy.start()
-    for copy in small + large:
+    for copy in copies:
         copy.wait()
-    faces = []
-    for s, layer in enumerate((0, layers - 1)):
-        at = pl.ds(layer, rows, stride=layers)
-        pore = mask_in[at] == 1
-        density = total([layer_in[s, k] for k in range(N)])
-        pot = potential_of(density, pore, wall_of(wet_in[at], wall_in))
-        faces.append((pot, jnp.where(pore, 1.0, 0.0)))
-    for i in range(2):
-        at = slice(i * rows, (i + 1) * rows)
-        a_ref[at], b_ref[at] = in_swap_order(pairs, faces[1][i], faces[0][i])
-    for s, row in enumerate((0, rows - 1)):
-        at = slice(row * layers, (row + 1) * layers)
-        pore = mask_in[at] == 1
+    for s, ref, _ in sides:
+        pore = mask_in[s] == 1
         density = total([row_in[s, k] for k in range(N)])
-        rows_ref[s, :layers] = potential_of(density, pore, wall_of(wet_in[at], wall_in))
-        rows_ref[s, layers:] = jnp.where(pore, 1.0, 0.0)
+        ref[:layers] = potential_of(density, pore, wall_of(wet_in[s], wall_in))
+        ref[layers:] = jnp.where(pore, 1.0, 0.0)
 
 
 def turn_kernel(raw_ref, mask_in, wet_in, wall_ref, rate_ref, f_ref, rates_ref, flat_ref, mask_ref, pot_ref):
@@ -219,29 +205,29 @@
             f_ref[k, i] = raw_ref[k, pl.ds(i, rows, stride=layers)]
 
 
-def start_pack_kernel(pairs, rows_ref, a_ref, b_ref, up_ref, down_ref, from_left, from_right):
-    size_x = rows_ref.shape[1] // 2
-    size_y = a_ref.shape[0] // 2
-    sort_received(pairs, a_ref, b_ref, from_left, from_right)
-    for s, ref, y in ((1, up_ref, size_y - 1), (0, down_ref, 0)):
-        ref[: 2 * size_x] = rows_ref[s]
-        ref[2 * size_x :] = jnp.zeros((TILE, ref.shape[1]), jnp.float32)
-        for i, side in enumerate((from_left, from_right)):
-            row = 2 * size_x + i
-            ref[row : row + 1] = side[y : y + 1]
-            ref[row + 2 : row + 3] = side[size_y + y : size_y + y + 1]
-
-
-def bits_kernel(mask_ref, x0l, x0r, bits_ref, pad_ref):
+def start_pack_kernel(pairs, pot_ref, mask_ref, from_below, from_above, a_ref, b_ref, left_ref, right_ref):
+    layers, rows = mask_ref.shape[0], mask_ref.shape[1]
+    for ref, layer in ((left_ref, 0), (right_ref, layers - 1)):
+        ref[:rows] = pot_ref[layer]
+        ref[rows : 2 * rows] = mask_ref[layer]
+        ref[2 * rows :] = jnp.zeros((TILE, ref.shape[1]), jnp.float32)
+        for i, side in enumerate((from_below, from_above)):
+            row = 2 * rows + i
+            ref[row : row + 1] = side[layer : layer + 1]
+            ref[row + 2 : row + 3] = side[layers + layer : layers + layer + 1]
+    a_ref[...], b_ref[...] = in_swap_order(pairs, right_ref[...], left_ref[...])
+
+
+def bits_kernel(mask_ref, from_below, from_above, bits_ref, pad_ref):
     size_x, size_y, size_z = mask_ref.shape
     nothing = jnp.zeros((TILE, size_z), jnp.float32)
-    for x in range(size_x + 2):
-        pad_ref[x, :TILE] = nothing
-        pad_ref[x, TILE + size_y :] = nothing
+    for x in (0, size_x + 1):
+        for y in range(0, size_y + PAD, TILE):
+            pad_ref[x, y : y + TILE] = nothing
     for x in range(size_x):
         pad_ref[1 + x, TILE : TILE + size_y] = mask_ref[x]
-    for x, side in ((0, x0l), (1 + size_x, x0r)):
-        pad_ref[x, TILE : TILE + size_y] = side[size_y:]
+        for y, side in ((TILE - 1, from_below), (TILE + size_y, from_above)):
+            pad_ref[1 + x, y : y + 1] = side[size_x + x : size_x + x + 1]
     for x in range(size_x):
         for y in range(0, size_y, TILE):
             bits = jnp.zeros((TILE, size_z), jnp.int32)
@@ -253,26 +239,29 @@
             bits_ref[x, y : y + TILE] = bits
 
 
-def more_bits_kernel(bits_in, y0d, y0u, bits_ref, pad_ref):
-    size_x, size_y, size_z = bits_ref.shape
-    row_of = lax.broadcasted_iota(jnp.int32, (TILE, size_z), 0)
-    found = []
-    for i, (side, ks) in enumerate(((y0d, UP), (y0u, DOWN))):
-        pad_ref[i, TILE : TILE + size_x] = side[size_x : 2 * size_x]
-        for row, x in ((TILE - 1, 2 * size_x + 2), (TILE + size_x, 2 * size_x + 3)):
-            pad_ref[i, row : row + 1] = side[x : x + 1]
-        bits = jnp.zeros((size_x, size_z), jnp.int32)
-        for k in ks:
-            ex, _, ez = SHIFT[k]
-            source = roll_z(pad_ref[i, TILE - ex : TILE - ex + size_x], ez)
-            bits = bits | jnp.where(source > 0.5, 1 << k, 0)
-        found.append(bits)
-    for x in range(size_x):
+def ring_kernel(pairs, bits_in, a_ref, b_ref, from_below, from_above, bits_ref, xl, xr, yd, yu, pad_ref):
+    size_x, size_y, _ = bits_ref.shape
+    sort_received(pairs, a_ref, b_ref, xl, xr)
+    corner = 2 * size_y
+    for i, (ref, side) in enumerate(((yd, from_below), (yu, from_above))):
+        ref[: 2 * size_x] = side[...]
+        ref[2 * size_x :] = jnp.zeros((TILE, ref.shape[1]), jnp.float32)
+        for j, layer in enumerate((xl, xr)):
+            row = 2 * size_x + j
+            ref[row : row + 1] = layer[corner + i : corner + i + 1]
+            ref[row + 2 : row + 3] = layer[corner + 2 + i : corner + 3 + i]
+    bits_ref[...] = bits_in[...]
+    for i, (side, ks, x) in enumerate(((xl, RIGHT, 0), (xr, LEFT, size_x - 1))):
+        pad_ref[i, TILE : TILE + size_y] = side[size_y : 2 * size_y]
+        for row, at in ((TILE - 1, corner + 2), (TILE + size_y, corner + 3)):
+            pad_ref[i, row : row + 1] = side[at : at + 1]
         for y in range(0, size_y, TILE):
             bits = bits_in[x, y : y + TILE]
-            for at, more in ((0, found[0]), (size_y - 1, found[1])):
-                if y <= at < y + TILE:
-                    bits = bits | jnp.where(row_of == at - y, more[x : x + 1], 0)
+            for k in ks:
+                _, ey, ez = SHIFT[k]
+                row = TILE + y - ey
+                source = roll_z(pad_ref[i, row : row + TILE], ez)
+                bits = bits | jnp.where(source > 0.5, 1 << k, 0)
             bits_ref[x, y : y + TILE] = bits
 
 
@@ -688,29 +677,24 @@
         wet_class.reshape(cells, size_z),
         wall_potential,
     )
-    start_rows = rows(2 * size_x + TILE)
-    a, b, row_faces = call(
-        functools.partial(face_kernel, pairs),
-        [rows(2 * size_y), rows(2 * size_y), ((2, 2 * size_x, size_z), f32)],
+    row_face = rows(2 * size_x)
+    layer_face = rows(2 * size_y + TILE)
+    ring_rows = rows(2 * size_x + TILE)
+    up, down = call(
+        face_kernel,
+        [row_face, row_face],
         [pltpu.with_memory_space_constraint(item, pltpu.HBM) for item in operands],
         special={i: HBM for i in range(4)},
         scratch=[
-            (2, N, size_y, size_z),
             (2, N, size_x, size_z),
-            pltpu.VMEM((cells, size_z), i32),
-            pltpu.VMEM((cells, size_z), i32),
+            pltpu.VMEM((2, size_x, size_z), i32),
+            pltpu.VMEM((2, size_x, size_z), i32),
             pltpu.SMEM(wall_potential.shape, f32),
-            pltpu.SemaphoreType.DMA((2, size_y)),
-            pltpu.SemaphoreType.DMA((2,)),
-            pltpu.SemaphoreType.DMA((3,)),
+            pltpu.SemaphoreType.DMA((7,)),
         ],
     )
-    a, b = exchange(a, b, "gy")
-    up, down, x0l, x0r = call(
-        functools.partial(start_pack_kernel, pairs),
-        [start_rows, start_rows, rows(2 * size_y), rows(2 * size_y)],
-        (row_faces, a, b),
-    )
+    *operands, up = lax.optimization_barrier((*operands, up))
+    below, above = shift(up, down, "gx")
     f, rates, flat_mask, mask, pot0 = call(
         turn_kernel,
         [fields(size_x), ((N, TILE, size_z), f32), flat(2), whole, whole],
@@ -718,11 +702,20 @@
         special={3: SMEM, 4: SMEM},
         cost=cost,
     )
-    y0d, y0u = shift(up, down, "gx")
-    whole_bits = [((size_x, size_y, size_z), i32)]
-    (bits,) = call(bits_kernel, whole_bits, (mask, x0l, x0r), scratch=[padded], cost=cost)
-    (bits,) = call(
-        more_bits_kernel, whole_bits, (bits, y0d, y0u), scratch=[(2, size_x + PAD, size_z)]
+    a, b = call(
+        functools.partial(start_pack_kernel, pairs),
+        [layer_face, layer_face],
+        (pot0, mask, below, above),
+        scratch=[layer_face[0]] * 2,
+    )
+    a, b = exchange(a, b, "gy")
+    whole_bits = ((size_x, size_y, size_z), i32)
+    (bits,) = call(bits_kernel, [whole_bits], (mask, below, above), scratch=[padded], cost=cost)
+    bits, x0l, x0r, y0d, y0u = call(
+        functools.partial(ring_kernel, pairs),
+        [whole_bits, layer_face, layer_face, ring_rows, ring_rows],
+        (bits, a, b, below, above),
+        scratch=[(2, size_y + PAD, size_z)],
     )
     edge2, edge1 = len(two_layers(size_x)), len(one_layer(size_x))
     held, sent = (f,), ()

time: 54.7 us -> 54.5 us (level)
    ppermute x5, starting transfers between devices: 6.94 us -> 8.24 us  [shift(): lax.ppermute(forward, axis, ahead)]
    ppermute x5, starting transfers between devices: 9.32 us -> 8.13 us  [swap(): b = lax.ppermute(b, axis, partners[1])]
where the time goes in v9:
time: 54.5 us; the launch traced here: 54.3 us
  starting transfers between devices  29.6 us (54%)
  waiting for transfers between devices  14.1 us (26%)
  Pallas kernels  9.77 us (18%)
  between operations  0.85 us (2%)
    ppermute x5, starting transfers between devices, shift(): lax.ppermute(backward, axis, [(b, a) for a, b in ahead])  12.5 us
    pallas_call x19, Pallas kernels, call(): pl.pallas_call(kernel, out_shape=[jax.ShapeDtypeStruct(shape, dtype) for...  9.77 us
    ppermute x5, starting transfers between devices, shift(): lax.ppermute(forward, axis, ahead)  8.24 us
    ppermute x5, starting transfers between devices, swap(): b = lax.ppermute(b, axis, partners[1])  8.13 us
    ppermute x5, waiting for transfers between devices, shift(): lax.ppermute(forward, axis, ahead)  7.95 us
    ppermute x5, waiting for transfers between devices, swap(): b = lax.ppermute(b, axis, partners[1])  4.57 us
    ppermute x5, waiting for transfers between devices, shift(): lax.ppermute(backward, axis, [(b, a) for a, b in ahead])  1.56 us
  transfers between devices with their start and end apart: 20, of which 15 were waited for; matrix products, arithmetic and copies ran while one was open for 0% of the time, Pallas kernels for 11%

profile of v9, /device:TPU:0, one launch (start us, length us, event | category | flops | bytes accessed | tf_op | source)
XLA Modules:
  0.0 54.3 jit_solution(13914382492277398137)
XLA Ops:
  0.6 0.0 copy-start.3
  0.6 0.0 copy-start.2
  0.7 0.0 copy-start.1
  0.7 0.0 copy-start
  0.7 0.0 copy-start.4
  0.7 1.2 %shard_map.68 = (f32[32,128]{1,0:T(8,128)S(1)}, f32[32,128]{1,0:T(8,128)S(1)}) custom-call(f32[19,128,128]{2,1,0:T(8,128)} %bitcast.5, s32[128,128]{1,0:T(8,128)} %bitcast.7, s32[128,128]{1,0:T(8,128)} %bitcast.9, f32[4]{0:T(128)} %wall_ref), custom_call_target="tpu_custom_call" | custom-call | tf_op jit(solution)/shard_map/pallas_call | solution.py:626
  1.9 3.1 %collective-permute-start = (f32[32,128]{1,0:T(8,128)S(1)}, f32[32,128]{1,0:T(8,128)S(1)}, u32[]{:S(2)}, u32[]{:S(2)}) collective-permute-start(f32[32,128]{1,0:T(8,128)S(1)} %get-tuple-element.95), channel_id=1, source_target_pairs={{0,4},{4,8},{8,12},{12,0},{1,5},{5,9},{9,13},{13,1},{2,6},{6,10},{... | collective-permute-start | bytes 49160 | tf_op jit(solution)/shard_map/ppermute | solution.py:644
  5.0 2.1 %collective-permute-start.1 = (f32[32,128]{1,0:T(8,128)S(1)}, f32[32,128]{1,0:T(8,128)S(1)}, u32[]{:S(2)}, u32[]{:S(2)}) collective-permute-start(f32[32,128]{1,0:T(8,128)S(1)} %get-tuple-element.96), channel_id=1, source_target_pairs={{4,0},{8,4},{12,8},{0,12},{5,1},{9,5},{13,9},{1,13},{6,2},{10,6},{... | collective-permute-start | bytes 49160 | tf_op jit(solution)/shard_map/ppermute | solution.py:645
  7.1 0.0 copy-done.3
  7.1 0.0 copy-done.2
  7.1 0.0 copy-done.1
  7.1 0.0 copy-done
  7.1 0.0 copy-done.4
  7.2 1.0 %shard_map.69 = (f32[19,16,8,128]{3,2,1,0:T(8,128)S(1)}, f32[19,8,128]{2,1,0:T(8,128)S(1)}, f32[2,128,128]{2,1,0:T(8,128)S(1)}, f32[16,8,128]{2,1,0:T(8,128)S(1)}, f32[16,8,128]{2,1,0:T(8,128)S(1)}) custom-call(f32[19,128,128]{2,1,0:T(8,128)S(1)} %bitcast.6, s32[128,128]{1,0:T(8,128)S(1)} %bitcast.8, s32[128,128]{1,0:T(8,128)S(1)} %bitcast.10, ...), custom_call_target="tpu_custom_call" | custom-call | flops 6553600 | bytes 1310720 | tf_op jit(solution)/shard_map/pallas_call | solution.py:626
  8.2 0.7 %collective-permute-done.from_below = f32[32,128]{1,0:T(8,128)S(1)} collective-permute-done((f32[32,128]{1,0:T(8,128)S(1)}, f32[32,128]{1,0:T(8,128)S(1)}, u32[]{:S(2)}, u32[]{:S(2)}) %collective-permute-start) | collective-permute-done | bytes 16416 | tf_op jit(solution)/shard_map/ppermute | solution.py:644
  8.9 0.1 collective-permute-done.1.from_above
  9.0 0.1 collective-permute-start.2
  9.1 1.6 %collective-permute-start.3 = (f32[24,128]{1,0:T(8,128)S(1)}, f32[24,128]{1,0:T(8,128)S(1)}, u32[]{:S(2)}, u32[]{:S(2)}) collective-permute-start(f32[24,128]{1,0:T(8,128)S(1)} %get-tuple-element.99), channel_id=1, source_target_pairs={{0,3},{1,2},{2,1},{3,0},{4,7},{5,6},{6,5},{7,4},{8,11},{9,10},{10,... | collective-permute-start | bytes 36872 | tf_op jit(solution)/shard_map/ppermute | solution.py:655
  10.7 0.2 shard_map.70.bits_in
  10.9 0.0 collective-permute-done.2.a_ref
  11.0 1.3 %collective-permute-done.3.b_ref = f32[24,128]{1,0:T(8,128)S(1)} collective-permute-done((f32[24,128]{1,0:T(8,128)S(1)}, f32[24,128]{1,0:T(8,128)S(1)}, u32[]{:S(2)}, u32[]{:S(2)}) %collective-permute-start.3) | collective-permute-done | bytes 12320 | tf_op jit(solution)/shard_map/ppermute | solution.py:655
  12.2 0.1 shard_map.72
  12.3 0.3 shard_map.73
  12.6 0.5 collective-permute-start.4
  13.1 1.2 %collective-permute-start.5 = (f32[56,128]{1,0:T(8,128)S(1)}, f32[56,128]{1,0:T(8,128)S(1)}, u32[]{:S(2)}, u32[]{:S(2)}) collective-permute-start(f32[56,128]{1,0:T(8,128)S(1)} %get-tuple-element.115), channel_id=1, source_target_pairs={{0,3},{1,2},{2,1},{3,0},{4,7},{5,6},{6,5},{7,4},{8,11},{9,10},{10,... | collective-permute-start | bytes 86024 | tf_op jit(solution)/shard_map/ppermute | solution.py:655
  14.4 0.8 %shard_map.74 = (f32[19,14,8,128]{3,2,1,0:T(8,128)S(1)}, f32[104,128]{1,0:T(8,128)S(1)}, f32[104,128]{1,0:T(8,128)S(1)}, f32[14,8,128]{2,1,0:T(8,128)S(1)}) custom-call(f32[19,8,128]{2,1,0:T(8,128)S(1)} %get-tuple-element.93.refs_0_, s32[16,8,128]{2,1,0:T(8,128)S(1)} %get-tuple-element.100.refs_1_.bits_ref, f32[18,24,128]{2,1,0:T(8,128)S(1)} %get-tuple-element.107.refs_2_, ...), custom_call_target="tpu_custom_call" | custom-call | flops 6553600 | bytes 1310720 | tf_op jit(solution)/shard_map/pallas_call | solution.py:626
  15.2 0.0 collective-permute-done.4.refs_2_
  15.2 1.3 %collective-permute-done.5.refs_3_ = f32[56,128]{1,0:T(8,128)S(1)} collective-permute-done((f32[56,128]{1,0:T(8,128)S(1)}, f32[56,128]{1,0:T(8,128)S(1)}, u32[]{:S(2)}, u32[]{:S(2)}) %collective-permute-start.5) | collective-permute-done | bytes 28704 | tf_op jit(solution)/shard_map/ppermute | solution.py:655
  16.5 1.5 %collective-permute-start.6 = (f32[104,128]{1,0:T(8,128)S(1)}, f32[104,128]{1,0:T(8,128)S(1)}, u32[]{:S(2)}, u32[]{:S(2)}) collective-permute-start(f32[104,128]{1,0:T(8,128)S(1)} %get-tuple-element.120.refs_17_), channel_id=1, source_target_pairs={{0,4},{4,8},{8,12},{12,0},{1,5},{5,9},{9,13},{13,1},{2,6},{6,10},{... | collective-permute-start | bytes 159752 | tf_op jit(solution)/shard_map/ppermute | solution.py:644
  18.0 2.4 %collective-permute-start.7 = (f32[104,128]{1,0:T(8,128)S(1)}, f32[104,128]{1,0:T(8,128)S(1)}, u32[]{:S(2)}, u32[]{:S(2)}) collective-permute-start(f32[104,128]{1,0:T(8,128)S(1)} %get-tuple-element.121.refs_18_), channel_id=1, source_target_pairs={{4,0},{8,4},{12,8},{0,12},{5,1},{9,5},{13,9},{1,13},{6,2},{10,6},{... | collective-permute-start | bytes 159752 | tf_op jit(solution)/shard_map/ppermute | solution.py:645
  20.4 2.1 %collective-permute-done.6.refs_13_.refs_7_ = f32[104,128]{1,0:T(8,128)S(1)} collective-permute-done((f32[104,128]{1,0:T(8,128)S(1)}, f32[104,128]{1,0:T(8,128)S(1)}, u32[]{:S(2)}, u32[]{:S(2)}) %collective-permute-start.6) | collective-permute-done | bytes 53280 | tf_op jit(solution)/shard_map/ppermute | solution.py:644
  22.5 0.5 collective-permute-done.7.refs_14_.refs_8_
  23.0 0.4 shard_map.76
  23.3 0.1 collective-permute-start.8
  23.4 1.7 %collective-permute-start.9 = (f32[56,128]{1,0:T(8,128)S(1)}, f32[56,128]{1,0:T(8,128)S(1)}, u32[]{:S(2)}, u32[]{:S(2)}) collective-permute-start(f32[56,128]{1,0:T(8,128)S(1)} %get-tuple-element.131), channel_id=1, source_target_pairs={{0,3},{1,2},{2,1},{3,0},{4,7},{5,6},{6,5},{7,4},{8,11},{9,10},{10,... | collective-permute-start | bytes 86024 | tf_op jit(solution)/shard_map/ppermute | solution.py:655
  25.2 0.9 %shard_map.77 = (f32[19,14,8,128]{3,2,1,0:T(8,128)S(1)}, f32[104,128]{1,0:T(8,128)S(1)}, f32[104,128]{1,0:T(8,128)S(1)}, f32[14,8,128]{2,1,0:T(8,128)S(1)}) custom-call(f32[19,8,128]{2,1,0:T(8,128)S(1)} %get-tuple-element.93.refs_0_, s32[16,8,128]{2,1,0:T(8,128)S(1)} %get-tuple-element.100.refs_1_.bits_ref, f32[18,24,128]{2,1,0:T(8,128)S(1)} %get-tuple-element.123.refs_2_, ...), custom_call_target="tpu_custom_call" | custom-call | flops 6553600 | bytes 1310720 | tf_op jit(solution)/shard_map/pallas_call | solution.py:626
  26.1 0.0 collective-permute-done.8.refs_2_
  26.1 0.7 %collective-permute-done.9.refs_3_ = f32[56,128]{1,0:T(8,128)S(1)} collective-permute-done((f32[56,128]{1,0:T(8,128)S(1)}, f32[56,128]{1,0:T(8,128)S(1)}, u32[]{:S(2)}, u32[]{:S(2)}) %collective-permute-start.9) | collective-permute-done | bytes 28704 | tf_op jit(solution)/shard_map/ppermute | solution.py:655
  26.8 1.2 %collective-permute-start.10 = (f32[104,128]{1,0:T(8,128)S(1)}, f32[104,128]{1,0:T(8,128)S(1)}, u32[]{:S(2)}, u32[]{:S(2)}) collective-permute-start(f32[104,128]{1,0:T(8,128)S(1)} %get-tuple-element.136.refs_17_), channel_id=1, source_target_pairs={{0,4},{4,8},{8,12},{12,0},{1,5},{5,9},{9,13},{13,1},{2,6},{6,10},{... | collective-permute-start | bytes 159752 | tf_op jit(solution)/shard_map/ppermute | solution.py:644
  28.0 2.7 %collective-permute-start.11 = (f32[104,128]{1,0:T(8,128)S(1)}, f32[104,128]{1,0:T(8,128)S(1)}, u32[]{:S(2)}, u32[]{:S(2)}) collective-permute-start(f32[104,128]{1,0:T(8,128)S(1)} %get-tuple-element.137.refs_18_), channel_id=1, source_target_pairs={{4,0},{8,4},{12,8},{0,12},{5,1},{9,5},{13,9},{1,13},{6,2},{10,6},{... | collective-permute-start | bytes 159752 | tf_op jit(solution)/shard_map/ppermute | solution.py:645
  30.7 2.2 %collective-permute-done.10.refs_13_.refs_7_ = f32[104,128]{1,0:T(8,128)S(1)} collective-permute-done((f32[104,128]{1,0:T(8,128)S(1)}, f32[104,128]{1,0:T(8,128)S(1)}, u32[]{:S(2)}, u32[]{:S(2)}) %collective-permute-start.10) | collective-permute-done | bytes 53280 | tf_op jit(solution)/shard_map/ppermute | solution.py:644
  32.9 0.3 collective-permute-done.11.refs_14_.refs_8_
  33.3 0.4 shard_map.79
  33.7 0.1 collective-permute-start.12
  33.8 1.7 %collective-permute-start.13 = (f32[56,128]{1,0:T(8,128)S(1)}, f32[56,128]{1,0:T(8,128)S(1)}, u32[]{:S(2)}, u32[]{:S(2)}) collective-permute-start(f32[56,128]{1,0:T(8,128)S(1)} %get-tuple-element.147), channel_id=1, source_target_pairs={{0,3},{1,2},{2,1},{3,0},{4,7},{5,6},{6,5},{7,4},{8,11},{9,10},{10,... | collective-permute-start | bytes 86024 | tf_op jit(solution)/shard_map/ppermute | solution.py:655
  35.5 0.9 %shard_map.80 = (f32[19,14,8,128]{3,2,1,0:T(8,128)S(1)}, f32[104,128]{1,0:T(8,128)S(1)}, f32[104,128]{1,0:T(8,128)S(1)}, f32[14,8,128]{2,1,0:T(8,128)S(1)}) custom-call(f32[19,8,128]{2,1,0:T(8,128)S(1)} %get-tuple-element.93.refs_0_, s32[16,8,128]{2,1,0:T(8,128)S(1)} %get-tuple-element.100.refs_1_.bits_ref, f32[18,24,128]{2,1,0:T(8,128)S(1)} %get-tuple-element.139.refs_2_, ...), custom_call_target="tpu_custom_call" | custom-call | flops 6553600 | bytes 1310720 | tf_op jit(solution)/shard_map/pallas_call | solution.py:626
  36.4 0.0 collective-permute-done.12.refs_2_
  36.4 0.7 %collective-permute-done.13.refs_3_ = f32[56,128]{1,0:T(8,128)S(1)} collective-permute-done((f32[56,128]{1,0:T(8,128)S(1)}, f32[56,128]{1,0:T(8,128)S(1)}, u32[]{:S(2)}, u32[]{:S(2)}) %collective-permute-start.13) | collective-permute-done | bytes 28704 | tf_op jit(solution)/shard_map/ppermute | solution.py:655
  37.2 1.3 %collective-permute-start.14 = (f32[104,128]{1,0:T(8,128)S(1)}, f32[104,128]{1,0:T(8,128)S(1)}, u32[]{:S(2)}, u32[]{:S(2)}) collective-permute-start(f32[104,128]{1,0:T(8,128)S(1)} %get-tuple-element.152.refs_17_), channel_id=1, source_target_pairs={{0,4},{4,8},{8,12},{12,0},{1,5},{5,9},{9,13},{13,1},{2,6},{6,10},{... | collective-permute-start | bytes 159752 | tf_op jit(solution)/shard_map/ppermute | solution.py:644
  38.5 2.6 %collective-permute-start.15 = (f32[104,128]{1,0:T(8,128)S(1)}, f32[104,128]{1,0:T(8,128)S(1)}, u32[]{:S(2)}, u32[]{:S(2)}) collective-permute-start(f32[104,128]{1,0:T(8,128)S(1)} %get-tuple-element.153.refs_18_), channel_id=1, source_target_pairs={{4,0},{8,4},{12,8},{0,12},{5,1},{9,5},{13,9},{1,13},{6,2},{10,6},{... | collective-permute-start | bytes 159752 | tf_op jit(solution)/shard_map/ppermute | solution.py:645
  41.0 2.2 %collective-permute-done.14.refs_13_.refs_7_ = f32[104,128]{1,0:T(8,128)S(1)} collective-permute-done((f32[104,128]{1,0:T(8,128)S(1)}, f32[104,128]{1,0:T(8,128)S(1)}, u32[]{:S(2)}, u32[]{:S(2)}) %collective-permute-start.14) | collective-permute-done | bytes 53280 | tf_op jit(solution)/shard_map/ppermute | solution.py:644
  43.3 0.5 collective-permute-done.15.refs_14_.refs_8_
  43.7 0.4 shard_map.82
  44.1 0.1 collective-permute-start.16
  44.2 1.7 %collective-permute-start.17 = (f32[48,128]{1,0:T(8,128)S(1)}, f32[48,128]{1,0:T(8,128)S(1)}, u32[]{:S(2)}, u32[]{:S(2)}) collective-permute-start(f32[48,128]{1,0:T(8,128)S(1)} %get-tuple-element.162), channel_id=1, source_target_pairs={{0,3},{1,2},{2,1},{3,0},{4,7},{5,6},{6,5},{7,4},{8,11},{9,10},{10,... | collective-permute-start | bytes 73736 | tf_op jit(solution)/shard_map/ppermute | solution.py:655
  46.0 0.9 %shard_map.83 = (f32[19,14,8,128]{3,2,1,0:T(8,128)S(1)}, f32[80,128]{1,0:T(8,128)S(1)}, f32[80,128]{1,0:T(8,128)S(1)}, f32[3,128,128]{2,1,0:T(8,128)S(1)}) custom-call(f32[19,8,128]{2,1,0:T(8,128)S(1)} %get-tuple-element.93.refs_0_, s32[16,8,128]{2,1,0:T(8,128)S(1)} %get-tuple-element.100.refs_1_.bits_ref, f32[18,24,128]{2,1,0:T(8,128)S(1)} %get-tuple-element.155.refs_2_, ...), custom_call_target="tpu_custom_call" | custom-call | flops 6553600 | bytes 1310720 | tf_op jit(solution)/shard_map/pallas_call | solution.py:626
  46.9 0.0 collective-permute-done.16.refs_2_
  46.9 0.6 %collective-permute-done.17.refs_3_ = f32[48,128]{1,0:T(8,128)S(1)} collective-permute-done((f32[48,128]{1,0:T(8,128)S(1)}, f32[48,128]{1,0:T(8,128)S(1)}, u32[]{:S(2)}, u32[]{:S(2)}) %collective-permute-start.17) | collective-permute-done | bytes 24608 | tf_op jit(solution)/shard_map/ppermute | solution.py:655
  47.5 1.2 %collective-permute-start.18 = (f32[80,128]{1,0:T(8,128)S(1)}, f32[80,128]{1,0:T(8,128)S(1)}, u32[]{:S(2)}, u32[]{:S(2)}) collective-permute-start(f32[80,128]{1,0:T(8,128)S(1)} %get-tuple-element.171), channel_id=1, source_target_pairs={{0,4},{4,8},{8,12},{12,0},{1,5},{5,9},{9,13},{13,1},{2,6},{6,10},{... | collective-permute-start | bytes 122888 | tf_op jit(solution)/shard_map/ppermute | solution.py:644
  48.7 2.7 %collective-permute-start.19 = (f32[80,128]{1,0:T(8,128)S(1)}, f32[80,128]{1,0:T(8,128)S(1)}, u32[]{:S(2)}, u32[]{:S(2)}) collective-permute-start(f32[80,128]{1,0:T(8,128)S(1)} %get-tuple-element.172), channel_id=1, source_target_pairs={{4,0},{8,4},{12,8},{0,12},{5,1},{9,5},{13,9},{1,13},{6,2},{10,6},{... | collective-permute-start | bytes 122888 | tf_op jit(solution)/shard_map/ppermute | solution.py:645
  51.4 1.3 %shard_map.85 = (f32[19,128,128]{2,1,0:T(8,128)}, f32[19,128,128]{2,1,0:T(8,128)S(1)}, f32[3,128,128]{2,1,0:T(8,128)}) custom-call(f32[19,2,8,128]{3,2,1,0:T(8,128)S(1)} %get-tuple-element.154.f_edge, f32[19,14,8,128]{3,2,1,0:T(8,128)S(1)} %get-tuple-element.158.f_middle, s32[16,8,128]{2,1,0:T(8,128)S(1)} %get-tuple-element.100.refs_1_.bits_ref, ...), custom_call_target="tpu_custom_call" | custom-call | flops 6553600 | bytes 1310720 | tf_op jit(solution)/shard_map/pallas_call | solution.py:626
  52.7 0.7 %collective-permute-done.18.yd = f32[80,128]{1,0:T(8,128)S(1)} collective-permute-done((f32[80,128]{1,0:T(8,128)S(1)}, f32[80,128]{1,0:T(8,128)S(1)}, u32[]{:S(2)}, u32[]{:S(2)}) %collective-permute-start.18) | collective-permute-done | bytes 40992 | tf_op jit(solution)/shard_map/ppermute | solution.py:644
  53.4 0.2 collective-permute-done.19.yu
  53.6 0.7 %shard_map.86 = f32[19,128,128]{2,1,0:T(8,128)} custom-call(f32[19,128,128]{2,1,0:T(8,128)} %get-tuple-element.168.out_in, f32[19,128,128]{2,1,0:T(8,128)S(1)} %get-tuple-element.169.flat_ref, f32[2,128,128]{2,1,0:T(8,128)S(1)} %get-tuple-element.170.mask_ref, f32[80,128]{1,0:T(8,128)S(1)} %collective-permute-done.18.yd, ...), custom_call_target="tpu_custom_call", output_to_operand_aliasing={{}: (0, {})} | custom-call | tf_op jit(solution)/shard_map/pallas_call | solution.py:626
  (5 shorter events, 0.1 us)
Async XLA Ops:
  0.6 6.5 %copy-start.3 = (f32[4]{0:T(128)S(1)}, f32[4]{0:T(128)}, u32[]{:S(2)}) copy-start(f32[4]{0:T(128)} %wall_ref) | copy-start | bytes 52
  0.6 6.5 %copy-start.2 = (s32[8,16,128]{2,1,0:T(8,128)S(1)}, s32[8,16,128]{2,1,0:T(8,128)}, u32[]{:S(2)}) copy-start(s32[8,16,128]{2,1,0:T(8,128)} %param.7) | copy-start | bytes 196612
  0.7 6.5 %copy-start.1 = (s32[8,16,128]{2,1,0:T(8,128)S(1)}, s32[8,16,128]{2,1,0:T(8,128)}, u32[]{:S(2)}) copy-start(s32[8,16,128]{2,1,0:T(8,128)} %param.6) | copy-start | bytes 196612
  0.7 6.5 %copy-start = (f32[19,8,16,128]{3,2,1,0:T(8,128)S(1)}, f32[19,8,16,128]{3,2,1,0:T(8,128)}, u32[]{:S(2)}) copy-start(f32[19,8,16,128]{3,2,1,0:T(8,128)} %param.5) | copy-start | bytes 3735556
  0.7 6.5 %copy-start.4 = (f32[19]{0:T(128)S(1)}, f32[19]{0:T(128)}, u32[]{:S(2)}) copy-start(f32[19]{0:T(128)} %rate_ref.1) | copy-start | bytes 232
  1.9 6.9 %collective-permute-start = (f32[32,128]{1,0:T(8,128)S(1)}, f32[32,128]{1,0:T(8,128)S(1)}, u32[]{:S(2)}, u32[]{:S(2)}) collective-permute-start(f32[32,128]{1,0:T(8,128)S(1)} %get-tuple-element.95), channel_id=1, source_target_pairs={{0,4},{4,8},{8,12},{12,0},{1,5},{5,9},{9,13},{13,1},{2,6},{6,10},{... | collective-permute-start | bytes 49160 | tf_op jit(solution)/shard_map/ppermute | solution.py:644
  5.0 3.9 %collective-permute-start.1 = (f32[32,128]{1,0:T(8,128)S(1)}, f32[32,128]{1,0:T(8,128)S(1)}, u32[]{:S(2)}, u32[]{:S(2)}) collective-permute-start(f32[32,128]{1,0:T(8,128)S(1)} %get-tuple-element.96), channel_id=1, source_target_pairs={{4,0},{8,4},{12,8},{0,12},{5,1},{9,5},{13,9},{1,13},{6,2},{10,6},{... | collective-permute-start | bytes 49160 | tf_op jit(solution)/shard_map/ppermute | solution.py:645
  9.0 2.0 %collective-permute-start.2 = (f32[24,128]{1,0:T(8,128)S(1)}, f32[24,128]{1,0:T(8,128)S(1)}, u32[]{:S(2)}, u32[]{:S(2)}) collective-permute-start(f32[24,128]{1,0:T(8,128)S(1)} %get-tuple-element.98), channel_id=1, source_target_pairs={{0,1},{1,0},{2,3},{3,2},{4,5},{5,4},{6,7},{7,6},{8,9},{9,8},{10,11... | collective-permute-start | bytes 36872 | tf_op jit(solution)/shard_map/ppermute | solution.py:656
  9.1 3.2 %collective-permute-start.3 = (f32[24,128]{1,0:T(8,128)S(1)}, f32[24,128]{1,0:T(8,128)S(1)}, u32[]{:S(2)}, u32[]{:S(2)}) collective-permute-start(f32[24,128]{1,0:T(8,128)S(1)} %get-tuple-element.99), channel_id=1, source_target_pairs={{0,3},{1,2},{2,1},{3,0},{4,7},{5,6},{6,5},{7,4},{8,11},{9,10},{10,... | collective-permute-start | bytes 36872 | tf_op jit(solution)/shard_map/ppermute | solution.py:655
  12.6 2.6 %collective-permute-start.4 = (f32[56,128]{1,0:T(8,128)S(1)}, f32[56,128]{1,0:T(8,128)S(1)}, u32[]{:S(2)}, u32[]{:S(2)}) collective-permute-start(f32[56,128]{1,0:T(8,128)S(1)} %get-tuple-element.114), channel_id=1, source_target_pairs={{0,1},{1,0},{2,3},{3,2},{4,5},{5,4},{6,7},{7,6},{8,9},{9,8},{10,11... | collective-permute-start | bytes 86024 | tf_op jit(solution)/shard_map/ppermute | solution.py:656
  13.1 3.3 %collective-permute-start.5 = (f32[56,128]{1,0:T(8,128)S(1)}, f32[56,128]{1,0:T(8,128)S(1)}, u32[]{:S(2)}, u32[]{:S(2)}) collective-permute-start(f32[56,128]{1,0:T(8,128)S(1)} %get-tuple-element.115), channel_id=1, source_target_pairs={{0,3},{1,2},{2,1},{3,0},{4,7},{5,6},{6,5},{7,4},{8,11},{9,10},{10,... | collective-permute-start | bytes 86024 | tf_op jit(solution)/shard_map/ppermute | solution.py:655
  16.5 6.0 %collective-permute-start.6 = (f32[104,128]{1,0:T(8,128)S(1)}, f32[104,128]{1,0:T(8,128)S(1)}, u32[]{:S(2)}, u32[]{:S(2)}) collective-permute-start(f32[104,128]{1,0:T(8,128)S(1)} %get-tuple-element.120.refs_17_), channel_id=1, source_target_pairs={{0,4},{4,8},{8,12},{12,0},{1,5},{5,9},{9,13},{13,1},{2,6},{6,10},{... | collective-permute-start | bytes 159752 | tf_op jit(solution)/shard_map/ppermute | solution.py:644
  18.0 5.0 %collective-permute-start.7 = (f32[104,128]{1,0:T(8,128)S(1)}, f32[104,128]{1,0:T(8,128)S(1)}, u32[]{:S(2)}, u32[]{:S(2)}) collective-permute-start(f32[104,128]{1,0:T(8,128)S(1)} %get-tuple-element.121.refs_18_), channel_id=1, source_target_pairs={{4,0},{8,4},{12,8},{0,12},{5,1},{9,5},{13,9},{1,13},{6,2},{10,6},{... | collective-permute-start | bytes 159752 | tf_op jit(solution)/shard_map/ppermute | solution.py:645
  23.3 2.7 %collective-permute-start.8 = (f32[56,128]{1,0:T(8,128)S(1)}, f32[56,128]{1,0:T(8,128)S(1)}, u32[]{:S(2)}, u32[]{:S(2)}) collective-permute-start(f32[56,128]{1,0:T(8,128)S(1)} %get-tuple-element.130), channel_id=1, source_target_pairs={{0,1},{1,0},{2,3},{3,2},{4,5},{5,4},{6,7},{7,6},{8,9},{9,8},{10,11... | collective-permute-start | bytes 86024 | tf_op jit(solution)/shard_map/ppermute | solution.py:656
  23.4 3.4 %collective-permute-start.9 = (f32[56,128]{1,0:T(8,128)S(1)}, f32[56,128]{1,0:T(8,128)S(1)}, u32[]{:S(2)}, u32[]{:S(2)}) collective-permute-start(f32[56,128]{1,0:T(8,128)S(1)} %get-tuple-element.131), channel_id=1, source_target_pairs={{0,3},{1,2},{2,1},{3,0},{4,7},{5,6},{6,5},{7,4},{8,11},{9,10},{10,... | collective-permute-start | bytes 86024 | tf_op jit(solution)/shard_map/ppermute | solution.py:655
  26.8 6.1 %collective-permute-start.10 = (f32[104,128]{1,0:T(8,128)S(1)}, f32[104,128]{1,0:T(8,128)S(1)}, u32[]{:S(2)}, u32[]{:S(2)}) collective-permute-start(f32[104,128]{1,0:T(8,128)S(1)} %get-tuple-element.136.refs_17_), channel_id=1, source_target_pairs={{0,4},{4,8},{8,12},{12,0},{1,5},{5,9},{9,13},{13,1},{2,6},{6,10},{... | collective-permute-start | bytes 159752 | tf_op jit(solution)/shard_map/ppermute | solution.py:644
  28.0 5.3 %collective-permute-start.11 = (f32[104,128]{1,0:T(8,128)S(1)}, f32[104,128]{1,0:T(8,128)S(1)}, u32[]{:S(2)}, u32[]{:S(2)}) collective-permute-start(f32[104,128]{1,0:T(8,128)S(1)} %get-tuple-element.137.refs_18_), channel_id=1, source_target_pairs={{4,0},{8,4},{12,8},{0,12},{5,1},{9,5},{13,9},{1,13},{6,2},{10,6},{... | collective-permute-start | bytes 159752 | tf_op jit(solution)/shard_map/ppermute | solution.py:645
  33.7 2.7 %collective-permute-start.12 = (f32[56,128]{1,0:T(8,128)S(1)}, f32[56,128]{1,0:T(8,128)S(1)}, u32[]{:S(2)}, u32[]{:S(2)}) collective-permute-start(f32[56,128]{1,0:T(8,128)S(1)} %get-tuple-element.146), channel_id=1, source_target_pairs={{0,1},{1,0},{2,3},{3,2},{4,5},{5,4},{6,7},{7,6},{8,9},{9,8},{10,11... | collective-permute-start | bytes 86024 | tf_op jit(solution)/shard_map/ppermute | solution.py:656
  33.8 3.4 %collective-permute-start.13 = (f32[56,128]{1,0:T(8,128)S(1)}, f32[56,128]{1,0:T(8,128)S(1)}, u32[]{:S(2)}, u32[]{:S(2)}) collective-permute-start(f32[56,128]{1,0:T(8,128)S(1)} %get-tuple-element.147), channel_id=1, source_target_pairs={{0,3},{1,2},{2,1},{3,0},{4,7},{5,6},{6,5},{7,4},{8,11},{9,10},{10,... | collective-permute-start | bytes 86024 | tf_op jit(solution)/shard_map/ppermute | solution.py:655
  37.2 6.1 %collective-permute-start.14 = (f32[104,128]{1,0:T(8,128)S(1)}, f32[104,128]{1,0:T(8,128)S(1)}, u32[]{:S(2)}, u32[]{:S(2)}) collective-permute-start(f32[104,128]{1,0:T(8,128)S(1)} %get-tuple-element.152.refs_17_), channel_id=1, source_target_pairs={{0,4},{4,8},{8,12},{12,0},{1,5},{5,9},{9,13},{13,1},{2,6},{6,10},{... | collective-permute-start | bytes 159752 | tf_op jit(solution)/shard_map/ppermute | solution.py:644
  38.5 5.3 %collective-permute-start.15 = (f32[104,128]{1,0:T(8,128)S(1)}, f32[104,128]{1,0:T(8,128)S(1)}, u32[]{:S(2)}, u32[]{:S(2)}) collective-permute-start(f32[104,128]{1,0:T(8,128)S(1)} %get-tuple-element.153.refs_18_), channel_id=1, source_target_pairs={{4,0},{8,4},{12,8},{0,12},{5,1},{9,5},{13,9},{1,13},{6,2},{10,6},{... | collective-permute-start | bytes 159752 | tf_op jit(solution)/shard_map/ppermute | solution.py:645
  44.1 2.8 %collective-permute-start.16 = (f32[48,128]{1,0:T(8,128)S(1)}, f32[48,128]{1,0:T(8,128)S(1)}, u32[]{:S(2)}, u32[]{:S(2)}) collective-permute-start(f32[48,128]{1,0:T(8,128)S(1)} %get-tuple-element.161), channel_id=1, source_target_pairs={{0,1},{1,0},{2,3},{3,2},{4,5},{5,4},{6,7},{7,6},{8,9},{9,8},{10,11... | collective-permute-start | bytes 73736 | tf_op jit(solution)/shard_map/ppermute | solution.py:656
  44.2 3.3 %collective-permute-start.17 = (f32[48,128]{1,0:T(8,128)S(1)}, f32[48,128]{1,0:T(8,128)S(1)}, u32[]{:S(2)}, u32[]{:S(2)}) collective-permute-start(f32[48,128]{1,0:T(8,128)S(1)} %get-tuple-element.162), channel_id=1, source_target_pairs={{0,3},{1,2},{2,1},{3,0},{4,7},{5,6},{6,5},{7,4},{8,11},{9,10},{10,... | collective-permute-start | bytes 73736 | tf_op jit(solution)/shard_map/ppermute | solution.py:655
  47.5 5.9 %collective-permute-start.18 = (f32[80,128]{1,0:T(8,128)S(1)}, f32[80,128]{1,0:T(8,128)S(1)}, u32[]{:S(2)}, u32[]{:S(2)}) collective-permute-start(f32[80,128]{1,0:T(8,128)S(1)} %get-tuple-element.171), channel_id=1, source_target_pairs={{0,4},{4,8},{8,12},{12,0},{1,5},{5,9},{9,13},{13,1},{2,6},{6,10},{... | collective-permute-start | bytes 122888 | tf_op jit(solution)/shard_map/ppermute | solution.py:644
  48.7 4.9 %collective-permute-start.19 = (f32[80,128]{1,0:T(8,128)S(1)}, f32[80,128]{1,0:T(8,128)S(1)}, u32[]{:S(2)}, u32[]{:S(2)}) collective-permute-start(f32[80,128]{1,0:T(8,128)S(1)} %get-tuple-element.172), channel_id=1, source_target_pairs={{4,0},{8,4},{12,8},{0,12},{5,1},{9,5},{13,9},{1,13},{6,2},{10,6},{... | collective-permute-start | bytes 122888 | tf_op jit(solution)/shard_map/ppermute | solution.py:645

commit v10 on v9

--- a/solution.py
+++ b/solution.py
@@ -187,22 +187,45 @@
         ref[layers:] = jnp.where(pore, 1.0, 0.0)
 
 
-def turn_kernel(raw_ref, mask_in, wet_in, wall_ref, rate_ref, f_ref, rates_ref, flat_ref, mask_ref, pot_ref):
+def turn_kernel(f_hbm, mask_hbm, wet_hbm, wall_hbm, rate_hbm, after_ref, *refs):
+    del after_ref
+    f_ref, rates_ref, flat_ref, mask_ref, pot_ref = refs[:5]
+    raw, mask_in, wet_in, wall_in, rate_in, f_sems, sems = refs[5:]
     layers, rows = f_ref.shape[1], f_ref.shape[2]
+    small = [
+        pltpu.make_async_copy(source, target, sems.at[i])
+        for i, (source, target) in enumerate(
+            (
+                (wall_hbm, wall_in),
+                (rate_hbm, rate_in),
+                (mask_hbm, mask_in),
+                (wet_hbm, wet_in),
+            )
+        )
+    ]
+    large = [pltpu.make_async_copy(f_hbm.at[k], raw.at[k], f_sems.at[k]) for k in range(N)]
+    for copy in small + large:
+        copy.start()
+    for copy in small:
+        copy.wait()
     for k in range(N):
-        rates_ref[k] = jnp.full(rates_ref.shape[1:], rate_ref[k], jnp.float32)
-    for i in range(0, layers * rows, TILE):
-        at = slice(i, i + TILE)
-        pore = mask_in[at] == 1
-        density = total([raw_ref[k, at] for k in range(N)])
-        flat_ref[0, at] = jnp.where(pore, 1.0, 0.0)
-        flat_ref[1, at] = potential_of(density, pore, wall_of(wet_in[at], wall_ref))
+        rates_ref[k] = jnp.full(rates_ref.shape[1:], rate_in[k], jnp.float32)
+    blocks = [slice(i, i + TILE) for i in range(0, layers * rows, TILE)]
+    for at in blocks:
+        flat_ref[0, at] = jnp.where(mask_in[at] == 1, 1.0, 0.0)
+        flat_ref[1, at] = wall_of(wet_in[at], wall_in)
+    density = None
+    for k, copy in enumerate(large):
+        copy.wait()
+        for i in range(layers):
+            f_ref[k, i] = raw[k, pl.ds(i, rows, stride=layers)]
+        here = [raw[k, at] for at in blocks]
+        density = here if density is None else [a + b for a, b in zip(density, here)]
+    for at, value in zip(blocks, density):
+        flat_ref[1, at] = potential_of(value, flat_ref[0, at] > 0.5, flat_ref[1, at])
     for i in range(layers):
         mask_ref[i] = flat_ref[0, pl.ds(i, rows, stride=layers)]
         pot_ref[i] = flat_ref[1, pl.ds(i, rows, stride=layers)]
-    for k in range(N):
-        for i in range(layers):
-            f_ref[k, i] = raw_ref[k, pl.ds(i, rows, stride=layers)]
 
 
 def start_pack_kernel(pairs, pot_ref, mask_ref, from_below, from_above, a_ref, b_ref, left_ref, right_ref):
@@ -617,7 +640,6 @@
 
 
 VMEM = pl.BlockSpec(memory_space=pltpu.VMEM)
-SMEM = pl.BlockSpec(memory_space=pltpu.SMEM)
 HBM = pl.BlockSpec(memory_space=pltpu.HBM)
 
 
@@ -671,19 +693,23 @@
     operations = 400 * cells * size_z
     cost = pl.CostEstimate(flops=operations, bytes_accessed=4 * operations // 20, transcendentals=0)
 
-    operands = (
-        populations.reshape(N, cells, size_z),
-        fluid_mask.reshape(cells, size_z),
-        wet_class.reshape(cells, size_z),
-        wall_potential,
-    )
+    operands = [
+        pltpu.with_memory_space_constraint(item, pltpu.HBM)
+        for item in (
+            populations.reshape(N, cells, size_z),
+            fluid_mask.reshape(cells, size_z),
+            wet_class.reshape(cells, size_z),
+            wall_potential,
+            relax_rates,
+        )
+    ]
     row_face = rows(2 * size_x)
     layer_face = rows(2 * size_y + TILE)
     ring_rows = rows(2 * size_x + TILE)
     up, down = call(
         face_kernel,
         [row_face, row_face],
-        [pltpu.with_memory_space_constraint(item, pltpu.HBM) for item in operands],
+        operands[:4],
         special={i: HBM for i in range(4)},
         scratch=[
             (2, N, size_x, size_z),
@@ -693,13 +719,21 @@
             pltpu.SemaphoreType.DMA((7,)),
         ],
     )
-    *operands, up = lax.optimization_barrier((*operands, up))
     below, above = shift(up, down, "gx")
     f, rates, flat_mask, mask, pot0 = call(
         turn_kernel,
         [fields(size_x), ((N, TILE, size_z), f32), flat(2), whole, whole],
-        (*operands, relax_rates),
-        special={3: SMEM, 4: SMEM},
+        (*operands, up),
+        special={i: HBM for i in range(5)},
+        scratch=[
+            flat(N)[0],
+            pltpu.VMEM((cells, size_z), i32),
+            pltpu.VMEM((cells, size_z), i32),
+            pltpu.SMEM(wall_potential.shape, f32),
+            pltpu.SMEM(relax_rates.shape, f32),
+            pltpu.SemaphoreType.DMA((N,)),
+            pltpu.SemaphoreType.DMA((4,)),
+        ],
         cost=cost,
     )
     a, b = call(

time: 54.5 us -> 57.7 us (1.059)
  waiting for transfers between devices: 14.1 us -> 17 us
  Pallas kernels: 9.77 us -> 10.7 us
  starting transfers between devices: 29.6 us -> 28.9 us
    ppermute x5, starting transfers between devices: 8.24 us -> 2.97 us  [shift(): lax.ppermute(forward, axis, ahead)]
    ppermute x5, starting transfers between devices: 12.5 us -> 17.7 us  [shift(): lax.ppermute(backward, axis, [(b, a) for a, b in ahead])]
    ppermute x5, waiting for transfers between devices: 7.95 us -> 11.1 us  [shift(): lax.ppermute(forward, axis, ahead)]
    pallas_call x19, Pallas kernels: 9.77 us -> 10.7 us  [call(): pl.pallas_call(kernel, out_shape=[jax.ShapeDtypeStruct(shape, dtype) for...]
    ppermute x5, waiting for transfers between devices: 1.56 us -> 0.69 us  [shift(): lax.ppermute(backward, axis, [(b, a) for a, b in ahead])]
    ppermute x5, starting transfers between devices: 8.13 us -> 7.54 us  [swap(): b = lax.ppermute(b, axis, partners[1])]
  transfers between devices with their start and end apart: 20 -> 20, of which waited for: 15 -> 12; matrix products, arithmetic and copies ran while one was open for 0% -> 0% of each run, Pallas kernels for 11% -> 12%
where the time goes in v10:
time: 57.7 us; the launch traced here: 57.5 us
  starting transfers between devices  28.9 us (50%)
  waiting for transfers between devices  17 us (29%)
  Pallas kernels  10.7 us (19%)
  between operations  0.82 us (1%)
    ppermute x5, starting transfers between devices, shift(): lax.ppermute(backward, axis, [(b, a) for a, b in ahead])  17.7 us
    ppermute x5, waiting for transfers between devices, shift(): lax.ppermute(forward, axis, ahead)  11.1 us
    pallas_call x19, Pallas kernels, call(): pl.pallas_call(kernel, out_shape=[jax.ShapeDtypeStruct(shape, dtype) for...  10.7 us
    ppermute x5, starting transfers between devices, swap(): b = lax.ppermute(b, axis, partners[1])  7.54 us
    ppermute x5, waiting for transfers between devices, swap(): b = lax.ppermute(b, axis, partners[1])  5.15 us
    ppermute x5, starting transfers between devices, shift(): lax.ppermute(forward, axis, ahead)  2.97 us
  transfers between devices with their start and end apart: 20, of which 12 were waited for; matrix products, arithmetic and copies ran while one was open for 0% of the time, Pallas kernels for 12%

profile of v10, /device:TPU:0, one launch (start us, length us, event | category | flops | bytes accessed | tf_op | source)
XLA Modules:
  0.0 57.5 jit_solution(11319950293188653478)
XLA Ops:
  0.6 1.1 %shard_map.68 = (f32[32,128]{1,0:T(8,128)S(1)}, f32[32,128]{1,0:T(8,128)S(1)}) custom-call(f32[19,128,128]{2,1,0:T(8,128)} %bitcast.5, s32[128,128]{1,0:T(8,128)} %bitcast.8, s32[128,128]{1,0:T(8,128)} %bitcast.10, f32[4]{0:T(128)} %wall_hbm.3), custom_call_target="tpu_custom_call" | custom-call | tf_op jit(solution)/shard_map/pallas_call | solution.py:648
  1.8 5.1 %collective-permute-start.1 = (f32[32,128]{1,0:T(8,128)S(1)}, f32[32,128]{1,0:T(8,128)S(1)}, u32[]{:S(2)}, u32[]{:S(2)}) collective-permute-start(f32[32,128]{1,0:T(8,128)S(1)} %get-tuple-element.86), channel_id=1, source_target_pairs={{4,0},{8,4},{12,8},{0,12},{5,1},{9,5},{13,9},{1,13},{6,2},{10,6},{... | collective-permute-start | bytes 49160 | tf_op jit(solution)/shard_map/ppermute | solution.py:667
  6.9 0.0 collective-permute-start
  6.9 2.1 %shard_map.69 = (f32[19,16,8,128]{3,2,1,0:T(8,128)S(1)}, f32[19,8,128]{2,1,0:T(8,128)S(1)}, f32[2,128,128]{2,1,0:T(8,128)S(1)}, f32[16,8,128]{2,1,0:T(8,128)S(1)}, f32[16,8,128]{2,1,0:T(8,128)S(1)}) custom-call(f32[19,128,128]{2,1,0:T(8,128)} %bitcast.6, s32[128,128]{1,0:T(8,128)} %bitcast.9, s32[128,128]{1,0:T(8,128)} %bitcast.11, f32[4]{0:T(128)} %wall_hbm.3, ...), custom_call_target="tpu_custom_call" | custom-call | flops 6553600 | bytes 1310720 | tf_op jit(solution)/shard_map/pallas_call | solution.py:648
  9.0 0.0 collective-permute-done.1.from_above
  9.0 3.4 %collective-permute-done.from_below = f32[32,128]{1,0:T(8,128)S(1)} collective-permute-done((f32[32,128]{1,0:T(8,128)S(1)}, f32[32,128]{1,0:T(8,128)S(1)}, u32[]{:S(2)}, u32[]{:S(2)}) %collective-permute-start) | collective-permute-done | bytes 16416 | tf_op jit(solution)/shard_map/ppermute | solution.py:666
  12.5 0.1 collective-permute-start.2
  12.5 1.6 %collective-permute-start.3 = (f32[24,128]{1,0:T(8,128)S(1)}, f32[24,128]{1,0:T(8,128)S(1)}, u32[]{:S(2)}, u32[]{:S(2)}) collective-permute-start(f32[24,128]{1,0:T(8,128)S(1)} %get-tuple-element.89), channel_id=1, source_target_pairs={{0,3},{1,2},{2,1},{3,0},{4,7},{5,6},{6,5},{7,4},{8,11},{9,10},{10,... | collective-permute-start | bytes 36872 | tf_op jit(solution)/shard_map/ppermute | solution.py:677
  14.1 0.2 shard_map.70.bits_in
  14.4 0.0 collective-permute-done.2.a_ref
  14.4 1.3 %collective-permute-done.3.b_ref = f32[24,128]{1,0:T(8,128)S(1)} collective-permute-done((f32[24,128]{1,0:T(8,128)S(1)}, f32[24,128]{1,0:T(8,128)S(1)}, u32[]{:S(2)}, u32[]{:S(2)}) %collective-permute-start.3) | collective-permute-done | bytes 12320 | tf_op jit(solution)/shard_map/ppermute | solution.py:677
  15.7 0.1 shard_map.72
  15.8 0.3 shard_map.73
  16.1 0.5 collective-permute-start.4
  16.6 1.2 %collective-permute-start.5 = (f32[56,128]{1,0:T(8,128)S(1)}, f32[56,128]{1,0:T(8,128)S(1)}, u32[]{:S(2)}, u32[]{:S(2)}) collective-permute-start(f32[56,128]{1,0:T(8,128)S(1)} %get-tuple-element.105), channel_id=1, source_target_pairs={{0,3},{1,2},{2,1},{3,0},{4,7},{5,6},{6,5},{7,4},{8,11},{9,10},{10,... | collective-permute-start | bytes 86024 | tf_op jit(solution)/shard_map/ppermute | solution.py:677
  17.8 0.8 %shard_map.74 = (f32[19,14,8,128]{3,2,1,0:T(8,128)S(1)}, f32[104,128]{1,0:T(8,128)S(1)}, f32[104,128]{1,0:T(8,128)S(1)}, f32[14,8,128]{2,1,0:T(8,128)S(1)}) custom-call(f32[19,8,128]{2,1,0:T(8,128)S(1)} %get-tuple-element.84.refs_0_, s32[16,8,128]{2,1,0:T(8,128)S(1)} %get-tuple-element.90.refs_1_.bits_ref, f32[18,24,128]{2,1,0:T(8,128)S(1)} %get-tuple-element.97.refs_2_, ...), custom_call_target="tpu_custom_call" | custom-call | flops 6553600 | bytes 1310720 | tf_op jit(solution)/shard_map/pallas_call | solution.py:648
  18.7 0.0 collective-permute-done.4.refs_2_
  18.7 1.3 %collective-permute-done.5.refs_3_ = f32[56,128]{1,0:T(8,128)S(1)} collective-permute-done((f32[56,128]{1,0:T(8,128)S(1)}, f32[56,128]{1,0:T(8,128)S(1)}, u32[]{:S(2)}, u32[]{:S(2)}) %collective-permute-start.5) | collective-permute-done | bytes 28704 | tf_op jit(solution)/shard_map/ppermute | solution.py:677
  20.0 0.1 collective-permute-start.6
  20.1 3.8 %collective-permute-start.7 = (f32[104,128]{1,0:T(8,128)S(1)}, f32[104,128]{1,0:T(8,128)S(1)}, u32[]{:S(2)}, u32[]{:S(2)}) collective-permute-start(f32[104,128]{1,0:T(8,128)S(1)} %get-tuple-element.111.refs_18_), channel_id=1, source_target_pairs={{4,0},{8,4},{12,8},{0,12},{5,1},{9,5},{13,9},{1,13},{6,2},{10,6},{... | collective-permute-start | bytes 159752 | tf_op jit(solution)/shard_map/ppermute | solution.py:667
  23.9 2.4 %collective-permute-done.6.refs_13_.refs_7_ = f32[104,128]{1,0:T(8,128)S(1)} collective-permute-done((f32[104,128]{1,0:T(8,128)S(1)}, f32[104,128]{1,0:T(8,128)S(1)}, u32[]{:S(2)}, u32[]{:S(2)}) %collective-permute-start.6) | collective-permute-done | bytes 53280 | tf_op jit(solution)/shard_map/ppermute | solution.py:666
  26.3 0.0 collective-permute-done.7.refs_14_.refs_8_
  26.3 0.4 shard_map.76
  26.7 0.1 collective-permute-start.8
  26.8 1.6 %collective-permute-start.9 = (f32[56,128]{1,0:T(8,128)S(1)}, f32[56,128]{1,0:T(8,128)S(1)}, u32[]{:S(2)}, u32[]{:S(2)}) collective-permute-start(f32[56,128]{1,0:T(8,128)S(1)} %get-tuple-element.121), channel_id=1, source_target_pairs={{0,3},{1,2},{2,1},{3,0},{4,7},{5,6},{6,5},{7,4},{8,11},{9,10},{10,... | collective-permute-start | bytes 86024 | tf_op jit(solution)/shard_map/ppermute | solution.py:677
  28.3 0.9 %shard_map.77 = (f32[19,14,8,128]{3,2,1,0:T(8,128)S(1)}, f32[104,128]{1,0:T(8,128)S(1)}, f32[104,128]{1,0:T(8,128)S(1)}, f32[14,8,128]{2,1,0:T(8,128)S(1)}) custom-call(f32[19,8,128]{2,1,0:T(8,128)S(1)} %get-tuple-element.84.refs_0_, s32[16,8,128]{2,1,0:T(8,128)S(1)} %get-tuple-element.90.refs_1_.bits_ref, f32[18,24,128]{2,1,0:T(8,128)S(1)} %get-tuple-element.113.refs_2_, ...), custom_call_target="tpu_custom_call" | custom-call | flops 6553600 | bytes 1310720 | tf_op jit(solution)/shard_map/pallas_call | solution.py:648
  29.2 0.0 collective-permute-done.8.refs_2_
  29.3 0.9 %collective-permute-done.9.refs_3_ = f32[56,128]{1,0:T(8,128)S(1)} collective-permute-done((f32[56,128]{1,0:T(8,128)S(1)}, f32[56,128]{1,0:T(8,128)S(1)}, u32[]{:S(2)}, u32[]{:S(2)}) %collective-permute-start.9) | collective-permute-done | bytes 28704 | tf_op jit(solution)/shard_map/ppermute | solution.py:677
  30.2 0.1 collective-permute-start.10
  30.2 3.8 %collective-permute-start.11 = (f32[104,128]{1,0:T(8,128)S(1)}, f32[104,128]{1,0:T(8,128)S(1)}, u32[]{:S(2)}, u32[]{:S(2)}) collective-permute-start(f32[104,128]{1,0:T(8,128)S(1)} %get-tuple-element.127.refs_18_), channel_id=1, source_target_pairs={{4,0},{8,4},{12,8},{0,12},{5,1},{9,5},{13,9},{1,13},{6,2},{10,6},{... | collective-permute-start | bytes 159752 | tf_op jit(solution)/shard_map/ppermute | solution.py:667
  34.0 2.2 %collective-permute-done.10.refs_13_.refs_7_ = f32[104,128]{1,0:T(8,128)S(1)} collective-permute-done((f32[104,128]{1,0:T(8,128)S(1)}, f32[104,128]{1,0:T(8,128)S(1)}, u32[]{:S(2)}, u32[]{:S(2)}) %collective-permute-start.10) | collective-permute-done | bytes 53280 | tf_op jit(solution)/shard_map/ppermute | solution.py:666
  36.3 0.0 collective-permute-done.11.refs_14_.refs_8_
  36.3 0.4 shard_map.79
  36.7 0.1 collective-permute-start.12
  36.7 1.6 %collective-permute-start.13 = (f32[56,128]{1,0:T(8,128)S(1)}, f32[56,128]{1,0:T(8,128)S(1)}, u32[]{:S(2)}, u32[]{:S(2)}) collective-permute-start(f32[56,128]{1,0:T(8,128)S(1)} %get-tuple-element.137), channel_id=1, source_target_pairs={{0,3},{1,2},{2,1},{3,0},{4,7},{5,6},{6,5},{7,4},{8,11},{9,10},{10,... | collective-permute-start | bytes 86024 | tf_op jit(solution)/shard_map/ppermute | solution.py:677
  38.3 0.9 %shard_map.80 = (f32[19,14,8,128]{3,2,1,0:T(8,128)S(1)}, f32[104,128]{1,0:T(8,128)S(1)}, f32[104,128]{1,0:T(8,128)S(1)}, f32[14,8,128]{2,1,0:T(8,128)S(1)}) custom-call(f32[19,8,128]{2,1,0:T(8,128)S(1)} %get-tuple-element.84.refs_0_, s32[16,8,128]{2,1,0:T(8,128)S(1)} %get-tuple-element.90.refs_1_.bits_ref, f32[18,24,128]{2,1,0:T(8,128)S(1)} %get-tuple-element.129.refs_2_, ...), custom_call_target="tpu_custom_call" | custom-call | flops 6553600 | bytes 1310720 | tf_op jit(solution)/shard_map/pallas_call | solution.py:648
  39.2 0.0 collective-permute-done.12.refs_2_
  39.2 0.9 %collective-permute-done.13.refs_3_ = f32[56,128]{1,0:T(8,128)S(1)} collective-permute-done((f32[56,128]{1,0:T(8,128)S(1)}, f32[56,128]{1,0:T(8,128)S(1)}, u32[]{:S(2)}, u32[]{:S(2)}) %collective-permute-start.13) | collective-permute-done | bytes 28704 | tf_op jit(solution)/shard_map/ppermute | solution.py:677
  40.1 1.7 %collective-permute-start.14 = (f32[104,128]{1,0:T(8,128)S(1)}, f32[104,128]{1,0:T(8,128)S(1)}, u32[]{:S(2)}, u32[]{:S(2)}) collective-permute-start(f32[104,128]{1,0:T(8,128)S(1)} %get-tuple-element.142.refs_17_), channel_id=1, source_target_pairs={{0,4},{4,8},{8,12},{12,0},{1,5},{5,9},{9,13},{13,1},{2,6},{6,10},{... | collective-permute-start | bytes 159752 | tf_op jit(solution)/shard_map/ppermute | solution.py:666
  41.8 2.2 %collective-permute-start.15 = (f32[104,128]{1,0:T(8,128)S(1)}, f32[104,128]{1,0:T(8,128)S(1)}, u32[]{:S(2)}, u32[]{:S(2)}) collective-permute-start(f32[104,128]{1,0:T(8,128)S(1)} %get-tuple-element.143.refs_18_), channel_id=1, source_target_pairs={{4,0},{8,4},{12,8},{0,12},{5,1},{9,5},{13,9},{1,13},{6,2},{10,6},{... | collective-permute-start | bytes 159752 | tf_op jit(solution)/shard_map/ppermute | solution.py:667
  44.0 2.4 %collective-permute-done.14.refs_13_.refs_7_ = f32[104,128]{1,0:T(8,128)S(1)} collective-permute-done((f32[104,128]{1,0:T(8,128)S(1)}, f32[104,128]{1,0:T(8,128)S(1)}, u32[]{:S(2)}, u32[]{:S(2)}) %collective-permute-start.14) | collective-permute-done | bytes 53280 | tf_op jit(solution)/shard_map/ppermute | solution.py:666
  46.4 0.5 collective-permute-done.15.refs_14_.refs_8_
  46.9 0.4 shard_map.82
  47.3 0.1 collective-permute-start.16
  47.3 1.6 %collective-permute-start.17 = (f32[48,128]{1,0:T(8,128)S(1)}, f32[48,128]{1,0:T(8,128)S(1)}, u32[]{:S(2)}, u32[]{:S(2)}) collective-permute-start(f32[48,128]{1,0:T(8,128)S(1)} %get-tuple-element.152), channel_id=1, source_target_pairs={{0,3},{1,2},{2,1},{3,0},{4,7},{5,6},{6,5},{7,4},{8,11},{9,10},{10,... | collective-permute-start | bytes 73736 | tf_op jit(solution)/shard_map/ppermute | solution.py:677
  48.9 0.9 %shard_map.83 = (f32[19,14,8,128]{3,2,1,0:T(8,128)S(1)}, f32[80,128]{1,0:T(8,128)S(1)}, f32[80,128]{1,0:T(8,128)S(1)}, f32[3,128,128]{2,1,0:T(8,128)S(1)}) custom-call(f32[19,8,128]{2,1,0:T(8,128)S(1)} %get-tuple-element.84.refs_0_, s32[16,8,128]{2,1,0:T(8,128)S(1)} %get-tuple-element.90.refs_1_.bits_ref, f32[18,24,128]{2,1,0:T(8,128)S(1)} %get-tuple-element.145.refs_2_, ...), custom_call_target="tpu_custom_call" | custom-call | flops 6553600 | bytes 1310720 | tf_op jit(solution)/shard_map/pallas_call | solution.py:648
  49.9 0.0 collective-permute-done.16.refs_2_
  49.9 0.8 %collective-permute-done.17.refs_3_ = f32[48,128]{1,0:T(8,128)S(1)} collective-permute-done((f32[48,128]{1,0:T(8,128)S(1)}, f32[48,128]{1,0:T(8,128)S(1)}, u32[]{:S(2)}, u32[]{:S(2)}) %collective-permute-start.17) | collective-permute-done | bytes 24608 | tf_op jit(solution)/shard_map/ppermute | solution.py:677
  50.7 1.2 %collective-permute-start.18 = (f32[80,128]{1,0:T(8,128)S(1)}, f32[80,128]{1,0:T(8,128)S(1)}, u32[]{:S(2)}, u32[]{:S(2)}) collective-permute-start(f32[80,128]{1,0:T(8,128)S(1)} %get-tuple-element.161), channel_id=1, source_target_pairs={{0,4},{4,8},{8,12},{12,0},{1,5},{5,9},{9,13},{13,1},{2,6},{6,10},{... | collective-permute-start | bytes 122888 | tf_op jit(solution)/shard_map/ppermute | solution.py:666
  51.9 2.7 %collective-permute-start.19 = (f32[80,128]{1,0:T(8,128)S(1)}, f32[80,128]{1,0:T(8,128)S(1)}, u32[]{:S(2)}, u32[]{:S(2)}) collective-permute-start(f32[80,128]{1,0:T(8,128)S(1)} %get-tuple-element.162), channel_id=1, source_target_pairs={{4,0},{8,4},{12,8},{0,12},{5,1},{9,5},{13,9},{1,13},{6,2},{10,6},{... | collective-permute-start | bytes 122888 | tf_op jit(solution)/shard_map/ppermute | solution.py:667
  54.6 1.3 %shard_map.85 = (f32[19,128,128]{2,1,0:T(8,128)}, f32[19,128,128]{2,1,0:T(8,128)S(1)}, f32[3,128,128]{2,1,0:T(8,128)}) custom-call(f32[19,2,8,128]{3,2,1,0:T(8,128)S(1)} %get-tuple-element.144.f_edge, f32[19,14,8,128]{3,2,1,0:T(8,128)S(1)} %get-tuple-element.148.f_middle, s32[16,8,128]{2,1,0:T(8,128)S(1)} %get-tuple-element.90.refs_1_.bits_ref, ...), custom_call_target="tpu_custom_call" | custom-call | flops 6553600 | bytes 1310720 | tf_op jit(solution)/shard_map/pallas_call | solution.py:648
  55.9 0.7 %collective-permute-done.18.yd = f32[80,128]{1,0:T(8,128)S(1)} collective-permute-done((f32[80,128]{1,0:T(8,128)S(1)}, f32[80,128]{1,0:T(8,128)S(1)}, u32[]{:S(2)}, u32[]{:S(2)}) %collective-permute-start.18) | collective-permute-done | bytes 40992 | tf_op jit(solution)/shard_map/ppermute | solution.py:666
  56.5 0.2 collective-permute-done.19.yu
  56.8 0.7 %shard_map.86 = f32[19,128,128]{2,1,0:T(8,128)} custom-call(f32[19,128,128]{2,1,0:T(8,128)} %get-tuple-element.158.out_in, f32[19,128,128]{2,1,0:T(8,128)S(1)} %get-tuple-element.159.flat_ref, f32[2,128,128]{2,1,0:T(8,128)S(1)} %get-tuple-element.160.mask_ref, f32[80,128]{1,0:T(8,128)S(1)} %collective-permute-done.18.yd, ...), custom_call_target="tpu_custom_call", output_to_operand_aliasing={{}: (0, {})} | custom-call | tf_op jit(solution)/shard_map/pallas_call | solution.py:648
  (5 shorter events, 0.1 us)
Async XLA Ops:
  1.8 7.2 %collective-permute-start.1 = (f32[32,128]{1,0:T(8,128)S(1)}, f32[32,128]{1,0:T(8,128)S(1)}, u32[]{:S(2)}, u32[]{:S(2)}) collective-permute-start(f32[32,128]{1,0:T(8,128)S(1)} %get-tuple-element.86), channel_id=1, source_target_pairs={{4,0},{8,4},{12,8},{0,12},{5,1},{9,5},{13,9},{1,13},{6,2},{10,6},{... | collective-permute-start | bytes 49160 | tf_op jit(solution)/shard_map/ppermute | solution.py:667
  6.9 5.5 %collective-permute-start = (f32[32,128]{1,0:T(8,128)S(1)}, f32[32,128]{1,0:T(8,128)S(1)}, u32[]{:S(2)}, u32[]{:S(2)}) collective-permute-start(f32[32,128]{1,0:T(8,128)S(1)} %get-tuple-element.83.after_ref), channel_id=1, source_target_pairs={{0,4},{4,8},{8,12},{12,0},{1,5},{5,9},{9,13},{13,1},{2,6},{6,10},{... | collective-permute-start | bytes 49160 | tf_op jit(solution)/shard_map/ppermute | solution.py:666
  12.5 1.9 %collective-permute-start.2 = (f32[24,128]{1,0:T(8,128)S(1)}, f32[24,128]{1,0:T(8,128)S(1)}, u32[]{:S(2)}, u32[]{:S(2)}) collective-permute-start(f32[24,128]{1,0:T(8,128)S(1)} %get-tuple-element.88), channel_id=1, source_target_pairs={{0,1},{1,0},{2,3},{3,2},{4,5},{5,4},{6,7},{7,6},{8,9},{9,8},{10,11... | collective-permute-start | bytes 36872 | tf_op jit(solution)/shard_map/ppermute | solution.py:678
  12.5 3.2 %collective-permute-start.3 = (f32[24,128]{1,0:T(8,128)S(1)}, f32[24,128]{1,0:T(8,128)S(1)}, u32[]{:S(2)}, u32[]{:S(2)}) collective-permute-start(f32[24,128]{1,0:T(8,128)S(1)} %get-tuple-element.89), channel_id=1, source_target_pairs={{0,3},{1,2},{2,1},{3,0},{4,7},{5,6},{6,5},{7,4},{8,11},{9,10},{10,... | collective-permute-start | bytes 36872 | tf_op jit(solution)/shard_map/ppermute | solution.py:677
  16.1 2.5 %collective-permute-start.4 = (f32[56,128]{1,0:T(8,128)S(1)}, f32[56,128]{1,0:T(8,128)S(1)}, u32[]{:S(2)}, u32[]{:S(2)}) collective-permute-start(f32[56,128]{1,0:T(8,128)S(1)} %get-tuple-element.104), channel_id=1, source_target_pairs={{0,1},{1,0},{2,3},{3,2},{4,5},{5,4},{6,7},{7,6},{8,9},{9,8},{10,11... | collective-permute-start | bytes 86024 | tf_op jit(solution)/shard_map/ppermute | solution.py:678
  16.6 3.3 %collective-permute-start.5 = (f32[56,128]{1,0:T(8,128)S(1)}, f32[56,128]{1,0:T(8,128)S(1)}, u32[]{:S(2)}, u32[]{:S(2)}) collective-permute-start(f32[56,128]{1,0:T(8,128)S(1)} %get-tuple-element.105), channel_id=1, source_target_pairs={{0,3},{1,2},{2,1},{3,0},{4,7},{5,6},{6,5},{7,4},{8,11},{9,10},{10,... | collective-permute-start | bytes 86024 | tf_op jit(solution)/shard_map/ppermute | solution.py:677
  20.0 6.3 %collective-permute-start.6 = (f32[104,128]{1,0:T(8,128)S(1)}, f32[104,128]{1,0:T(8,128)S(1)}, u32[]{:S(2)}, u32[]{:S(2)}) collective-permute-start(f32[104,128]{1,0:T(8,128)S(1)} %get-tuple-element.110.refs_17_), channel_id=1, source_target_pairs={{0,4},{4,8},{8,12},{12,0},{1,5},{5,9},{9,13},{13,1},{2,6},{6,10},{... | collective-permute-start | bytes 159752 | tf_op jit(solution)/shard_map/ppermute | solution.py:666
  20.1 6.2 %collective-permute-start.7 = (f32[104,128]{1,0:T(8,128)S(1)}, f32[104,128]{1,0:T(8,128)S(1)}, u32[]{:S(2)}, u32[]{:S(2)}) collective-permute-start(f32[104,128]{1,0:T(8,128)S(1)} %get-tuple-element.111.refs_18_), channel_id=1, source_target_pairs={{4,0},{8,4},{12,8},{0,12},{5,1},{9,5},{13,9},{1,13},{6,2},{10,6},{... | collective-permute-start | bytes 159752 | tf_op jit(solution)/shard_map/ppermute | solution.py:667
  26.7 2.6 %collective-permute-start.8 = (f32[56,128]{1,0:T(8,128)S(1)}, f32[56,128]{1,0:T(8,128)S(1)}, u32[]{:S(2)}, u32[]{:S(2)}) collective-permute-start(f32[56,128]{1,0:T(8,128)S(1)} %get-tuple-element.120), channel_id=1, source_target_pairs={{0,1},{1,0},{2,3},{3,2},{4,5},{5,4},{6,7},{7,6},{8,9},{9,8},{10,11... | collective-permute-start | bytes 86024 | tf_op jit(solution)/shard_map/ppermute | solution.py:678
  26.8 3.4 %collective-permute-start.9 = (f32[56,128]{1,0:T(8,128)S(1)}, f32[56,128]{1,0:T(8,128)S(1)}, u32[]{:S(2)}, u32[]{:S(2)}) collective-permute-start(f32[56,128]{1,0:T(8,128)S(1)} %get-tuple-element.121), channel_id=1, source_target_pairs={{0,3},{1,2},{2,1},{3,0},{4,7},{5,6},{6,5},{7,4},{8,11},{9,10},{10,... | collective-permute-start | bytes 86024 | tf_op jit(solution)/shard_map/ppermute | solution.py:677
  30.2 6.1 %collective-permute-start.10 = (f32[104,128]{1,0:T(8,128)S(1)}, f32[104,128]{1,0:T(8,128)S(1)}, u32[]{:S(2)}, u32[]{:S(2)}) collective-permute-start(f32[104,128]{1,0:T(8,128)S(1)} %get-tuple-element.126.refs_17_), channel_id=1, source_target_pairs={{0,4},{4,8},{8,12},{12,0},{1,5},{5,9},{9,13},{13,1},{2,6},{6,10},{... | collective-permute-start | bytes 159752 | tf_op jit(solution)/shard_map/ppermute | solution.py:666
  30.2 6.0 %collective-permute-start.11 = (f32[104,128]{1,0:T(8,128)S(1)}, f32[104,128]{1,0:T(8,128)S(1)}, u32[]{:S(2)}, u32[]{:S(2)}) collective-permute-start(f32[104,128]{1,0:T(8,128)S(1)} %get-tuple-element.127.refs_18_), channel_id=1, source_target_pairs={{4,0},{8,4},{12,8},{0,12},{5,1},{9,5},{13,9},{1,13},{6,2},{10,6},{... | collective-permute-start | bytes 159752 | tf_op jit(solution)/shard_map/ppermute | solution.py:667
  36.7 2.6 %collective-permute-start.12 = (f32[56,128]{1,0:T(8,128)S(1)}, f32[56,128]{1,0:T(8,128)S(1)}, u32[]{:S(2)}, u32[]{:S(2)}) collective-permute-start(f32[56,128]{1,0:T(8,128)S(1)} %get-tuple-element.136), channel_id=1, source_target_pairs={{0,1},{1,0},{2,3},{3,2},{4,5},{5,4},{6,7},{7,6},{8,9},{9,8},{10,11... | collective-permute-start | bytes 86024 | tf_op jit(solution)/shard_map/ppermute | solution.py:678
  36.7 3.4 %collective-permute-start.13 = (f32[56,128]{1,0:T(8,128)S(1)}, f32[56,128]{1,0:T(8,128)S(1)}, u32[]{:S(2)}, u32[]{:S(2)}) collective-permute-start(f32[56,128]{1,0:T(8,128)S(1)} %get-tuple-element.137), channel_id=1, source_target_pairs={{0,3},{1,2},{2,1},{3,0},{4,7},{5,6},{6,5},{7,4},{8,11},{9,10},{10,... | collective-permute-start | bytes 86024 | tf_op jit(solution)/shard_map/ppermute | solution.py:677
  40.1 6.3 %collective-permute-start.14 = (f32[104,128]{1,0:T(8,128)S(1)}, f32[104,128]{1,0:T(8,128)S(1)}, u32[]{:S(2)}, u32[]{:S(2)}) collective-permute-start(f32[104,128]{1,0:T(8,128)S(1)} %get-tuple-element.142.refs_17_), channel_id=1, source_target_pairs={{0,4},{4,8},{8,12},{12,0},{1,5},{5,9},{9,13},{13,1},{2,6},{6,10},{... | collective-permute-start | bytes 159752 | tf_op jit(solution)/shard_map/ppermute | solution.py:666
  41.8 5.1 %collective-permute-start.15 = (f32[104,128]{1,0:T(8,128)S(1)}, f32[104,128]{1,0:T(8,128)S(1)}, u32[]{:S(2)}, u32[]{:S(2)}) collective-permute-start(f32[104,128]{1,0:T(8,128)S(1)} %get-tuple-element.143.refs_18_), channel_id=1, source_target_pairs={{4,0},{8,4},{12,8},{0,12},{5,1},{9,5},{13,9},{1,13},{6,2},{10,6},{... | collective-permute-start | bytes 159752 | tf_op jit(solution)/shard_map/ppermute | solution.py:667
  47.3 2.6 %collective-permute-start.16 = (f32[48,128]{1,0:T(8,128)S(1)}, f32[48,128]{1,0:T(8,128)S(1)}, u32[]{:S(2)}, u32[]{:S(2)}) collective-permute-start(f32[48,128]{1,0:T(8,128)S(1)} %get-tuple-element.151), channel_id=1, source_target_pairs={{0,1},{1,0},{2,3},{3,2},{4,5},{5,4},{6,7},{7,6},{8,9},{9,8},{10,11... | collective-permute-start | bytes 73736 | tf_op jit(solution)/shard_map/ppermute | solution.py:678
  47.3 3.3 %collective-permute-start.17 = (f32[48,128]{1,0:T(8,128)S(1)}, f32[48,128]{1,0:T(8,128)S(1)}, u32[]{:S(2)}, u32[]{:S(2)}) collective-permute-start(f32[48,128]{1,0:T(8,128)S(1)} %get-tuple-element.152), channel_id=1, source_target_pairs={{0,3},{1,2},{2,1},{3,0},{4,7},{5,6},{6,5},{7,4},{8,11},{9,10},{10,... | collective-permute-start | bytes 73736 | tf_op jit(solution)/shard_map/ppermute | solution.py:677
  50.7 5.9 %collective-permute-start.18 = (f32[80,128]{1,0:T(8,128)S(1)}, f32[80,128]{1,0:T(8,128)S(1)}, u32[]{:S(2)}, u32[]{:S(2)}) collective-permute-start(f32[80,128]{1,0:T(8,128)S(1)} %get-tuple-element.161), channel_id=1, source_target_pairs={{0,4},{4,8},{8,12},{12,0},{1,5},{5,9},{9,13},{13,1},{2,6},{6,10},{... | collective-permute-start | bytes 122888 | tf_op jit(solution)/shard_map/ppermute | solution.py:666
  51.9 4.9 %collective-permute-start.19 = (f32[80,128]{1,0:T(8,128)S(1)}, f32[80,128]{1,0:T(8,128)S(1)}, u32[]{:S(2)}, u32[]{:S(2)}) collective-permute-start(f32[80,128]{1,0:T(8,128)S(1)} %get-tuple-element.162), channel_id=1, source_target_pairs={{4,0},{8,4},{12,8},{0,12},{5,1},{9,5},{13,9},{1,13},{6,2},{10,6},{... | collective-permute-start | bytes 122888 | tf_op jit(solution)/shard_map/ppermute | solution.py:667

commit v11 on v9

--- a/solution.py
+++ b/solution.py
@@ -703,16 +703,16 @@
         cost=cost,
     )
     a, b = call(
-        functools.partial(start_pack_kernel, pairs),
+        functools.partial(start_pack_kernel, False),
         [layer_face, layer_face],
         (pot0, mask, below, above),
         scratch=[layer_face[0]] * 2,
     )
-    a, b = exchange(a, b, "gy")
+    a, b = shift(a, b, "gy")
     whole_bits = ((size_x, size_y, size_z), i32)
     (bits,) = call(bits_kernel, [whole_bits], (mask, below, above), scratch=[padded], cost=cost)
     bits, x0l, x0r, y0d, y0u = call(
-        functools.partial(ring_kernel, pairs),
+        functools.partial(ring_kernel, False),
         [whole_bits, layer_face, layer_face, ring_rows, ring_rows],
         (bits, a, b, below, above),
         scratch=[(2, size_y + PAD, size_z)],

time: 54.5 us -> 55.7 us (1.022)
  waiting for transfers between devices: 14.1 us -> 18.9 us
  starting transfers between devices: 29.6 us -> 26.1 us
    ppermute x5 -> x4, starting transfers between devices: 8.13 us -> 1.61 us  [swap(): b = lax.ppermute(b, axis, partners[1])]
    ppermute x5 -> x4, waiting for transfers between devices: 4.57 us -> 8.17 us  [swap(): b = lax.ppermute(b, axis, partners[1])]
    ppermute x5 -> x6, starting transfers between devices: 12.5 us -> 14.3 us  [shift(): lax.ppermute(backward, axis, [(b, a) for a, b in ahead])]
    ppermute x5 -> x6, waiting for transfers between devices: 7.95 us -> 9.11 us  [shift(): lax.ppermute(forward, axis, ahead)]
    ppermute x5 -> x4, starting transfers between devices: 0.78 us -> 1.9 us  [swap(): return (lax.ppermute(a, axis, partners[0]), b)]
    ppermute x5 -> x6, waiting for transfers between devices: 1.56 us -> 1.6 us  [shift(): lax.ppermute(backward, axis, [(b, a) for a, b in ahead])]
    ppermute x5 -> x6, starting transfers between devices: 8.24 us -> 8.25 us  [shift(): lax.ppermute(forward, axis, ahead)]
where the time goes in v11:
time: 55.7 us; the launch traced here: 55.6 us
  starting transfers between devices  26.1 us (47%)
  waiting for transfers between devices  18.9 us (34%)
  Pallas kernels  9.76 us (18%)
  between operations  0.84 us (2%)
    ppermute x6, starting transfers between devices, shift(): lax.ppermute(backward, axis, [(b, a) for a, b in ahead])  14.3 us
    pallas_call x19, Pallas kernels, call(): pl.pallas_call(kernel, out_shape=[jax.ShapeDtypeStruct(shape, dtype) for...  9.76 us
    ppermute x6, waiting for transfers between devices, shift(): lax.ppermute(forward, axis, ahead)  9.11 us
    ppermute x6, starting transfers between devices, shift(): lax.ppermute(forward, axis, ahead)  8.25 us
    ppermute x4, waiting for transfers between devices, swap(): b = lax.ppermute(b, axis, partners[1])  8.17 us
    ppermute x4, starting transfers between devices, swap(): return (lax.ppermute(a, axis, partners[0]), b)  1.9 us
    ppermute x4, starting transfers between devices, swap(): b = lax.ppermute(b, axis, partners[1])  1.61 us
    ppermute x6, waiting for transfers between devices, shift(): lax.ppermute(backward, axis, [(b, a) for a, b in ahead])  1.6 us
  transfers between devices with their start and end apart: 20, of which 15 were waited for; matrix products, arithmetic and copies ran while one was open for 0% of the time, Pallas kernels for 11%

profile of v11, /device:TPU:0, one launch (start us, length us, event | category | flops | bytes accessed | tf_op | source)
XLA Modules:
  0.0 55.6 jit_solution(7497860903668625156)
XLA Ops:
  0.6 0.0 copy-start.3
  0.6 0.0 copy-start.2
  0.7 0.0 copy-start.1
  0.7 0.0 copy-start
  0.7 0.0 copy-start.4
  0.7 1.2 %shard_map.68 = (f32[32,128]{1,0:T(8,128)S(1)}, f32[32,128]{1,0:T(8,128)S(1)}) custom-call(f32[19,128,128]{2,1,0:T(8,128)} %bitcast.5, s32[128,128]{1,0:T(8,128)} %bitcast.7, s32[128,128]{1,0:T(8,128)} %bitcast.9, f32[4]{0:T(128)} %wall_ref), custom_call_target="tpu_custom_call" | custom-call | tf_op jit(solution)/shard_map/pallas_call | solution.py:626
  1.9 3.1 %collective-permute-start = (f32[32,128]{1,0:T(8,128)S(1)}, f32[32,128]{1,0:T(8,128)S(1)}, u32[]{:S(2)}, u32[]{:S(2)}) collective-permute-start(f32[32,128]{1,0:T(8,128)S(1)} %get-tuple-element.95), channel_id=1, source_target_pairs={{0,4},{4,8},{8,12},{12,0},{1,5},{5,9},{9,13},{13,1},{2,6},{6,10},{... | collective-permute-start | bytes 49160 | tf_op jit(solution)/shard_map/ppermute | solution.py:644
  5.0 2.1 %collective-permute-start.1 = (f32[32,128]{1,0:T(8,128)S(1)}, f32[32,128]{1,0:T(8,128)S(1)}, u32[]{:S(2)}, u32[]{:S(2)}) collective-permute-start(f32[32,128]{1,0:T(8,128)S(1)} %get-tuple-element.96), channel_id=1, source_target_pairs={{4,0},{8,4},{12,8},{0,12},{5,1},{9,5},{13,9},{1,13},{6,2},{10,6},{... | collective-permute-start | bytes 49160 | tf_op jit(solution)/shard_map/ppermute | solution.py:645
  7.1 0.0 copy-done.3
  7.1 0.0 copy-done.2
  7.1 0.0 copy-done.1
  7.1 0.0 copy-done
  7.1 0.0 copy-done.4
  7.2 1.0 %shard_map.69 = (f32[19,16,8,128]{3,2,1,0:T(8,128)S(1)}, f32[19,8,128]{2,1,0:T(8,128)S(1)}, f32[2,128,128]{2,1,0:T(8,128)S(1)}, f32[16,8,128]{2,1,0:T(8,128)S(1)}, f32[16,8,128]{2,1,0:T(8,128)S(1)}) custom-call(f32[19,128,128]{2,1,0:T(8,128)S(1)} %bitcast.6, s32[128,128]{1,0:T(8,128)S(1)} %bitcast.8, s32[128,128]{1,0:T(8,128)S(1)} %bitcast.10, ...), custom_call_target="tpu_custom_call" | custom-call | flops 6553600 | bytes 1310720 | tf_op jit(solution)/shard_map/pallas_call | solution.py:626
  8.2 0.7 %collective-permute-done.from_below = f32[32,128]{1,0:T(8,128)S(1)} collective-permute-done((f32[32,128]{1,0:T(8,128)S(1)}, f32[32,128]{1,0:T(8,128)S(1)}, u32[]{:S(2)}, u32[]{:S(2)}) %collective-permute-start) | collective-permute-done | bytes 16416 | tf_op jit(solution)/shard_map/ppermute | solution.py:644
  8.9 0.1 collective-permute-done.1.from_above
  9.0 0.1 collective-permute-start.2
  9.0 1.7 %collective-permute-start.3 = (f32[24,128]{1,0:T(8,128)S(1)}, f32[24,128]{1,0:T(8,128)S(1)}, u32[]{:S(2)}, u32[]{:S(2)}) collective-permute-start(f32[24,128]{1,0:T(8,128)S(1)} %get-tuple-element.99), channel_id=1, source_target_pairs={{1,0},{2,1},{3,2},{0,3},{5,4},{6,5},{7,6},{4,7},{9,8},{10,9},{11,1... | collective-permute-start | bytes 36872 | tf_op jit(solution)/shard_map/ppermute | solution.py:645
  10.8 0.2 shard_map.70.bits_in
  11.0 1.1 %collective-permute-done.2.a_ref = f32[24,128]{1,0:T(8,128)S(1)} collective-permute-done((f32[24,128]{1,0:T(8,128)S(1)}, f32[24,128]{1,0:T(8,128)S(1)}, u32[]{:S(2)}, u32[]{:S(2)}) %collective-permute-start.2) | collective-permute-done | bytes 12320 | tf_op jit(solution)/shard_map/ppermute | solution.py:644
  12.1 0.0 collective-permute-done.3.b_ref
  12.2 0.1 shard_map.72
  12.2 0.3 shard_map.73
  12.6 1.7 %collective-permute-start.4 = (f32[56,128]{1,0:T(8,128)S(1)}, f32[56,128]{1,0:T(8,128)S(1)}, u32[]{:S(2)}, u32[]{:S(2)}) collective-permute-start(f32[56,128]{1,0:T(8,128)S(1)} %get-tuple-element.114), channel_id=1, source_target_pairs={{0,1},{1,0},{2,3},{3,2},{4,5},{5,4},{6,7},{7,6},{8,9},{9,8},{10,11... | collective-permute-start | bytes 86024 | tf_op jit(solution)/shard_map/ppermute | solution.py:656
  14.3 0.2 collective-permute-start.5
  14.4 0.8 %shard_map.74 = (f32[19,14,8,128]{3,2,1,0:T(8,128)S(1)}, f32[104,128]{1,0:T(8,128)S(1)}, f32[104,128]{1,0:T(8,128)S(1)}, f32[14,8,128]{2,1,0:T(8,128)S(1)}) custom-call(f32[19,8,128]{2,1,0:T(8,128)S(1)} %get-tuple-element.93.refs_0_, s32[16,8,128]{2,1,0:T(8,128)S(1)} %get-tuple-element.100.refs_1_.bits_ref, f32[18,24,128]{2,1,0:T(8,128)S(1)} %get-tuple-element.107.refs_2_, ...), custom_call_target="tpu_custom_call" | custom-call | flops 6553600 | bytes 1310720 | tf_op jit(solution)/shard_map/pallas_call | solution.py:626
  15.3 0.0 collective-permute-done.4.refs_2_
  15.3 2.3 %collective-permute-done.5.refs_3_ = f32[56,128]{1,0:T(8,128)S(1)} collective-permute-done((f32[56,128]{1,0:T(8,128)S(1)}, f32[56,128]{1,0:T(8,128)S(1)}, u32[]{:S(2)}, u32[]{:S(2)}) %collective-permute-start.5) | collective-permute-done | bytes 28704 | tf_op jit(solution)/shard_map/ppermute | solution.py:655
  17.6 1.4 %collective-permute-start.6 = (f32[104,128]{1,0:T(8,128)S(1)}, f32[104,128]{1,0:T(8,128)S(1)}, u32[]{:S(2)}, u32[]{:S(2)}) collective-permute-start(f32[104,128]{1,0:T(8,128)S(1)} %get-tuple-element.120.refs_17_), channel_id=1, source_target_pairs={{0,4},{4,8},{8,12},{12,0},{1,5},{5,9},{9,13},{13,1},{2,6},{6,10},{... | collective-permute-start | bytes 159752 | tf_op jit(solution)/shard_map/ppermute | solution.py:644
  19.0 2.5 %collective-permute-start.7 = (f32[104,128]{1,0:T(8,128)S(1)}, f32[104,128]{1,0:T(8,128)S(1)}, u32[]{:S(2)}, u32[]{:S(2)}) collective-permute-start(f32[104,128]{1,0:T(8,128)S(1)} %get-tuple-element.121.refs_18_), channel_id=1, source_target_pairs={{4,0},{8,4},{12,8},{0,12},{5,1},{9,5},{13,9},{1,13},{6,2},{10,6},{... | collective-permute-start | bytes 159752 | tf_op jit(solution)/shard_map/ppermute | solution.py:645
  21.6 2.1 %collective-permute-done.6.refs_13_.refs_7_ = f32[104,128]{1,0:T(8,128)S(1)} collective-permute-done((f32[104,128]{1,0:T(8,128)S(1)}, f32[104,128]{1,0:T(8,128)S(1)}, u32[]{:S(2)}, u32[]{:S(2)}) %collective-permute-start.6) | collective-permute-done | bytes 53280 | tf_op jit(solution)/shard_map/ppermute | solution.py:644
  23.7 0.5 collective-permute-done.7.refs_14_.refs_8_
  24.2 0.4 shard_map.76
  24.6 0.1 collective-permute-start.8
  24.7 0.5 collective-permute-start.9
  25.1 0.9 %shard_map.77 = (f32[19,14,8,128]{3,2,1,0:T(8,128)S(1)}, f32[104,128]{1,0:T(8,128)S(1)}, f32[104,128]{1,0:T(8,128)S(1)}, f32[14,8,128]{2,1,0:T(8,128)S(1)}) custom-call(f32[19,8,128]{2,1,0:T(8,128)S(1)} %get-tuple-element.93.refs_0_, s32[16,8,128]{2,1,0:T(8,128)S(1)} %get-tuple-element.100.refs_1_.bits_ref, f32[18,24,128]{2,1,0:T(8,128)S(1)} %get-tuple-element.123.refs_2_, ...), custom_call_target="tpu_custom_call" | custom-call | flops 6553600 | bytes 1310720 | tf_op jit(solution)/shard_map/pallas_call | solution.py:626
  26.0 0.0 collective-permute-done.8.refs_2_
  26.0 2.0 %collective-permute-done.9.refs_3_ = f32[56,128]{1,0:T(8,128)S(1)} collective-permute-done((f32[56,128]{1,0:T(8,128)S(1)}, f32[56,128]{1,0:T(8,128)S(1)}, u32[]{:S(2)}, u32[]{:S(2)}) %collective-permute-start.9) | collective-permute-done | bytes 28704 | tf_op jit(solution)/shard_map/ppermute | solution.py:655
  28.1 1.2 %collective-permute-start.10 = (f32[104,128]{1,0:T(8,128)S(1)}, f32[104,128]{1,0:T(8,128)S(1)}, u32[]{:S(2)}, u32[]{:S(2)}) collective-permute-start(f32[104,128]{1,0:T(8,128)S(1)} %get-tuple-element.136.refs_17_), channel_id=1, source_target_pairs={{0,4},{4,8},{8,12},{12,0},{1,5},{5,9},{9,13},{13,1},{2,6},{6,10},{... | collective-permute-start | bytes 159752 | tf_op jit(solution)/shard_map/ppermute | solution.py:644
  29.2 2.7 %collective-permute-start.11 = (f32[104,128]{1,0:T(8,128)S(1)}, f32[104,128]{1,0:T(8,128)S(1)}, u32[]{:S(2)}, u32[]{:S(2)}) collective-permute-start(f32[104,128]{1,0:T(8,128)S(1)} %get-tuple-element.137.refs_18_), channel_id=1, source_target_pairs={{4,0},{8,4},{12,8},{0,12},{5,1},{9,5},{13,9},{1,13},{6,2},{10,6},{... | collective-permute-start | bytes 159752 | tf_op jit(solution)/shard_map/ppermute | solution.py:645
  31.9 2.2 %collective-permute-done.10.refs_13_.refs_7_ = f32[104,128]{1,0:T(8,128)S(1)} collective-permute-done((f32[104,128]{1,0:T(8,128)S(1)}, f32[104,128]{1,0:T(8,128)S(1)}, u32[]{:S(2)}, u32[]{:S(2)}) %collective-permute-start.10) | collective-permute-done | bytes 53280 | tf_op jit(solution)/shard_map/ppermute | solution.py:644
  34.2 0.3 collective-permute-done.11.refs_14_.refs_8_
  34.5 0.4 shard_map.79
  34.9 0.1 collective-permute-start.12
  35.0 0.5 collective-permute-start.13
  35.5 0.9 %shard_map.80 = (f32[19,14,8,128]{3,2,1,0:T(8,128)S(1)}, f32[104,128]{1,0:T(8,128)S(1)}, f32[104,128]{1,0:T(8,128)S(1)}, f32[14,8,128]{2,1,0:T(8,128)S(1)}) custom-call(f32[19,8,128]{2,1,0:T(8,128)S(1)} %get-tuple-element.93.refs_0_, s32[16,8,128]{2,1,0:T(8,128)S(1)} %get-tuple-element.100.refs_1_.bits_ref, f32[18,24,128]{2,1,0:T(8,128)S(1)} %get-tuple-element.139.refs_2_, ...), custom_call_target="tpu_custom_call" | custom-call | flops 6553600 | bytes 1310720 | tf_op jit(solution)/shard_map/pallas_call | solution.py:626
  36.3 0.0 collective-permute-done.12.refs_2_
  36.4 2.0 %collective-permute-done.13.refs_3_ = f32[56,128]{1,0:T(8,128)S(1)} collective-permute-done((f32[56,128]{1,0:T(8,128)S(1)}, f32[56,128]{1,0:T(8,128)S(1)}, u32[]{:S(2)}, u32[]{:S(2)}) %collective-permute-start.13) | collective-permute-done | bytes 28704 | tf_op jit(solution)/shard_map/ppermute | solution.py:655
  38.4 1.3 %collective-permute-start.14 = (f32[104,128]{1,0:T(8,128)S(1)}, f32[104,128]{1,0:T(8,128)S(1)}, u32[]{:S(2)}, u32[]{:S(2)}) collective-permute-start(f32[104,128]{1,0:T(8,128)S(1)} %get-tuple-element.152.refs_17_), channel_id=1, source_target_pairs={{0,4},{4,8},{8,12},{12,0},{1,5},{5,9},{9,13},{13,1},{2,6},{6,10},{... | collective-permute-start | bytes 159752 | tf_op jit(solution)/shard_map/ppermute | solution.py:644
  39.7 2.6 %collective-permute-start.15 = (f32[104,128]{1,0:T(8,128)S(1)}, f32[104,128]{1,0:T(8,128)S(1)}, u32[]{:S(2)}, u32[]{:S(2)}) collective-permute-start(f32[104,128]{1,0:T(8,128)S(1)} %get-tuple-element.153.refs_18_), channel_id=1, source_target_pairs={{4,0},{8,4},{12,8},{0,12},{5,1},{9,5},{13,9},{1,13},{6,2},{10,6},{... | collective-permute-start | bytes 159752 | tf_op jit(solution)/shard_map/ppermute | solution.py:645
  42.3 2.2 %collective-permute-done.14.refs_13_.refs_7_ = f32[104,128]{1,0:T(8,128)S(1)} collective-permute-done((f32[104,128]{1,0:T(8,128)S(1)}, f32[104,128]{1,0:T(8,128)S(1)}, u32[]{:S(2)}, u32[]{:S(2)}) %collective-permute-start.14) | collective-permute-done | bytes 53280 | tf_op jit(solution)/shard_map/ppermute | solution.py:644
  44.5 0.5 collective-permute-done.15.refs_14_.refs_8_
  45.0 0.4 shard_map.82
  45.4 0.1 collective-permute-start.16
  45.4 0.5 collective-permute-start.17
  45.9 0.9 %shard_map.83 = (f32[19,14,8,128]{3,2,1,0:T(8,128)S(1)}, f32[80,128]{1,0:T(8,128)S(1)}, f32[80,128]{1,0:T(8,128)S(1)}, f32[3,128,128]{2,1,0:T(8,128)S(1)}) custom-call(f32[19,8,128]{2,1,0:T(8,128)S(1)} %get-tuple-element.93.refs_0_, s32[16,8,128]{2,1,0:T(8,128)S(1)} %get-tuple-element.100.refs_1_.bits_ref, f32[18,24,128]{2,1,0:T(8,128)S(1)} %get-tuple-element.155.refs_2_, ...), custom_call_target="tpu_custom_call" | custom-call | flops 6553600 | bytes 1310720 | tf_op jit(solution)/shard_map/pallas_call | solution.py:626
  46.9 0.0 collective-permute-done.16.refs_2_
  46.9 1.9 %collective-permute-done.17.refs_3_ = f32[48,128]{1,0:T(8,128)S(1)} collective-permute-done((f32[48,128]{1,0:T(8,128)S(1)}, f32[48,128]{1,0:T(8,128)S(1)}, u32[]{:S(2)}, u32[]{:S(2)}) %collective-permute-start.17) | collective-permute-done | bytes 24608 | tf_op jit(solution)/shard_map/ppermute | solution.py:655
  48.8 1.2 %collective-permute-start.18 = (f32[80,128]{1,0:T(8,128)S(1)}, f32[80,128]{1,0:T(8,128)S(1)}, u32[]{:S(2)}, u32[]{:S(2)}) collective-permute-start(f32[80,128]{1,0:T(8,128)S(1)} %get-tuple-element.171), channel_id=1, source_target_pairs={{0,4},{4,8},{8,12},{12,0},{1,5},{5,9},{9,13},{13,1},{2,6},{6,10},{... | collective-permute-start | bytes 122888 | tf_op jit(solution)/shard_map/ppermute | solution.py:644
  50.0 2.7 %collective-permute-start.19 = (f32[80,128]{1,0:T(8,128)S(1)}, f32[80,128]{1,0:T(8,128)S(1)}, u32[]{:S(2)}, u32[]{:S(2)}) collective-permute-start(f32[80,128]{1,0:T(8,128)S(1)} %get-tuple-element.172), channel_id=1, source_target_pairs={{4,0},{8,4},{12,8},{0,12},{5,1},{9,5},{13,9},{1,13},{6,2},{10,6},{... | collective-permute-start | bytes 122888 | tf_op jit(solution)/shard_map/ppermute | solution.py:645
  52.7 1.3 %shard_map.85 = (f32[19,128,128]{2,1,0:T(8,128)}, f32[19,128,128]{2,1,0:T(8,128)S(1)}, f32[3,128,128]{2,1,0:T(8,128)}) custom-call(f32[19,2,8,128]{3,2,1,0:T(8,128)S(1)} %get-tuple-element.154.f_edge, f32[19,14,8,128]{3,2,1,0:T(8,128)S(1)} %get-tuple-element.158.f_middle, s32[16,8,128]{2,1,0:T(8,128)S(1)} %get-tuple-element.100.refs_1_.bits_ref, ...), custom_call_target="tpu_custom_call" | custom-call | flops 6553600 | bytes 1310720 | tf_op jit(solution)/shard_map/pallas_call | solution.py:626
  53.9 0.7 %collective-permute-done.18.yd = f32[80,128]{1,0:T(8,128)S(1)} collective-permute-done((f32[80,128]{1,0:T(8,128)S(1)}, f32[80,128]{1,0:T(8,128)S(1)}, u32[]{:S(2)}, u32[]{:S(2)}) %collective-permute-start.18) | collective-permute-done | bytes 40992 | tf_op jit(solution)/shard_map/ppermute | solution.py:644
  54.6 0.2 collective-permute-done.19.yu
  54.8 0.7 %shard_map.86 = f32[19,128,128]{2,1,0:T(8,128)} custom-call(f32[19,128,128]{2,1,0:T(8,128)} %get-tuple-element.168.out_in, f32[19,128,128]{2,1,0:T(8,128)S(1)} %get-tuple-element.169.flat_ref, f32[2,128,128]{2,1,0:T(8,128)S(1)} %get-tuple-element.170.mask_ref, f32[80,128]{1,0:T(8,128)S(1)} %collective-permute-done.18.yd, ...), custom_call_target="tpu_custom_call", output_to_operand_aliasing={{}: (0, {})} | custom-call | tf_op jit(solution)/shard_map/pallas_call | solution.py:626
  (5 shorter events, 0.1 us)
Async XLA Ops:
  0.6 6.5 %copy-start.3 = (f32[4]{0:T(128)S(1)}, f32[4]{0:T(128)}, u32[]{:S(2)}) copy-start(f32[4]{0:T(128)} %wall_ref) | copy-start | bytes 52
  0.6 6.5 %copy-start.2 = (s32[8,16,128]{2,1,0:T(8,128)S(1)}, s32[8,16,128]{2,1,0:T(8,128)}, u32[]{:S(2)}) copy-start(s32[8,16,128]{2,1,0:T(8,128)} %param.7) | copy-start | bytes 196612
  0.7 6.5 %copy-start.1 = (s32[8,16,128]{2,1,0:T(8,128)S(1)}, s32[8,16,128]{2,1,0:T(8,128)}, u32[]{:S(2)}) copy-start(s32[8,16,128]{2,1,0:T(8,128)} %param.6) | copy-start | bytes 196612
  0.7 6.5 %copy-start = (f32[19,8,16,128]{3,2,1,0:T(8,128)S(1)}, f32[19,8,16,128]{3,2,1,0:T(8,128)}, u32[]{:S(2)}) copy-start(f32[19,8,16,128]{3,2,1,0:T(8,128)} %param.5) | copy-start | bytes 3735556
  0.7 6.5 %copy-start.4 = (f32[19]{0:T(128)S(1)}, f32[19]{0:T(128)}, u32[]{:S(2)}) copy-start(f32[19]{0:T(128)} %rate_ref.1) | copy-start | bytes 232
  1.9 6.9 %collective-permute-start = (f32[32,128]{1,0:T(8,128)S(1)}, f32[32,128]{1,0:T(8,128)S(1)}, u32[]{:S(2)}, u32[]{:S(2)}) collective-permute-start(f32[32,128]{1,0:T(8,128)S(1)} %get-tuple-element.95), channel_id=1, source_target_pairs={{0,4},{4,8},{8,12},{12,0},{1,5},{5,9},{9,13},{13,1},{2,6},{6,10},{... | collective-permute-start | bytes 49160 | tf_op jit(solution)/shard_map/ppermute | solution.py:644
  5.0 3.9 %collective-permute-start.1 = (f32[32,128]{1,0:T(8,128)S(1)}, f32[32,128]{1,0:T(8,128)S(1)}, u32[]{:S(2)}, u32[]{:S(2)}) collective-permute-start(f32[32,128]{1,0:T(8,128)S(1)} %get-tuple-element.96), channel_id=1, source_target_pairs={{4,0},{8,4},{12,8},{0,12},{5,1},{9,5},{13,9},{1,13},{6,2},{10,6},{... | collective-permute-start | bytes 49160 | tf_op jit(solution)/shard_map/ppermute | solution.py:645
  9.0 3.2 %collective-permute-start.2 = (f32[24,128]{1,0:T(8,128)S(1)}, f32[24,128]{1,0:T(8,128)S(1)}, u32[]{:S(2)}, u32[]{:S(2)}) collective-permute-start(f32[24,128]{1,0:T(8,128)S(1)} %get-tuple-element.98), channel_id=1, source_target_pairs={{0,1},{1,2},{2,3},{3,0},{4,5},{5,6},{6,7},{7,4},{8,9},{9,10},{10,1... | collective-permute-start | bytes 36872 | tf_op jit(solution)/shard_map/ppermute | solution.py:644
  9.0 3.1 %collective-permute-start.3 = (f32[24,128]{1,0:T(8,128)S(1)}, f32[24,128]{1,0:T(8,128)S(1)}, u32[]{:S(2)}, u32[]{:S(2)}) collective-permute-start(f32[24,128]{1,0:T(8,128)S(1)} %get-tuple-element.99), channel_id=1, source_target_pairs={{1,0},{2,1},{3,2},{0,3},{5,4},{6,5},{7,6},{4,7},{9,8},{10,9},{11,1... | collective-permute-start | bytes 36872 | tf_op jit(solution)/shard_map/ppermute | solution.py:645
  12.6 2.7 %collective-permute-start.4 = (f32[56,128]{1,0:T(8,128)S(1)}, f32[56,128]{1,0:T(8,128)S(1)}, u32[]{:S(2)}, u32[]{:S(2)}) collective-permute-start(f32[56,128]{1,0:T(8,128)S(1)} %get-tuple-element.114), channel_id=1, source_target_pairs={{0,1},{1,0},{2,3},{3,2},{4,5},{5,4},{6,7},{7,6},{8,9},{9,8},{10,11... | collective-permute-start | bytes 86024 | tf_op jit(solution)/shard_map/ppermute | solution.py:656
  14.3 3.3 %collective-permute-start.5 = (f32[56,128]{1,0:T(8,128)S(1)}, f32[56,128]{1,0:T(8,128)S(1)}, u32[]{:S(2)}, u32[]{:S(2)}) collective-permute-start(f32[56,128]{1,0:T(8,128)S(1)} %get-tuple-element.115), channel_id=1, source_target_pairs={{0,3},{1,2},{2,1},{3,0},{4,7},{5,6},{6,5},{7,4},{8,11},{9,10},{10,... | collective-permute-start | bytes 86024 | tf_op jit(solution)/shard_map/ppermute | solution.py:655
  17.6 6.1 %collective-permute-start.6 = (f32[104,128]{1,0:T(8,128)S(1)}, f32[104,128]{1,0:T(8,128)S(1)}, u32[]{:S(2)}, u32[]{:S(2)}) collective-permute-start(f32[104,128]{1,0:T(8,128)S(1)} %get-tuple-element.120.refs_17_), channel_id=1, source_target_pairs={{0,4},{4,8},{8,12},{12,0},{1,5},{5,9},{9,13},{13,1},{2,6},{6,10},{... | collective-permute-start | bytes 159752 | tf_op jit(solution)/shard_map/ppermute | solution.py:644
  19.0 5.2 %collective-permute-start.7 = (f32[104,128]{1,0:T(8,128)S(1)}, f32[104,128]{1,0:T(8,128)S(1)}, u32[]{:S(2)}, u32[]{:S(2)}) collective-permute-start(f32[104,128]{1,0:T(8,128)S(1)} %get-tuple-element.121.refs_18_), channel_id=1, source_target_pairs={{4,0},{8,4},{12,8},{0,12},{5,1},{9,5},{13,9},{1,13},{6,2},{10,6},{... | collective-permute-start | bytes 159752 | tf_op jit(solution)/shard_map/ppermute | solution.py:645
  24.6 1.5 %collective-permute-start.8 = (f32[56,128]{1,0:T(8,128)S(1)}, f32[56,128]{1,0:T(8,128)S(1)}, u32[]{:S(2)}, u32[]{:S(2)}) collective-permute-start(f32[56,128]{1,0:T(8,128)S(1)} %get-tuple-element.130), channel_id=1, source_target_pairs={{0,1},{1,0},{2,3},{3,2},{4,5},{5,4},{6,7},{7,6},{8,9},{9,8},{10,11... | collective-permute-start | bytes 86024 | tf_op jit(solution)/shard_map/ppermute | solution.py:656
  24.7 3.4 %collective-permute-start.9 = (f32[56,128]{1,0:T(8,128)S(1)}, f32[56,128]{1,0:T(8,128)S(1)}, u32[]{:S(2)}, u32[]{:S(2)}) collective-permute-start(f32[56,128]{1,0:T(8,128)S(1)} %get-tuple-element.131), channel_id=1, source_target_pairs={{0,3},{1,2},{2,1},{3,0},{4,7},{5,6},{6,5},{7,4},{8,11},{9,10},{10,... | collective-permute-start | bytes 86024 | tf_op jit(solution)/shard_map/ppermute | solution.py:655
  28.1 6.1 %collective-permute-start.10 = (f32[104,128]{1,0:T(8,128)S(1)}, f32[104,128]{1,0:T(8,128)S(1)}, u32[]{:S(2)}, u32[]{:S(2)}) collective-permute-start(f32[104,128]{1,0:T(8,128)S(1)} %get-tuple-element.136.refs_17_), channel_id=1, source_target_pairs={{0,4},{4,8},{8,12},{12,0},{1,5},{5,9},{9,13},{13,1},{2,6},{6,10},{... | collective-permute-start | bytes 159752 | tf_op jit(solution)/shard_map/ppermute | solution.py:644
  29.2 5.3 %collective-permute-start.11 = (f32[104,128]{1,0:T(8,128)S(1)}, f32[104,128]{1,0:T(8,128)S(1)}, u32[]{:S(2)}, u32[]{:S(2)}) collective-permute-start(f32[104,128]{1,0:T(8,128)S(1)} %get-tuple-element.137.refs_18_), channel_id=1, source_target_pairs={{4,0},{8,4},{12,8},{0,12},{5,1},{9,5},{13,9},{1,13},{6,2},{10,6},{... | collective-permute-start | bytes 159752 | tf_op jit(solution)/shard_map/ppermute | solution.py:645
  34.9 1.4 %collective-permute-start.12 = (f32[56,128]{1,0:T(8,128)S(1)}, f32[56,128]{1,0:T(8,128)S(1)}, u32[]{:S(2)}, u32[]{:S(2)}) collective-permute-start(f32[56,128]{1,0:T(8,128)S(1)} %get-tuple-element.146), channel_id=1, source_target_pairs={{0,1},{1,0},{2,3},{3,2},{4,5},{5,4},{6,7},{7,6},{8,9},{9,8},{10,11... | collective-permute-start | bytes 86024 | tf_op jit(solution)/shard_map/ppermute | solution.py:656
  35.0 3.4 %collective-permute-start.13 = (f32[56,128]{1,0:T(8,128)S(1)}, f32[56,128]{1,0:T(8,128)S(1)}, u32[]{:S(2)}, u32[]{:S(2)}) collective-permute-start(f32[56,128]{1,0:T(8,128)S(1)} %get-tuple-element.147), channel_id=1, source_target_pairs={{0,3},{1,2},{2,1},{3,0},{4,7},{5,6},{6,5},{7,4},{8,11},{9,10},{10,... | collective-permute-start | bytes 86024 | tf_op jit(solution)/shard_map/ppermute | solution.py:655
  38.4 6.1 %collective-permute-start.14 = (f32[104,128]{1,0:T(8,128)S(1)}, f32[104,128]{1,0:T(8,128)S(1)}, u32[]{:S(2)}, u32[]{:S(2)}) collective-permute-start(f32[104,128]{1,0:T(8,128)S(1)} %get-tuple-element.152.refs_17_), channel_id=1, source_target_pairs={{0,4},{4,8},{8,12},{12,0},{1,5},{5,9},{9,13},{13,1},{2,6},{6,10},{... | collective-permute-start | bytes 159752 | tf_op jit(solution)/shard_map/ppermute | solution.py:644
  39.7 5.3 %collective-permute-start.15 = (f32[104,128]{1,0:T(8,128)S(1)}, f32[104,128]{1,0:T(8,128)S(1)}, u32[]{:S(2)}, u32[]{:S(2)}) collective-permute-start(f32[104,128]{1,0:T(8,128)S(1)} %get-tuple-element.153.refs_18_), channel_id=1, source_target_pairs={{4,0},{8,4},{12,8},{0,12},{5,1},{9,5},{13,9},{1,13},{6,2},{10,6},{... | collective-permute-start | bytes 159752 | tf_op jit(solution)/shard_map/ppermute | solution.py:645
  45.4 1.5 %collective-permute-start.16 = (f32[48,128]{1,0:T(8,128)S(1)}, f32[48,128]{1,0:T(8,128)S(1)}, u32[]{:S(2)}, u32[]{:S(2)}) collective-permute-start(f32[48,128]{1,0:T(8,128)S(1)} %get-tuple-element.161), channel_id=1, source_target_pairs={{0,1},{1,0},{2,3},{3,2},{4,5},{5,4},{6,7},{7,6},{8,9},{9,8},{10,11... | collective-permute-start | bytes 73736 | tf_op jit(solution)/shard_map/ppermute | solution.py:656
  45.4 3.3 %collective-permute-start.17 = (f32[48,128]{1,0:T(8,128)S(1)}, f32[48,128]{1,0:T(8,128)S(1)}, u32[]{:S(2)}, u32[]{:S(2)}) collective-permute-start(f32[48,128]{1,0:T(8,128)S(1)} %get-tuple-element.162), channel_id=1, source_target_pairs={{0,3},{1,2},{2,1},{3,0},{4,7},{5,6},{6,5},{7,4},{8,11},{9,10},{10,... | collective-permute-start | bytes 73736 | tf_op jit(solution)/shard_map/ppermute | solution.py:655
  48.8 5.9 %collective-permute-start.18 = (f32[80,128]{1,0:T(8,128)S(1)}, f32[80,128]{1,0:T(8,128)S(1)}, u32[]{:S(2)}, u32[]{:S(2)}) collective-permute-start(f32[80,128]{1,0:T(8,128)S(1)} %get-tuple-element.171), channel_id=1, source_target_pairs={{0,4},{4,8},{8,12},{12,0},{1,5},{5,9},{9,13},{13,1},{2,6},{6,10},{... | collective-permute-start | bytes 122888 | tf_op jit(solution)/shard_map/ppermute | solution.py:644
  50.0 4.9 %collective-permute-start.19 = (f32[80,128]{1,0:T(8,128)S(1)}, f32[80,128]{1,0:T(8,128)S(1)}, u32[]{:S(2)}, u32[]{:S(2)}) collective-permute-start(f32[80,128]{1,0:T(8,128)S(1)} %get-tuple-element.172), channel_id=1, source_target_pairs={{4,0},{8,4},{12,8},{0,12},{5,1},{9,5},{13,9},{1,13},{6,2},{10,6},{... | collective-permute-start | bytes 122888 | tf_op jit(solution)/shard_map/ppermute | solution.py:645
